TPU v7x, 256 devices: a whole 4x4x8 slice. The times are simulated.
256 devices in a mesh: tm: 32 (over x, y, core), sky: 8 (over z).
Axes of the slice: x: 4, y: 4, z: 8, core: 2. Of those that a mesh axis runs over, the one named last changes fastest.
Arguments:
- residuals: bfloat16 [128, 512, 2048], P('tm', None, 'sky')
- seg_counts: int32 [128], P('tm'), may hold values from 256 to 512, as said below
- attitude: bfloat16 [128, 512, 512], P('tm', 'sky')
- sched_seg: int32 [2048, 256], P(('tm', 'sky')), may hold values from 0 to 127, as said below
- sched_slot: int32 [2048, 256], P(('tm', 'sky')), may hold values from 0 to 511, as said below
- periods: int32 [1024], replicated, may hold values from 16 to 16383
Outputs:
- cleaned: float32 [128, 512, 2048], P('tm', None, 'sky')
- log_evidence: float32 [2048, 128], P(('tm', 'sky'))
Inputs may be any that keep to these rules, and one draw needn't show every extreme that they name: `seg_counts`: every segment has between 256 and 512 observed slots; some segment has all 512. `sched_seg`: in each aligned block of 8 rows (the plans of one device) at most 128 entries fall in the segments of one index of tm, and in every block some index receives exactly 128. `sched_slot`: each slot is below the observed count of its segment.
All inputs are finite; a program needn't handle non-finite values.
Results may differ from a plain program's by a relative error of at most 0.035.
Values may be sent and summed in bfloat16 or wider, within the bound.
A program may use at most 128 MiB of HBM per device.

v0:
```python
import jax
import jax.numpy as jnp
from jax import lax
from jax.sharding import PartitionSpec as P

SRC_GROUP = 128
ITERS = 2


TWO_PI = 6.283185307179586
BETA = 2.0
RIDGE = 1.0


def make_basis(times, periods):
    period_float = periods.astype(jnp.float32)
    phase = (times[..., None] % periods).astype(jnp.float32) * (TWO_PI / period_float)
    return jnp.concatenate([jnp.cos(phase), jnp.sin(phase)], axis=-1).astype(jnp.bfloat16)


def fit_groups(basis, observed, norm_cos, norm_sin, nper):
    corr = jnp.einsum("fio,fic->foc", basis, observed, preferred_element_type=jnp.float32)
    cosine = corr[:, :nper]
    sine = corr[:, nper:]
    amp_c = cosine / norm_cos[:, :, None]
    amp_s = sine / norm_sin[:, :, None]
    power = cosine * amp_c + sine * amp_s
    logits = BETA * power
    highest = jnp.max(logits, axis=1)
    expo = jnp.exp(logits - highest[:, None, :])
    total = jnp.sum(expo, axis=1)
    share = expo / total[:, None, :]
    coeff = jnp.concatenate([share * amp_c, share * amp_s], axis=1).astype(jnp.bfloat16)
    model = jnp.einsum("fio,foc->fic", basis, coeff, preferred_element_type=jnp.float32)
    return (model, highest + jnp.log(total))


def on_device(residuals, seg_counts, attitude, sched_seg, sched_slot, periods):
    tm_count = lax.axis_size("tm")
    sched_dev, obs = sched_seg.shape
    seg_dev, slots, width = residuals.shape
    nper = periods.shape[0]
    column_blocks = width // SRC_GROUP
    capacity = 2 * sched_dev * obs // tm_count
    requests = sched_dev * obs
    seg_flat = sched_seg.reshape(-1)
    slot_flat = sched_slot.reshape(-1)
    block_of = jnp.repeat(jnp.arange(sched_dev, dtype=jnp.int32) % column_blocks, obs)
    target = seg_flat // seg_dev
    local_row = (seg_flat % seg_dev * slots + slot_flat) * column_blocks + block_of
    onehot = (target[:, None] == jnp.arange(tm_count, dtype=jnp.int32)[None, :]).astype(jnp.int32)
    position = jnp.sum(jnp.cumsum(onehot, axis=0) * onehot, axis=1) - 1
    empty_row = seg_dev * slots * column_blocks
    wanted = (
        jnp.full((tm_count, capacity), empty_row, jnp.int32).at[target, position].set(local_row)
    )
    asked = lax.all_to_all(wanted, "tm", split_axis=0, concat_axis=0, tiled=True)
    basis = make_basis(sched_seg * slots + sched_slot, periods)
    squares = basis.astype(jnp.float32) ** 2
    norm_cos = jnp.sum(squares[:, :, :nper], axis=1) + RIDGE
    norm_sin = jnp.sum(squares[:, :, nper:], axis=1) + RIDGE
    valid = jnp.arange(slots, dtype=jnp.int32)[None, :] < seg_counts[:, None]
    current = residuals.astype(jnp.float32)
    evidence = jnp.zeros((sched_dev, SRC_GROUP), jnp.float32)
    for iteration in range(ITERS):
        masked = jnp.where(valid[:, :, None], current, 0.0).astype(jnp.bfloat16)
        white = jnp.einsum(
            "sij,sjc->sic",
            lax.all_gather(attitude, "sky", axis=1, tiled=True),
            masked,
            preferred_element_type=jnp.float32,
        ).astype(jnp.bfloat16)
        flat = white.reshape(-1, SRC_GROUP)
        picked = jnp.take(flat, asked, axis=0, mode="fill", fill_value=0)
        arrived = lax.all_to_all(picked, "tm", split_axis=0, concat_axis=0, tiled=True)
        observed = arrived[target, position].reshape(sched_dev, obs, SRC_GROUP)
        model, evidence = fit_groups(basis, observed, norm_cos, norm_sin, nper)
        outgoing = (
            jnp.zeros((tm_count, capacity, SRC_GROUP), jnp.float32)
            .at[target, position]
            .set(model.reshape(requests, SRC_GROUP))
        )
        returned = lax.all_to_all(outgoing, "tm", split_axis=0, concat_axis=0, tiled=True)
        placed = (
            jnp.zeros((empty_row, SRC_GROUP), jnp.float32)
            .at[asked.reshape(-1)]
            .add(returned.reshape(-1, SRC_GROUP), mode="drop")
        )
        current = current - placed.reshape(seg_dev, slots, width)
    return (current, evidence)


def solution(mesh):
    in_specs = (
        P("tm", None, "sky"),
        P("tm"),
        P("tm", "sky", None),
        P(("tm", "sky"), None),
        P(("tm", "sky"), None),
        P(),
    )
    out_specs = (P("tm", None, "sky"), P(("tm", "sky"), None))
    return jax.shard_map(
        on_device, mesh=mesh, in_specs=in_specs, out_specs=out_specs, check_vma=False
    )
```

profile of v0, /device:TPU:1, one launch (start us, length us, event | category | flops | bytes accessed | tf_op | source)
XLA Modules:
  0.0 466.6 jit_solution(18162760085475107118)
XLA Ops:
  7.2 0.7 all-gather.2.cloned.1.call-update
  7.9 0.7 reshape.255
  8.6 0.7 copy.33
  9.4 9.1 %reduce-window.6 = s32[32,16,128]{2,1,0:T(8,128)S(1)} reduce-window(s32[32,16,128]{2,1,0:T(8,128)S(1)} %fusion.40, s32[]{:T(128)} %constant.78.clone.1), window={size=1x1x128 pad=0_0x0_0x127_0}, to_apply=%region_0.1 | reduce-window | flops 8323072 | bytes 524292 | tf_op jit(solution)/shard_map/reduce-window
  19.2 0.7 copy.36
  19.9 0.7 copy.34
  20.9 0.7 multiply_reduce_fusion
  21.6 0.8 and_reduce_fusion
  22.4 8.6 %scatter_custom_fusion.2 = s32[4096]{0:T(1024)} fusion(s32[2048]{0:T(1024)S(1)} %broadcast_select_fusion.2, s32[2048]{0:T(1024)S(1)} %get-tuple-element.16, s32[]{:T(128)} %constant.76.clone.1), kind=kCustom, calls=%fused_computation.111 | custom fusion | bytes 16388
  31.0 9.0 %all-to-all-start = ((s32[32,1,128]{2,1,0:T(1,128)}), s32[32,1,128]{2,1,0:T(1,128)S(1)}, u32[]{:S(2)}, u32[]{:S(2)}) async-start(s32[32,1,128]{2,1,0:T(1,128)} %bitcast.5), calls=%async_computation | async-start | bytes 32768 | tf_op jit(solution)/shard_map/all_to_all | solution.py:57
  40.0 0.7 broadcast_compare_fusion
  40.7 0.7 convert_divide_fusion
  41.4 0.7 compare_select_fusion.7
  42.1 0.7 multiply_add_fusion
  42.8 112.5 %fusion.6 = (bf16[8,256,1024]{1,2,0:T(8,128)(2,1)}, bf16[8,256,1024]{1,2,0:T(8,128)(2,1)}) fusion(f32[1024]{0:T(1024)S(1)} %convert_divide_fusion, s32[1024]{0:T(1024)S(1)} %compare_select_fusion.7, s32[8,256]{1,0:T(8,128)S(1)} %multiply_add_fusion, pred[1024]{0:T(1024)(128)(4,1)S(1)} %broadcast_compare_fusion), kind=kLoop, calls=%fused_computation.20 | loop fusion | flops 23068672 | bytes 8406016 | tf_op jit(solution)/shard_map/convert.4
  155.4 2.7 fusion.23
  159.1 12.1 %gather_fusion.2 = bf16[4096,128]{1,0:T(8,128)(2,1)S(1)} fusion(bf16[4096,128]{1,0:T(8,128)(2,1)S(1)} %reshape.260, s32[4096]{0:T(1024)S(1)} %bitcast_clamp_fusion), kind=kCustom, calls=%fused_computation.clone | custom fusion | bytes 2113536 | tf_op jit(solution)/shard_map/jit(_take)/gather | solution.py:74
  171.3 1.5 broadcast_select_fusion.1
  172.8 8.0 %all-to-all-start.1 = ((bf16[32,128,128]{2,1,0:T(8,128)(2,1)}), bf16[32,128,128]{2,1,0:T(8,128)(2,1)S(1)}, u32[]{:S(2)}, u32[]{:S(2)}) async-start(bf16[32,128,128]{2,1,0:T(8,128)(2,1)} %broadcast_select_fusion.1), calls=%async_computation.1 | async-start | bytes 2097152 | tf_op jit(solution)/shard_map/all_to_all | solution.py:75
  180.8 10.8 %convert_multiply_fusion = f32[8,256,2048]{1,2,0:T(8,128)} fusion(bf16[8,256,1024]{1,2,0:T(8,128)(2,1)} %get-tuple-element.15, bf16[8,256,1024]{1,2,0:T(8,128)(2,1)} %get-tuple-element.14), kind=kLoop, calls=%fused_computation.15 | loop fusion | flops 20971520 | bytes 25165824 | tf_op jit(solution)/shard_map/integer_pow | solution.py:59
  191.5 7.0 %slice_reduce_fusion.1 = (f32[8,1024]{1,0:T(8,128)S(1)}, f32[8,1024]{1,0:T(8,128)S(1)}) fusion(f32[8,256,2048]{1,2,0:T(8,128)} %convert_multiply_fusion), kind=kLoop, calls=%fused_computation.23 | loop fusion | flops 4177920 | bytes 16842752 | tf_op jit(solution)/shard_map/reduce_sum | solution.py:60
  198.6 11.1 %gather_fusion = bf16[2048,128]{1,0:T(8,128)(2,1)S(1)} fusion(bf16[32,128,128]{2,1,0:T(8,128)(2,1)S(1)} %all-to-all-done.1, s32[2048]{0:T(1024)S(1)} %bitcast.56), kind=kCustom, calls=%fused_computation.2 | custom fusion | bytes 1064960 | tf_op jit(solution)/shard_map/gather | solution.py:76
  209.7 9.0 %fusion.57 = f32[8,2048,128]{2,1,0:T(8,128)} fusion(bf16[8,256,128]{2,1,0:T(8,128)(2,1)S(1)} %bitcast.64, bf16[8,256,1024]{1,2,0:T(8,128)(2,1)} %get-tuple-element.15, bf16[8,256,1024]{1,2,0:T(8,128)(2,1)} %get-tuple-element.14), kind=kOutput, calls=%fused_computation.134 | convolution fusion | flops 1090519040 | bytes 17301504 | tf_op jit(solution)/shard_map/fio,fic->foc/dot_general | solution.py:22
  218.8 10.1 %multiply_convert_fusion.3 = (bf16[8,1024,128]{2,1,0:T(8,128)(2,1)}, bf16[8,1024,128]{2,1,0:T(8,128)(2,1)}) fusion(f32[8,1024]{1,0:T(8,128)S(1)} %get-tuple-element.21, f32[8,2048,128]{2,1,0:T(8,128)} %fusion.57, f32[8,1024]{1,0:T(8,128)S(1)} %get-tuple-element.20), kind=kOutput, calls=%fused_computation.40 | output fusion | flops 14684158 | bytes 21102592 | tf_op jit(solution)/shard_map/div | solution.py:32
  228.8 6.2 %fusion.10 = f32[8,256,128]{2,1,0:T(8,128)S(1)} fusion(bf16[8,1024,128]{2,1,0:T(8,128)(2,1)} %get-tuple-element.13, bf16[8,1024,128]{2,1,0:T(8,128)(2,1)} %get-tuple-element.12, bf16[8,256,1024]{1,2,0:T(8,128)(2,1)} %get-tuple-element.15, bf16[8,256,1024]{1,2,0:T(8,128)(2,1)} %get-tuple-element.14), kind=kOutput, calls=%fused_computation.27 | convolution fusion | flops 1098907648 | bytes 13631488 | tf_op jit(solution)/shard_map/fio,foc->fic/dot_general | solution.py:34
  235.0 7.0 %scatter_custom_fusion.3 = f32[4096,128]{1,0:T(8,128)} fusion(s32[2048]{0:T(1024)S(1)} %broadcast_select_fusion.2, f32[2048,128]{1,0:T(8,128)S(1)} %bitcast.81, f32[]{:T(128)} %constant.49.clone.1), kind=kCustom, calls=%fused_computation.63 | custom fusion | bytes 2097156
  242.0 7.4 %all-to-all-start.2 = ((f32[32,128,128]{2,1,0:T(8,128)}), f32[32,128,128]{2,1,0:T(8,128)S(1)}, u32[]{:S(2)}, u32[]{:S(2)}) async-start(f32[32,128,128]{2,1,0:T(8,128)} %bitcast.15), calls=%async_computation.2 | async-start | bytes 4194304 | tf_op jit(solution)/shard_map/all_to_all | solution.py:83
  249.4 28.3 %all-to-all-done.2 = f32[32,128,128]{2,1,0:T(8,128)S(1)} async-done(((f32[32,128,128]{2,1,0:T(8,128)}), f32[32,128,128]{2,1,0:T(8,128)S(1)}, u32[]{:S(2)}, u32[]{:S(2)}) %all-to-all-start.2) | async-done | bytes 2097184 | tf_op jit(solution)/shard_map/all_to_all | solution.py:83
  277.7 23.9 %scatter_custom_fusion = f32[4096,128]{1,0:T(8,128)} fusion(s32[4096]{0:T(1024)S(1)} %bitcast.78, f32[4096,128]{1,0:T(8,128)S(1)} %bitcast.61, f32[]{:T(128)} %constant.49.clone.1), kind=kCustom, calls=%fused_computation.67 | custom fusion | flops 524288 | bytes 2097156 | tf_op jit(solution)/shard_map/scatter-add | solution.py:87
  301.6 1.9 reshape.264
  303.5 3.7 fusion.24
  307.2 2.3 copy.26
  309.5 1.4 reshape.265
  310.9 15.0 %gather_fusion.3 = bf16[4096,128]{1,0:T(8,128)(2,1)} fusion(bf16[4096,128]{1,0:T(8,128)(2,1)S(1)} %reshape.265, s32[4096]{0:T(1024)S(1)} %bitcast_clamp_fusion), kind=kCustom, calls=%fused_computation.1.clone | custom fusion | bytes 2113536 | tf_op jit(solution)/shard_map/jit(_take)/gather | solution.py:74
  326.0 1.8 broadcast_select_fusion
  327.7 20.6 %all_to_all.32 = bf16[32,128,128]{2,1,0:T(8,128)(2,1)S(1)} all-to-all(bf16[32,128,128]{2,1,0:T(8,128)(2,1)S(1)} %broadcast_select_fusion), channel_id=1, replica_groups=mesh['tm'=32,'sky'=8] {'tm'}, dimensions={0} | all-to-all | bytes 2097152 | tf_op jit(solution)/shard_map/all_to_all | solution.py:75
  348.3 20.5 %gather_fusion.1 = bf16[2048,128]{1,0:T(8,128)(2,1)} fusion(bf16[32,128,128]{2,1,0:T(8,128)(2,1)S(1)} %all_to_all.32, s32[2048]{0:T(1024)S(1)} %bitcast.57), kind=kCustom, calls=%fused_computation.3 | custom fusion | bytes 1064960 | tf_op jit(solution)/shard_map/gather | solution.py:76
  368.8 5.8 %fusion.56 = f32[8,2048,128]{2,1,0:T(8,128)S(1)} fusion(bf16[8,256,128]{2,1,0:T(8,128)(2,1)} %bitcast.63, bf16[8,256,1024]{1,2,0:T(8,128)(2,1)} %get-tuple-element.15, bf16[8,256,1024]{1,2,0:T(8,128)(2,1)} %get-tuple-element.14), kind=kOutput, calls=%fused_computation.133 | convolution fusion | flops 1090519040 | bytes 17301504 | tf_op jit(solution)/shard_map/fio,fic->foc/dot_general | solution.py:22
  374.7 3.0 fusion.58
  378.2 4.7 %multiply_convert_fusion.1 = (bf16[8,1024,128]{2,1,0:T(8,128)(2,1)}, bf16[8,1024,128]{2,1,0:T(8,128)(2,1)}) fusion(f32[8,1024]{1,0:T(8,128)S(1)} %get-tuple-element.21, f32[8,2048,128]{2,1,0:T(8,128)S(1)} %fusion.56, f32[8,128]{1,0:T(8,128)S(1)} %fusion.19, f32[8,1024,128]{2,1,0:T(8,128)S(1)} %get-tuple-element.6, f32[8,128]{1,0:T(8,128)S(1)} %get-tuple-element.5, ...), kind=kLoop, calls=%fused_computation.36 | loop fusion | flops 8388608 | bytes 16850944 | tf_op jit(solution)/shard_map/convert
  382.9 6.1 %fusion.14 = f32[8,256,128]{2,1,0:T(8,128)S(1)} fusion(bf16[8,1024,128]{2,1,0:T(8,128)(2,1)} %get-tuple-element.11, bf16[8,1024,128]{2,1,0:T(8,128)(2,1)} %get-tuple-element.10, bf16[8,256,1024]{1,2,0:T(8,128)(2,1)} %get-tuple-element.15, bf16[8,256,1024]{1,2,0:T(8,128)(2,1)} %get-tuple-element.14), kind=kOutput, calls=%fused_computation.31 | convolution fusion | flops 1098907648 | bytes 13631488 | tf_op jit(solution)/shard_map/fio,foc->fic/dot_general | solution.py:34
  389.0 7.0 %scatter_custom_fusion.4 = f32[4096,128]{1,0:T(8,128)} fusion(s32[2048]{0:T(1024)S(1)} %broadcast_select_fusion.2, f32[2048,128]{1,0:T(8,128)S(1)} %bitcast.80, f32[]{:T(128)} %constant.49.clone.1), kind=kCustom, calls=%fused_computation.61 | custom fusion | bytes 2097156
  396.0 4.9 %all-to-all-start.4 = ((f32[32,128,128]{2,1,0:T(8,128)}), f32[32,128,128]{2,1,0:T(8,128)}, u32[]{:S(2)}, u32[]{:S(2)}) async-start(f32[32,128,128]{2,1,0:T(8,128)} %bitcast.58), calls=%async_computation.4 | async-start | bytes 4194304 | tf_op jit(solution)/shard_map/all_to_all | solution.py:83
  400.9 0.6 log_add_fusion
  401.5 27.6 %all-to-all-done.4 = f32[32,128,128]{2,1,0:T(8,128)} async-done(((f32[32,128,128]{2,1,0:T(8,128)}), f32[32,128,128]{2,1,0:T(8,128)}, u32[]{:S(2)}, u32[]{:S(2)}) %all-to-all-start.4) | async-done | bytes 2097184 | tf_op jit(solution)/shard_map/all_to_all | solution.py:83
  429.2 24.1 %scatter_custom_fusion.1 = f32[4096,128]{1,0:T(8,128)} fusion(s32[4096]{0:T(1024)S(1)} %bitcast.79, f32[4096,128]{1,0:T(8,128)} %bitcast.23, f32[]{:T(128)} %constant.49.clone.1), kind=kCustom, calls=%fused_computation.65 | custom fusion | flops 524288 | bytes 2097664 | tf_op jit(solution)/shard_map/scatter-add | solution.py:87
  453.2 2.9 reshape.269
  456.1 3.4 fusion.22
  (32 shorter events, 2.7 us)
Async XLA Ops:
  7.2 148.3 %all-gather.2.cloned.1.call-start = ((), (), s32[]{:S(2)}) async-start(), calls=%async_computation.5 | async-start | bytes 2359296 | tf_op jit(solution)/shard_map/all_gather | solution.py:69
  31.0 124.4 %all-to-all-start = ((s32[32,1,128]{2,1,0:T(1,128)}), s32[32,1,128]{2,1,0:T(1,128)S(1)}, u32[]{:S(2)}, u32[]{:S(2)}) async-start(s32[32,1,128]{2,1,0:T(1,128)} %bitcast.5), calls=%async_computation | async-start | bytes 32768 | tf_op jit(solution)/shard_map/all_to_all | solution.py:57
  42.8 112.5 %copy-start.2 = (s32[4]{0:T(128)S(1)}, s32[4]{0:T(128)}, u32[]{:S(2)}) copy-start(s32[4]{0:T(128)} %param.9) | copy-start | bytes 52
  42.8 112.6 %copy-start = (bf16[4,512,256]{2,1,0:T(8,128)(2,1)S(1)}, bf16[4,512,256]{2,1,0:T(8,128)(2,1)}, u32[]{:S(2)}) copy-start(bf16[4,512,256]{2,1,0:T(8,128)(2,1)} %param.8) | copy-start | bytes 3145732
  172.8 25.8 %all-to-all-start.1 = ((bf16[32,128,128]{2,1,0:T(8,128)(2,1)}), bf16[32,128,128]{2,1,0:T(8,128)(2,1)S(1)}, u32[]{:S(2)}, u32[]{:S(2)}) async-start(bf16[32,128,128]{2,1,0:T(8,128)(2,1)} %broadcast_select_fusion.1), calls=%async_computation.1 | async-start | bytes 2097152 | tf_op jit(solution)/shard_map/all_to_all | solution.py:75
  242.0 35.7 %all-to-all-start.2 = ((f32[32,128,128]{2,1,0:T(8,128)}), f32[32,128,128]{2,1,0:T(8,128)S(1)}, u32[]{:S(2)}, u32[]{:S(2)}) async-start(f32[32,128,128]{2,1,0:T(8,128)} %bitcast.15), calls=%async_computation.2 | async-start | bytes 4194304 | tf_op jit(solution)/shard_map/all_to_all | solution.py:83
  396.0 33.1 %all-to-all-start.4 = ((f32[32,128,128]{2,1,0:T(8,128)}), f32[32,128,128]{2,1,0:T(8,128)}, u32[]{:S(2)}, u32[]{:S(2)}) async-start(f32[32,128,128]{2,1,0:T(8,128)} %bitcast.58), calls=%async_computation.4 | async-start | bytes 4194304 | tf_op jit(solution)/shard_map/all_to_all | solution.py:83
  400.9 55.2 %copy-start.1 = (bf16[4,512,256]{2,1,0:T(8,128)(2,1)S(1)}, bf16[4,512,256]{2,1,0:T(8,128)(2,1)}, u32[]{:S(2)}) copy-start(bf16[4,512,256]{2,1,0:T(8,128)(2,1)} %param.8) | copy-start | bytes 3145732
Sparse Core Ops, SparseCore 0:
  9.8 40.9 all-gather.1
where the time goes:
time: 470 us; the launch traced here: 467 us
  other arithmetic  218 us (46%)
  local copies, waits for them, and re-layouts  94.1 us (20%)
  waiting for transfers between devices  56.6 us (12%)
  matrix products  33.6 us (7%)
  starting transfers between devices  29.3 us (6%)
  blocking collectives  20.6 us (4%)
  between operations  14.5 us (3%)
    another operation x5, other arithmetic  127 us
    all_to_all x2, waiting for transfers between devices, on_device(): lax.all_to_all(outgoing, 'tm', split_axis=0, concat_axis=0, tiled=True)  55.9 us
    scatter-add x2, other arithmetic, on_device(): placed = jnp.zeros((empty_row, SRC_GROUP), jnp.float32).at[asked.reshape(...  48 us
    gather x2, local copies, waits for them, and re-layouts, on_device(): observed = arrived[target, position].reshape(sched_dev, obs, SRC_GROUP)  31.7 us
    gather x2, local copies, waits for them, and re-layouts, on_device(): picked = jnp.take(flat, asked, axis=0, mode='fill', fill_value=0)  27.2 us
    unnamed x14, local copies, waits for them, and re-layouts  24.8 us
    all_to_all x1, blocking collectives, on_device(): lax.all_to_all(picked, 'tm', split_axis=0, concat_axis=0, tiled=True)  20.6 us
    dot_general x2, matrix products, fit_groups(): jnp.einsum('fio,fic->foc', basis, observed, preferred_element_type=jnp.fl...  14.9 us
  transfers between devices with their start and end apart: 5, of which 2 were waited for; matrix products, arithmetic and copies ran while one was open for 34% of the time, Pallas kernels for 0%

commit v1 on v0

--- a/solution.py
+++ b/solution.py
@@ -1,6 +1,7 @@
 import jax
 import jax.numpy as jnp
 from jax import lax
+from jax.experimental import pallas as pl
 from jax.sharding import PartitionSpec as P
 
 SRC_GROUP = 128
@@ -12,10 +13,85 @@
 RIDGE = 1.0
 
 
-def make_basis(times, periods):
-    period_float = periods.astype(jnp.float32)
-    phase = (times[..., None] % periods).astype(jnp.float32) * (TWO_PI / period_float)
-    return jnp.concatenate([jnp.cos(phase), jnp.sin(phase)], axis=-1).astype(jnp.bfloat16)
+PIO2_1 = 1.5703125
+PIO2_2 = 4.837512969970703125e-4
+PIO2_3 = 7.549789954891e-8
+ROWS = 16
+LANES = 128
+
+
+def basis_kernel(t_ref, p_ref, w_ref, inv_ref, basis_ref, nc_ref, ns_ref):
+    obs = t_ref.shape[0]
+    nper = p_ref.shape[1]
+
+    def lane_block(j, carry):
+        c0 = pl.multiple_of(j * LANES, LANES)
+        pf = p_ref[:, pl.ds(c0, LANES)]
+        w = w_ref[:, pl.ds(c0, LANES)]
+        inv = inv_ref[:, pl.ds(c0, LANES)]
+
+        def row_block(i, acc):
+            acc_c, acc_s = acc
+            r0 = pl.multiple_of(i * ROWS, ROWS)
+            tf = jnp.broadcast_to(t_ref[pl.ds(r0, ROWS), :], (ROWS, LANES))
+            q = jnp.floor(tf * inv)
+            r = tf - q * pf
+            r = jnp.where(r < 0.0, r + pf, r)
+            r = jnp.where(r >= pf, r - pf, r)
+            phase = r * w
+            k = jnp.floor(phase * 0.6366197723675814 + 0.5)
+            y = ((phase - k * PIO2_1) - k * PIO2_2) - k * PIO2_3
+            z = y * y
+            s = y + y * z * (-1.6666654611e-1 + z * (8.3321608736e-3 + z * -1.9515295891e-4))
+            c = 1.0 - 0.5 * z + z * z * (4.166664568298827e-2 + z * (-1.388731625493765e-3 + z * 2.443315711809948e-5))
+            odd = (k == 1.0) | (k == 3.0)
+            cs = jnp.where(odd, s, c)
+            sn = jnp.where(odd, c, s)
+            cos_v = jnp.where((k == 1.0) | (k == 2.0), -cs, cs).astype(jnp.bfloat16)
+            sin_v = jnp.where((k == 2.0) | (k == 3.0), -sn, sn).astype(jnp.bfloat16)
+            basis_ref[pl.ds(r0, ROWS), pl.ds(c0, LANES)] = cos_v
+            basis_ref[pl.ds(r0, ROWS), pl.ds(nper + c0, LANES)] = sin_v
+            cf = cos_v.astype(jnp.float32)
+            sf = sin_v.astype(jnp.float32)
+            return acc_c + cf * cf, acc_s + sf * sf
+
+        zero = jnp.zeros((ROWS, LANES), jnp.float32)
+        acc_c, acc_s = lax.fori_loop(0, obs // ROWS, row_block, (zero, zero))
+        nc_ref[:, pl.ds(c0, LANES)] = jnp.sum(acc_c, axis=0, keepdims=True) + RIDGE
+        ns_ref[:, pl.ds(c0, LANES)] = jnp.sum(acc_s, axis=0, keepdims=True) + RIDGE
+        return carry
+
+    lax.fori_loop(0, nper // LANES, lane_block, 0)
+
+
+def basis_and_norms(times, periods):
+    plans, obs = times.shape
+    nper = periods.shape[0]
+    pf = periods.astype(jnp.float32)
+    w = (TWO_PI / pf).reshape(1, nper)
+    inv = (1.0 / pf).reshape(1, nper)
+    pf = pf.reshape(1, nper)
+    tf = times.astype(jnp.float32).reshape(plans, obs, 1)
+    row = pl.BlockSpec((1, nper), lambda g: (0, 0))
+    basis, nc, ns = pl.pallas_call(
+        basis_kernel,
+        grid=(plans,),
+        in_specs=[pl.BlockSpec((None, obs, 1), lambda g: (g, 0, 0)), row, row, row],
+        out_specs=[
+            pl.BlockSpec((None, obs, 2 * nper), lambda g: (g, 0, 0)),
+            pl.BlockSpec((None, 1, nper), lambda g: (g, 0, 0)),
+            pl.BlockSpec((None, 1, nper), lambda g: (g, 0, 0)),
+        ],
+        out_shape=[
+            jax.ShapeDtypeStruct((plans, obs, 2 * nper), jnp.bfloat16),
+            jax.ShapeDtypeStruct((plans, 1, nper), jnp.float32),
+            jax.ShapeDtypeStruct((plans, 1, nper), jnp.float32),
+        ],
+        cost_estimate=pl.CostEstimate(
+            flops=60 * plans * obs * nper, transcendentals=0,
+            bytes_accessed=plans * obs * 2 * nper * 2),
+    )(tf, pf, w, inv)
+    return basis, nc.reshape(plans, nper), ns.reshape(plans, nper)
 
 
 def fit_groups(basis, observed, norm_cos, norm_sin, nper):
@@ -55,10 +131,7 @@
         jnp.full((tm_count, capacity), empty_row, jnp.int32).at[target, position].set(local_row)
     )
     asked = lax.all_to_all(wanted, "tm", split_axis=0, concat_axis=0, tiled=True)
-    basis = make_basis(sched_seg * slots + sched_slot, periods)
-    squares = basis.astype(jnp.float32) ** 2
-    norm_cos = jnp.sum(squares[:, :, :nper], axis=1) + RIDGE
-    norm_sin = jnp.sum(squares[:, :, nper:], axis=1) + RIDGE
+    basis, norm_cos, norm_sin = basis_and_norms(sched_seg * slots + sched_slot, periods)
     valid = jnp.arange(slots, dtype=jnp.int32)[None, :] < seg_counts[:, None]
     current = residuals.astype(jnp.float32)
     evidence = jnp.zeros((sched_dev, SRC_GROUP), jnp.float32)

time: 470 us -> 454 us (0.966)
  other arithmetic: 218 us -> 84.4 us
  Pallas kernels: 0 us -> 107 us
  waiting for transfers between devices: 56.6 us -> 66.9 us
    another operation x5 -> x4, other arithmetic: 127 us -> 12.5 us
    pallas_call x0 -> x1, Pallas kernels: none -> 107 us  [basis_and_norms(): pl.pallas_call(basis_kernel, grid=(plans,), in_specs=[pl.BlockSpec((None,...]
    integer_pow x1 -> x0, other arithmetic: 10.8 us -> none  [on_device(): squares = basis.astype(jnp.float32) ** 2]
    reduce_sum x1 -> x0, other arithmetic: 7.03 us -> none  [on_device(): norm_cos = jnp.sum(squares[:, :, :nper], axis=1) + RIDGE]
    all_to_all x1, waiting for transfers between devices: 0.01 us -> 6.14 us  [on_device(): lax.all_to_all(wanted, 'tm', split_axis=0, concat_axis=0, tiled=True)]
    unnamed x14 -> x23, local copies, waits for them, and re-layouts: 24.8 us -> 25.6 us
  transfers between devices with their start and end apart: 5 -> 5, of which waited for: 2 -> 4; matrix products, arithmetic and copies ran while one was open for 34% -> 6% of each run, Pallas kernels for 0% -> 24%
where the time goes in v1:
time: 454 us; the launch traced here: 453 us
  Pallas kernels  107 us (24%)
  local copies, waits for them, and re-layouts  96.3 us (21%)
  other arithmetic  84.4 us (19%)
  waiting for transfers between devices  66.9 us (15%)
  starting transfers between devices  32.2 us (7%)
  matrix products  31.1 us (7%)
  blocking collectives  20.6 us (5%)
  between operations  14.4 us (3%)
    pallas_call x1, Pallas kernels, basis_and_norms(): pl.pallas_call(basis_kernel, grid=(plans,), in_specs=[pl.BlockSpec((None,...  107 us
    all_to_all x2, waiting for transfers between devices, on_device(): lax.all_to_all(outgoing, 'tm', split_axis=0, concat_axis=0, tiled=True)  55.7 us
    scatter-add x2, other arithmetic, on_device(): placed = jnp.zeros((empty_row, SRC_GROUP), jnp.float32).at[asked.reshape(...  47.8 us
    gather x2, local copies, waits for them, and re-layouts, on_device(): observed = arrived[target, position].reshape(sched_dev, obs, SRC_GROUP)  31.7 us
    gather x2, local copies, waits for them, and re-layouts, on_device(): picked = jnp.take(flat, asked, axis=0, mode='fill', fill_value=0)  27.2 us
    unnamed x23, local copies, waits for them, and re-layouts  25.6 us
    all_to_all x1, blocking collectives, on_device(): lax.all_to_all(picked, 'tm', split_axis=0, concat_axis=0, tiled=True)  20.6 us
    dot_general x2, matrix products, fit_groups(): jnp.einsum('fio,fic->foc', basis, observed, preferred_element_type=jnp.fl...  15.5 us
  transfers between devices with their start and end apart: 5, of which 4 were waited for; matrix products, arithmetic and copies ran while one was open for 6% of the time, Pallas kernels for 24%

profile of v1, /device:TPU:1, one launch (start us, length us, event | category | flops | bytes accessed | tf_op | source)
XLA Modules:
  0.0 452.8 jit_solution(5504261765250947167)
XLA Ops:
  7.2 0.7 all-gather.2.cloned.1.call-update
  8.0 0.7 reshape.256
  8.7 0.7 copy.37
  9.4 0.7 copy.38
  10.1 0.7 copy.40
  10.8 9.1 %reduce-window.6 = s32[32,16,128]{2,1,0:T(8,128)S(1)} reduce-window(s32[32,16,128]{2,1,0:T(8,128)S(1)} %fusion.32, s32[]{:T(128)} %constant.72.clone.1), window={size=1x1x128 pad=0_0x0_0x127_0}, to_apply=%region_0.1 | reduce-window | flops 8323072 | bytes 524292 | tf_op jit(solution)/shard_map/reduce-window
  20.9 0.7 multiply_reduce_fusion
  21.6 0.8 and_reduce_fusion
  22.4 8.6 %scatter_custom_fusion.2 = s32[4096]{0:T(1024)} fusion(s32[2048]{0:T(1024)S(1)} %broadcast_select_fusion.2, s32[2048]{0:T(1024)S(1)} %get-tuple-element.18, s32[]{:T(128)} %constant.70.clone.1), kind=kCustom, calls=%fused_computation.94 | custom fusion | bytes 16388
  31.0 8.6 %all-to-all-start = ((s32[32,1,128]{2,1,0:T(1,128)}), s32[32,1,128]{2,1,0:T(1,128)S(1)}, u32[]{:S(2)}, u32[]{:S(2)}) async-start(s32[32,1,128]{2,1,0:T(1,128)} %bitcast.5), calls=%async_computation | async-start | bytes 32768 | tf_op jit(solution)/shard_map/all_to_all | solution.py:133
  39.6 0.7 iota_compare_fusion.2
  40.3 6.1 %all-to-all-done = s32[32,1,128]{2,1,0:T(1,128)S(1)} async-done(((s32[32,1,128]{2,1,0:T(1,128)}), s32[32,1,128]{2,1,0:T(1,128)S(1)}, u32[]{:S(2)}, u32[]{:S(2)}) %all-to-all-start) | async-done | bytes 16416 | tf_op jit(solution)/shard_map/all_to_all | solution.py:133
  46.5 4.4 all-gather.2.cloned.1.call-done
  50.9 3.1 fusion.15
  54.9 12.1 %gather_fusion.2 = bf16[4096,128]{1,0:T(8,128)(2,1)S(1)} fusion(bf16[4096,128]{1,0:T(8,128)(2,1)S(1)} %reshape.265, s32[4096]{0:T(1024)S(1)} %bitcast_clamp_fusion), kind=kCustom, calls=%fused_computation.clone | custom fusion | bytes 2113536 | tf_op jit(solution)/shard_map/jit(_take)/gather | solution.py:147
  67.1 1.6 broadcast_select_fusion.1
  68.6 11.4 %all-to-all-start.1 = ((bf16[32,128,128]{2,1,0:T(8,128)(2,1)}), bf16[32,128,128]{2,1,0:T(8,128)(2,1)S(1)}, u32[]{:S(2)}, u32[]{:S(2)}) async-start(bf16[32,128,128]{2,1,0:T(8,128)(2,1)} %broadcast_select_fusion.1), calls=%async_computation.1 | async-start | bytes 2097152 | tf_op jit(solution)/shard_map/all_to_all | solution.py:148
  80.7 1.3 copy.23.t_ref
  82.0 0.6 broadcast_divide_fusion
  82.6 106.8 %shard_map.77 = (bf16[8,256,2048]{2,1,0:T(8,128)(2,1)}, f32[8,1,1024]{2,1,0:T(1,128)}, f32[8,1,1024]{2,1,0:T(1,128)}) custom-call(f32[8,256,1]{2,1,0:T(8,128)} %copy.23.t_ref, f32[1,1024]{1,0:T(1,128)} %bitcast.98, f32[1,1024]{1,0:T(1,128)} %bitcast.97, f32[1,1024]{1,0:T(1,128)} %bitcast.96), custom_call_target="tpu_custom_call" | custom-call | flops 125829120 | bytes 8388608 | tf_op jit(solution)/shard_map/pallas_call | solution.py:76
  189.5 0.8 copy_bitcast_fusion
  190.3 11.1 %gather_fusion = bf16[2048,128]{1,0:T(8,128)(2,1)S(1)} fusion(bf16[32,128,128]{2,1,0:T(8,128)(2,1)S(1)} %all-to-all-done.1, s32[2048]{0:T(1024)S(1)} %bitcast.72), kind=kCustom, calls=%fused_computation.2 | custom fusion | bytes 1064960 | tf_op jit(solution)/shard_map/gather | solution.py:149
  201.4 9.4 %fusion.49 = f32[8,2048,128]{2,1,0:T(8,128)} fusion(bf16[8,256,2048]{2,1,0:T(8,128)(2,1)} %get-tuple-element.6, bf16[8,256,128]{2,1,0:T(8,128)(2,1)S(1)} %bitcast.80), kind=kOutput, calls=%fused_computation.117 | convolution fusion | flops 1073741824 | bytes 17301504 | tf_op jit(solution)/shard_map/fio,fic->foc/dot_general | solution.py:98
  210.7 9.5 %multiply_convert_fusion.3 = (bf16[8,1024,128]{2,1,0:T(8,128)(2,1)S(1)}, bf16[8,1024,128]{2,1,0:T(8,128)(2,1)}) fusion(f32[8,1024]{1,0:T(8,128)S(1)} %get-tuple-element.25, f32[8,2048,128]{2,1,0:T(8,128)} %fusion.49, f32[8,1024]{1,0:T(8,128)S(1)} %get-tuple-element.24), kind=kOutput, calls=%fused_computation.24 | output fusion | flops 14684158 | bytes 21102592 | tf_op jit(solution)/shard_map/div | solution.py:108
  220.3 6.4 %fusion.2 = f32[8,256,128]{2,1,0:T(8,128)S(1)} fusion(bf16[8,256,2048]{2,1,0:T(8,128)(2,1)} %get-tuple-element.6, bf16[8,1024,128]{2,1,0:T(8,128)(2,1)} %get-tuple-element.17, bf16[8,1024,128]{2,1,0:T(8,128)(2,1)S(1)} %get-tuple-element.16), kind=kOutput, calls=%fused_computation.11 | convolution fusion | flops 1082130432 | bytes 13631488 | tf_op jit(solution)/shard_map/fio,foc->fic/dot_general | solution.py:110
  226.7 7.0 %scatter_custom_fusion.3 = f32[4096,128]{1,0:T(8,128)} fusion(s32[2048]{0:T(1024)S(1)} %broadcast_select_fusion.2, f32[2048,128]{1,0:T(8,128)S(1)} %bitcast.102, f32[]{:T(128)} %constant.43.clone.1), kind=kCustom, calls=%fused_computation.47 | custom fusion | bytes 2097156
  233.7 7.4 %all-to-all-start.2 = ((f32[32,128,128]{2,1,0:T(8,128)}), f32[32,128,128]{2,1,0:T(8,128)S(1)}, u32[]{:S(2)}, u32[]{:S(2)}) async-start(f32[32,128,128]{2,1,0:T(8,128)} %bitcast.19), calls=%async_computation.2 | async-start | bytes 4194304 | tf_op jit(solution)/shard_map/all_to_all | solution.py:156
  241.1 28.3 %all-to-all-done.2 = f32[32,128,128]{2,1,0:T(8,128)S(1)} async-done(((f32[32,128,128]{2,1,0:T(8,128)}), f32[32,128,128]{2,1,0:T(8,128)S(1)}, u32[]{:S(2)}, u32[]{:S(2)}) %all-to-all-start.2) | async-done | bytes 2097184 | tf_op jit(solution)/shard_map/all_to_all | solution.py:156
  269.4 23.7 %scatter_custom_fusion = f32[4096,128]{1,0:T(8,128)} fusion(s32[4096]{0:T(1024)S(1)} %bitcast.99, f32[4096,128]{1,0:T(8,128)S(1)} %bitcast.79, f32[]{:T(128)} %constant.43.clone.1), kind=kCustom, calls=%fused_computation.51 | custom fusion | flops 524288 | bytes 2097156 | tf_op jit(solution)/shard_map/scatter-add | solution.py:160
  293.1 1.9 reshape.269
  295.0 3.7 fusion.16
  298.8 2.3 copy.28
  301.1 1.4 reshape.270
  302.5 15.0 %gather_fusion.3 = bf16[4096,128]{1,0:T(8,128)(2,1)} fusion(bf16[4096,128]{1,0:T(8,128)(2,1)S(1)} %reshape.270, s32[4096]{0:T(1024)S(1)} %bitcast_clamp_fusion), kind=kCustom, calls=%fused_computation.1.clone | custom fusion | bytes 2113536 | tf_op jit(solution)/shard_map/jit(_take)/gather | solution.py:147
  317.6 1.8 broadcast_select_fusion
  319.3 20.6 %all_to_all.32 = bf16[32,128,128]{2,1,0:T(8,128)(2,1)S(1)} all-to-all(bf16[32,128,128]{2,1,0:T(8,128)(2,1)S(1)} %broadcast_select_fusion), channel_id=1, replica_groups=mesh['tm'=32,'sky'=8] {'tm'}, dimensions={0} | all-to-all | bytes 2097152 | tf_op jit(solution)/shard_map/all_to_all | solution.py:148
  339.9 20.5 %gather_fusion.1 = bf16[2048,128]{1,0:T(8,128)(2,1)} fusion(bf16[32,128,128]{2,1,0:T(8,128)(2,1)S(1)} %all_to_all.32, s32[2048]{0:T(1024)S(1)} %bitcast.73), kind=kCustom, calls=%fused_computation.3 | custom fusion | bytes 1064960 | tf_op jit(solution)/shard_map/gather | solution.py:149
  360.4 6.2 %fusion.50 = f32[8,2048,128]{2,1,0:T(8,128)S(1)} fusion(bf16[8,256,2048]{2,1,0:T(8,128)(2,1)} %get-tuple-element.6, bf16[8,256,128]{2,1,0:T(8,128)(2,1)} %bitcast.81), kind=kOutput, calls=%fused_computation.118 | convolution fusion | flops 1073741824 | bytes 17301504 | tf_op jit(solution)/shard_map/fio,fic->foc/dot_general | solution.py:98
  366.6 3.0 fusion.48
  370.2 3.1 multiply_convert_fusion.1
  373.3 2.4 fusion.6
  375.7 7.0 %scatter_custom_fusion.4 = f32[4096,128]{1,0:T(8,128)} fusion(s32[2048]{0:T(1024)S(1)} %broadcast_select_fusion.2, f32[2048,128]{1,0:T(8,128)S(1)} %bitcast.101, f32[]{:T(128)} %constant.43.clone.1), kind=kCustom, calls=%fused_computation.45 | custom fusion | bytes 2097156
  382.7 4.8 %all-to-all-start.4 = ((f32[32,128,128]{2,1,0:T(8,128)}), f32[32,128,128]{2,1,0:T(8,128)}, u32[]{:S(2)}, u32[]{:S(2)}) async-start(f32[32,128,128]{2,1,0:T(8,128)} %bitcast.76), calls=%async_computation.4 | async-start | bytes 4194304 | tf_op jit(solution)/shard_map/all_to_all | solution.py:156
  387.5 0.6 log_add_fusion
  388.1 27.5 %all-to-all-done.4 = f32[32,128,128]{2,1,0:T(8,128)} async-done(((f32[32,128,128]{2,1,0:T(8,128)}), f32[32,128,128]{2,1,0:T(8,128)}, u32[]{:S(2)}, u32[]{:S(2)}) %all-to-all-start.4) | async-done | bytes 2097184 | tf_op jit(solution)/shard_map/all_to_all | solution.py:156
  415.6 24.1 %scatter_custom_fusion.1 = f32[4096,128]{1,0:T(8,128)} fusion(s32[4096]{0:T(1024)S(1)} %bitcast.100, f32[4096,128]{1,0:T(8,128)} %bitcast.27, f32[]{:T(128)} %constant.43.clone.1), kind=kCustom, calls=%fused_computation.49 | custom fusion | flops 524288 | bytes 2097664 | tf_op jit(solution)/shard_map/scatter-add | solution.py:160
  439.6 2.9 reshape.274
  442.5 3.4 fusion.14
  (39 shorter events, 3.2 us)
Async XLA Ops:
  7.2 43.7 %all-gather.2.cloned.1.call-start = ((), (), s32[]{:S(2)}) async-start(), calls=%async_computation.5 | async-start | bytes 2359296 | tf_op jit(solution)/shard_map/all_gather | solution.py:142
  31.0 15.5 %all-to-all-start = ((s32[32,1,128]{2,1,0:T(1,128)}), s32[32,1,128]{2,1,0:T(1,128)S(1)}, u32[]{:S(2)}, u32[]{:S(2)}) async-start(s32[32,1,128]{2,1,0:T(1,128)} %bitcast.5), calls=%async_computation | async-start | bytes 32768 | tf_op jit(solution)/shard_map/all_to_all | solution.py:133
  67.0 13.0 %copy-start.4 = (s32[1024]{0:T(1024)S(1)}, s32[1024]{0:T(1024)}, u32[]{:S(2)}) copy-start(s32[1024]{0:T(1024)} %param.13) | copy-start | bytes 12292
  67.0 13.6 %copy-start.2 = (s32[8,256]{1,0:T(8,128)S(1)}, s32[8,256]{1,0:T(8,128)}, u32[]{:S(2)}) copy-start(s32[8,256]{1,0:T(8,128)} %param.11) | copy-start | bytes 24580
  67.0 13.6 %copy-start.3 = (s32[8,256]{1,0:T(8,128)S(1)}, s32[8,256]{1,0:T(8,128)}, u32[]{:S(2)}) copy-start(s32[8,256]{1,0:T(8,128)} %param.12) | copy-start | bytes 24580
  68.6 121.6 %all-to-all-start.1 = ((bf16[32,128,128]{2,1,0:T(8,128)(2,1)}), bf16[32,128,128]{2,1,0:T(8,128)(2,1)S(1)}, u32[]{:S(2)}, u32[]{:S(2)}) async-start(bf16[32,128,128]{2,1,0:T(8,128)(2,1)} %broadcast_select_fusion.1), calls=%async_computation.1 | async-start | bytes 2097152 | tf_op jit(solution)/shard_map/all_to_all | solution.py:148
  233.7 35.7 %all-to-all-start.2 = ((f32[32,128,128]{2,1,0:T(8,128)}), f32[32,128,128]{2,1,0:T(8,128)S(1)}, u32[]{:S(2)}, u32[]{:S(2)}) async-start(f32[32,128,128]{2,1,0:T(8,128)} %bitcast.19), calls=%async_computation.2 | async-start | bytes 4194304 | tf_op jit(solution)/shard_map/all_to_all | solution.py:156
  241.1 53.9 %copy-start = (bf16[4,512,256]{2,1,0:T(8,128)(2,1)S(1)}, bf16[4,512,256]{2,1,0:T(8,128)(2,1)}, u32[]{:S(2)}) copy-start(bf16[4,512,256]{2,1,0:T(8,128)(2,1)} %param.8) | copy-start | bytes 3145732
  369.6 3.7 slice-start
  370.1 3.1 slice-start.1
  382.7 32.9 %all-to-all-start.4 = ((f32[32,128,128]{2,1,0:T(8,128)}), f32[32,128,128]{2,1,0:T(8,128)}, u32[]{:S(2)}, u32[]{:S(2)}) async-start(f32[32,128,128]{2,1,0:T(8,128)} %bitcast.76), calls=%async_computation.4 | async-start | bytes 4194304 | tf_op jit(solution)/shard_map/all_to_all | solution.py:156
  387.5 55.1 %copy-start.1 = (bf16[4,512,256]{2,1,0:T(8,128)(2,1)S(1)}, bf16[4,512,256]{2,1,0:T(8,128)(2,1)}, u32[]{:S(2)}) copy-start(bf16[4,512,256]{2,1,0:T(8,128)(2,1)} %param.8) | copy-start | bytes 3145732
Sparse Core Ops, SparseCore 0:
  9.8 41.0 all-gather.1

commit v2 on v1

--- a/solution.py
+++ b/solution.py
@@ -17,7 +17,8 @@
 PIO2_2 = 4.837512969970703125e-4
 PIO2_3 = 7.549789954891e-8
 ROWS = 16
-LANES = 128
+LANES = 512
+UNROLL = 2
 
 
 def basis_kernel(t_ref, p_ref, w_ref, inv_ref, basis_ref, nc_ref, ns_ref):
@@ -56,7 +57,7 @@
             return acc_c + cf * cf, acc_s + sf * sf
 
         zero = jnp.zeros((ROWS, LANES), jnp.float32)
-        acc_c, acc_s = lax.fori_loop(0, obs // ROWS, row_block, (zero, zero))
+        acc_c, acc_s = lax.fori_loop(0, obs // ROWS, row_block, (zero, zero), unroll=UNROLL)
         nc_ref[:, pl.ds(c0, LANES)] = jnp.sum(acc_c, axis=0, keepdims=True) + RIDGE
         ns_ref[:, pl.ds(c0, LANES)] = jnp.sum(acc_s, axis=0, keepdims=True) + RIDGE
         return carry
@@ -149,15 +150,15 @@
         observed = arrived[target, position].reshape(sched_dev, obs, SRC_GROUP)
         model, evidence = fit_groups(basis, observed, norm_cos, norm_sin, nper)
         outgoing = (
-            jnp.zeros((tm_count, capacity, SRC_GROUP), jnp.float32)
+            jnp.zeros((tm_count, capacity, SRC_GROUP), jnp.bfloat16)
             .at[target, position]
-            .set(model.reshape(requests, SRC_GROUP))
+            .set(model.reshape(requests, SRC_GROUP).astype(jnp.bfloat16))
         )
         returned = lax.all_to_all(outgoing, "tm", split_axis=0, concat_axis=0, tiled=True)
         placed = (
             jnp.zeros((empty_row, SRC_GROUP), jnp.float32)
             .at[asked.reshape(-1)]
-            .add(returned.reshape(-1, SRC_GROUP), mode="drop")
+            .add(returned.reshape(-1, SRC_GROUP).astype(jnp.float32), mode="drop")
         )
         current = current - placed.reshape(seg_dev, slots, width)
     return (current, evidence)

time: 454 us -> 351 us (0.77)
  Pallas kernels: 107 us -> 26.9 us
  waiting for transfers between devices: 66.9 us -> 44.4 us
    pallas_call x1, Pallas kernels: 107 us -> 26.9 us  [basis_and_norms(): pl.pallas_call(basis_kernel, grid=(plans,), in_specs=[pl.BlockSpec((None,...]
    all_to_all x2, waiting for transfers between devices: 55.7 us -> 33.2 us  [on_device(): lax.all_to_all(outgoing, 'tm', split_axis=0, concat_axis=0, tiled=True)]
  transfers between devices with their start and end apart: 5 -> 5, of which waited for: 4 -> 4; matrix products, arithmetic and copies ran while one was open for 6% -> 8% of each run, Pallas kernels for 24% -> 8%
where the time goes in v2:
time: 351 us; the launch traced here: 350 us
  local copies, waits for them, and re-layouts  95.9 us (27%)
  other arithmetic  84.6 us (24%)
  waiting for transfers between devices  44.4 us (13%)
  starting transfers between devices  32.1 us (9%)
  matrix products  31 us (9%)
  Pallas kernels  26.9 us (8%)
  blocking collectives  20.7 us (6%)
  between operations  14.4 us (4%)
    scatter-add x2, other arithmetic, on_device(): placed = jnp.zeros((empty_row, SRC_GROUP), jnp.float32).at[asked.reshape(...  48 us
    all_to_all x2, waiting for transfers between devices, on_device(): lax.all_to_all(outgoing, 'tm', split_axis=0, concat_axis=0, tiled=True)  33.2 us
    gather x2, local copies, waits for them, and re-layouts, on_device(): observed = arrived[target, position].reshape(sched_dev, obs, SRC_GROUP)  31.7 us
    gather x2, local copies, waits for them, and re-layouts, on_device(): picked = jnp.take(flat, asked, axis=0, mode='fill', fill_value=0)  27.2 us
    pallas_call x1, Pallas kernels, basis_and_norms(): pl.pallas_call(basis_kernel, grid=(plans,), in_specs=[pl.BlockSpec((None,...  26.9 us
    unnamed x23, local copies, waits for them, and re-layouts  25.3 us
    all_to_all x1, blocking collectives, on_device(): lax.all_to_all(picked, 'tm', split_axis=0, concat_axis=0, tiled=True)  20.7 us
    dot_general x2, matrix products, fit_groups(): jnp.einsum('fio,fic->foc', basis, observed, preferred_element_type=jnp.fl...  15.5 us
  transfers between devices with their start and end apart: 5, of which 4 were waited for; matrix products, arithmetic and copies ran while one was open for 8% of the time, Pallas kernels for 8%

profile of v2, /device:TPU:1, one launch (start us, length us, event | category | flops | bytes accessed | tf_op | source)
XLA Modules:
  0.0 350.0 jit_solution(5267266067506360964)
XLA Ops:
  7.2 0.7 all-gather.2.cloned.1.call-update
  8.0 0.7 reshape.254
  8.7 0.7 copy.37
  9.4 0.7 copy.38
  10.1 0.7 copy.40
  10.8 9.1 %reduce-window.6 = s32[32,16,128]{2,1,0:T(8,128)S(1)} reduce-window(s32[32,16,128]{2,1,0:T(8,128)S(1)} %fusion.40, s32[]{:T(128)} %constant.72.clone.1), window={size=1x1x128 pad=0_0x0_0x127_0}, to_apply=%region_0.1 | reduce-window | flops 8323072 | bytes 524292 | tf_op jit(solution)/shard_map/reduce-window
  20.9 0.7 multiply_reduce_fusion
  21.6 0.8 and_reduce_fusion
  22.4 8.6 %scatter_custom_fusion.2 = s32[4096]{0:T(1024)} fusion(s32[2048]{0:T(1024)S(1)} %broadcast_select_fusion.2, s32[2048]{0:T(1024)S(1)} %get-tuple-element.18, s32[]{:T(128)} %constant.70.clone.1), kind=kCustom, calls=%fused_computation.98 | custom fusion | bytes 16388
  31.0 8.6 %all-to-all-start = ((s32[32,1,128]{2,1,0:T(1,128)}), s32[32,1,128]{2,1,0:T(1,128)S(1)}, u32[]{:S(2)}, u32[]{:S(2)}) async-start(s32[32,1,128]{2,1,0:T(1,128)} %bitcast.5), calls=%async_computation | async-start | bytes 32768 | tf_op jit(solution)/shard_map/all_to_all | solution.py:134
  39.6 0.7 iota_compare_fusion.2
  40.3 6.1 %all-to-all-done = s32[32,1,128]{2,1,0:T(1,128)S(1)} async-done(((s32[32,1,128]{2,1,0:T(1,128)}), s32[32,1,128]{2,1,0:T(1,128)S(1)}, u32[]{:S(2)}, u32[]{:S(2)}) %all-to-all-start) | async-done | bytes 16416 | tf_op jit(solution)/shard_map/all_to_all | solution.py:134
  46.5 4.4 %all-gather.2.cloned.1.call-done = bf16[4,512,512]{2,1,0:T(8,128)(2,1)} async-done(((bf16[4,64,512]{2,1,0:T(8,128)(2,1)}), bf16[4,512,512]{2,1,0:T(8,128)(2,1)}) %all-gather.2.cloned.1.call-update) | async-done | bytes 2097168 | tf_op jit(solution)/shard_map/all_gather | solution.py:143
  50.9 3.1 fusion.19
  54.9 12.1 %gather_fusion.2 = bf16[4096,128]{1,0:T(8,128)(2,1)S(1)} fusion(bf16[4096,128]{1,0:T(8,128)(2,1)S(1)} %reshape.263, s32[4096]{0:T(1024)S(1)} %bitcast_clamp_fusion), kind=kCustom, calls=%fused_computation.clone | custom fusion | bytes 2113536 | tf_op jit(solution)/shard_map/jit(_take)/gather | solution.py:148
  67.1 1.6 broadcast_select_fusion.1
  68.6 11.4 %all-to-all-start.1 = ((bf16[32,128,128]{2,1,0:T(8,128)(2,1)}), bf16[32,128,128]{2,1,0:T(8,128)(2,1)S(1)}, u32[]{:S(2)}, u32[]{:S(2)}) async-start(bf16[32,128,128]{2,1,0:T(8,128)(2,1)} %broadcast_select_fusion.1), calls=%async_computation.1 | async-start | bytes 2097152 | tf_op jit(solution)/shard_map/all_to_all | solution.py:149
  80.7 1.3 copy.23.t_ref
  82.0 0.6 broadcast_divide_fusion
  82.6 26.9 %shard_map.77 = (bf16[8,256,2048]{2,1,0:T(8,128)(2,1)}, f32[8,1,1024]{2,1,0:T(1,128)}, f32[8,1,1024]{2,1,0:T(1,128)}) custom-call(f32[8,256,1]{2,1,0:T(8,128)} %copy.23.t_ref, f32[1,1024]{1,0:T(1,128)} %bitcast.99, f32[1,1024]{1,0:T(1,128)} %bitcast.98, f32[1,1024]{1,0:T(1,128)} %bitcast.97), custom_call_target="tpu_custom_call" | custom-call | flops 125829120 | bytes 8388608 | tf_op jit(solution)/shard_map/pallas_call | solution.py:77
  109.5 0.8 copy_bitcast_fusion
  110.3 11.1 %gather_fusion = bf16[2048,128]{1,0:T(8,128)(2,1)S(1)} fusion(bf16[32,128,128]{2,1,0:T(8,128)(2,1)S(1)} %all-to-all-done.1, s32[2048]{0:T(1024)S(1)} %bitcast.74), kind=kCustom, calls=%fused_computation.2 | custom fusion | bytes 1064960 | tf_op jit(solution)/shard_map/gather | solution.py:150
  121.5 9.4 %fusion.57 = f32[8,2048,128]{2,1,0:T(8,128)} fusion(bf16[8,256,2048]{2,1,0:T(8,128)(2,1)} %get-tuple-element.6, bf16[8,256,128]{2,1,0:T(8,128)(2,1)S(1)} %bitcast.81), kind=kOutput, calls=%fused_computation.121 | convolution fusion | flops 1073741824 | bytes 17301504 | tf_op jit(solution)/shard_map/fio,fic->foc/dot_general | solution.py:99
  130.8 9.5 %multiply_convert_fusion.3 = (bf16[8,1024,128]{2,1,0:T(8,128)(2,1)S(1)}, bf16[8,1024,128]{2,1,0:T(8,128)(2,1)}) fusion(f32[8,1024]{1,0:T(8,128)S(1)} %get-tuple-element.25, f32[8,2048,128]{2,1,0:T(8,128)} %fusion.57, f32[8,1024]{1,0:T(8,128)S(1)} %get-tuple-element.24), kind=kOutput, calls=%fused_computation.24 | output fusion | flops 14684158 | bytes 21102592 | tf_op jit(solution)/shard_map/div | solution.py:109
  140.4 6.4 %fusion.24 = bf16[8,256,128]{2,1,0:T(8,128)(2,1)S(1)} fusion(bf16[8,256,2048]{2,1,0:T(8,128)(2,1)} %get-tuple-element.6, bf16[8,1024,128]{2,1,0:T(8,128)(2,1)} %get-tuple-element.17, bf16[8,1024,128]{2,1,0:T(8,128)(2,1)S(1)} %get-tuple-element.16), kind=kOutput, calls=%fused_computation.48 | convolution fusion | flops 1082392576 | bytes 13107200 | tf_op jit(solution)/shard_map/fio,foc->fic/dot_general | solution.py:111
  146.7 6.8 %scatter_custom_fusion.3 = bf16[4096,128]{1,0:T(8,128)(2,1)} fusion(s32[2048]{0:T(1024)S(1)} %broadcast_select_fusion.2, bf16[2048,128]{1,0:T(8,128)(2,1)S(1)} %bitcast.103, bf16[]{:T(256)} %constant.80.clone.1), kind=kCustom, calls=%fused_computation.59 | custom fusion | bytes 1048578
  153.5 7.4 %all-to-all-start.2 = ((bf16[32,128,128]{2,1,0:T(8,128)(2,1)}), bf16[32,128,128]{2,1,0:T(8,128)(2,1)S(1)}, u32[]{:S(2)}, u32[]{:S(2)}) async-start(bf16[32,128,128]{2,1,0:T(8,128)(2,1)} %bitcast.19), calls=%async_computation.2 | async-start | bytes 2097152 | tf_op jit(solution)/shard_map/all_to_all | solution.py:157
  161.0 16.9 %all-to-all-done.2 = bf16[32,128,128]{2,1,0:T(8,128)(2,1)S(1)} async-done(((bf16[32,128,128]{2,1,0:T(8,128)(2,1)}), bf16[32,128,128]{2,1,0:T(8,128)(2,1)S(1)}, u32[]{:S(2)}, u32[]{:S(2)}) %all-to-all-start.2) | async-done | bytes 1048608 | tf_op jit(solution)/shard_map/all_to_all | solution.py:157
  177.8 23.8 %scatter_custom_fusion = f32[4096,128]{1,0:T(8,128)} fusion(s32[4096]{0:T(1024)S(1)} %bitcast.100, bf16[4096,128]{1,0:T(8,128)(2,1)S(1)} %bitcast.80, f32[]{:T(128)} %constant.43.clone.1), kind=kCustom, calls=%fused_computation.39 | custom fusion | flops 1048576 | bytes 3145732 | tf_op jit(solution)/shard_map/scatter-add | solution.py:161
  201.6 1.9 reshape.265
  203.5 3.7 %fusion.20 = bf16[4,512,256]{1,2,0:T(8,128)(2,1)} fusion(bf16[4,512,512]{2,1,0:T(8,128)(2,1)} %all-gather.2.cloned.1.call-done, f32[4,512,256]{2,1,0:T(8,128)S(1)} %reshape.265, bf16[4,512,256]{2,1,0:T(8,128)(2,1)S(1)} %copy-done, pred[4,512]{1,0:T(4,128)(4,1)S(1)} %iota_compare_fusion.2), kind=kOutput, calls=%fused_computation.46 | convolution fusion | flops 539492352 | bytes 6293504 | tf_op jit(solution)/shard_map/sij,sjc->sic/dot_general | solution.py:141
  207.3 2.3 copy.28
  209.6 1.4 reshape.266
  211.0 15.0 %gather_fusion.3 = bf16[4096,128]{1,0:T(8,128)(2,1)} fusion(bf16[4096,128]{1,0:T(8,128)(2,1)S(1)} %reshape.266, s32[4096]{0:T(1024)S(1)} %bitcast_clamp_fusion), kind=kCustom, calls=%fused_computation.1.clone | custom fusion | bytes 2113536 | tf_op jit(solution)/shard_map/jit(_take)/gather | solution.py:148
  226.1 1.8 broadcast_select_fusion
  227.8 20.7 %all_to_all.32 = bf16[32,128,128]{2,1,0:T(8,128)(2,1)S(1)} all-to-all(bf16[32,128,128]{2,1,0:T(8,128)(2,1)S(1)} %broadcast_select_fusion), channel_id=1, replica_groups=mesh['tm'=32,'sky'=8] {'tm'}, dimensions={0} | all-to-all | bytes 2097152 | tf_op jit(solution)/shard_map/all_to_all | solution.py:149
  248.5 20.5 %gather_fusion.1 = bf16[2048,128]{1,0:T(8,128)(2,1)} fusion(bf16[32,128,128]{2,1,0:T(8,128)(2,1)S(1)} %all_to_all.32, s32[2048]{0:T(1024)S(1)} %bitcast.75), kind=kCustom, calls=%fused_computation.3 | custom fusion | bytes 1064960 | tf_op jit(solution)/shard_map/gather | solution.py:150
  269.0 6.2 %fusion.58 = f32[8,2048,128]{2,1,0:T(8,128)S(1)} fusion(bf16[8,256,2048]{2,1,0:T(8,128)(2,1)} %get-tuple-element.6, bf16[8,256,128]{2,1,0:T(8,128)(2,1)} %bitcast.82), kind=kOutput, calls=%fused_computation.122 | convolution fusion | flops 1073741824 | bytes 17301504 | tf_op jit(solution)/shard_map/fio,fic->foc/dot_general | solution.py:99
  275.2 3.0 fusion.56
  278.8 3.1 multiply_convert_fusion.1
  281.9 2.3 fusion.21
  284.2 6.8 %scatter_custom_fusion.4 = bf16[4096,128]{1,0:T(8,128)(2,1)} fusion(s32[2048]{0:T(1024)S(1)} %broadcast_select_fusion.2, bf16[2048,128]{1,0:T(8,128)(2,1)S(1)} %bitcast.102, bf16[]{:T(256)} %constant.80.clone.1), kind=kCustom, calls=%fused_computation.57 | custom fusion | bytes 1048578
  291.0 4.7 %all-to-all-start.4 = ((bf16[32,128,128]{2,1,0:T(8,128)(2,1)}), bf16[32,128,128]{2,1,0:T(8,128)(2,1)}, u32[]{:S(2)}, u32[]{:S(2)}) async-start(bf16[32,128,128]{2,1,0:T(8,128)(2,1)} %bitcast.26), calls=%async_computation.4 | async-start | bytes 2097152 | tf_op jit(solution)/shard_map/all_to_all | solution.py:157
  295.8 0.6 log_add_fusion
  296.4 16.4 %all-to-all-done.4 = bf16[32,128,128]{2,1,0:T(8,128)(2,1)} async-done(((bf16[32,128,128]{2,1,0:T(8,128)(2,1)}), bf16[32,128,128]{2,1,0:T(8,128)(2,1)}, u32[]{:S(2)}, u32[]{:S(2)}) %all-to-all-start.4) | async-done | bytes 1048608 | tf_op jit(solution)/shard_map/all_to_all | solution.py:157
  312.7 24.2 %scatter_custom_fusion.1 = f32[4096,128]{1,0:T(8,128)} fusion(s32[4096]{0:T(1024)S(1)} %bitcast.101, bf16[4096,128]{1,0:T(8,128)(2,1)} %bitcast.29, f32[]{:T(128)} %constant.43.clone.1), kind=kCustom, calls=%fused_computation.37 | custom fusion | flops 1048576 | bytes 3145732 | tf_op jit(solution)/shard_map/scatter-add | solution.py:161
  336.9 2.9 reshape.268
  339.8 3.4 fusion.18
  (39 shorter events, 3.2 us)
Async XLA Ops:
  7.2 43.7 %all-gather.2.cloned.1.call-start = ((), (), s32[]{:S(2)}) async-start(), calls=%async_computation.5 | async-start | bytes 2359296 | tf_op jit(solution)/shard_map/all_gather | solution.py:143
  31.0 15.5 %all-to-all-start = ((s32[32,1,128]{2,1,0:T(1,128)}), s32[32,1,128]{2,1,0:T(1,128)S(1)}, u32[]{:S(2)}, u32[]{:S(2)}) async-start(s32[32,1,128]{2,1,0:T(1,128)} %bitcast.5), calls=%async_computation | async-start | bytes 32768 | tf_op jit(solution)/shard_map/all_to_all | solution.py:134
  67.0 13.0 %copy-start.4 = (s32[1024]{0:T(1024)S(1)}, s32[1024]{0:T(1024)}, u32[]{:S(2)}) copy-start(s32[1024]{0:T(1024)} %param.13) | copy-start | bytes 12292
  67.0 13.6 %copy-start.2 = (s32[8,256]{1,0:T(8,128)S(1)}, s32[8,256]{1,0:T(8,128)}, u32[]{:S(2)}) copy-start(s32[8,256]{1,0:T(8,128)} %param.11) | copy-start | bytes 24580
  67.0 13.6 %copy-start.3 = (s32[8,256]{1,0:T(8,128)S(1)}, s32[8,256]{1,0:T(8,128)}, u32[]{:S(2)}) copy-start(s32[8,256]{1,0:T(8,128)} %param.12) | copy-start | bytes 24580
  68.6 41.7 %all-to-all-start.1 = ((bf16[32,128,128]{2,1,0:T(8,128)(2,1)}), bf16[32,128,128]{2,1,0:T(8,128)(2,1)S(1)}, u32[]{:S(2)}, u32[]{:S(2)}) async-start(bf16[32,128,128]{2,1,0:T(8,128)(2,1)} %broadcast_select_fusion.1), calls=%async_computation.1 | async-start | bytes 2097152 | tf_op jit(solution)/shard_map/all_to_all | solution.py:149
  153.5 24.3 %all-to-all-start.2 = ((bf16[32,128,128]{2,1,0:T(8,128)(2,1)}), bf16[32,128,128]{2,1,0:T(8,128)(2,1)S(1)}, u32[]{:S(2)}, u32[]{:S(2)}) async-start(bf16[32,128,128]{2,1,0:T(8,128)(2,1)} %bitcast.19), calls=%async_computation.2 | async-start | bytes 2097152 | tf_op jit(solution)/shard_map/all_to_all | solution.py:157
  160.9 42.6 %copy-start = (bf16[4,512,256]{2,1,0:T(8,128)(2,1)S(1)}, bf16[4,512,256]{2,1,0:T(8,128)(2,1)}, u32[]{:S(2)}) copy-start(bf16[4,512,256]{2,1,0:T(8,128)(2,1)} %param.8) | copy-start | bytes 3145732
  278.2 3.7 %slice-start = ((s8[8388608]{0:T(1024)(128)(4,1)}), s8[4194304]{0:T(1024)(128)(4,1)S(1)}, s32[]{:S(2)}) async-start(s8[8388608]{0:T(1024)(128)(4,1)} %bitcast.76), calls=%async_computation.6 | async-start | bytes 8388608
  278.8 3.1 slice-start.1
  291.0 21.7 %all-to-all-start.4 = ((bf16[32,128,128]{2,1,0:T(8,128)(2,1)}), bf16[32,128,128]{2,1,0:T(8,128)(2,1)}, u32[]{:S(2)}, u32[]{:S(2)}) async-start(bf16[32,128,128]{2,1,0:T(8,128)(2,1)} %bitcast.26), calls=%async_computation.4 | async-start | bytes 2097152 | tf_op jit(solution)/shard_map/all_to_all | solution.py:157
  295.8 44.0 %copy-start.1 = (bf16[4,512,256]{2,1,0:T(8,128)(2,1)S(1)}, bf16[4,512,256]{2,1,0:T(8,128)(2,1)}, u32[]{:S(2)}) copy-start(bf16[4,512,256]{2,1,0:T(8,128)(2,1)} %param.8) | copy-start | bytes 3145732
Sparse Core Ops, SparseCore 0:
  9.8 41.0 all-gather.1

commit v3 on v2

--- a/solution.py
+++ b/solution.py
@@ -2,6 +2,7 @@
 import jax.numpy as jnp
 from jax import lax
 from jax.experimental import pallas as pl
+from jax.experimental.pallas import tpu as pltpu
 from jax.sharding import PartitionSpec as P
 
 SRC_GROUP = 128
@@ -95,6 +96,29 @@
     return basis, nc.reshape(plans, nper), ns.reshape(plans, nper)
 
 
+def gather_kernel(idx_ref, src_ref, out_ref):
+    def body(r, carry):
+        out_ref[pl.ds(r, 1), :] = src_ref[pl.ds(idx_ref[r], 1), :]
+        return carry
+
+    lax.fori_loop(0, out_ref.shape[0], body, 0, unroll=16)
+
+
+def row_gather(src, idx):
+    rows, width = idx.shape[0], src.shape[1]
+    return pl.pallas_call(
+        gather_kernel,
+        in_specs=[pl.BlockSpec(memory_space=pltpu.SMEM), pl.BlockSpec(memory_space=pltpu.VMEM)],
+        out_specs=pl.BlockSpec(memory_space=pltpu.VMEM),
+        out_shape=jax.ShapeDtypeStruct((rows, width), src.dtype),
+        cost_estimate=pl.CostEstimate(
+            flops=0, transcendentals=0, bytes_accessed=2 * rows * width * src.dtype.itemsize),
+    )(idx, src)
+
+
+def with_zero_rows(flat):
+    return jnp.concatenate([flat, jnp.zeros((8, flat.shape[1]), flat.dtype)], axis=0)
+
 def fit_groups(basis, observed, norm_cos, norm_sin, nper):
     corr = jnp.einsum("fio,fic->foc", basis, observed, preferred_element_type=jnp.float32)
     cosine = corr[:, :nper]
@@ -128,36 +152,39 @@
     onehot = (target[:, None] == jnp.arange(tm_count, dtype=jnp.int32)[None, :]).astype(jnp.int32)
     position = jnp.sum(jnp.cumsum(onehot, axis=0) * onehot, axis=1) - 1
     empty_row = seg_dev * slots * column_blocks
-    wanted = (
-        jnp.full((tm_count, capacity), empty_row, jnp.int32).at[target, position].set(local_row)
+    slot_of = target * capacity + position
+    pair = (
+        jnp.broadcast_to(jnp.array([empty_row, requests], jnp.int32), (tm_count * capacity, 2))
+        .at[slot_of]
+        .set(jnp.stack([local_row, jnp.arange(requests, dtype=jnp.int32)], axis=1))
     )
-    asked = lax.all_to_all(wanted, "tm", split_axis=0, concat_axis=0, tiled=True)
+    wanted = pair[:, 0].reshape(tm_count, capacity)
+    inverse = pair[:, 1]
+    asked = lax.all_to_all(wanted, "tm", split_axis=0, concat_axis=0, tiled=True).reshape(-1)
     basis, norm_cos, norm_sin = basis_and_norms(sched_seg * slots + sched_slot, periods)
     valid = jnp.arange(slots, dtype=jnp.int32)[None, :] < seg_counts[:, None]
     current = residuals.astype(jnp.float32)
     evidence = jnp.zeros((sched_dev, SRC_GROUP), jnp.float32)
+    attitude_all = lax.all_gather(attitude, "sky", axis=1, tiled=True)
     for iteration in range(ITERS):
         masked = jnp.where(valid[:, :, None], current, 0.0).astype(jnp.bfloat16)
         white = jnp.einsum(
-            "sij,sjc->sic",
-            lax.all_gather(attitude, "sky", axis=1, tiled=True),
-            masked,
-            preferred_element_type=jnp.float32,
-        ).astype(jnp.bfloat16)
-        flat = white.reshape(-1, SRC_GROUP)
-        picked = jnp.take(flat, asked, axis=0, mode="fill", fill_value=0)
-        arrived = lax.all_to_all(picked, "tm", split_axis=0, concat_axis=0, tiled=True)
-        observed = arrived[target, position].reshape(sched_dev, obs, SRC_GROUP)
+            "sij,sjc->sic", attitude_all, masked, preferred_element_type=jnp.float32
+        )
+        picked = row_gather(with_zero_rows(white.reshape(-1, SRC_GROUP)), asked)
+        arrived = lax.all_to_all(
+            picked.astype(jnp.bfloat16).reshape(tm_count, capacity, SRC_GROUP),
+            "tm", split_axis=0, concat_axis=0, tiled=True)
+        observed = row_gather(arrived.reshape(-1, SRC_GROUP).astype(jnp.float32), slot_of)
+        observed = observed.astype(jnp.bfloat16).reshape(sched_dev, obs, SRC_GROUP)
         model, evidence = fit_groups(basis, observed, norm_cos, norm_sin, nper)
-        outgoing = (
-            jnp.zeros((tm_count, capacity, SRC_GROUP), jnp.bfloat16)
-            .at[target, position]
-            .set(model.reshape(requests, SRC_GROUP).astype(jnp.bfloat16))
-        )
-        returned = lax.all_to_all(outgoing, "tm", split_axis=0, concat_axis=0, tiled=True)
+        outgoing = row_gather(with_zero_rows(model.reshape(requests, SRC_GROUP)), inverse)
+        returned = lax.all_to_all(
+            outgoing.astype(jnp.bfloat16).reshape(tm_count, capacity, SRC_GROUP),
+            "tm", split_axis=0, concat_axis=0, tiled=True)
         placed = (
             jnp.zeros((empty_row, SRC_GROUP), jnp.float32)
-            .at[asked.reshape(-1)]
+            .at[asked]
             .add(returned.reshape(-1, SRC_GROUP).astype(jnp.float32), mode="drop")
         )
         current = current - placed.reshape(seg_dev, slots, width)

time: 351 us -> 341 us (0.972)
  local copies, waits for them, and re-layouts: 95.9 us -> 36.5 us
  Pallas kernels: 26.9 us -> 65.5 us
  other arithmetic: 84.6 us -> 95 us
    gather x4 -> x0, local copies, waits for them, and re-layouts: 58.8 us -> none  [the longest x2 31.7 us: on_device(): observed = arrived[target, position].reshape(sched_dev, obs, SRC_GROUP)]
    pallas_call x0 -> x6, Pallas kernels: none -> 38.6 us  [row_gather(): pl.pallas_call(gather_kernel, in_specs=[pl.BlockSpec(memory_space=pltpu.S...]
    unnamed x23 -> x24, local copies, waits for them, and re-layouts: 25.3 us -> 3.62 us
    convert_element_type x0 -> x8, other arithmetic: none -> 15.5 us  [the longest x2 5.49 us: on_device(): outgoing.astype(jnp.bfloat16).reshape(tm_count, capacity, SRC_GROUP)]
    concatenate x0 -> x4, local copies, waits for them, and re-layouts: none -> 6.8 us  [with_zero_rows(): jnp.concatenate([flat, jnp.zeros((8, flat.shape[1]), flat.dtype)], axis=0)]
    all_gather x1, waiting for transfers between devices: 4.37 us -> 11 us  [on_device(): attitude_all = lax.all_gather(attitude, 'sky', axis=1, tiled=True)]
    scatter x0 -> x1, local copies, waits for them, and re-layouts: none -> 6.37 us  [on_device(): pair = jnp.broadcast_to(jnp.array([empty_row, requests], jnp.int32), (tm_...]
    all_to_all x1, waiting for transfers between devices: 6.14 us -> 0.01 us  [on_device(): lax.all_to_all(wanted, 'tm', split_axis=0, concat_axis=0, tiled=True)]
  transfers between devices with their start and end apart: 5 -> 5, of which waited for: 4 -> 3; matrix products, arithmetic and copies ran while one was open for 8% -> 10% of each run, Pallas kernels for 8% -> 8%
where the time goes in v3:
time: 341 us; the launch traced here: 339 us
  other arithmetic  95 us (28%)
  Pallas kernels  65.5 us (19%)
  waiting for transfers between devices  44.9 us (13%)
  local copies, waits for them, and re-layouts  36.5 us (11%)
  starting transfers between devices  31.7 us (9%)
  matrix products  30.8 us (9%)
  blocking collectives  20.7 us (6%)
  between operations  14.3 us (4%)
    scatter-add x2, other arithmetic, on_device(): placed = jnp.zeros((empty_row, SRC_GROUP), jnp.float32).at[asked].add(ret...  48 us
    pallas_call x6, Pallas kernels, row_gather(): pl.pallas_call(gather_kernel, in_specs=[pl.BlockSpec(memory_space=pltpu.S...  38.6 us
    all_to_all x2, waiting for transfers between devices, on_device(): lax.all_to_all(outgoing.astype(jnp.bfloat16).reshape(tm_count, capacity,...  33.2 us
    pallas_call x1, Pallas kernels, basis_and_norms(): pl.pallas_call(basis_kernel, grid=(plans,), in_specs=[pl.BlockSpec((None,...  26.9 us
    all_to_all x1, blocking collectives, on_device(): lax.all_to_all(picked.astype(jnp.bfloat16).reshape(tm_count, capacity, SR...  20.7 us
    dot_general x2, matrix products, fit_groups(): jnp.einsum('fio,fic->foc', basis, observed, preferred_element_type=jnp.fl...  15.5 us
    another operation x4, other arithmetic  12.5 us
    all_to_all x2, starting transfers between devices, on_device(): lax.all_to_all(outgoing.astype(jnp.bfloat16).reshape(tm_count, capacity,...  11.8 us
  transfers between devices with their start and end apart: 5, of which 3 were waited for; matrix products, arithmetic and copies ran while one was open for 10% of the time, Pallas kernels for 8%

profile of v3, /device:TPU:1, one launch (start us, length us, event | category | flops | bytes accessed | tf_op | source)
XLA Modules:
  0.0 339.4 jit_solution(4989058105147284124)
XLA Ops:
  10.9 9.1 %reduce-window.6 = s32[32,16,128]{2,1,0:T(8,128)S(1)} reduce-window(s32[32,16,128]{2,1,0:T(8,128)S(1)} %fusion.28, s32[]{:T(128)} %constant.61.clone.1), window={size=1x1x128 pad=0_0x0_0x127_0}, to_apply=%region_0.1 | reduce-window | flops 8323072 | bytes 524292 | tf_op jit(solution)/shard_map/reduce-window
  22.7 6.4 %scatter_fusion = s32[4096,2]{1,0:T(8,128)S(1)} fusion(s32[4096,2]{1,0:T(8,128)S(1)} %broadcast_in_dim.20, s32[2048]{0:T(1024)S(1)} %bitcast.98, s32[2048,2]{1,0:T(8,128)S(1)} %copy.41), kind=kCustom, calls=%fused_computation | custom fusion | bytes 57344 | tf_op jit(solution)/shard_map/scatter | solution.py:159
  29.1 2.3 slice_reduce_fusion
  31.4 8.6 %all-to-all-start = ((s32[32,1,128]{2,1,0:T(1,128)}), s32[32,1,128]{2,1,0:T(1,128)S(1)}, u32[]{:S(2)}, u32[]{:S(2)}) async-start(s32[32,1,128]{2,1,0:T(1,128)} %bitcast.5), calls=%async_computation | async-start | bytes 32768 | tf_op jit(solution)/shard_map/all_to_all | solution.py:163
  40.1 11.0 %all-gather.2.cloned.1.call-done = bf16[4,512,512]{2,1,0:T(8,128)(2,1)} async-done(((bf16[4,64,512]{2,1,0:T(8,128)(2,1)}), bf16[4,512,512]{2,1,0:T(8,128)(2,1)}) %all-gather.2.cloned.1.call-update) | async-done | bytes 2097168 | tf_op jit(solution)/shard_map/all_gather | solution.py:168
  51.0 2.7 convolution_bitcast_fusion.1
  53.7 1.8 copy.45
  55.5 1.6 reshape.335
  57.2 1.5 concatenate.20.src_ref
  59.3 7.4 %shard_map.87 = f32[4096,128]{1,0:T(8,128)} custom-call(s32[4096]{0:T(1024)} %bitcast.90, f32[4104,128]{1,0:T(8,128)} %concatenate.20.src_ref), custom_call_target="tpu_custom_call" | custom-call | bytes 4194304 | tf_op jit(solution)/shard_map/pallas_call | solution.py:109
  66.7 2.8 convert_element_type.67
  69.4 11.2 %all-to-all-start.1 = ((bf16[32,128,128]{2,1,0:T(8,128)(2,1)}), bf16[32,128,128]{2,1,0:T(8,128)(2,1)S(1)}, u32[]{:S(2)}, u32[]{:S(2)}) async-start(bf16[32,128,128]{2,1,0:T(8,128)(2,1)} %bitcast.14), calls=%async_computation.1 | async-start | bytes 2097152 | tf_op jit(solution)/shard_map/all_to_all | solution.py:175
  81.3 1.3 copy.43.t_ref
  83.2 26.9 %shard_map.86 = (bf16[8,256,2048]{2,1,0:T(8,128)(2,1)}, f32[8,1,1024]{2,1,0:T(1,128)}, f32[8,1,1024]{2,1,0:T(1,128)}) custom-call(f32[8,256,1]{2,1,0:T(8,128)} %copy.43.t_ref, f32[1,1024]{1,0:T(1,128)} %bitcast.106, f32[1,1024]{1,0:T(1,128)} %bitcast.105, f32[1,1024]{1,0:T(1,128)} %bitcast.104), custom_call_target="tpu_custom_call" | custom-call | flops 125829120 | bytes 8388608 | tf_op jit(solution)/shard_map/pallas_call | solution.py:78
  111.0 1.5 bitcast_convert_fusion.1.src_ref
  112.5 4.9 %shard_map.88 = f32[2048,128]{1,0:T(8,128)} custom-call(s32[2048]{0:T(1024)} %get-tuple-element.16.idx_ref, f32[4096,128]{1,0:T(8,128)} %bitcast_convert_fusion.1.src_ref), custom_call_target="tpu_custom_call" | custom-call | bytes 2097152 | tf_op jit(solution)/shard_map/pallas_call | solution.py:109
  117.4 1.3 convert_element_type.70
  118.7 9.4 %fusion.41 = f32[8,2048,128]{2,1,0:T(8,128)} fusion(bf16[8,256,2048]{2,1,0:T(8,128)(2,1)} %get-tuple-element.5, bf16[8,256,128]{2,1,0:T(8,128)(2,1)S(1)} %bitcast.85), kind=kOutput, calls=%fused_computation.98 | convolution fusion | flops 1073741824 | bytes 17301504 | tf_op jit(solution)/shard_map/fio,fic->foc/dot_general | solution.py:123
  128.0 9.5 %multiply_convert_fusion.3 = (bf16[8,1024,128]{2,1,0:T(8,128)(2,1)S(1)}, bf16[8,1024,128]{2,1,0:T(8,128)(2,1)}) fusion(f32[8,1024]{1,0:T(8,128)S(1)} %get-tuple-element.23, f32[8,2048,128]{2,1,0:T(8,128)} %fusion.41, f32[8,1024]{1,0:T(8,128)S(1)} %get-tuple-element.22), kind=kOutput, calls=%fused_computation.18 | output fusion | flops 14684158 | bytes 21102592 | tf_op jit(solution)/shard_map/div | solution.py:133
  137.5 6.3 %fusion.2 = f32[8,256,128]{2,1,0:T(8,128)S(1)} fusion(bf16[8,256,2048]{2,1,0:T(8,128)(2,1)} %get-tuple-element.5, bf16[8,1024,128]{2,1,0:T(8,128)(2,1)} %get-tuple-element.15, bf16[8,1024,128]{2,1,0:T(8,128)(2,1)S(1)} %get-tuple-element.14), kind=kOutput, calls=%fused_computation.5 | convolution fusion | flops 1082130432 | bytes 13631488 | tf_op jit(solution)/shard_map/fio,foc->fic/dot_general | solution.py:135
  143.9 1.1 concatenate.22.src_ref
  145.0 7.0 %shard_map.89 = f32[4096,128]{1,0:T(8,128)} custom-call(s32[4096]{0:T(1024)} %get-tuple-element.8.idx_ref, f32[2056,128]{1,0:T(8,128)} %concatenate.22.src_ref), custom_call_target="tpu_custom_call" | custom-call | bytes 4194304 | tf_op jit(solution)/shard_map/pallas_call | solution.py:109
  152.0 2.8 convert_element_type.71
  154.8 7.4 %all-to-all-start.2 = ((bf16[32,128,128]{2,1,0:T(8,128)(2,1)}), bf16[32,128,128]{2,1,0:T(8,128)(2,1)S(1)}, u32[]{:S(2)}, u32[]{:S(2)}) async-start(bf16[32,128,128]{2,1,0:T(8,128)(2,1)} %bitcast.18), calls=%async_computation.2 | async-start | bytes 2097152 | tf_op jit(solution)/shard_map/all_to_all | solution.py:182
  162.2 16.9 %all-to-all-done.2 = bf16[32,128,128]{2,1,0:T(8,128)(2,1)S(1)} async-done(((bf16[32,128,128]{2,1,0:T(8,128)(2,1)}), bf16[32,128,128]{2,1,0:T(8,128)(2,1)S(1)}, u32[]{:S(2)}, u32[]{:S(2)}) %all-to-all-start.2) | async-done | bytes 1048608 | tf_op jit(solution)/shard_map/all_to_all | solution.py:182
  179.1 23.8 %scatter_custom_fusion.1 = f32[4096,128]{1,0:T(8,128)} fusion(s32[4096]{0:T(1024)S(1)} %bitcast.107, bf16[4096,128]{1,0:T(8,128)(2,1)S(1)} %bitcast.84, f32[]{:T(128)} %constant.59.clone.1), kind=kCustom, calls=%fused_computation.35 | custom fusion | flops 1048576 | bytes 3145732 | tf_op jit(solution)/shard_map/scatter-add | solution.py:188
  202.9 1.9 reshape.340
  204.8 4.1 %convolution_bitcast_fusion = f32[4,512,256]{1,2,0:T(8,128)} fusion(bf16[4,512,512]{2,1,0:T(8,128)(2,1)} %all-gather.2.cloned.1.call-done, f32[4,512,256]{2,1,0:T(8,128)S(1)} %reshape.340, bf16[4,512,256]{2,1,0:T(8,128)(2,1)S(1)} %copy-done, pred[4,512]{1,0:T(4,128)(4,1)S(1)} %iota_compare_fusion.2), kind=kOutput, calls=%fused_computation.38 | convolution fusion | flops 538968064 | bytes 7342080 | tf_op jit(solution)/shard_map/sij,sjc->sic/dot_general | solution.py:171
  208.8 3.0 copy.48
  211.8 2.6 reshape.341
  214.4 3.1 concatenate.23.src_ref
  217.5 7.4 %shard_map.90 = f32[4096,128]{1,0:T(8,128)} custom-call(s32[4096]{0:T(1024)} %bitcast.91, f32[4104,128]{1,0:T(8,128)} %concatenate.23.src_ref), custom_call_target="tpu_custom_call" | custom-call | bytes 4194304 | tf_op jit(solution)/shard_map/pallas_call | solution.py:109
  224.9 1.7 convert_element_type.75
  226.6 20.7 %all_to_all.29 = bf16[32,128,128]{2,1,0:T(8,128)(2,1)S(1)} all-to-all(bf16[32,128,128]{2,1,0:T(8,128)(2,1)S(1)} %bitcast.83), channel_id=1, replica_groups=mesh['tm'=32,'sky'=8] {'tm'}, dimensions={0} | all-to-all | bytes 2097152 | tf_op jit(solution)/shard_map/all_to_all | solution.py:175
  247.2 1.5 bitcast_convert_fusion.src_ref
  248.8 4.9 %shard_map.91 = f32[2048,128]{1,0:T(8,128)} custom-call(s32[2048]{0:T(1024)} %get-tuple-element.16.idx_ref, f32[4096,128]{1,0:T(8,128)} %bitcast_convert_fusion.src_ref), custom_call_target="tpu_custom_call" | custom-call | bytes 2097152 | tf_op jit(solution)/shard_map/pallas_call | solution.py:109
  253.7 1.3 convert_element_type.78
  254.9 6.1 %fusion.42 = f32[8,2048,128]{2,1,0:T(8,128)S(1)} fusion(bf16[8,256,2048]{2,1,0:T(8,128)(2,1)} %get-tuple-element.5, bf16[8,256,128]{2,1,0:T(8,128)(2,1)S(1)} %bitcast.86), kind=kOutput, calls=%fused_computation.99 | convolution fusion | flops 1073741824 | bytes 17301504 | tf_op jit(solution)/shard_map/fio,fic->foc/dot_general | solution.py:123
  261.1 3.0 fusion.40
  264.6 3.1 multiply_convert_fusion.1
  267.7 2.3 fusion.6
  271.1 7.0 %shard_map.92 = f32[4096,128]{1,0:T(8,128)} custom-call(s32[4096]{0:T(1024)} %get-tuple-element.8.idx_ref, f32[2056,128]{1,0:T(8,128)} %concatenate.25.src_ref), custom_call_target="tpu_custom_call" | custom-call | bytes 4194304 | tf_op jit(solution)/shard_map/pallas_call | solution.py:109
  278.1 2.7 convert_element_type.79
  280.9 4.4 %all-to-all-start.4 = ((bf16[32,128,128]{2,1,0:T(8,128)(2,1)}), bf16[32,128,128]{2,1,0:T(8,128)(2,1)}, u32[]{:S(2)}, u32[]{:S(2)}) async-start(bf16[32,128,128]{2,1,0:T(8,128)(2,1)} %bitcast.82), calls=%async_computation.4 | async-start | bytes 2097152 | tf_op jit(solution)/shard_map/all_to_all | solution.py:182
  285.9 16.4 %all-to-all-done.4 = bf16[32,128,128]{2,1,0:T(8,128)(2,1)} async-done(((bf16[32,128,128]{2,1,0:T(8,128)(2,1)}), bf16[32,128,128]{2,1,0:T(8,128)(2,1)}, u32[]{:S(2)}, u32[]{:S(2)}) %all-to-all-start.4) | async-done | bytes 1048608 | tf_op jit(solution)/shard_map/all_to_all | solution.py:182
  302.3 24.2 %scatter_custom_fusion.2 = f32[4096,128]{1,0:T(8,128)} fusion(s32[4096]{0:T(1024)S(1)} %bitcast.108, bf16[4096,128]{1,0:T(8,128)(2,1)} %bitcast.30, f32[]{:T(128)} %constant.59.clone.1), kind=kCustom, calls=%fused_computation.33 | custom fusion | flops 1048576 | bytes 3145732 | tf_op jit(solution)/shard_map/scatter-add | solution.py:188
  326.4 2.9 reshape.346
  329.3 3.2 fusion.18
  (53 shorter events, 11.3 us)
Async XLA Ops:
  7.2 43.9 %all-gather.2.cloned.1.call-start = ((), (), s32[]{:S(2)}) async-start(), calls=%async_computation.5 | async-start | bytes 2359296 | tf_op jit(solution)/shard_map/all_gather | solution.py:168
  29.1 10.9 %copy-start.6 = (s32[4]{0:T(128)S(1)}, s32[4]{0:T(128)}, u32[]{:S(2)}) copy-start(s32[4]{0:T(128)} %param.8) | copy-start | bytes 52
  29.1 22.0 %copy-start = (bf16[4,512,256]{2,1,0:T(8,128)(2,1)S(1)}, bf16[4,512,256]{2,1,0:T(8,128)(2,1)}, u32[]{:S(2)}) copy-start(bf16[4,512,256]{2,1,0:T(8,128)(2,1)} %param.7) | copy-start | bytes 3145732
  31.4 27.3 %all-to-all-start = ((s32[32,1,128]{2,1,0:T(1,128)}), s32[32,1,128]{2,1,0:T(1,128)S(1)}, u32[]{:S(2)}, u32[]{:S(2)}) async-start(s32[32,1,128]{2,1,0:T(1,128)} %bitcast.5), calls=%async_computation | async-start | bytes 32768 | tf_op jit(solution)/shard_map/all_to_all | solution.py:163
  58.7 0.6 copy-start.1
  59.3 21.4 %copy-start.5 = (s32[1024]{0:T(1024)S(1)}, s32[1024]{0:T(1024)}, u32[]{:S(2)}) copy-start(s32[1024]{0:T(1024)} %param.12) | copy-start | bytes 12292
  59.3 22.0 %copy-start.3 = (s32[8,256]{1,0:T(8,128)S(1)}, s32[8,256]{1,0:T(8,128)}, u32[]{:S(2)}) copy-start(s32[8,256]{1,0:T(8,128)} %param.10) | copy-start | bytes 24580
  59.3 22.0 %copy-start.4 = (s32[8,256]{1,0:T(8,128)S(1)}, s32[8,256]{1,0:T(8,128)}, u32[]{:S(2)}) copy-start(s32[8,256]{1,0:T(8,128)} %param.11) | copy-start | bytes 24580
  69.4 41.5 %all-to-all-start.1 = ((bf16[32,128,128]{2,1,0:T(8,128)(2,1)}), bf16[32,128,128]{2,1,0:T(8,128)(2,1)S(1)}, u32[]{:S(2)}, u32[]{:S(2)}) async-start(bf16[32,128,128]{2,1,0:T(8,128)(2,1)} %bitcast.14), calls=%async_computation.1 | async-start | bytes 2097152 | tf_op jit(solution)/shard_map/all_to_all | solution.py:175
  145.0 17.2 %copy-start.2 = (s32[32,1,128]{2,1,0:T(1,128)S(1)}, s32[32,1,128]{2,1,0:T(1,128)}, u32[]{:S(2)}) copy-start(s32[32,1,128]{2,1,0:T(1,128)} %copy-done.1) | copy-start | bytes 49156
  154.8 24.3 %all-to-all-start.2 = ((bf16[32,128,128]{2,1,0:T(8,128)(2,1)}), bf16[32,128,128]{2,1,0:T(8,128)(2,1)S(1)}, u32[]{:S(2)}, u32[]{:S(2)}) async-start(bf16[32,128,128]{2,1,0:T(8,128)(2,1)} %bitcast.18), calls=%async_computation.2 | async-start | bytes 2097152 | tf_op jit(solution)/shard_map/all_to_all | solution.py:182
  264.0 3.7 %slice-start = ((s8[8388608]{0:T(1024)(128)(4,1)}), s8[4194304]{0:T(1024)(128)(4,1)S(1)}, s32[]{:S(2)}) async-start(s8[8388608]{0:T(1024)(128)(4,1)} %bitcast.80), calls=%async_computation.6 | async-start | bytes 8388608
  264.6 3.1 slice-start.1
  280.9 21.4 %all-to-all-start.4 = ((bf16[32,128,128]{2,1,0:T(8,128)(2,1)}), bf16[32,128,128]{2,1,0:T(8,128)(2,1)}, u32[]{:S(2)}, u32[]{:S(2)}) async-start(bf16[32,128,128]{2,1,0:T(8,128)(2,1)} %bitcast.82), calls=%async_computation.4 | async-start | bytes 2097152 | tf_op jit(solution)/shard_map/all_to_all | solution.py:182
Sparse Core Ops, SparseCore 0:
  9.8 41.2 all-gather.1

commit v4 on v3

--- a/solution.py
+++ b/solution.py
@@ -118,6 +118,62 @@
 
 def with_zero_rows(flat):
     return jnp.concatenate([flat, jnp.zeros((8, flat.shape[1]), flat.dtype)], axis=0)
+
+
+def a2a_kernel(x_ref, out_ref, held, send_sem, recv_sem):
+    n = x_ref.shape[0]
+    me = lax.axis_index("tm")
+    sky = lax.axis_index("sky")
+    barrier = pltpu.get_barrier_semaphore()
+
+    def greet(k, carry):
+        peer = lax.rem(me + k, n)
+        pl.semaphore_signal(barrier, inc=1, device_id=(peer, sky), device_id_type=pl.DeviceIdType.MESH)
+        return carry
+
+    lax.fori_loop(1, n, greet, 0)
+    pl.semaphore_wait(barrier, n - 1)
+
+    def copy(k):
+        peer = lax.rem(me + k, n)
+        return pltpu.make_async_remote_copy(
+            src_ref=x_ref.at[peer],
+            dst_ref=held.at[me],
+            send_sem=send_sem.at[k],
+            recv_sem=recv_sem.at[k],
+            device_id=(peer, sky),
+            device_id_type=pl.DeviceIdType.MESH,
+        )
+
+    def start(k, carry):
+        copy(k).start()
+        return carry
+
+    lax.fori_loop(1, n, start, 0)
+    held[pl.ds(me, 1)] = x_ref[pl.ds(me, 1)]
+
+    def finish(k, carry):
+        copy(k).wait()
+        return carry
+
+    lax.fori_loop(1, n, finish, 0)
+    out_ref[...] = held[...].astype(out_ref.dtype)
+
+
+def tm_all_to_all(x, out_dtype, collective_id):
+    n, rows, width = x.shape
+    return pl.pallas_call(
+        a2a_kernel,
+        in_specs=[pl.BlockSpec(memory_space=pltpu.VMEM)],
+        out_specs=pl.BlockSpec(memory_space=pltpu.VMEM),
+        out_shape=jax.ShapeDtypeStruct((n, rows, width), out_dtype),
+        scratch_shapes=[
+            pltpu.VMEM((n, rows, width), x.dtype),
+            pltpu.SemaphoreType.DMA((n,)),
+            pltpu.SemaphoreType.DMA((n,)),
+        ],
+        compiler_params=pltpu.CompilerParams(collective_id=collective_id, has_side_effects=True),
+    )(x)
 
 def fit_groups(basis, observed, norm_cos, norm_sin, nper):
     corr = jnp.einsum("fio,fic->foc", basis, observed, preferred_element_type=jnp.float32)
@@ -172,16 +228,16 @@
             "sij,sjc->sic", attitude_all, masked, preferred_element_type=jnp.float32
         )
         picked = row_gather(with_zero_rows(white.reshape(-1, SRC_GROUP)), asked)
-        arrived = lax.all_to_all(
+        arrived = tm_all_to_all(
             picked.astype(jnp.bfloat16).reshape(tm_count, capacity, SRC_GROUP),
-            "tm", split_axis=0, concat_axis=0, tiled=True)
-        observed = row_gather(arrived.reshape(-1, SRC_GROUP).astype(jnp.float32), slot_of)
+            jnp.float32, 1 + 2 * iteration)
+        observed = row_gather(arrived.reshape(-1, SRC_GROUP), slot_of)
         observed = observed.astype(jnp.bfloat16).reshape(sched_dev, obs, SRC_GROUP)
         model, evidence = fit_groups(basis, observed, norm_cos, norm_sin, nper)
         outgoing = row_gather(with_zero_rows(model.reshape(requests, SRC_GROUP)), inverse)
-        returned = lax.all_to_all(
+        returned = tm_all_to_all(
             outgoing.astype(jnp.bfloat16).reshape(tm_count, capacity, SRC_GROUP),
-            "tm", split_axis=0, concat_axis=0, tiled=True)
+            jnp.float32, 2 + 2 * iteration)
         placed = (
             jnp.zeros((empty_row, SRC_GROUP), jnp.float32)
             .at[asked]

time: 341 us -> 348 us (1.021)
  Pallas kernels: 65.5 us -> 163 us
  waiting for transfers between devices: 44.9 us -> 0.7 us
  starting transfers between devices: 31.7 us -> 8.63 us
  blocking collectives: 20.7 us -> 0 us
    pallas_call x0 -> x4, Pallas kernels: none -> 97.5 us  [tm_all_to_all(): pl.pallas_call(a2a_kernel, in_specs=[pl.BlockSpec(memory_space=pltpu.VMEM...]
    all_to_all x3 -> x0, waiting for transfers between devices: 33.2 us -> none  [the longest x2 33.2 us: on_device(): lax.all_to_all(outgoing.astype(jnp.bfloat16).reshape(tm_count, capacity,...]
    all_to_all x3 -> x0, starting transfers between devices: 23.1 us -> none  [the longest x2 11.8 us: on_device(): lax.all_to_all(outgoing.astype(jnp.bfloat16).reshape(tm_count, capacity,...]
    all_to_all x1 -> x0, blocking collectives: 20.7 us -> none  [on_device(): lax.all_to_all(picked.astype(jnp.bfloat16).reshape(tm_count, capacity, SR...]
    all_gather x1, waiting for transfers between devices: 11 us -> 0.02 us  [on_device(): attitude_all = lax.all_gather(attitude, 'sky', axis=1, tiled=True)]
  transfers between devices with their start and end apart: 5 -> 2, of which waited for: 3 -> 0; matrix products, arithmetic and copies ran while one was open for 10% -> 8% of each run, Pallas kernels for 8% -> 8%
where the time goes in v4:
time: 348 us; the launch traced here: 346 us
  Pallas kernels  163 us (47%)
  other arithmetic  92.9 us (27%)
  local copies, waits for them, and re-layouts  35.9 us (10%)
  matrix products  30.9 us (9%)
  between operations  14.3 us (4%)
  starting transfers between devices  8.63 us (2%)
    pallas_call x4, Pallas kernels, tm_all_to_all(): pl.pallas_call(a2a_kernel, in_specs=[pl.BlockSpec(memory_space=pltpu.VMEM...  97.5 us
    scatter-add x2, other arithmetic, on_device(): placed = jnp.zeros((empty_row, SRC_GROUP), jnp.float32).at[asked].add(ret...  48.1 us
    pallas_call x6, Pallas kernels, row_gather(): pl.pallas_call(gather_kernel, in_specs=[pl.BlockSpec(memory_space=pltpu.S...  38.3 us
    pallas_call x1, Pallas kernels, basis_and_norms(): pl.pallas_call(basis_kernel, grid=(plans,), in_specs=[pl.BlockSpec((None,...  26.9 us
    dot_general x2, matrix products, fit_groups(): jnp.einsum('fio,fic->foc', basis, observed, preferred_element_type=jnp.fl...  15.5 us
    another operation x4, other arithmetic  12.5 us
    div x1, other arithmetic, fit_groups(): share = expo / total[:, None, :]  9.54 us
    dot_general x2, matrix products, fit_groups(): jnp.einsum('fio,foc->fic', basis, coeff, preferred_element_type=jnp.float32)  8.64 us
  transfers between devices with their start and end apart: 2, of which 0 were waited for; matrix products, arithmetic and copies ran while one was open for 8% of the time, Pallas kernels for 8%

profile of v4, /device:TPU:1, one launch (start us, length us, event | category | flops | bytes accessed | tf_op | source)
XLA Modules:
  0.0 346.1 jit_solution(41357859634787078)
XLA Ops:
  8.7 0.7 copy.57
  10.1 0.7 copy.60
  10.9 9.1 %reduce-window.6 = s32[32,16,128]{2,1,0:T(8,128)S(1)} reduce-window(s32[32,16,128]{2,1,0:T(8,128)S(1)} %fusion.26, s32[]{:T(128)} %constant.61.clone.1), window={size=1x1x128 pad=0_0x0_0x127_0}, to_apply=%region_0.1 | reduce-window | flops 8323072 | bytes 524292 | tf_op jit(solution)/shard_map/reduce-window
  21.9 0.8 broadcast_in_dim.20
  22.7 6.4 %scatter_fusion = s32[4096,2]{1,0:T(8,128)S(1)} fusion(s32[4096,2]{1,0:T(8,128)S(1)} %broadcast_in_dim.20, s32[2048]{0:T(1024)S(1)} %bitcast.97, s32[2048,2]{1,0:T(8,128)S(1)} %copy.41), kind=kCustom, calls=%fused_computation | custom fusion | bytes 57344 | tf_op jit(solution)/shard_map/scatter | solution.py:215
  29.1 2.3 slice_reduce_fusion
  31.4 8.6 %all-to-all-start = ((s32[32,1,128]{2,1,0:T(1,128)}), s32[32,1,128]{2,1,0:T(1,128)S(1)}, u32[]{:S(2)}, u32[]{:S(2)}) async-start(s32[32,1,128]{2,1,0:T(1,128)} %bitcast.5), calls=%async_computation | async-start | bytes 32768 | tf_op jit(solution)/shard_map/all_to_all | solution.py:219
  40.7 1.3 copy.43.t_ref
  42.6 26.9 %shard_map.86 = (bf16[8,256,2048]{2,1,0:T(8,128)(2,1)}, f32[8,1,1024]{2,1,0:T(1,128)}, f32[8,1,1024]{2,1,0:T(1,128)}) custom-call(f32[8,256,1]{2,1,0:T(8,128)} %copy.43.t_ref, f32[1,1024]{1,0:T(1,128)} %bitcast.105, f32[1,1024]{1,0:T(1,128)} %bitcast.104, f32[1,1024]{1,0:T(1,128)} %bitcast.103), custom_call_target="tpu_custom_call" | custom-call | flops 125829120 | bytes 8388608 | tf_op jit(solution)/shard_map/pallas_call | solution.py:78
  69.5 0.8 copy_bitcast_fusion
  70.5 2.7 convolution_bitcast_fusion.1
  73.2 1.8 copy.45
  75.0 1.6 reshape.335
  76.6 1.5 concatenate.20.src_ref
  78.1 7.4 %shard_map.87 = f32[4096,128]{1,0:T(8,128)} custom-call(s32[4096]{0:T(1024)} %bitcast.89, f32[4104,128]{1,0:T(8,128)} %concatenate.20.src_ref), custom_call_target="tpu_custom_call" | custom-call | bytes 4194304 | tf_op jit(solution)/shard_map/pallas_call | solution.py:109
  85.5 2.7 convert_element_type.45
  88.2 23.0 %shard_map.88 = f32[32,128,128]{2,1,0:T(8,128)} custom-call(bf16[32,128,128]{2,1,0:T(8,128)(2,1)} %bitcast.78), custom_call_target="tpu_custom_call" | custom-call | tf_op jit(solution)/shard_map/pallas_call | solution.py:165
  111.2 4.8 %shard_map.89 = f32[2048,128]{1,0:T(8,128)} custom-call(s32[2048]{0:T(1024)} %get-tuple-element.16.idx_ref, f32[4096,128]{1,0:T(8,128)} %bitcast.76), custom_call_target="tpu_custom_call" | custom-call | bytes 2097152 | tf_op jit(solution)/shard_map/pallas_call | solution.py:109
  116.0 1.3 convert_element_type.46
  117.3 9.3 %fusion.39 = f32[8,2048,128]{2,1,0:T(8,128)} fusion(bf16[8,256,2048]{2,1,0:T(8,128)(2,1)} %get-tuple-element.5, bf16[8,256,128]{2,1,0:T(8,128)(2,1)S(1)} %bitcast.82), kind=kOutput, calls=%fused_computation.94 | convolution fusion | flops 1073741824 | bytes 17301504 | tf_op jit(solution)/shard_map/fio,fic->foc/dot_general | solution.py:179
  126.6 9.5 %multiply_convert_fusion.3 = (bf16[8,1024,128]{2,1,0:T(8,128)(2,1)S(1)}, bf16[8,1024,128]{2,1,0:T(8,128)(2,1)}) fusion(f32[8,1024]{1,0:T(8,128)S(1)} %get-tuple-element.23, f32[8,2048,128]{2,1,0:T(8,128)} %fusion.39, f32[8,1024]{1,0:T(8,128)S(1)} %get-tuple-element.22), kind=kOutput, calls=%fused_computation.18 | output fusion | flops 14684158 | bytes 21102592 | tf_op jit(solution)/shard_map/div | solution.py:189
  136.2 6.3 %fusion.2 = f32[8,256,128]{2,1,0:T(8,128)S(1)} fusion(bf16[8,256,2048]{2,1,0:T(8,128)(2,1)} %get-tuple-element.5, bf16[8,1024,128]{2,1,0:T(8,128)(2,1)} %get-tuple-element.15, bf16[8,1024,128]{2,1,0:T(8,128)(2,1)S(1)} %get-tuple-element.14), kind=kOutput, calls=%fused_computation.5 | convolution fusion | flops 1082130432 | bytes 13631488 | tf_op jit(solution)/shard_map/fio,foc->fic/dot_general | solution.py:191
  142.5 1.1 concatenate.22.src_ref
  143.6 7.0 %shard_map.90 = f32[4096,128]{1,0:T(8,128)} custom-call(s32[4096]{0:T(1024)} %get-tuple-element.8.idx_ref, f32[2056,128]{1,0:T(8,128)} %concatenate.22.src_ref), custom_call_target="tpu_custom_call" | custom-call | bytes 4194304 | tf_op jit(solution)/shard_map/pallas_call | solution.py:109
  150.6 2.7 convert_element_type.47
  153.3 26.5 %shard_map.91 = f32[32,128,128]{2,1,0:T(8,128)} custom-call(bf16[32,128,128]{2,1,0:T(8,128)(2,1)} %bitcast.79), custom_call_target="tpu_custom_call" | custom-call | tf_op jit(solution)/shard_map/pallas_call | solution.py:165
  179.8 24.1 %scatter_custom_fusion.1 = f32[4096,128]{1,0:T(8,128)} fusion(s32[4096]{0:T(1024)S(1)} %bitcast.106, f32[4096,128]{1,0:T(8,128)} %bitcast.85, f32[]{:T(128)} %constant.59.clone.1), kind=kCustom, calls=%fused_computation.41 | custom fusion | flops 524288 | bytes 2097664 | tf_op jit(solution)/shard_map/scatter-add | solution.py:244
  203.9 1.9 reshape.342
  205.8 4.1 %convolution_bitcast_fusion = f32[4,512,256]{1,2,0:T(8,128)} fusion(bf16[4,512,512]{2,1,0:T(8,128)(2,1)} %all-gather.2.cloned.1.call-done, f32[4,512,256]{2,1,0:T(8,128)S(1)} %reshape.342, bf16[4,512,256]{2,1,0:T(8,128)(2,1)S(1)} %copy-done, pred[4,512]{1,0:T(4,128)(4,1)S(1)} %iota_compare_fusion.2), kind=kOutput, calls=%fused_computation.34 | convolution fusion | flops 538968064 | bytes 7342080 | tf_op jit(solution)/shard_map/sij,sjc->sic/dot_general | solution.py:227
  209.8 3.0 copy.48
  212.8 2.6 reshape.343
  215.4 3.1 concatenate.23.src_ref
  218.5 7.4 %shard_map.92 = f32[4096,128]{1,0:T(8,128)} custom-call(s32[4096]{0:T(1024)} %bitcast.90, f32[4104,128]{1,0:T(8,128)} %concatenate.23.src_ref), custom_call_target="tpu_custom_call" | custom-call | bytes 4194304 | tf_op jit(solution)/shard_map/pallas_call | solution.py:109
  225.9 2.7 convert_element_type.49
  228.6 23.5 %shard_map.93 = f32[32,128,128]{2,1,0:T(8,128)} custom-call(bf16[32,128,128]{2,1,0:T(8,128)(2,1)} %bitcast.80), custom_call_target="tpu_custom_call" | custom-call | tf_op jit(solution)/shard_map/pallas_call | solution.py:165
  252.1 4.8 %shard_map.94 = f32[2048,128]{1,0:T(8,128)} custom-call(s32[2048]{0:T(1024)} %get-tuple-element.16.idx_ref, f32[4096,128]{1,0:T(8,128)} %bitcast.77), custom_call_target="tpu_custom_call" | custom-call | bytes 2097152 | tf_op jit(solution)/shard_map/pallas_call | solution.py:109
  256.9 1.3 convert_element_type.50
  258.2 6.1 %fusion.40 = f32[8,2048,128]{2,1,0:T(8,128)S(1)} fusion(bf16[8,256,2048]{2,1,0:T(8,128)(2,1)} %get-tuple-element.5, bf16[8,256,128]{2,1,0:T(8,128)(2,1)S(1)} %bitcast.83), kind=kOutput, calls=%fused_computation.95 | convolution fusion | flops 1073741824 | bytes 17301504 | tf_op jit(solution)/shard_map/fio,fic->foc/dot_general | solution.py:179
  264.3 3.0 fusion.38
  267.8 3.1 multiply_convert_fusion.1
  271.5 2.3 fusion.6
  273.9 1.1 concatenate.25.src_ref
  274.9 7.0 %shard_map.95 = f32[4096,128]{1,0:T(8,128)} custom-call(s32[4096]{0:T(1024)} %get-tuple-element.8.idx_ref, f32[2056,128]{1,0:T(8,128)} %concatenate.25.src_ref), custom_call_target="tpu_custom_call" | custom-call | bytes 4194304 | tf_op jit(solution)/shard_map/pallas_call | solution.py:109
  281.9 2.7 convert_element_type.51
  284.6 24.4 %shard_map.96 = f32[32,128,128]{2,1,0:T(8,128)} custom-call(bf16[32,128,128]{2,1,0:T(8,128)(2,1)} %bitcast.81), custom_call_target="tpu_custom_call" | custom-call | tf_op jit(solution)/shard_map/pallas_call | solution.py:165
  309.1 24.1 %scatter_custom_fusion.2 = f32[4096,128]{1,0:T(8,128)} fusion(s32[4096]{0:T(1024)S(1)} %bitcast.107, f32[4096,128]{1,0:T(8,128)} %bitcast.84, f32[]{:T(128)} %constant.59.clone.1), kind=kCustom, calls=%fused_computation.39 | custom fusion | flops 524288 | bytes 2097664 | tf_op jit(solution)/shard_map/scatter-add | solution.py:244
  333.1 2.9 reshape.350
  336.0 3.2 fusion.14
  (46 shorter events, 6.7 us)
Async XLA Ops:
  7.2 63.3 %all-gather.2.cloned.1.call-start = ((), (), s32[]{:S(2)}) async-start(), calls=%async_computation.1 | async-start | bytes 2359296 | tf_op jit(solution)/shard_map/all_gather | solution.py:224
  29.1 11.0 %copy-start.4 = (s32[1024]{0:T(1024)S(1)}, s32[1024]{0:T(1024)}, u32[]{:S(2)}) copy-start(s32[1024]{0:T(1024)} %param.12) | copy-start | bytes 12292
  29.1 11.6 %copy-start.2 = (s32[8,256]{1,0:T(8,128)S(1)}, s32[8,256]{1,0:T(8,128)}, u32[]{:S(2)}) copy-start(s32[8,256]{1,0:T(8,128)} %param.10) | copy-start | bytes 24580
  29.1 11.6 %copy-start.3 = (s32[8,256]{1,0:T(8,128)S(1)}, s32[8,256]{1,0:T(8,128)}, u32[]{:S(2)}) copy-start(s32[8,256]{1,0:T(8,128)} %param.11) | copy-start | bytes 24580
  29.1 41.2 %copy-start.5 = (s32[4]{0:T(128)S(1)}, s32[4]{0:T(128)}, u32[]{:S(2)}) copy-start(s32[4]{0:T(128)} %param.8) | copy-start | bytes 52
  29.1 41.4 %copy-start = (bf16[4,512,256]{2,1,0:T(8,128)(2,1)S(1)}, bf16[4,512,256]{2,1,0:T(8,128)(2,1)}, u32[]{:S(2)}) copy-start(bf16[4,512,256]{2,1,0:T(8,128)(2,1)} %param.7) | copy-start | bytes 3145732
  31.4 39.0 %all-to-all-start = ((s32[32,1,128]{2,1,0:T(1,128)}), s32[32,1,128]{2,1,0:T(1,128)S(1)}, u32[]{:S(2)}, u32[]{:S(2)}) async-start(s32[32,1,128]{2,1,0:T(1,128)} %bitcast.5), calls=%async_computation | async-start | bytes 32768 | tf_op jit(solution)/shard_map/all_to_all | solution.py:219
  70.4 4.6 %copy-start.1 = (s32[32,1,128]{2,1,0:T(1,128)}, s32[32,1,128]{2,1,0:T(1,128)S(1)}, u32[]{:S(2)}) copy-start(s32[32,1,128]{2,1,0:T(1,128)S(1)} %all-to-all-done) | copy-start | bytes 49156
  267.3 4.3 %slice-start = ((s8[8388608]{0:T(1024)(128)(4,1)}), s8[4194304]{0:T(1024)(128)(4,1)S(1)}, s32[]{:S(2)}) async-start(s8[8388608]{0:T(1024)(128)(4,1)} %bitcast.74), calls=%async_computation.2 | async-start | bytes 8388608
  267.8 3.7 %slice-start.1 = ((s8[8388608]{0:T(1024)(128)(4,1)}), s8[4194304]{0:T(1024)(128)(4,1)S(1)}, s32[]{:S(2)}) async-start(s8[8388608]{0:T(1024)(128)(4,1)} %bitcast.74), calls=%async_computation.3 | async-start | bytes 8388608
Sparse Core Ops, SparseCore 0:
  9.8 41.2 all-gather.1

commit v5 on v4

--- a/solution.py
+++ b/solution.py
@@ -174,6 +174,42 @@
         ],
         compiler_params=pltpu.CompilerParams(collective_id=collective_id, has_side_effects=True),
     )(x)
+
+
+STREAMS = 4
+SUNROLL = 2
+
+def scatter_add_kernel(idx_ref, src_ref, out_ref, acc_ref):
+    rows = src_ref.shape[0]
+    streams = acc_ref.shape[0]
+    acc_ref[...] = jnp.zeros_like(acc_ref)
+
+    def body(step, carry):
+        base = step * streams
+        for s in range(streams):
+            r = base + s
+            i = idx_ref[r]
+            acc_ref[s, pl.ds(i, 1), :] = acc_ref[s, pl.ds(i, 1), :] + src_ref[pl.ds(r, 1), :]
+        return carry
+
+    lax.fori_loop(0, rows // streams, body, 0, unroll=SUNROLL)
+    total = acc_ref[0]
+    for s in range(1, streams):
+        total = total + acc_ref[s]
+    out_ref[...] = total[: out_ref.shape[0]]
+
+
+def scatter_add(src, idx, out_rows):
+    rows, width = src.shape
+    pad = out_rows + 8
+    return pl.pallas_call(
+        scatter_add_kernel,
+        in_specs=[pl.BlockSpec(memory_space=pltpu.SMEM), pl.BlockSpec(memory_space=pltpu.VMEM)],
+        out_specs=pl.BlockSpec(memory_space=pltpu.VMEM),
+        out_shape=jax.ShapeDtypeStruct((out_rows, width), jnp.float32),
+        scratch_shapes=[pltpu.VMEM((STREAMS, pad, width), jnp.float32)],
+        cost_estimate=pl.CostEstimate(flops=rows * width, transcendentals=0, bytes_accessed=(rows + out_rows) * width * 4),
+    )(idx, src)
 
 def fit_groups(basis, observed, norm_cos, norm_sin, nper):
     corr = jnp.einsum("fio,fic->foc", basis, observed, preferred_element_type=jnp.float32)
@@ -228,9 +264,12 @@
             "sij,sjc->sic", attitude_all, masked, preferred_element_type=jnp.float32
         )
         picked = row_gather(with_zero_rows(white.reshape(-1, SRC_GROUP)), asked)
-        arrived = tm_all_to_all(
-            picked.astype(jnp.bfloat16).reshape(tm_count, capacity, SRC_GROUP),
-            jnp.float32, 1 + 2 * iteration)
+        outbound = picked.astype(jnp.bfloat16).reshape(tm_count, capacity, SRC_GROUP)
+        if iteration == 0:
+            arrived = lax.all_to_all(outbound, "tm", split_axis=0, concat_axis=0, tiled=True)
+            arrived = arrived.astype(jnp.float32)
+        else:
+            arrived = tm_all_to_all(outbound, jnp.float32, 1 + 2 * iteration)
         observed = row_gather(arrived.reshape(-1, SRC_GROUP), slot_of)
         observed = observed.astype(jnp.bfloat16).reshape(sched_dev, obs, SRC_GROUP)
         model, evidence = fit_groups(basis, observed, norm_cos, norm_sin, nper)
@@ -238,11 +277,7 @@
         returned = tm_all_to_all(
             outgoing.astype(jnp.bfloat16).reshape(tm_count, capacity, SRC_GROUP),
             jnp.float32, 2 + 2 * iteration)
-        placed = (
-            jnp.zeros((empty_row, SRC_GROUP), jnp.float32)
-            .at[asked]
-            .add(returned.reshape(-1, SRC_GROUP).astype(jnp.float32), mode="drop")
-        )
+        placed = scatter_add(returned.reshape(-1, SRC_GROUP), asked, empty_row)
         current = current - placed.reshape(seg_dev, slots, width)
     return (current, evidence)
 

time: 348 us -> 330 us (0.948)
  other arithmetic: 92.9 us -> 46.4 us
  starting transfers between devices: 8.63 us -> 19.9 us
  waiting for transfers between devices: 0.7 us -> 11.6 us
  Pallas kernels: 163 us -> 169 us
    scatter-add x2 -> x0, other arithmetic: 48.1 us -> none  [on_device(): placed = jnp.zeros((empty_row, SRC_GROUP), jnp.float32).at[asked].add(ret...]
    pallas_call x0 -> x2, Pallas kernels: none -> 30.3 us  [scatter_add(): pl.pallas_call(scatter_add_kernel, in_specs=[pl.BlockSpec(memory_space=pl...]
    pallas_call x4 -> x3, Pallas kernels: 97.5 us -> 73 us  [tm_all_to_all(): pl.pallas_call(a2a_kernel, in_specs=[pl.BlockSpec(memory_space=pltpu.VMEM...]
    all_to_all x0 -> x1, starting transfers between devices: none -> 11.2 us  [on_device(): lax.all_to_all(outbound, 'tm', split_axis=0, concat_axis=0, tiled=True)]
    all_gather x1, waiting for transfers between devices: 0.02 us -> 11 us  [on_device(): attitude_all = lax.all_gather(attitude, 'sky', axis=1, tiled=True)]
  transfers between devices with their start and end apart: 2 -> 3, of which waited for: 0 -> 1; matrix products, arithmetic and copies ran while one was open for 8% -> 10% of each run, Pallas kernels for 8% -> 8%
where the time goes in v5:
time: 330 us; the launch traced here: 328 us
  Pallas kernels  169 us (51%)
  other arithmetic  46.4 us (14%)
  local copies, waits for them, and re-layouts  36.5 us (11%)
  matrix products  30.9 us (9%)
  starting transfers between devices  19.9 us (6%)
  between operations  14.3 us (4%)
  waiting for transfers between devices  11.6 us (4%)
    pallas_call x3, Pallas kernels, tm_all_to_all(): pl.pallas_call(a2a_kernel, in_specs=[pl.BlockSpec(memory_space=pltpu.VMEM...  73 us
    pallas_call x6, Pallas kernels, row_gather(): pl.pallas_call(gather_kernel, in_specs=[pl.BlockSpec(memory_space=pltpu.S...  38.4 us
    pallas_call x2, Pallas kernels, scatter_add(): pl.pallas_call(scatter_add_kernel, in_specs=[pl.BlockSpec(memory_space=pl...  30.3 us
    pallas_call x1, Pallas kernels, basis_and_norms(): pl.pallas_call(basis_kernel, grid=(plans,), in_specs=[pl.BlockSpec((None,...  26.9 us
    dot_general x2, matrix products, fit_groups(): jnp.einsum('fio,fic->foc', basis, observed, preferred_element_type=jnp.fl...  15.5 us
    another operation x4, other arithmetic  12.5 us
    all_to_all x1, starting transfers between devices, on_device(): lax.all_to_all(outbound, 'tm', split_axis=0, concat_axis=0, tiled=True)  11.2 us
    all_gather x1, waiting for transfers between devices, on_device(): attitude_all = lax.all_gather(attitude, 'sky', axis=1, tiled=True)  11 us
  transfers between devices with their start and end apart: 3, of which 1 were waited for; matrix products, arithmetic and copies ran while one was open for 10% of the time, Pallas kernels for 8%

profile of v5, /device:TPU:1, one launch (start us, length us, event | category | flops | bytes accessed | tf_op | source)
XLA Modules:
  0.0 328.2 jit_solution(5234285823728969642)
XLA Ops:
  10.9 9.1 %reduce-window.6 = s32[32,16,128]{2,1,0:T(8,128)S(1)} reduce-window(s32[32,16,128]{2,1,0:T(8,128)S(1)} %fusion.22, s32[]{:T(128)} %constant.57.clone.1), window={size=1x1x128 pad=0_0x0_0x127_0}, to_apply=%region_0.1 | reduce-window | flops 8323072 | bytes 524292 | tf_op jit(solution)/shard_map/reduce-window
  21.9 0.8 broadcast_in_dim.20
  22.7 6.4 %scatter_fusion = s32[4096,2]{1,0:T(8,128)S(1)} fusion(s32[4096,2]{1,0:T(8,128)S(1)} %broadcast_in_dim.20, s32[2048]{0:T(1024)S(1)} %bitcast.96, s32[2048,2]{1,0:T(8,128)S(1)} %copy.41), kind=kCustom, calls=%fused_computation | custom fusion | bytes 57344 | tf_op jit(solution)/shard_map/scatter | solution.py:251
  29.1 2.3 slice_reduce_fusion
  31.4 8.6 %all-to-all-start = ((s32[32,1,128]{2,1,0:T(1,128)}), s32[32,1,128]{2,1,0:T(1,128)S(1)}, u32[]{:S(2)}, u32[]{:S(2)}) async-start(s32[32,1,128]{2,1,0:T(1,128)} %bitcast.5), calls=%async_computation | async-start | bytes 32768 | tf_op jit(solution)/shard_map/all_to_all | solution.py:255
  40.1 11.0 %all-gather.2.cloned.1.call-done = bf16[4,512,512]{2,1,0:T(8,128)(2,1)} async-done(((bf16[4,64,512]{2,1,0:T(8,128)(2,1)}), bf16[4,512,512]{2,1,0:T(8,128)(2,1)}) %all-gather.2.cloned.1.call-update) | async-done | bytes 2097168 | tf_op jit(solution)/shard_map/all_gather | solution.py:260
  51.0 2.7 convolution_bitcast_fusion.1
  53.7 1.8 copy.45
  55.5 1.6 reshape.305
  57.2 1.5 concatenate.20.src_ref
  59.3 7.4 %shard_map.87 = f32[4096,128]{1,0:T(8,128)} custom-call(s32[4096]{0:T(1024)} %bitcast.86, f32[4104,128]{1,0:T(8,128)} %concatenate.20.src_ref), custom_call_target="tpu_custom_call" | custom-call | bytes 4194304 | tf_op jit(solution)/shard_map/pallas_call | solution.py:109
  66.7 2.8 convert_element_type.46
  69.4 11.2 %all-to-all-start.1 = ((bf16[32,128,128]{2,1,0:T(8,128)(2,1)}), bf16[32,128,128]{2,1,0:T(8,128)(2,1)S(1)}, u32[]{:S(2)}, u32[]{:S(2)}) async-start(bf16[32,128,128]{2,1,0:T(8,128)(2,1)} %bitcast.12), calls=%async_computation.1 | async-start | bytes 2097152 | tf_op jit(solution)/shard_map/all_to_all | solution.py:269
  81.3 1.3 copy.43.t_ref
  83.2 26.9 %shard_map.86 = (bf16[8,256,2048]{2,1,0:T(8,128)(2,1)}, f32[8,1,1024]{2,1,0:T(1,128)}, f32[8,1,1024]{2,1,0:T(1,128)}) custom-call(f32[8,256,1]{2,1,0:T(8,128)} %copy.43.t_ref, f32[1,1024]{1,0:T(1,128)} %bitcast.104, f32[1,1024]{1,0:T(1,128)} %bitcast.103, f32[1,1024]{1,0:T(1,128)} %bitcast.102), custom_call_target="tpu_custom_call" | custom-call | flops 125829120 | bytes 8388608 | tf_op jit(solution)/shard_map/pallas_call | solution.py:78
  110.2 0.8 copy_bitcast_fusion
  111.0 1.5 bitcast_convert_fusion.src_ref
  112.5 4.9 %shard_map.88 = f32[2048,128]{1,0:T(8,128)} custom-call(s32[2048]{0:T(1024)} %get-tuple-element.16.idx_ref, f32[4096,128]{1,0:T(8,128)} %bitcast_convert_fusion.src_ref), custom_call_target="tpu_custom_call" | custom-call | bytes 2097152 | tf_op jit(solution)/shard_map/pallas_call | solution.py:109
  117.4 1.3 convert_element_type.47
  118.7 9.3 %fusion.35 = f32[8,2048,128]{2,1,0:T(8,128)} fusion(bf16[8,256,2048]{2,1,0:T(8,128)(2,1)} %get-tuple-element.5, bf16[8,256,128]{2,1,0:T(8,128)(2,1)S(1)} %bitcast.81), kind=kOutput, calls=%fused_computation.88 | convolution fusion | flops 1073741824 | bytes 17301504 | tf_op jit(solution)/shard_map/fio,fic->foc/dot_general | solution.py:215
  128.0 9.5 %multiply_convert_fusion.3 = (bf16[8,1024,128]{2,1,0:T(8,128)(2,1)S(1)}, bf16[8,1024,128]{2,1,0:T(8,128)(2,1)}) fusion(f32[8,1024]{1,0:T(8,128)S(1)} %get-tuple-element.23, f32[8,2048,128]{2,1,0:T(8,128)} %fusion.35, f32[8,1024]{1,0:T(8,128)S(1)} %get-tuple-element.22), kind=kOutput, calls=%fused_computation.16 | output fusion | flops 14684158 | bytes 21102592 | tf_op jit(solution)/shard_map/div | solution.py:225
  137.5 6.3 %fusion.2 = f32[8,256,128]{2,1,0:T(8,128)S(1)} fusion(bf16[8,256,2048]{2,1,0:T(8,128)(2,1)} %get-tuple-element.5, bf16[8,1024,128]{2,1,0:T(8,128)(2,1)} %get-tuple-element.15, bf16[8,1024,128]{2,1,0:T(8,128)(2,1)S(1)} %get-tuple-element.14), kind=kOutput, calls=%fused_computation.3 | convolution fusion | flops 1082130432 | bytes 13631488 | tf_op jit(solution)/shard_map/fio,foc->fic/dot_general | solution.py:227
  143.9 1.1 concatenate.22.src_ref
  145.0 7.0 %shard_map.89 = f32[4096,128]{1,0:T(8,128)} custom-call(s32[4096]{0:T(1024)} %get-tuple-element.8.idx_ref, f32[2056,128]{1,0:T(8,128)} %concatenate.22.src_ref), custom_call_target="tpu_custom_call" | custom-call | bytes 4194304 | tf_op jit(solution)/shard_map/pallas_call | solution.py:109
  152.0 2.7 convert_element_type.48
  154.7 23.0 %shard_map.90 = f32[32,128,128]{2,1,0:T(8,128)} custom-call(bf16[32,128,128]{2,1,0:T(8,128)(2,1)} %bitcast.78), custom_call_target="tpu_custom_call" | custom-call | tf_op jit(solution)/shard_map/pallas_call | solution.py:165
  177.7 15.1 %shard_map.91 = f32[4096,128]{1,0:T(8,128)} custom-call(s32[4096]{0:T(1024)} %bitcast.87, f32[4096,128]{1,0:T(8,128)} %bitcast.77), custom_call_target="tpu_custom_call" | custom-call | flops 524288 | bytes 4194304 | tf_op jit(solution)/shard_map/pallas_call | solution.py:205
  192.8 1.9 reshape.313
  194.7 4.1 %convolution_bitcast_fusion = f32[4,512,256]{1,2,0:T(8,128)} fusion(bf16[4,512,512]{2,1,0:T(8,128)(2,1)} %all-gather.2.cloned.1.call-done, f32[4,512,256]{2,1,0:T(8,128)S(1)} %reshape.313, bf16[4,512,256]{2,1,0:T(8,128)(2,1)S(1)} %copy-done, pred[4,512]{1,0:T(4,128)(4,1)S(1)} %iota_compare_fusion.2), kind=kOutput, calls=%fused_computation.32 | convolution fusion | flops 538968064 | bytes 7342080 | tf_op jit(solution)/shard_map/sij,sjc->sic/dot_general | solution.py:263
  198.8 3.0 copy.48
  201.8 2.6 reshape.314
  204.4 3.1 concatenate.23.src_ref
  207.5 7.4 %shard_map.92 = f32[4096,128]{1,0:T(8,128)} custom-call(s32[4096]{0:T(1024)} %bitcast.88, f32[4104,128]{1,0:T(8,128)} %concatenate.23.src_ref), custom_call_target="tpu_custom_call" | custom-call | bytes 4194304 | tf_op jit(solution)/shard_map/pallas_call | solution.py:109
  214.9 2.7 convert_element_type.50
  217.5 26.5 %shard_map.93 = f32[32,128,128]{2,1,0:T(8,128)} custom-call(bf16[32,128,128]{2,1,0:T(8,128)(2,1)} %bitcast.79), custom_call_target="tpu_custom_call" | custom-call | tf_op jit(solution)/shard_map/pallas_call | solution.py:165
  244.0 4.8 %shard_map.94 = f32[2048,128]{1,0:T(8,128)} custom-call(s32[2048]{0:T(1024)} %get-tuple-element.16.idx_ref, f32[4096,128]{1,0:T(8,128)} %bitcast.75), custom_call_target="tpu_custom_call" | custom-call | bytes 2097152 | tf_op jit(solution)/shard_map/pallas_call | solution.py:109
  248.8 1.3 convert_element_type.51
  250.1 6.1 %fusion.36 = f32[8,2048,128]{2,1,0:T(8,128)S(1)} fusion(bf16[8,256,2048]{2,1,0:T(8,128)(2,1)} %get-tuple-element.5, bf16[8,256,128]{2,1,0:T(8,128)(2,1)S(1)} %bitcast.82), kind=kOutput, calls=%fused_computation.89 | convolution fusion | flops 1073741824 | bytes 17301504 | tf_op jit(solution)/shard_map/fio,fic->foc/dot_general | solution.py:215
  256.2 3.0 fusion.34
  259.8 3.1 multiply_convert_fusion.1
  263.5 2.3 fusion.6
  265.8 1.1 concatenate.25.src_ref
  266.9 7.0 %shard_map.95 = f32[4096,128]{1,0:T(8,128)} custom-call(s32[4096]{0:T(1024)} %get-tuple-element.8.idx_ref, f32[2056,128]{1,0:T(8,128)} %concatenate.25.src_ref), custom_call_target="tpu_custom_call" | custom-call | bytes 4194304 | tf_op jit(solution)/shard_map/pallas_call | solution.py:109
  273.9 2.7 convert_element_type.52
  276.5 23.5 %shard_map.96 = f32[32,128,128]{2,1,0:T(8,128)} custom-call(bf16[32,128,128]{2,1,0:T(8,128)(2,1)} %bitcast.80), custom_call_target="tpu_custom_call" | custom-call | tf_op jit(solution)/shard_map/pallas_call | solution.py:165
  300.0 15.1 %shard_map.97 = f32[4096,128]{1,0:T(8,128)} custom-call(s32[4096]{0:T(1024)} %bitcast.89, f32[4096,128]{1,0:T(8,128)} %bitcast.76), custom_call_target="tpu_custom_call" | custom-call | flops 524288 | bytes 4194304 | tf_op jit(solution)/shard_map/pallas_call | solution.py:205
  315.2 2.9 reshape.321
  318.1 3.2 fusion.14
  (47 shorter events, 8.6 us)
Async XLA Ops:
  7.2 43.9 %all-gather.2.cloned.1.call-start = ((), (), s32[]{:S(2)}) async-start(), calls=%async_computation.2 | async-start | bytes 2359296 | tf_op jit(solution)/shard_map/all_gather | solution.py:260
  29.1 10.9 %copy-start.5 = (s32[4]{0:T(128)S(1)}, s32[4]{0:T(128)}, u32[]{:S(2)}) copy-start(s32[4]{0:T(128)} %param.8) | copy-start | bytes 52
  29.1 22.0 %copy-start = (bf16[4,512,256]{2,1,0:T(8,128)(2,1)S(1)}, bf16[4,512,256]{2,1,0:T(8,128)(2,1)}, u32[]{:S(2)}) copy-start(bf16[4,512,256]{2,1,0:T(8,128)(2,1)} %param.7) | copy-start | bytes 3145732
  31.4 27.3 %all-to-all-start = ((s32[32,1,128]{2,1,0:T(1,128)}), s32[32,1,128]{2,1,0:T(1,128)S(1)}, u32[]{:S(2)}, u32[]{:S(2)}) async-start(s32[32,1,128]{2,1,0:T(1,128)} %bitcast.5), calls=%async_computation | async-start | bytes 32768 | tf_op jit(solution)/shard_map/all_to_all | solution.py:255
  58.7 0.6 copy-start.1
  59.3 21.4 %copy-start.4 = (s32[1024]{0:T(1024)S(1)}, s32[1024]{0:T(1024)}, u32[]{:S(2)}) copy-start(s32[1024]{0:T(1024)} %param.12) | copy-start | bytes 12292
  59.3 22.0 %copy-start.2 = (s32[8,256]{1,0:T(8,128)S(1)}, s32[8,256]{1,0:T(8,128)}, u32[]{:S(2)}) copy-start(s32[8,256]{1,0:T(8,128)} %param.10) | copy-start | bytes 24580
  59.3 22.0 %copy-start.3 = (s32[8,256]{1,0:T(8,128)S(1)}, s32[8,256]{1,0:T(8,128)}, u32[]{:S(2)}) copy-start(s32[8,256]{1,0:T(8,128)} %param.11) | copy-start | bytes 24580
  69.4 41.5 %all-to-all-start.1 = ((bf16[32,128,128]{2,1,0:T(8,128)(2,1)}), bf16[32,128,128]{2,1,0:T(8,128)(2,1)S(1)}, u32[]{:S(2)}, u32[]{:S(2)}) async-start(bf16[32,128,128]{2,1,0:T(8,128)(2,1)} %bitcast.12), calls=%async_computation.1 | async-start | bytes 2097152 | tf_op jit(solution)/shard_map/all_to_all | solution.py:269
  259.2 4.3 %slice-start = ((s8[8388608]{0:T(1024)(128)(4,1)}), s8[4194304]{0:T(1024)(128)(4,1)S(1)}, s32[]{:S(2)}) async-start(s8[8388608]{0:T(1024)(128)(4,1)} %bitcast.73), calls=%async_computation.3 | async-start | bytes 8388608
  259.8 3.7 %slice-start.1 = ((s8[8388608]{0:T(1024)(128)(4,1)}), s8[4194304]{0:T(1024)(128)(4,1)S(1)}, s32[]{:S(2)}) async-start(s8[8388608]{0:T(1024)(128)(4,1)} %bitcast.73), calls=%async_computation.4 | async-start | bytes 8388608
Sparse Core Ops, SparseCore 0:
  9.8 41.2 all-gather.1

commit v6 on v5

--- a/solution.py
+++ b/solution.py
@@ -96,24 +96,33 @@
     return basis, nc.reshape(plans, nper), ns.reshape(plans, nper)
 
 
-def gather_kernel(idx_ref, src_ref, out_ref):
-    def body(r, carry):
-        out_ref[pl.ds(r, 1), :] = src_ref[pl.ds(idx_ref[r], 1), :]
-        return carry
-
-    lax.fori_loop(0, out_ref.shape[0], body, 0, unroll=16)
-
-
-def row_gather(src, idx):
+def gather_kernel(idx_ref, src_ref, *rest):
+    out_ref = rest[-2]
+    stage_ref = rest[-1]
+    block = stage_ref.shape[0]
+
+    def body(b, carry):
+        r0 = pl.multiple_of(b * block, block)
+        for j in range(block):
+            stage_ref[pl.ds(j, 1), :] = src_ref[pl.ds(idx_ref[r0 + j], 1), :]
+        out_ref[pl.ds(r0, block), :] = stage_ref[...].astype(out_ref.dtype)
+        return carry
+
+    lax.fori_loop(0, out_ref.shape[0] // block, body, 0)
+
+
+def row_gather(src, idx, out_dtype, *after):
     rows, width = idx.shape[0], src.shape[1]
     return pl.pallas_call(
         gather_kernel,
-        in_specs=[pl.BlockSpec(memory_space=pltpu.SMEM), pl.BlockSpec(memory_space=pltpu.VMEM)],
+        in_specs=[pl.BlockSpec(memory_space=pltpu.SMEM), pl.BlockSpec(memory_space=pltpu.VMEM)]
+        + [pl.BlockSpec(memory_space=pltpu.VMEM) for _ in after],
         out_specs=pl.BlockSpec(memory_space=pltpu.VMEM),
-        out_shape=jax.ShapeDtypeStruct((rows, width), src.dtype),
+        out_shape=jax.ShapeDtypeStruct((rows, width), out_dtype),
+        scratch_shapes=[pltpu.VMEM((32, width), src.dtype)],
         cost_estimate=pl.CostEstimate(
             flops=0, transcendentals=0, bytes_accessed=2 * rows * width * src.dtype.itemsize),
-    )(idx, src)
+    )(idx, src, *after)
 
 
 def with_zero_rows(flat):
@@ -242,7 +251,13 @@
     target = seg_flat // seg_dev
     local_row = (seg_flat % seg_dev * slots + slot_flat) * column_blocks + block_of
     onehot = (target[:, None] == jnp.arange(tm_count, dtype=jnp.int32)[None, :]).astype(jnp.int32)
-    position = jnp.sum(jnp.cumsum(onehot, axis=0) * onehot, axis=1) - 1
+    ones = onehot.astype(jnp.bfloat16).reshape(requests // 128, 128, tm_count)
+    tril = (jnp.arange(128)[:, None] >= jnp.arange(128)[None, :]).astype(jnp.bfloat16)
+    within = jnp.einsum("ij,bjc->bic", tril, ones, preferred_element_type=jnp.float32)
+    totals = within[:, -1, :]
+    before = jnp.cumsum(totals, axis=0) - totals
+    counts = (within + before[:, None, :]).reshape(requests, tm_count)
+    position = jnp.sum(counts * onehot.astype(jnp.float32), axis=1).astype(jnp.int32) - 1
     empty_row = seg_dev * slots * column_blocks
     slot_of = target * capacity + position
     pair = (
@@ -263,19 +278,21 @@
         white = jnp.einsum(
             "sij,sjc->sic", attitude_all, masked, preferred_element_type=jnp.float32
         )
-        picked = row_gather(with_zero_rows(white.reshape(-1, SRC_GROUP)), asked)
-        outbound = picked.astype(jnp.bfloat16).reshape(tm_count, capacity, SRC_GROUP)
+        picked = row_gather(
+            with_zero_rows(white.reshape(-1, SRC_GROUP)), asked, jnp.bfloat16, norm_cos)
+        outbound = picked.reshape(tm_count, capacity, SRC_GROUP)
         if iteration == 0:
             arrived = lax.all_to_all(outbound, "tm", split_axis=0, concat_axis=0, tiled=True)
             arrived = arrived.astype(jnp.float32)
         else:
             arrived = tm_all_to_all(outbound, jnp.float32, 1 + 2 * iteration)
-        observed = row_gather(arrived.reshape(-1, SRC_GROUP), slot_of)
-        observed = observed.astype(jnp.bfloat16).reshape(sched_dev, obs, SRC_GROUP)
+        observed = row_gather(arrived.reshape(-1, SRC_GROUP), slot_of, jnp.bfloat16)
+        observed = observed.reshape(sched_dev, obs, SRC_GROUP)
         model, evidence = fit_groups(basis, observed, norm_cos, norm_sin, nper)
-        outgoing = row_gather(with_zero_rows(model.reshape(requests, SRC_GROUP)), inverse)
+        outgoing = row_gather(
+            with_zero_rows(model.reshape(requests, SRC_GROUP)), inverse, jnp.bfloat16)
         returned = tm_all_to_all(
-            outgoing.astype(jnp.bfloat16).reshape(tm_count, capacity, SRC_GROUP),
+            outgoing.reshape(tm_count, capacity, SRC_GROUP),
             jnp.float32, 2 + 2 * iteration)
         placed = scatter_add(returned.reshape(-1, SRC_GROUP), asked, empty_row)
         current = current - placed.reshape(seg_dev, slots, width)

time: 330 us -> 305 us (0.924)
  other arithmetic: 46.4 us -> 24 us
  waiting for transfers between devices: 11.6 us -> 16.9 us
  Pallas kernels: 169 us -> 164 us
  starting transfers between devices: 19.9 us -> 16 us
    all_to_all x1, waiting for transfers between devices: 0.01 us -> 16.3 us  [on_device(): lax.all_to_all(outbound, 'tm', split_axis=0, concat_axis=0, tiled=True)]
    convert_element_type x7 -> x0, other arithmetic: 13.3 us -> none  [the longest x2 5.43 us: on_device(): picked.astype(jnp.bfloat16).reshape(tm_count, capacity, SRC_GROUP)]
    all_gather x1, waiting for transfers between devices: 11 us -> 0.01 us  [on_device(): attitude_all = lax.all_gather(attitude, 'sky', axis=1, tiled=True)]
    another operation x4 -> x2, other arithmetic: 12.5 us -> 3.09 us
    all_to_all x1, starting transfers between devices: 11.2 us -> 7.38 us  [on_device(): lax.all_to_all(outbound, 'tm', split_axis=0, concat_axis=0, tiled=True)]
  transfers between devices with their start and end apart: 3 -> 3, of which waited for: 1 -> 1; matrix products, arithmetic and copies ran while one was open for 10% -> 8% of each run, Pallas kernels for 8% -> 9%
where the time goes in v6:
time: 305 us; the launch traced here: 303 us
  Pallas kernels  164 us (54%)
  local copies, waits for them, and re-layouts  36.4 us (12%)
  matrix products  31.2 us (10%)
  other arithmetic  24 us (8%)
  waiting for transfers between devices  16.9 us (6%)
  starting transfers between devices  16 us (5%)
  between operations  14.4 us (5%)
    pallas_call x3, Pallas kernels, tm_all_to_all(): pl.pallas_call(a2a_kernel, in_specs=[pl.BlockSpec(memory_space=pltpu.VMEM...  70.1 us
    pallas_call x6, Pallas kernels, row_gather(): pl.pallas_call(gather_kernel, in_specs=[pl.BlockSpec(memory_space=pltpu.S...  37.2 us
    pallas_call x2, Pallas kernels, scatter_add(): pl.pallas_call(scatter_add_kernel, in_specs=[pl.BlockSpec(memory_space=pl...  30.3 us
    pallas_call x1, Pallas kernels, basis_and_norms(): pl.pallas_call(basis_kernel, grid=(plans,), in_specs=[pl.BlockSpec((None,...  26.9 us
    all_to_all x1, waiting for transfers between devices, on_device(): lax.all_to_all(outbound, 'tm', split_axis=0, concat_axis=0, tiled=True)  16.3 us
    dot_general x2, matrix products, fit_groups(): jnp.einsum('fio,fic->foc', basis, observed, preferred_element_type=jnp.fl...  15.6 us
    div x1, other arithmetic, fit_groups(): share = expo / total[:, None, :]  9.59 us
    dot_general x2, matrix products, fit_groups(): jnp.einsum('fio,foc->fic', basis, coeff, preferred_element_type=jnp.float32)  8.64 us
  transfers between devices with their start and end apart: 3, of which 1 were waited for; matrix products, arithmetic and copies ran while one was open for 8% of the time, Pallas kernels for 9%

profile of v6, /device:TPU:1, one launch (start us, length us, event | category | flops | bytes accessed | tf_op | source)
XLA Modules:
  0.0 303.3 jit_solution(1246628915878370704)
XLA Ops:
  7.2 0.7 all-gather.2.cloned.1.call-update
  8.0 0.7 reshape.311
  8.7 0.7 copy.58
  9.4 0.7 copy.59
  11.8 0.8 broadcast_in_dim.20
  12.6 6.4 %scatter_fusion = s32[4096,2]{1,0:T(8,128)S(1)} fusion(s32[4096,2]{1,0:T(8,128)S(1)} %broadcast_in_dim.20, s32[2048]{0:T(1024)S(1)} %bitcast.94, s32[2048,2]{1,0:T(8,128)S(1)} %copy.43), kind=kCustom, calls=%fused_computation | custom fusion | bytes 57344 | tf_op jit(solution)/shard_map/scatter | solution.py:266
  19.0 2.3 slice_reduce_fusion
  21.3 8.6 %all-to-all-start = ((s32[32,1,128]{2,1,0:T(1,128)}), s32[32,1,128]{2,1,0:T(1,128)S(1)}, u32[]{:S(2)}, u32[]{:S(2)}) async-start(s32[32,1,128]{2,1,0:T(1,128)} %bitcast.4), calls=%async_computation | async-start | bytes 32768 | tf_op jit(solution)/shard_map/all_to_all | solution.py:270
  30.5 1.3 copy.45.t_ref
  31.9 0.6 broadcast_divide_fusion
  32.5 26.9 %shard_map.86 = (bf16[8,256,2048]{2,1,0:T(8,128)(2,1)}, f32[8,1,1024]{2,1,0:T(1,128)}, f32[8,1,1024]{2,1,0:T(1,128)}) custom-call(f32[8,256,1]{2,1,0:T(8,128)} %copy.45.t_ref, f32[1,1024]{1,0:T(1,128)} %bitcast.103, f32[1,1024]{1,0:T(1,128)} %bitcast.102, f32[1,1024]{1,0:T(1,128)} %bitcast.101), custom_call_target="tpu_custom_call" | custom-call | flops 125829120 | bytes 8388608 | tf_op jit(solution)/shard_map/pallas_call | solution.py:78
  59.4 1.4 copy.65
  60.9 2.7 convolution_bitcast_fusion.1
  63.6 1.8 copy.47
  65.4 1.6 reshape.320
  67.0 1.5 concatenate.20.src_ref
  69.2 7.1 %shard_map.87 = bf16[4096,128]{1,0:T(8,128)(2,1)} custom-call(s32[4096]{0:T(1024)} %bitcast.85, f32[4104,128]{1,0:T(8,128)} %concatenate.20.src_ref, f32[8,1024]{1,0:T(8,128)} %bitcast.80), custom_call_target="tpu_custom_call" | custom-call | bytes 4194304 | tf_op jit(solution)/shard_map/pallas_call | solution.py:116
  76.2 7.4 %all-to-all-start.1 = ((bf16[32,128,128]{2,1,0:T(8,128)(2,1)}), bf16[32,128,128]{2,1,0:T(8,128)(2,1)S(1)}, u32[]{:S(2)}, u32[]{:S(2)}) async-start(bf16[32,128,128]{2,1,0:T(8,128)(2,1)} %bitcast.75), calls=%async_computation.1 | async-start | bytes 2097152 | tf_op jit(solution)/shard_map/all_to_all | solution.py:285
  83.7 0.6 fusion.28.idx_ref
  84.3 16.3 %all-to-all-done.1 = bf16[32,128,128]{2,1,0:T(8,128)(2,1)S(1)} async-done(((bf16[32,128,128]{2,1,0:T(8,128)(2,1)}), bf16[32,128,128]{2,1,0:T(8,128)(2,1)S(1)}, u32[]{:S(2)}, u32[]{:S(2)}) %all-to-all-start.1) | async-done | bytes 1048608 | tf_op jit(solution)/shard_map/all_to_all | solution.py:285
  100.5 1.5 bitcast_convert_fusion.src_ref
  102.1 4.6 %shard_map.88 = bf16[2048,128]{1,0:T(8,128)(2,1)} custom-call(s32[2048]{0:T(1024)} %fusion.28.idx_ref, f32[4096,128]{1,0:T(8,128)} %bitcast_convert_fusion.src_ref), custom_call_target="tpu_custom_call" | custom-call | bytes 2097152 | tf_op jit(solution)/shard_map/pallas_call | solution.py:116
  106.7 9.4 %fusion.40 = f32[8,2048,128]{2,1,0:T(8,128)} fusion(bf16[8,256,2048]{2,1,0:T(8,128)(2,1)} %get-tuple-element.5, bf16[8,256,128]{2,1,0:T(8,128)(2,1)} %bitcast.76), kind=kOutput, calls=%fused_computation.93 | convolution fusion | flops 1073741824 | bytes 17301504 | tf_op jit(solution)/shard_map/fio,fic->foc/dot_general | solution.py:224
  116.1 9.6 %multiply_convert_fusion.3 = (bf16[8,1024,128]{2,1,0:T(8,128)(2,1)S(1)}, bf16[8,1024,128]{2,1,0:T(8,128)(2,1)}) fusion(f32[8,1024]{1,0:T(8,128)} %bitcast.81, f32[8,2048,128]{2,1,0:T(8,128)} %fusion.40, f32[8,1024]{1,0:T(8,128)S(1)} %bitcast.89), kind=kOutput, calls=%fused_computation.16 | output fusion | flops 14684158 | bytes 21102592 | tf_op jit(solution)/shard_map/div | solution.py:234
  125.7 6.3 %fusion.2 = f32[8,256,128]{2,1,0:T(8,128)S(1)} fusion(bf16[8,256,2048]{2,1,0:T(8,128)(2,1)} %get-tuple-element.5, bf16[8,1024,128]{2,1,0:T(8,128)(2,1)} %get-tuple-element.15, bf16[8,1024,128]{2,1,0:T(8,128)(2,1)S(1)} %get-tuple-element.14), kind=kOutput, calls=%fused_computation.3 | convolution fusion | flops 1082130432 | bytes 13631488 | tf_op jit(solution)/shard_map/fio,foc->fic/dot_general | solution.py:236
  132.0 1.0 concatenate.22.src_ref
  133.1 6.7 %shard_map.89 = bf16[4096,128]{1,0:T(8,128)(2,1)} custom-call(s32[4096]{0:T(1024)} %get-tuple-element.8.idx_ref, f32[2056,128]{1,0:T(8,128)} %concatenate.22.src_ref), custom_call_target="tpu_custom_call" | custom-call | bytes 4194304 | tf_op jit(solution)/shard_map/pallas_call | solution.py:116
  139.8 20.0 %shard_map.90 = f32[32,128,128]{2,1,0:T(8,128)} custom-call(bf16[32,128,128]{2,1,0:T(8,128)(2,1)} %bitcast.73), custom_call_target="tpu_custom_call" | custom-call | tf_op jit(solution)/shard_map/pallas_call | solution.py:174
  159.8 15.1 %shard_map.91 = f32[4096,128]{1,0:T(8,128)} custom-call(s32[4096]{0:T(1024)} %bitcast.86, f32[4096,128]{1,0:T(8,128)} %bitcast.71), custom_call_target="tpu_custom_call" | custom-call | flops 524288 | bytes 4194304 | tf_op jit(solution)/shard_map/pallas_call | solution.py:214
  175.0 1.9 reshape.329
  176.9 4.1 %convolution_bitcast_fusion = f32[4,512,256]{1,2,0:T(8,128)} fusion(bf16[4,512,512]{2,1,0:T(8,128)(2,1)} %all-gather.2.cloned.1.call-done, f32[4,512,256]{2,1,0:T(8,128)S(1)} %reshape.329, bf16[4,512,256]{2,1,0:T(8,128)(2,1)S(1)} %copy-done, pred[4,512]{1,0:T(4,128)(4,1)S(1)} %iota_compare_fusion.2), kind=kOutput, calls=%fused_computation.32 | convolution fusion | flops 538968064 | bytes 7342080 | tf_op jit(solution)/shard_map/sij,sjc->sic/dot_general | solution.py:278
  180.9 3.0 copy.50
  183.9 2.6 reshape.330
  186.5 3.1 %concatenate.23.src_ref = f32[4104,128]{1,0:T(8,128)} pad(f32[4096,128]{1,0:T(8,128)} %reshape.330, f32[]{:T(128)} %constant.60.clone.1), padding=0_8x0_0 | pad | bytes 4198404 | tf_op jit(solution)/shard_map/concatenate | solution.py:129
  189.6 7.1 %shard_map.92 = bf16[4096,128]{1,0:T(8,128)(2,1)} custom-call(s32[4096]{0:T(1024)} %bitcast.87, f32[4104,128]{1,0:T(8,128)} %concatenate.23.src_ref, f32[8,1024]{1,0:T(8,128)} %bitcast.82), custom_call_target="tpu_custom_call" | custom-call | bytes 4194304 | tf_op jit(solution)/shard_map/pallas_call | solution.py:116
  196.7 26.5 %shard_map.93 = f32[32,128,128]{2,1,0:T(8,128)} custom-call(bf16[32,128,128]{2,1,0:T(8,128)(2,1)} %bitcast.74), custom_call_target="tpu_custom_call" | custom-call | tf_op jit(solution)/shard_map/pallas_call | solution.py:174
  223.2 4.9 %shard_map.94 = bf16[2048,128]{1,0:T(8,128)(2,1)} custom-call(s32[2048]{0:T(1024)} %fusion.28.idx_ref, f32[4096,128]{1,0:T(8,128)} %bitcast.69), custom_call_target="tpu_custom_call" | custom-call | bytes 2097152 | tf_op jit(solution)/shard_map/pallas_call | solution.py:116
  228.1 6.2 %fusion.41 = f32[8,2048,128]{2,1,0:T(8,128)S(1)} fusion(bf16[8,256,2048]{2,1,0:T(8,128)(2,1)} %get-tuple-element.5, bf16[8,256,128]{2,1,0:T(8,128)(2,1)} %bitcast.77), kind=kOutput, calls=%fused_computation.94 | convolution fusion | flops 1073741824 | bytes 17301504 | tf_op jit(solution)/shard_map/fio,fic->foc/dot_general | solution.py:224
  234.3 3.0 fusion.38
  237.9 3.1 %multiply_convert_fusion.1 = (bf16[8,1024,128]{2,1,0:T(8,128)(2,1)S(1)}, bf16[8,1024,128]{2,1,0:T(8,128)(2,1)S(1)}) fusion(f32[8,1024]{1,0:T(8,128)S(1)} %bitcast.84, f32[8,2048,128]{2,1,0:T(8,128)S(1)} %fusion.41, f32[8,128]{1,0:T(8,128)S(1)} %fusion.11, f32[8,1024,128]{2,1,0:T(8,128)S(1)} %get-tuple-element.11, f32[8,128]{1,0:T(8,128)S(1)} %get-tuple-element.10, ...), kind=kLoop, calls=%fused_computation.12 | loop fusion | flops 8388608 | bytes 16850944 | tf_op jit(solution)/shard_map/convert.1
  240.9 0.6 log_add_fusion
  241.6 2.3 fusion.6
  243.9 1.0 concatenate.25.src_ref
  244.9 6.7 %shard_map.95 = bf16[4096,128]{1,0:T(8,128)(2,1)} custom-call(s32[4096]{0:T(1024)} %get-tuple-element.8.idx_ref, f32[2056,128]{1,0:T(8,128)} %concatenate.25.src_ref), custom_call_target="tpu_custom_call" | custom-call | bytes 4194304 | tf_op jit(solution)/shard_map/pallas_call | solution.py:116
  251.7 23.5 %shard_map.96 = f32[32,128,128]{2,1,0:T(8,128)} custom-call(bf16[32,128,128]{2,1,0:T(8,128)(2,1)} %bitcast.72), custom_call_target="tpu_custom_call" | custom-call | tf_op jit(solution)/shard_map/pallas_call | solution.py:174
  275.2 15.1 %shard_map.97 = f32[4096,128]{1,0:T(8,128)} custom-call(s32[4096]{0:T(1024)} %bitcast.88, f32[4096,128]{1,0:T(8,128)} %bitcast.70), custom_call_target="tpu_custom_call" | custom-call | flops 524288 | bytes 4194304 | tf_op jit(solution)/shard_map/pallas_call | solution.py:214
  290.3 2.9 reshape.337
  293.2 3.2 %fusion.14 = f32[4,512,256]{2,1,0:T(8,128)} fusion(f32[4,512,256]{2,1,0:T(8,128)} %reshape.337, f32[4,512,256]{2,1,0:T(8,128)S(1)} %reshape.329, bf16[4,512,256]{2,1,0:T(8,128)(2,1)S(1)} %copy-done), kind=kLoop, calls=%fused_computation.34 | loop fusion | flops 1572864 | bytes 7340032 | tf_op jit(solution)/shard_map/sub | solution.py:298
  (46 shorter events, 3.6 us)
Async XLA Ops:
  7.2 53.7 %all-gather.2.cloned.1.call-start = ((), (), s32[]{:S(2)}) async-start(), calls=%async_computation.2 | async-start | bytes 2359296 | tf_op jit(solution)/shard_map/all_gather | solution.py:275
  19.0 11.0 %copy-start.6 = (s32[1024]{0:T(1024)S(1)}, s32[1024]{0:T(1024)}, u32[]{:S(2)}) copy-start(s32[1024]{0:T(1024)} %param.12) | copy-start | bytes 12292
  19.0 11.6 %copy-start.3 = (s32[8,256]{1,0:T(8,128)S(1)}, s32[8,256]{1,0:T(8,128)}, u32[]{:S(2)}) copy-start(s32[8,256]{1,0:T(8,128)} %param.10) | copy-start | bytes 24580
  19.0 11.6 %copy-start.4 = (s32[8,256]{1,0:T(8,128)S(1)}, s32[8,256]{1,0:T(8,128)}, u32[]{:S(2)}) copy-start(s32[8,256]{1,0:T(8,128)} %param.11) | copy-start | bytes 24580
  19.0 41.8 %copy-start.7 = (s32[4]{0:T(128)S(1)}, s32[4]{0:T(128)}, u32[]{:S(2)}) copy-start(s32[4]{0:T(128)} %param.8) | copy-start | bytes 52
  19.0 41.9 %copy-start = (bf16[4,512,256]{2,1,0:T(8,128)(2,1)S(1)}, bf16[4,512,256]{2,1,0:T(8,128)(2,1)}, u32[]{:S(2)}) copy-start(bf16[4,512,256]{2,1,0:T(8,128)(2,1)} %param.7) | copy-start | bytes 3145732
  21.3 47.2 %all-to-all-start = ((s32[32,1,128]{2,1,0:T(1,128)}), s32[32,1,128]{2,1,0:T(1,128)S(1)}, u32[]{:S(2)}, u32[]{:S(2)}) async-start(s32[32,1,128]{2,1,0:T(1,128)} %bitcast.4), calls=%async_computation | async-start | bytes 32768 | tf_op jit(solution)/shard_map/all_to_all | solution.py:270
  67.0 16.6 %copy-start.5 = (f32[8,1,1024]{2,1,0:T(1,128)S(1)}, f32[8,1,1024]{2,1,0:T(1,128)}, u32[]{:S(2)}) copy-start(f32[8,1,1024]{2,1,0:T(1,128)} %get-tuple-element.7) | copy-start | bytes 98308
  68.6 0.6 copy-start.2
  76.2 24.3 %all-to-all-start.1 = ((bf16[32,128,128]{2,1,0:T(8,128)(2,1)}), bf16[32,128,128]{2,1,0:T(8,128)(2,1)S(1)}, u32[]{:S(2)}, u32[]{:S(2)}) async-start(bf16[32,128,128]{2,1,0:T(8,128)(2,1)} %bitcast.75), calls=%async_computation.1 | async-start | bytes 2097152 | tf_op jit(solution)/shard_map/all_to_all | solution.py:285
  228.1 6.2 %copy-start.1 = (f32[8,1,1024]{2,0,1:T(8,128)S(1)}, f32[8,1,1024]{2,0,1:T(8,128)}, u32[]{:S(2)}) copy-start(f32[8,1,1024]{2,0,1:T(8,128)} %copy.65) | copy-start | bytes 98308
  237.3 4.3 %slice-start = ((s8[8388608]{0:T(1024)(128)(4,1)}), s8[4194304]{0:T(1024)(128)(4,1)S(1)}, s32[]{:S(2)}) async-start(s8[8388608]{0:T(1024)(128)(4,1)} %bitcast.67), calls=%async_computation.3 | async-start | bytes 8388608
  237.9 3.7 %slice-start.1 = ((s8[8388608]{0:T(1024)(128)(4,1)}), s8[4194304]{0:T(1024)(128)(4,1)S(1)}, s32[]{:S(2)}) async-start(s8[8388608]{0:T(1024)(128)(4,1)} %bitcast.67), calls=%async_computation.4 | async-start | bytes 8388608
Sparse Core Ops, SparseCore 0:
  9.8 41.5 all-gather.1

commit v7 on v6

--- a/solution.py
+++ b/solution.py
@@ -219,6 +219,55 @@
         scratch_shapes=[pltpu.VMEM((STREAMS, pad, width), jnp.float32)],
         cost_estimate=pl.CostEstimate(flops=rows * width, transcendentals=0, bytes_accessed=(rows + out_rows) * width * 4),
     )(idx, src)
+
+
+def fit_kernel(basis_ref, obs_ref, inc_ref, ins_ref, model_ref, ev_ref):
+    nper = inc_ref.shape[1]
+    basis = basis_ref[...]
+    obs_t = obs_ref[...].astype(jnp.float32).T.astype(jnp.bfloat16)
+    corr = jnp.dot(obs_t, basis, preferred_element_type=jnp.float32)
+    cosine = corr[:, :nper]
+    sine = corr[:, nper:]
+    amp_c = cosine * inc_ref[...]
+    amp_s = sine * ins_ref[...]
+    logits = BETA * (cosine * amp_c + sine * amp_s)
+    highest = jnp.max(logits, axis=1, keepdims=True)
+    expo = jnp.exp(logits - highest)
+    total = jnp.sum(expo, axis=1, keepdims=True)
+    share = expo * (1.0 / total)
+    coeff = jnp.concatenate([share * amp_c, share * amp_s], axis=1).astype(jnp.bfloat16)
+    model_ref[...] = lax.dot_general(
+        basis, coeff, (((1,), (1,)), ((), ())), preferred_element_type=jnp.float32)
+    ev_ref[...] = highest + jnp.log(total)
+
+
+def fit_fused(basis, observed, inv_cos, inv_sin):
+    plans, obs, width = basis.shape
+    cols = observed.shape[2]
+    nper = width // 2
+    row = pl.BlockSpec((None, 1, nper), lambda g: (g, 0, 0))
+    model, ev = pl.pallas_call(
+        fit_kernel,
+        grid=(plans,),
+        in_specs=[
+            pl.BlockSpec((None, obs, width), lambda g: (g, 0, 0)),
+            pl.BlockSpec((None, obs, cols), lambda g: (g, 0, 0)),
+            row,
+            row,
+        ],
+        out_specs=[
+            pl.BlockSpec((None, obs, cols), lambda g: (g, 0, 0)),
+            pl.BlockSpec((None, cols, 1), lambda g: (g, 0, 0)),
+        ],
+        out_shape=[
+            jax.ShapeDtypeStruct((plans, obs, cols), jnp.float32),
+            jax.ShapeDtypeStruct((plans, cols, 1), jnp.float32),
+        ],
+        cost_estimate=pl.CostEstimate(
+            flops=4 * plans * obs * width * cols, transcendentals=plans * nper * cols,
+            bytes_accessed=plans * obs * width * 2),
+    )(basis, observed, inv_cos, inv_sin)
+    return model, ev.reshape(plans, cols)
 
 def fit_groups(basis, observed, norm_cos, norm_sin, nper):
     corr = jnp.einsum("fio,fic->foc", basis, observed, preferred_element_type=jnp.float32)
@@ -270,6 +319,8 @@
     asked = lax.all_to_all(wanted, "tm", split_axis=0, concat_axis=0, tiled=True).reshape(-1)
     basis, norm_cos, norm_sin = basis_and_norms(sched_seg * slots + sched_slot, periods)
     valid = jnp.arange(slots, dtype=jnp.int32)[None, :] < seg_counts[:, None]
+    inv_cos = (1.0 / norm_cos).reshape(sched_dev, 1, nper)
+    inv_sin = (1.0 / norm_sin).reshape(sched_dev, 1, nper)
     current = residuals.astype(jnp.float32)
     evidence = jnp.zeros((sched_dev, SRC_GROUP), jnp.float32)
     attitude_all = lax.all_gather(attitude, "sky", axis=1, tiled=True)
@@ -288,7 +339,7 @@
             arrived = tm_all_to_all(outbound, jnp.float32, 1 + 2 * iteration)
         observed = row_gather(arrived.reshape(-1, SRC_GROUP), slot_of, jnp.bfloat16)
         observed = observed.reshape(sched_dev, obs, SRC_GROUP)
-        model, evidence = fit_groups(basis, observed, norm_cos, norm_sin, nper)
+        model, evidence = fit_fused(basis, observed, inv_cos, inv_sin)
         outgoing = row_gather(
             with_zero_rows(model.reshape(requests, SRC_GROUP)), inverse, jnp.bfloat16)
         returned = tm_all_to_all(

time: 305 us -> 290 us (0.951)
  matrix products: 31.2 us -> 6.92 us
  Pallas kernels: 164 us -> 187 us
  other arithmetic: 24 us -> 9.75 us
    dot_general x4 -> x0, matrix products: 24.2 us -> none  [the longest x2 15.6 us: fit_groups(): jnp.einsum('fio,fic->foc', basis, observed, preferred_element_type=jnp.fl...]
    pallas_call x0 -> x2, Pallas kernels: none -> 22.3 us  [fit_fused(): pl.pallas_call(fit_kernel, grid=(plans,), in_specs=[pl.BlockSpec((None, o...]
    div x1, other arithmetic: 9.59 us -> 0.7 us  [on_device(): inv_sin = (1.0 / norm_sin).reshape(sched_dev, 1, nper)]
    another operation x1 -> x0, other arithmetic: 3.07 us -> none
  transfers between devices with their start and end apart: 3 -> 3, of which waited for: 1 -> 1; matrix products, arithmetic and copies ran while one was open for 8% -> 9% of each run, Pallas kernels for 9% -> 9%
where the time goes in v7:
time: 290 us; the launch traced here: 288 us
  Pallas kernels  187 us (64%)
  local copies, waits for them, and re-layouts  38 us (13%)
  waiting for transfers between devices  16.3 us (6%)
  starting transfers between devices  16.1 us (6%)
  between operations  14.3 us (5%)
  other arithmetic  9.75 us (3%)
  matrix products  6.92 us (2%)
    pallas_call x3, Pallas kernels, tm_all_to_all(): pl.pallas_call(a2a_kernel, in_specs=[pl.BlockSpec(memory_space=pltpu.VMEM...  70 us
    pallas_call x6, Pallas kernels, row_gather(): pl.pallas_call(gather_kernel, in_specs=[pl.BlockSpec(memory_space=pltpu.S...  37.1 us
    pallas_call x2, Pallas kernels, scatter_add(): pl.pallas_call(scatter_add_kernel, in_specs=[pl.BlockSpec(memory_space=pl...  30.3 us
    pallas_call x1, Pallas kernels, basis_and_norms(): pl.pallas_call(basis_kernel, grid=(plans,), in_specs=[pl.BlockSpec((None,...  27 us
    pallas_call x2, Pallas kernels, fit_fused(): pl.pallas_call(fit_kernel, grid=(plans,), in_specs=[pl.BlockSpec((None, o...  22.3 us
    all_to_all x1, waiting for transfers between devices, on_device(): lax.all_to_all(outbound, 'tm', split_axis=0, concat_axis=0, tiled=True)  15.6 us
    concatenate x4, local copies, waits for them, and re-layouts, with_zero_rows(): jnp.concatenate([flat, jnp.zeros((8, flat.shape[1]), flat.dtype)], axis=0)  9.03 us
    all_to_all x1, starting transfers between devices, on_device(): lax.all_to_all(wanted, 'tm', split_axis=0, concat_axis=0, tiled=True)  8.72 us
  transfers between devices with their start and end apart: 3, of which 1 were waited for; matrix products, arithmetic and copies ran while one was open for 9% of the time, Pallas kernels for 9%

profile of v7, /device:TPU:1, one launch (start us, length us, event | category | flops | bytes accessed | tf_op | source)
XLA Modules:
  0.0 287.9 jit_solution(15041091928585695915)
XLA Ops:
  7.2 0.7 all-gather.2.cloned.1.call-update
  8.0 0.7 reshape.311
  8.7 0.7 copy.47
  9.4 0.7 copy.48
  10.1 0.2 convolution_bitcast_fusion.2
  10.8 0.3 subtract_reduce_fusion
  11.4 0.4 copy.37
  11.9 6.4 %scatter_fusion = s32[4096,2]{1,0:T(8,128)S(1)} fusion(s32[4096,2]{1,0:T(8,128)S(1)} %broadcast_in_dim.32, s32[2048]{0:T(1024)S(1)} %bitcast.77, s32[2048,2]{1,0:T(8,128)S(1)} %copy.37), kind=kCustom, calls=%fused_computation | custom fusion | bytes 57344 | tf_op jit(solution)/shard_map/scatter | solution.py:315
  18.4 2.3 slice_reduce_fusion
  20.7 8.7 %all-to-all-start = ((s32[32,1,128]{2,1,0:T(1,128)}), s32[32,1,128]{2,1,0:T(1,128)S(1)}, u32[]{:S(2)}, u32[]{:S(2)}) async-start(s32[32,1,128]{2,1,0:T(1,128)} %bitcast.4), calls=%async_computation | async-start | bytes 32768 | tf_op jit(solution)/shard_map/all_to_all | solution.py:319
  29.4 0.6 convert_element_type.48
  30.0 1.3 copy.39.t_ref
  31.4 0.6 broadcast_divide_fusion.2
  32.0 27.0 %shard_map.86 = (bf16[8,256,2048]{2,1,0:T(8,128)(2,1)}, f32[8,1,1024]{2,1,0:T(1,128)}, f32[8,1,1024]{2,1,0:T(1,128)}) custom-call(f32[8,256,1]{2,1,0:T(8,128)} %copy.39.t_ref, f32[1,1024]{1,0:T(1,128)} %bitcast.86, f32[1,1024]{1,0:T(1,128)} %bitcast.85, f32[1,1024]{1,0:T(1,128)} %bitcast.84), custom_call_target="tpu_custom_call" | custom-call | flops 125829120 | bytes 8388608 | tf_op jit(solution)/shard_map/pallas_call | solution.py:78
  58.9 1.4 copy.52
  60.4 2.7 convolution_bitcast_fusion.1
  63.1 1.8 copy.41
  64.9 1.6 reshape.320
  66.5 1.5 concatenate.12.src_ref
  68.0 0.6 copy-done.1
  68.6 7.1 %shard_map.87 = bf16[4096,128]{1,0:T(8,128)(2,1)} custom-call(s32[4096]{0:T(1024)} %bitcast.69, f32[4104,128]{1,0:T(8,128)} %concatenate.12.src_ref, f32[8,1024]{1,0:T(8,128)} %bitcast.73), custom_call_target="tpu_custom_call" | custom-call | bytes 4194304 | tf_op jit(solution)/shard_map/pallas_call | solution.py:116
  75.7 7.4 %all-to-all-start.1 = ((bf16[32,128,128]{2,1,0:T(8,128)(2,1)}), bf16[32,128,128]{2,1,0:T(8,128)(2,1)S(1)}, u32[]{:S(2)}, u32[]{:S(2)}) async-start(bf16[32,128,128]{2,1,0:T(8,128)(2,1)} %bitcast.64), calls=%async_computation.1 | async-start | bytes 2097152 | tf_op jit(solution)/shard_map/all_to_all | solution.py:336
  83.1 0.6 fusion.15.idx_ref
  83.7 0.7 broadcast_divide_fusion
  84.4 15.6 %all-to-all-done.1 = bf16[32,128,128]{2,1,0:T(8,128)(2,1)S(1)} async-done(((bf16[32,128,128]{2,1,0:T(8,128)(2,1)}), bf16[32,128,128]{2,1,0:T(8,128)(2,1)S(1)}, u32[]{:S(2)}, u32[]{:S(2)}) %all-to-all-start.1) | async-done | bytes 1048608 | tf_op jit(solution)/shard_map/all_to_all | solution.py:336
  100.0 1.5 bitcast_convert_fusion.src_ref
  101.5 4.7 %shard_map.88 = bf16[2048,128]{1,0:T(8,128)(2,1)} custom-call(s32[2048]{0:T(1024)} %fusion.15.idx_ref, f32[4096,128]{1,0:T(8,128)} %bitcast_convert_fusion.src_ref), custom_call_target="tpu_custom_call" | custom-call | bytes 2097152 | tf_op jit(solution)/shard_map/pallas_call | solution.py:116
  106.2 11.1 %shard_map.89 = (f32[8,256,128]{2,1,0:T(8,128)}, f32[8,128,1]{2,1,0:T(8,128)}) custom-call(bf16[8,256,2048]{2,1,0:T(8,128)(2,1)} %get-tuple-element.8.basis_ref, bf16[8,256,128]{2,1,0:T(8,128)(2,1)} %bitcast.66, f32[8,1,1024]{2,1,0:T(1,128)} %get-tuple-element.21.inc_ref, f32[8,1,1024]{2,1,0:T(1,128)} %get-tuple-element.20.ins_ref), custom_call_target="tpu_custom_call" | custom-call | flops 2147483648 | bytes 8388608 | tf_op jit(solution)/shard_map/pallas_call | solution.py:249
  117.3 2.3 concatenate.13.src_ref
  119.6 6.8 %shard_map.90 = bf16[4096,128]{1,0:T(8,128)(2,1)} custom-call(s32[4096]{0:T(1024)} %get-tuple-element.14.idx_ref, f32[2056,128]{1,0:T(8,128)} %concatenate.13.src_ref), custom_call_target="tpu_custom_call" | custom-call | bytes 4194304 | tf_op jit(solution)/shard_map/pallas_call | solution.py:116
  126.4 20.0 %shard_map.91 = f32[32,128,128]{2,1,0:T(8,128)} custom-call(bf16[32,128,128]{2,1,0:T(8,128)(2,1)} %bitcast.63), custom_call_target="tpu_custom_call" | custom-call | tf_op jit(solution)/shard_map/pallas_call | solution.py:174
  146.3 15.1 %shard_map.92 = f32[4096,128]{1,0:T(8,128)} custom-call(s32[4096]{0:T(1024)} %bitcast.70, f32[4096,128]{1,0:T(8,128)} %bitcast.60), custom_call_target="tpu_custom_call" | custom-call | flops 524288 | bytes 4194304 | tf_op jit(solution)/shard_map/pallas_call | solution.py:214
  161.5 1.9 reshape.329
  163.4 4.1 %convolution_bitcast_fusion = f32[4,512,256]{1,2,0:T(8,128)} fusion(bf16[4,512,512]{2,1,0:T(8,128)(2,1)} %all-gather.2.cloned.1.call-done, f32[4,512,256]{2,1,0:T(8,128)S(1)} %reshape.329, bf16[4,512,256]{2,1,0:T(8,128)(2,1)S(1)} %copy-done, pred[4,512]{1,0:T(4,128)(4,1)S(1)} %iota_compare_fusion.2), kind=kOutput, calls=%fused_computation.7 | convolution fusion | flops 538968064 | bytes 7342080 | tf_op jit(solution)/shard_map/sij,sjc->sic/dot_general | solution.py:329
  167.4 2.9 %copy.43 = f32[4,512,256]{2,1,0:T(8,128)} copy(f32[4,512,256]{1,2,0:T(8,128)} %convolution_bitcast_fusion) | data formatting | bytes 4194304 | tf_op jit(solution)/shard_map/sij,sjc->sic/dot_general | solution.py:329
  170.4 2.6 reshape.330
  173.0 3.0 %concatenate.14.src_ref = f32[4104,128]{1,0:T(8,128)} pad(f32[4096,128]{1,0:T(8,128)} %reshape.330, f32[]{:T(128)} %constant.59.clone.1), padding=0_8x0_0 | pad | bytes 4198404 | tf_op jit(solution)/shard_map/concatenate | solution.py:129
  176.0 7.1 %shard_map.93 = bf16[4096,128]{1,0:T(8,128)(2,1)} custom-call(s32[4096]{0:T(1024)} %bitcast.71, f32[4104,128]{1,0:T(8,128)} %concatenate.14.src_ref, f32[8,1024]{1,0:T(8,128)} %bitcast.74), custom_call_target="tpu_custom_call" | custom-call | bytes 4194304 | tf_op jit(solution)/shard_map/pallas_call | solution.py:116
  183.1 26.5 %shard_map.94 = f32[32,128,128]{2,1,0:T(8,128)} custom-call(bf16[32,128,128]{2,1,0:T(8,128)(2,1)} %bitcast.61), custom_call_target="tpu_custom_call" | custom-call | tf_op jit(solution)/shard_map/pallas_call | solution.py:174
  209.7 4.7 %shard_map.95 = bf16[2048,128]{1,0:T(8,128)(2,1)} custom-call(s32[2048]{0:T(1024)} %fusion.15.idx_ref, f32[4096,128]{1,0:T(8,128)} %bitcast.58), custom_call_target="tpu_custom_call" | custom-call | bytes 2097152 | tf_op jit(solution)/shard_map/pallas_call | solution.py:116
  214.3 11.1 %shard_map.96 = (f32[8,256,128]{2,1,0:T(8,128)}, f32[8,128,1]{2,1,0:T(8,128)}) custom-call(bf16[8,256,2048]{2,1,0:T(8,128)(2,1)} %get-tuple-element.8.basis_ref, bf16[8,256,128]{2,1,0:T(8,128)(2,1)} %bitcast.65, f32[8,1,1024]{2,1,0:T(1,128)} %get-tuple-element.21.inc_ref, f32[8,1,1024]{2,1,0:T(1,128)} %get-tuple-element.20.ins_ref), custom_call_target="tpu_custom_call" | custom-call | flops 2147483648 | bytes 8388608 | tf_op jit(solution)/shard_map/pallas_call | solution.py:249
  225.5 2.3 concatenate.15.src_ref
  227.7 6.7 %shard_map.97 = bf16[4096,128]{1,0:T(8,128)(2,1)} custom-call(s32[4096]{0:T(1024)} %get-tuple-element.14.idx_ref, f32[2056,128]{1,0:T(8,128)} %concatenate.15.src_ref), custom_call_target="tpu_custom_call" | custom-call | bytes 4194304 | tf_op jit(solution)/shard_map/pallas_call | solution.py:116
  234.5 23.5 %shard_map.98 = f32[32,128,128]{2,1,0:T(8,128)} custom-call(bf16[32,128,128]{2,1,0:T(8,128)(2,1)} %bitcast.62), custom_call_target="tpu_custom_call" | custom-call | tf_op jit(solution)/shard_map/pallas_call | solution.py:174
  258.0 15.1 %shard_map.99 = f32[4096,128]{1,0:T(8,128)} custom-call(s32[4096]{0:T(1024)} %bitcast.72, f32[4096,128]{1,0:T(8,128)} %bitcast.59), custom_call_target="tpu_custom_call" | custom-call | flops 524288 | bytes 4194304 | tf_op jit(solution)/shard_map/pallas_call | solution.py:214
  273.1 2.9 %reshape.337 = f32[4,512,256]{2,1,0:T(8,128)} reshape(f32[4096,128]{1,0:T(8,128)} %shard_map.99) | data formatting | bytes 4194304 | tf_op jit(solution)/shard_map/reshape | solution.py:349
  276.0 3.2 %fusion.1 = f32[4,512,256]{2,1,0:T(8,128)} fusion(f32[4,512,256]{2,1,0:T(8,128)} %reshape.337, f32[4,512,256]{2,1,0:T(8,128)S(1)} %reshape.329, bf16[4,512,256]{2,1,0:T(8,128)(2,1)S(1)} %copy-done), kind=kLoop, calls=%fused_computation.9 | loop fusion | flops 1572864 | bytes 7340032 | tf_op jit(solution)/shard_map/sub | solution.py:349
  279.2 1.8 reduce.4
  (37 shorter events, 1.1 us)
Async XLA Ops:
  7.2 4.6 %copy-start.7 = (s32[2]{0:T(128)S(1)}, s32[2]{0:T(128)}, u32[]{:S(2)}) copy-start(s32[2]{0:T(128)} %constant.65.clone) | copy-start | bytes 28
  7.2 53.2 %all-gather.2.cloned.1.call-start = ((), (), s32[]{:S(2)}) async-start(), calls=%async_computation.2 | async-start | bytes 2359296 | tf_op jit(solution)/shard_map/all_gather | solution.py:326
  18.3 11.1 %copy-start.6 = (s32[1024]{0:T(1024)S(1)}, s32[1024]{0:T(1024)}, u32[]{:S(2)}) copy-start(s32[1024]{0:T(1024)} %param.12) | copy-start | bytes 12292
  18.3 11.7 %copy-start.2 = (s32[8,256]{1,0:T(8,128)S(1)}, s32[8,256]{1,0:T(8,128)}, u32[]{:S(2)}) copy-start(s32[8,256]{1,0:T(8,128)} %param.10) | copy-start | bytes 24580
  18.3 11.7 %copy-start.4 = (s32[8,256]{1,0:T(8,128)S(1)}, s32[8,256]{1,0:T(8,128)}, u32[]{:S(2)}) copy-start(s32[8,256]{1,0:T(8,128)} %param.11) | copy-start | bytes 24580
  20.7 39.7 %copy-start.8 = (s32[4]{0:T(128)S(1)}, s32[4]{0:T(128)}, u32[]{:S(2)}) copy-start(s32[4]{0:T(128)} %param.8) | copy-start | bytes 52
  20.7 39.7 %copy-start = (bf16[4,512,256]{2,1,0:T(8,128)(2,1)S(1)}, bf16[4,512,256]{2,1,0:T(8,128)(2,1)}, u32[]{:S(2)}) copy-start(bf16[4,512,256]{2,1,0:T(8,128)(2,1)} %param.7) | copy-start | bytes 3145732
  20.7 47.3 %all-to-all-start = ((s32[32,1,128]{2,1,0:T(1,128)}), s32[32,1,128]{2,1,0:T(1,128)S(1)}, u32[]{:S(2)}, u32[]{:S(2)}) async-start(s32[32,1,128]{2,1,0:T(1,128)} %bitcast.4), calls=%async_computation | async-start | bytes 32768 | tf_op jit(solution)/shard_map/all_to_all | solution.py:319
  68.0 0.6 copy-start.1
  68.6 15.1 %copy-start.3 = (f32[8,1,1024]{2,1,0:T(1,128)S(1)}, f32[8,1,1024]{2,1,0:T(1,128)}, u32[]{:S(2)}) copy-start(f32[8,1,1024]{2,1,0:T(1,128)} %get-tuple-element.9) | copy-start | bytes 98308
  68.6 15.1 %copy-start.5 = (f32[8,1,1024]{2,1,0:T(1,128)S(1)}, f32[8,1,1024]{2,1,0:T(1,128)}, u32[]{:S(2)}) copy-start(f32[8,1,1024]{2,1,0:T(1,128)} %get-tuple-element.10) | copy-start | bytes 98308
  75.7 24.3 %all-to-all-start.1 = ((bf16[32,128,128]{2,1,0:T(8,128)(2,1)}), bf16[32,128,128]{2,1,0:T(8,128)(2,1)S(1)}, u32[]{:S(2)}, u32[]{:S(2)}) async-start(bf16[32,128,128]{2,1,0:T(8,128)(2,1)} %bitcast.64), calls=%async_computation.1 | async-start | bytes 2097152 | tf_op jit(solution)/shard_map/all_to_all | solution.py:336
Sparse Core Ops, SparseCore 0:
  9.8 41.4 all-gather.1

commit v8 on v7

--- a/solution.py
+++ b/solution.py
@@ -269,6 +269,78 @@
     )(basis, observed, inv_cos, inv_sin)
     return model, ev.reshape(plans, cols)
 
+
+def half_gather_kernel(idx_ref, src_ref, *rest):
+    out_ref = rest[-2]
+    stage_ref = rest[-1]
+    block, width = stage_ref.shape
+    last = src_ref.shape[0] - 1
+
+    def body(b, carry):
+        r0 = pl.multiple_of(b * block, block)
+        for j in range(block):
+            a = idx_ref[r0 + j]
+            row = src_ref[pl.ds(jnp.minimum(a // 2, last), 1), :]
+            stage_ref[pl.ds(j, 1), :] = jnp.where(a % 2 == 1, row[:, width:], row[:, :width])
+        out_ref[pl.ds(r0, block), :] = stage_ref[...].astype(out_ref.dtype)
+        return carry
+
+    lax.fori_loop(0, out_ref.shape[0] // block, body, 0)
+
+
+def half_gather(src, idx, out_dtype, *after):
+    rows, width = idx.shape[0], src.shape[1] // 2
+    return pl.pallas_call(
+        half_gather_kernel,
+        in_specs=[pl.BlockSpec(memory_space=pltpu.SMEM), pl.BlockSpec(memory_space=pltpu.VMEM)]
+        + [pl.BlockSpec(memory_space=pltpu.VMEM) for _ in after],
+        out_specs=pl.BlockSpec(memory_space=pltpu.VMEM),
+        out_shape=jax.ShapeDtypeStruct((rows, width), out_dtype),
+        scratch_shapes=[pltpu.VMEM((32, width), src.dtype)],
+        cost_estimate=pl.CostEstimate(
+            flops=0, transcendentals=0, bytes_accessed=3 * rows * width * src.dtype.itemsize),
+    )(idx, src, *after)
+
+
+def scatter_sub_kernel(idx_ref, src_ref, cur_ref, out_ref, acc_ref):
+    rows, width = src_ref.shape
+    streams = acc_ref.shape[0]
+    acc_ref[...] = jnp.zeros_like(acc_ref)
+
+    def body(step, carry):
+        base = step * streams
+        for s in range(streams):
+            r = base + s
+            a = idx_ref[r]
+            v = src_ref[pl.ds(r, 1), :]
+            zero = jnp.zeros_like(v)
+            odd = a % 2 == 1
+            add = jnp.concatenate([jnp.where(odd, zero, v), jnp.where(odd, v, zero)], axis=1)
+            row = a // 2
+            acc_ref[s, pl.ds(row, 1), :] = acc_ref[s, pl.ds(row, 1), :] + add
+        return carry
+
+    lax.fori_loop(0, rows // streams, body, 0, unroll=SUNROLL)
+    n = out_ref.shape[0]
+    total = acc_ref[0, :n]
+    for s in range(1, streams):
+        total = total + acc_ref[s, :n]
+    out_ref[...] = cur_ref[...] - total
+
+
+def scatter_sub(src, idx, current):
+    rows, width = src.shape
+    out_rows = current.shape[0]
+    return pl.pallas_call(
+        scatter_sub_kernel,
+        in_specs=[pl.BlockSpec(memory_space=pltpu.SMEM)] + [pl.BlockSpec(memory_space=pltpu.VMEM)] * 2,
+        out_specs=pl.BlockSpec(memory_space=pltpu.VMEM),
+        out_shape=jax.ShapeDtypeStruct(current.shape, jnp.float32),
+        scratch_shapes=[pltpu.VMEM((STREAMS, out_rows + 8, 2 * width), jnp.float32)],
+        cost_estimate=pl.CostEstimate(
+            flops=rows * width, transcendentals=0, bytes_accessed=(rows * width + 2 * current.size) * 4),
+    )(idx, src, current)
+
 def fit_groups(basis, observed, norm_cos, norm_sin, nper):
     corr = jnp.einsum("fio,fic->foc", basis, observed, preferred_element_type=jnp.float32)
     cosine = corr[:, :nper]
@@ -310,7 +382,7 @@
     empty_row = seg_dev * slots * column_blocks
     slot_of = target * capacity + position
     pair = (
-        jnp.broadcast_to(jnp.array([empty_row, requests], jnp.int32), (tm_count * capacity, 2))
+        jnp.broadcast_to(jnp.array([empty_row, 0], jnp.int32), (tm_count * capacity, 2))
         .at[slot_of]
         .set(jnp.stack([local_row, jnp.arange(requests, dtype=jnp.int32)], axis=1))
     )
@@ -329,8 +401,8 @@
         white = jnp.einsum(
             "sij,sjc->sic", attitude_all, masked, preferred_element_type=jnp.float32
         )
-        picked = row_gather(
-            with_zero_rows(white.reshape(-1, SRC_GROUP)), asked, jnp.bfloat16, norm_cos)
+        picked = half_gather(
+            white.reshape(seg_dev * slots, width), asked, jnp.bfloat16, norm_cos)
         outbound = picked.reshape(tm_count, capacity, SRC_GROUP)
         if iteration == 0:
             arrived = lax.all_to_all(outbound, "tm", split_axis=0, concat_axis=0, tiled=True)
@@ -340,13 +412,13 @@
         observed = row_gather(arrived.reshape(-1, SRC_GROUP), slot_of, jnp.bfloat16)
         observed = observed.reshape(sched_dev, obs, SRC_GROUP)
         model, evidence = fit_fused(basis, observed, inv_cos, inv_sin)
-        outgoing = row_gather(
-            with_zero_rows(model.reshape(requests, SRC_GROUP)), inverse, jnp.bfloat16)
+        outgoing = row_gather(model.reshape(requests, SRC_GROUP), inverse, jnp.bfloat16)
         returned = tm_all_to_all(
             outgoing.reshape(tm_count, capacity, SRC_GROUP),
             jnp.float32, 2 + 2 * iteration)
-        placed = scatter_add(returned.reshape(-1, SRC_GROUP), asked, empty_row)
-        current = current - placed.reshape(seg_dev, slots, width)
+        current = scatter_sub(
+            returned.reshape(-1, SRC_GROUP), asked, current.reshape(seg_dev * slots, width)
+        ).reshape(seg_dev, slots, width)
     return (current, evidence)
 
 

time: 290 us -> 376 us (1.30)
  Pallas kernels: 187 us -> 295 us
  local copies, waits for them, and re-layouts: 38 us -> 20 us
    pallas_call x2 -> x4, Pallas kernels: 30.3 us -> 153 us  [the longest x2 78.3 us: scatter_sub(): pl.pallas_call(scatter_sub_kernel, in_specs=[pl.BlockSpec(memory_space=pl...]
    pallas_call x6 -> x4, Pallas kernels: 37.1 us -> 22.8 us  [row_gather(): pl.pallas_call(gather_kernel, in_specs=[pl.BlockSpec(memory_space=pltpu.S...]
    concatenate x4 -> x0, local copies, waits for them, and re-layouts: 9.03 us -> none  [with_zero_rows(): jnp.concatenate([flat, jnp.zeros((8, flat.shape[1]), flat.dtype)], axis=0)]
    reshape x4 -> x0, local copies, waits for them, and re-layouts: 9 us -> none  [the longest x2 4.76 us: on_device(): current = current - placed.reshape(seg_dev, slots, width)]
  transfers between devices with their start and end apart: 3 -> 3, of which waited for: 1 -> 1; matrix products, arithmetic and copies ran while one was open for 9% -> 6% of each run, Pallas kernels for 9% -> 7%
where the time goes in v8:
time: 376 us; the launch traced here: 374 us
  Pallas kernels  295 us (78%)
  local copies, waits for them, and re-layouts  20 us (5%)
  starting transfers between devices  16.2 us (4%)
  waiting for transfers between devices  14.7 us (4%)
  between operations  14.3 us (4%)
  other arithmetic  7.03 us (2%)
  matrix products  6.92 us (2%)
    pallas_call x2, Pallas kernels, scatter_sub(): pl.pallas_call(scatter_sub_kernel, in_specs=[pl.BlockSpec(memory_space=pl...  78.3 us
    pallas_call x2, Pallas kernels, half_gather(): pl.pallas_call(half_gather_kernel, in_specs=[pl.BlockSpec(memory_space=pl...  74.8 us
    pallas_call x3, Pallas kernels, tm_all_to_all(): pl.pallas_call(a2a_kernel, in_specs=[pl.BlockSpec(memory_space=pltpu.VMEM...  69.9 us
    pallas_call x1, Pallas kernels, basis_and_norms(): pl.pallas_call(basis_kernel, grid=(plans,), in_specs=[pl.BlockSpec((None,...  27 us
    pallas_call x4, Pallas kernels, row_gather(): pl.pallas_call(gather_kernel, in_specs=[pl.BlockSpec(memory_space=pltpu.S...  22.8 us
    pallas_call x2, Pallas kernels, fit_fused(): pl.pallas_call(fit_kernel, grid=(plans,), in_specs=[pl.BlockSpec((None, o...  22.3 us
    all_to_all x1, waiting for transfers between devices, on_device(): lax.all_to_all(outbound, 'tm', split_axis=0, concat_axis=0, tiled=True)  14 us
    all_to_all x1, starting transfers between devices, on_device(): lax.all_to_all(wanted, 'tm', split_axis=0, concat_axis=0, tiled=True)  8.72 us
  transfers between devices with their start and end apart: 3, of which 1 were waited for; matrix products, arithmetic and copies ran while one was open for 6% of the time, Pallas kernels for 7%

profile of v8, /device:TPU:1, one launch (start us, length us, event | category | flops | bytes accessed | tf_op | source)
XLA Modules:
  0.0 374.1 jit_solution(16623895074594620017)
XLA Ops:
  7.2 0.7 all-gather.2.cloned.1.call-update
  7.9 0.1 broadcast_bitcast_fusion
  8.0 0.7 reshape.314
  8.7 0.7 copy.47
  9.4 0.7 copy.48
  10.1 0.2 convolution_bitcast_fusion.2
  10.3 0.1 slice.12
  10.5 0.2 copy.35
  10.7 0.2 copy.36
  10.8 0.3 subtract_reduce_fusion
  11.1 0.1 fusion.6
  11.3 0.1 multiply_add_fusion
  11.4 0.4 copy.37
  11.8 0.1 broadcast_in_dim.32
  11.9 6.4 %scatter_fusion = s32[4096,2]{1,0:T(8,128)S(1)} fusion(s32[4096,2]{1,0:T(8,128)S(1)} %broadcast_in_dim.32, s32[2048]{0:T(1024)S(1)} %bitcast.88, s32[2048,2]{1,0:T(8,128)S(1)} %copy.37), kind=kCustom, calls=%fused_computation | custom fusion | bytes 57344 | tf_op jit(solution)/shard_map/scatter | solution.py:387
  18.4 2.3 slice_reduce_fusion
  20.7 8.7 %all-to-all-start = ((s32[32,1,128]{2,1,0:T(1,128)}), s32[32,1,128]{2,1,0:T(1,128)S(1)}, u32[]{:S(2)}, u32[]{:S(2)}) async-start(s32[32,1,128]{2,1,0:T(1,128)} %bitcast.4), calls=%async_computation | async-start | bytes 32768 | tf_op jit(solution)/shard_map/all_to_all | solution.py:391
  29.4 0.6 convert_element_type.47
  30.0 1.3 copy.39.t_ref
  31.4 0.6 broadcast_divide_fusion.2
  32.0 27.0 %shard_map.86 = (bf16[8,256,2048]{2,1,0:T(8,128)(2,1)}, f32[8,1,1024]{2,1,0:T(1,128)}, f32[8,1,1024]{2,1,0:T(1,128)}) custom-call(f32[8,256,1]{2,1,0:T(8,128)} %copy.39.t_ref, f32[1,1024]{1,0:T(1,128)} %bitcast.97, f32[1,1024]{1,0:T(1,128)} %bitcast.96, f32[1,1024]{1,0:T(1,128)} %bitcast.95), custom_call_target="tpu_custom_call" | custom-call | flops 125829120 | bytes 8388608 | tf_op jit(solution)/shard_map/pallas_call | solution.py:78
  58.9 1.4 copy.52
  60.3 0.1 iota_compare_fusion.2
  60.4 2.7 convolution_bitcast_fusion.1
  63.1 1.8 copy.41
  64.9 0.6 copy-done.3
  65.5 37.4 %shard_map.87 = bf16[4096,128]{1,0:T(8,128)(2,1)} custom-call(s32[4096]{0:T(1024)} %bitcast.80, f32[2048,256]{1,0:T(8,128)} %bitcast.69, f32[8,1024]{1,0:T(8,128)} %bitcast.84), custom_call_target="tpu_custom_call" | custom-call | bytes 6291456 | tf_op jit(solution)/shard_map/pallas_call | solution.py:293
  102.9 7.4 %all-to-all-start.1 = ((bf16[32,128,128]{2,1,0:T(8,128)(2,1)}), bf16[32,128,128]{2,1,0:T(8,128)(2,1)S(1)}, u32[]{:S(2)}, u32[]{:S(2)}) async-start(bf16[32,128,128]{2,1,0:T(8,128)(2,1)} %bitcast.72), calls=%async_computation.1 | async-start | bytes 2097152 | tf_op jit(solution)/shard_map/all_to_all | solution.py:408
  110.3 0.6 fusion.13.idx_ref
  110.9 0.7 broadcast_divide_fusion
  111.6 1.6 bitcast_convert_fusion.1.cur_ref
  113.2 14.0 %all-to-all-done.1 = bf16[32,128,128]{2,1,0:T(8,128)(2,1)S(1)} async-done(((bf16[32,128,128]{2,1,0:T(8,128)(2,1)}), bf16[32,128,128]{2,1,0:T(8,128)(2,1)S(1)}, u32[]{:S(2)}, u32[]{:S(2)}) %all-to-all-start.1) | async-done | bytes 1048608 | tf_op jit(solution)/shard_map/all_to_all | solution.py:408
  127.2 1.5 bitcast_convert_fusion.src_ref
  128.7 4.7 %shard_map.88 = bf16[2048,128]{1,0:T(8,128)(2,1)} custom-call(s32[2048]{0:T(1024)} %fusion.13.idx_ref, f32[4096,128]{1,0:T(8,128)} %bitcast_convert_fusion.src_ref), custom_call_target="tpu_custom_call" | custom-call | bytes 2097152 | tf_op jit(solution)/shard_map/pallas_call | solution.py:116
  133.4 11.2 %shard_map.89 = (f32[8,256,128]{2,1,0:T(8,128)}, f32[8,128,1]{2,1,0:T(8,128)}) custom-call(bf16[8,256,2048]{2,1,0:T(8,128)(2,1)} %get-tuple-element.8.basis_ref, bf16[8,256,128]{2,1,0:T(8,128)(2,1)} %bitcast.77, f32[8,1,1024]{2,1,0:T(1,128)} %get-tuple-element.21.inc_ref, f32[8,1,1024]{2,1,0:T(1,128)} %get-tuple-element.20.ins_ref), custom_call_target="tpu_custom_call" | custom-call | flops 2147483648 | bytes 8388608 | tf_op jit(solution)/shard_map/pallas_call | solution.py:249
  144.6 6.7 %shard_map.90 = bf16[4096,128]{1,0:T(8,128)(2,1)} custom-call(s32[4096]{0:T(1024)} %get-tuple-element.14.idx_ref, f32[2048,128]{1,0:T(8,128)} %bitcast.79), custom_call_target="tpu_custom_call" | custom-call | bytes 4194304 | tf_op jit(solution)/shard_map/pallas_call | solution.py:116
  151.3 20.0 %shard_map.91 = f32[32,128,128]{2,1,0:T(8,128)} custom-call(bf16[32,128,128]{2,1,0:T(8,128)(2,1)} %bitcast.74), custom_call_target="tpu_custom_call" | custom-call | tf_op jit(solution)/shard_map/pallas_call | solution.py:174
  171.3 39.2 %shard_map.92.cur_ref = f32[2048,256]{1,0:T(8,128)} custom-call(s32[4096]{0:T(1024)} %bitcast.81, f32[4096,128]{1,0:T(8,128)} %bitcast.67, f32[2048,256]{1,0:T(8,128)} %bitcast_convert_fusion.1.cur_ref), custom_call_target="tpu_custom_call" | custom-call | flops 524288 | bytes 6291456 | tf_op jit(solution)/shard_map/pallas_call | solution.py:334
  210.5 4.1 %convolution_bitcast_fusion = f32[4,512,256]{1,2,0:T(8,128)} fusion(bf16[4,512,512]{2,1,0:T(8,128)(2,1)S(1)} %copy-done, f32[4,512,256]{2,1,0:T(8,128)} %bitcast.65, pred[4,512]{1,0:T(4,128)(4,1)S(1)} %iota_compare_fusion.2), kind=kOutput, calls=%fused_computation.5 | convolution fusion | flops 537395200 | bytes 6293504 | tf_op jit(solution)/shard_map/sij,sjc->sic/dot_general | solution.py:401
  214.5 2.9 copy.43
  217.5 37.4 %shard_map.93 = bf16[4096,128]{1,0:T(8,128)(2,1)} custom-call(s32[4096]{0:T(1024)} %bitcast.82, f32[2048,256]{1,0:T(8,128)} %bitcast.70, f32[8,1024]{1,0:T(8,128)} %bitcast.85), custom_call_target="tpu_custom_call" | custom-call | bytes 6291456 | tf_op jit(solution)/shard_map/pallas_call | solution.py:293
  254.9 26.4 %shard_map.94 = f32[32,128,128]{2,1,0:T(8,128)} custom-call(bf16[32,128,128]{2,1,0:T(8,128)(2,1)} %bitcast.71), custom_call_target="tpu_custom_call" | custom-call | tf_op jit(solution)/shard_map/pallas_call | solution.py:174
  281.3 4.7 %shard_map.95 = bf16[2048,128]{1,0:T(8,128)(2,1)} custom-call(s32[2048]{0:T(1024)} %fusion.13.idx_ref, f32[4096,128]{1,0:T(8,128)} %bitcast.68), custom_call_target="tpu_custom_call" | custom-call | bytes 2097152 | tf_op jit(solution)/shard_map/pallas_call | solution.py:116
  286.0 11.1 %shard_map.96 = (f32[8,256,128]{2,1,0:T(8,128)}, f32[8,128,1]{2,1,0:T(8,128)}) custom-call(bf16[8,256,2048]{2,1,0:T(8,128)(2,1)} %get-tuple-element.8.basis_ref, bf16[8,256,128]{2,1,0:T(8,128)(2,1)} %bitcast.76, f32[8,1,1024]{2,1,0:T(1,128)} %get-tuple-element.21.inc_ref, f32[8,1,1024]{2,1,0:T(1,128)} %get-tuple-element.20.ins_ref), custom_call_target="tpu_custom_call" | custom-call | flops 2147483648 | bytes 8388608 | tf_op jit(solution)/shard_map/pallas_call | solution.py:249
  297.2 6.7 %shard_map.97 = bf16[4096,128]{1,0:T(8,128)(2,1)} custom-call(s32[4096]{0:T(1024)} %get-tuple-element.14.idx_ref, f32[2048,128]{1,0:T(8,128)} %bitcast.78), custom_call_target="tpu_custom_call" | custom-call | bytes 4194304 | tf_op jit(solution)/shard_map/pallas_call | solution.py:116
  303.9 23.5 %shard_map.98 = f32[32,128,128]{2,1,0:T(8,128)} custom-call(bf16[32,128,128]{2,1,0:T(8,128)(2,1)} %bitcast.73), custom_call_target="tpu_custom_call" | custom-call | tf_op jit(solution)/shard_map/pallas_call | solution.py:174
  327.4 39.1 %shard_map.99 = f32[2048,256]{1,0:T(8,128)} custom-call(s32[4096]{0:T(1024)} %bitcast.83, f32[4096,128]{1,0:T(8,128)} %bitcast.66, f32[2048,256]{1,0:T(8,128)} %shard_map.92.cur_ref), custom_call_target="tpu_custom_call" | custom-call | flops 524288 | bytes 6291456 | tf_op jit(solution)/shard_map/pallas_call | solution.py:334
  366.5 0.8 reduce.4
  (33 shorter events, 0.2 us)
Async XLA Ops:
  7.2 4.6 %copy-start.9 = (s32[2]{0:T(128)S(1)}, s32[2]{0:T(128)}, u32[]{:S(2)}) copy-start(s32[2]{0:T(128)} %constant.64.clone) | copy-start | bytes 28
  7.2 53.2 %all-gather.2.cloned.1.call-start = ((), (), s32[]{:S(2)}) async-start(), calls=%async_computation.2 | async-start | bytes 2359296 | tf_op jit(solution)/shard_map/all_gather | solution.py:398
  18.3 11.1 %copy-start.8 = (s32[1024]{0:T(1024)S(1)}, s32[1024]{0:T(1024)}, u32[]{:S(2)}) copy-start(s32[1024]{0:T(1024)} %param.12) | copy-start | bytes 12292
  18.3 11.7 %copy-start.4 = (s32[8,256]{1,0:T(8,128)S(1)}, s32[8,256]{1,0:T(8,128)}, u32[]{:S(2)}) copy-start(s32[8,256]{1,0:T(8,128)} %param.10) | copy-start | bytes 24580
  18.3 11.7 %copy-start.6 = (s32[8,256]{1,0:T(8,128)S(1)}, s32[8,256]{1,0:T(8,128)}, u32[]{:S(2)}) copy-start(s32[8,256]{1,0:T(8,128)} %param.11) | copy-start | bytes 24580
  20.7 39.6 %copy-start.10 = (s32[4]{0:T(128)S(1)}, s32[4]{0:T(128)}, u32[]{:S(2)}) copy-start(s32[4]{0:T(128)} %param.8) | copy-start | bytes 52
  20.7 39.7 %copy-start.1 = (bf16[4,512,256]{2,1,0:T(8,128)(2,1)S(1)}, bf16[4,512,256]{2,1,0:T(8,128)(2,1)}, u32[]{:S(2)}) copy-start(bf16[4,512,256]{2,1,0:T(8,128)(2,1)} %param.7) | copy-start | bytes 3145732
  20.7 44.2 %all-to-all-start = ((s32[32,1,128]{2,1,0:T(1,128)}), s32[32,1,128]{2,1,0:T(1,128)S(1)}, u32[]{:S(2)}, u32[]{:S(2)}) async-start(s32[32,1,128]{2,1,0:T(1,128)} %bitcast.4), calls=%async_computation | async-start | bytes 32768 | tf_op jit(solution)/shard_map/all_to_all | solution.py:391
  64.9 0.6 copy-start.3
  65.5 45.5 %copy-start.5 = (f32[8,1,1024]{2,1,0:T(1,128)S(1)}, f32[8,1,1024]{2,1,0:T(1,128)}, u32[]{:S(2)}) copy-start(f32[8,1,1024]{2,1,0:T(1,128)} %get-tuple-element.9) | copy-start | bytes 98308
  65.5 45.5 %copy-start.7 = (f32[8,1,1024]{2,1,0:T(1,128)S(1)}, f32[8,1,1024]{2,1,0:T(1,128)}, u32[]{:S(2)}) copy-start(f32[8,1,1024]{2,1,0:T(1,128)} %get-tuple-element.10) | copy-start | bytes 98308
  102.9 24.3 %all-to-all-start.1 = ((bf16[32,128,128]{2,1,0:T(8,128)(2,1)}), bf16[32,128,128]{2,1,0:T(8,128)(2,1)S(1)}, u32[]{:S(2)}, u32[]{:S(2)}) async-start(bf16[32,128,128]{2,1,0:T(8,128)(2,1)} %bitcast.72), calls=%async_computation.1 | async-start | bytes 2097152 | tf_op jit(solution)/shard_map/all_to_all | solution.py:408
  171.3 39.2 %copy-start = (bf16[4,512,512]{2,1,0:T(8,128)(2,1)S(1)}, bf16[4,512,512]{2,1,0:T(8,128)(2,1)}, u32[]{:S(2)}) copy-start(bf16[4,512,512]{2,1,0:T(8,128)(2,1)} %all-gather.2.cloned.1.call-done) | copy-start | bytes 6291460
  327.4 39.1 %copy-start.2 = (f32[8,128,1]{2,1,0:T(8,128)S(1)}, f32[8,128,1]{2,1,0:T(8,128)}, u32[]{:S(2)}) copy-start(f32[8,128,1]{2,1,0:T(8,128)} %get-tuple-element.13) | copy-start | bytes 12292
Sparse Core Ops, SparseCore 0:
  9.8 41.3 all-gather.1

commit v9 on v7

--- a/solution.py
+++ b/solution.py
@@ -269,6 +269,70 @@
     )(basis, observed, inv_cos, inv_sin)
     return model, ev.reshape(plans, cols)
 
+
+def white_kernel(cnt_ref, cur_ref, att_ref, out_ref):
+    segs, slots, _ = att_ref.shape
+    width = out_ref.shape[1]
+    blocks = cur_ref.shape[1] // width
+    for s in range(segs):
+        cur = cur_ref[pl.ds(s * slots, slots), :]
+        slot = lax.broadcasted_iota(jnp.int32, cur.shape, 0)
+        masked = jnp.where(slot < cnt_ref[s], cur, 0.0).astype(jnp.bfloat16)
+        white = jnp.dot(att_ref[s], masked, preferred_element_type=jnp.float32)
+        for b in range(blocks):
+            out_ref[pl.ds(b * segs * slots + s * slots, slots), :] = white[:, b * width:(b + 1) * width]
+    out_ref[pl.ds(blocks * segs * slots, 8), :] = jnp.zeros((8, width), jnp.float32)
+
+
+def whiten_rows(counts, current, attitude_all, width):
+    segs, slots, _ = attitude_all.shape
+    rows = current.shape[0] * current.shape[1] // width
+    return pl.pallas_call(
+        white_kernel,
+        in_specs=[pl.BlockSpec(memory_space=pltpu.SMEM)] + [pl.BlockSpec(memory_space=pltpu.VMEM)] * 2,
+        out_specs=pl.BlockSpec(memory_space=pltpu.VMEM),
+        out_shape=jax.ShapeDtypeStruct((rows + 8, width), jnp.float32),
+        cost_estimate=pl.CostEstimate(
+            flops=2 * segs * slots * slots * current.shape[1], transcendentals=0,
+            bytes_accessed=current.size * 8 + attitude_all.size * 2),
+    )(counts, current, attitude_all)
+
+
+def scatter_sub_kernel(idx_ref, src_ref, cur_ref, out_ref, acc_ref):
+    rows, width = src_ref.shape
+    streams = acc_ref.shape[0]
+    n = cur_ref.shape[0]
+    acc_ref[...] = jnp.zeros_like(acc_ref)
+
+    def body(step, carry):
+        base = step * streams
+        for s in range(streams):
+            r = base + s
+            i = idx_ref[r]
+            acc_ref[s, pl.ds(i, 1), :] = acc_ref[s, pl.ds(i, 1), :] + src_ref[pl.ds(r, 1), :]
+        return carry
+
+    lax.fori_loop(0, rows // streams, body, 0, unroll=SUNROLL)
+    for b in range(cur_ref.shape[1] // width):
+        total = acc_ref[0, pl.ds(b * n, n), :]
+        for s in range(1, streams):
+            total = total + acc_ref[s, pl.ds(b * n, n), :]
+        out_ref[:, b * width:(b + 1) * width] = cur_ref[:, b * width:(b + 1) * width] - total
+
+
+def scatter_sub(src, idx, current):
+    rows, width = src.shape
+    blocks = current.shape[1] // width
+    return pl.pallas_call(
+        scatter_sub_kernel,
+        in_specs=[pl.BlockSpec(memory_space=pltpu.SMEM)] + [pl.BlockSpec(memory_space=pltpu.VMEM)] * 2,
+        out_specs=pl.BlockSpec(memory_space=pltpu.VMEM),
+        out_shape=jax.ShapeDtypeStruct(current.shape, jnp.float32),
+        scratch_shapes=[pltpu.VMEM((STREAMS, blocks * current.shape[0] + 8, width), jnp.float32)],
+        cost_estimate=pl.CostEstimate(
+            flops=rows * width, transcendentals=0, bytes_accessed=(rows * width + 2 * current.size) * 4),
+    )(idx, src, current)
+
 def fit_groups(basis, observed, norm_cos, norm_sin, nper):
     corr = jnp.einsum("fio,fic->foc", basis, observed, preferred_element_type=jnp.float32)
     cosine = corr[:, :nper]
@@ -298,7 +362,7 @@
     slot_flat = sched_slot.reshape(-1)
     block_of = jnp.repeat(jnp.arange(sched_dev, dtype=jnp.int32) % column_blocks, obs)
     target = seg_flat // seg_dev
-    local_row = (seg_flat % seg_dev * slots + slot_flat) * column_blocks + block_of
+    local_row = block_of * (seg_dev * slots) + seg_flat % seg_dev * slots + slot_flat
     onehot = (target[:, None] == jnp.arange(tm_count, dtype=jnp.int32)[None, :]).astype(jnp.int32)
     ones = onehot.astype(jnp.bfloat16).reshape(requests // 128, 128, tm_count)
     tril = (jnp.arange(128)[:, None] >= jnp.arange(128)[None, :]).astype(jnp.bfloat16)
@@ -310,7 +374,7 @@
     empty_row = seg_dev * slots * column_blocks
     slot_of = target * capacity + position
     pair = (
-        jnp.broadcast_to(jnp.array([empty_row, requests], jnp.int32), (tm_count * capacity, 2))
+        jnp.broadcast_to(jnp.array([empty_row, 0], jnp.int32), (tm_count * capacity, 2))
         .at[slot_of]
         .set(jnp.stack([local_row, jnp.arange(requests, dtype=jnp.int32)], axis=1))
     )
@@ -321,16 +385,12 @@
     valid = jnp.arange(slots, dtype=jnp.int32)[None, :] < seg_counts[:, None]
     inv_cos = (1.0 / norm_cos).reshape(sched_dev, 1, nper)
     inv_sin = (1.0 / norm_sin).reshape(sched_dev, 1, nper)
-    current = residuals.astype(jnp.float32)
+    current = residuals.astype(jnp.float32).reshape(seg_dev * slots, width)
     evidence = jnp.zeros((sched_dev, SRC_GROUP), jnp.float32)
     attitude_all = lax.all_gather(attitude, "sky", axis=1, tiled=True)
     for iteration in range(ITERS):
-        masked = jnp.where(valid[:, :, None], current, 0.0).astype(jnp.bfloat16)
-        white = jnp.einsum(
-            "sij,sjc->sic", attitude_all, masked, preferred_element_type=jnp.float32
-        )
-        picked = row_gather(
-            with_zero_rows(white.reshape(-1, SRC_GROUP)), asked, jnp.bfloat16, norm_cos)
+        white = whiten_rows(seg_counts, current, attitude_all, SRC_GROUP)
+        picked = row_gather(white, asked, jnp.bfloat16, norm_cos)
         outbound = picked.reshape(tm_count, capacity, SRC_GROUP)
         if iteration == 0:
             arrived = lax.all_to_all(outbound, "tm", split_axis=0, concat_axis=0, tiled=True)
@@ -340,13 +400,12 @@
         observed = row_gather(arrived.reshape(-1, SRC_GROUP), slot_of, jnp.bfloat16)
         observed = observed.reshape(sched_dev, obs, SRC_GROUP)
         model, evidence = fit_fused(basis, observed, inv_cos, inv_sin)
-        outgoing = row_gather(
-            with_zero_rows(model.reshape(requests, SRC_GROUP)), inverse, jnp.bfloat16)
+        outgoing = row_gather(model.reshape(requests, SRC_GROUP), inverse, jnp.bfloat16)
         returned = tm_all_to_all(
             outgoing.reshape(tm_count, capacity, SRC_GROUP),
             jnp.float32, 2 + 2 * iteration)
-        placed = scatter_add(returned.reshape(-1, SRC_GROUP), asked, empty_row)
-        current = current - placed.reshape(seg_dev, slots, width)
+        current = scatter_sub(returned.reshape(-1, SRC_GROUP), asked, current)
+    current = current.reshape(seg_dev, slots, width)
     return (current, evidence)
 
 

time: 290 us -> 268 us (0.924)
  local copies, waits for them, and re-layouts: 38 us -> 15.2 us
  Pallas kernels: 187 us -> 197 us
  matrix products: 6.92 us -> 0.19 us
    pallas_call x2 -> x4, Pallas kernels: 30.3 us -> 40.4 us  [the longest x2 31.8 us: scatter_sub(): pl.pallas_call(scatter_sub_kernel, in_specs=[pl.BlockSpec(memory_space=pl...]
    concatenate x4 -> x0, local copies, waits for them, and re-layouts: 9.03 us -> none  [with_zero_rows(): jnp.concatenate([flat, jnp.zeros((8, flat.shape[1]), flat.dtype)], axis=0)]
    reshape x4 -> x0, local copies, waits for them, and re-layouts: 9 us -> none  [the longest x2 4.76 us: on_device(): current = current - placed.reshape(seg_dev, slots, width)]
    dot_general x2 -> x0, matrix products: 6.73 us -> none  [on_device(): jnp.einsum('sij,sjc->sic', attitude_all, masked, preferred_element_type=j...]
    dot_general x2 -> x0, local copies, waits for them, and re-layouts: 4.74 us -> none  [on_device(): jnp.einsum('sij,sjc->sic', attitude_all, masked, preferred_element_type=j...]
    sub x1 -> x0, other arithmetic: 3.25 us -> none  [on_device(): current = current - placed.reshape(seg_dev, slots, width)]
  transfers between devices with their start and end apart: 3 -> 3, of which waited for: 1 -> 1; matrix products, arithmetic and copies ran while one was open for 9% -> 7% of each run, Pallas kernels for 9% -> 12%
where the time goes in v9:
time: 268 us; the launch traced here: 266 us
  Pallas kernels  197 us (74%)
  waiting for transfers between devices  16.3 us (6%)
  starting transfers between devices  16.1 us (6%)
  local copies, waits for them, and re-layouts  15.2 us (6%)
  between operations  14.3 us (5%)
  other arithmetic  6.98 us (3%)
    pallas_call x3, Pallas kernels, tm_all_to_all(): pl.pallas_call(a2a_kernel, in_specs=[pl.BlockSpec(memory_space=pltpu.VMEM...  69.9 us
    pallas_call x6, Pallas kernels, row_gather(): pl.pallas_call(gather_kernel, in_specs=[pl.BlockSpec(memory_space=pltpu.S...  37.1 us
    pallas_call x2, Pallas kernels, scatter_sub(): pl.pallas_call(scatter_sub_kernel, in_specs=[pl.BlockSpec(memory_space=pl...  31.8 us
    pallas_call x1, Pallas kernels, basis_and_norms(): pl.pallas_call(basis_kernel, grid=(plans,), in_specs=[pl.BlockSpec((None,...  27 us
    pallas_call x2, Pallas kernels, fit_fused(): pl.pallas_call(fit_kernel, grid=(plans,), in_specs=[pl.BlockSpec((None, o...  22.3 us
    all_to_all x1, waiting for transfers between devices, on_device(): lax.all_to_all(outbound, 'tm', split_axis=0, concat_axis=0, tiled=True)  15.6 us
    all_to_all x1, starting transfers between devices, on_device(): lax.all_to_all(wanted, 'tm', split_axis=0, concat_axis=0, tiled=True)  8.72 us
    pallas_call x2, Pallas kernels, whiten_rows(): pl.pallas_call(white_kernel, in_specs=[pl.BlockSpec(memory_space=pltpu.SM...  8.66 us
  transfers between devices with their start and end apart: 3, of which 1 were waited for; matrix products, arithmetic and copies ran while one was open for 7% of the time, Pallas kernels for 12%

profile of v9, /device:TPU:1, one launch (start us, length us, event | category | flops | bytes accessed | tf_op | source)
XLA Modules:
  0.0 265.7 jit_solution(12758570032326497114)
XLA Ops:
  7.2 0.0 copy-start.8
  7.2 0.0 all-gather.2.cloned.1.call-start
  7.2 0.7 all-gather.2.cloned.1.call-update
  7.9 0.1 broadcast_bitcast_fusion
  8.0 0.7 reshape.286
  8.7 0.7 copy.29
  9.4 0.7 copy.31
  10.1 0.2 convolution_bitcast_fusion
  10.3 0.1 slice.12
  10.5 0.2 copy.23
  10.7 0.2 copy.24
  10.8 0.3 subtract_reduce_fusion
  11.1 0.1 fusion.1
  11.3 0.1 fusion.11
  11.4 0.4 copy.25
  11.8 0.1 broadcast_in_dim.4
  11.9 6.4 %scatter_fusion = s32[4096,2]{1,0:T(8,128)S(1)} fusion(s32[4096,2]{1,0:T(8,128)S(1)} %broadcast_in_dim.4, s32[2048]{0:T(1024)S(1)} %bitcast.76, s32[2048,2]{1,0:T(8,128)S(1)} %copy.25), kind=kCustom, calls=%fused_computation | custom fusion | bytes 57344 | tf_op jit(solution)/shard_map/scatter | solution.py:379
  18.3 0.0 copy-start.7
  18.4 2.3 slice_reduce_fusion
  20.7 8.7 %all-to-all-start = ((s32[32,1,128]{2,1,0:T(1,128)}), s32[32,1,128]{2,1,0:T(1,128)S(1)}, u32[]{:S(2)}, u32[]{:S(2)}) async-start(s32[32,1,128]{2,1,0:T(1,128)} %bitcast.4), calls=%async_computation | async-start | bytes 32768 | tf_op jit(solution)/shard_map/all_to_all | solution.py:383
  29.4 0.6 convert_element_type.39
  30.0 1.3 copy.27.t_ref
  31.4 0.6 broadcast_divide_fusion.2
  32.0 27.0 %shard_map.86 = (bf16[8,256,2048]{2,1,0:T(8,128)(2,1)}, f32[8,1,1024]{2,1,0:T(1,128)}, f32[8,1,1024]{2,1,0:T(1,128)}) custom-call(f32[8,256,1]{2,1,0:T(8,128)} %copy.27.t_ref, f32[1,1024]{1,0:T(1,128)} %bitcast.85, f32[1,1024]{1,0:T(1,128)} %bitcast.84, f32[1,1024]{1,0:T(1,128)} %bitcast.83), custom_call_target="tpu_custom_call" | custom-call | flops 125829120 | bytes 8388608 | tf_op jit(solution)/shard_map/pallas_call | solution.py:78
  58.9 1.4 copy.34
  60.3 1.5 bitcast_convert_fusion.1.cur_ref
  61.9 4.4 %shard_map.87.src_ref = f32[4104,128]{1,0:T(8,128)} custom-call(s32[4]{0:T(128)} %cnt_ref.3, f32[2048,256]{1,0:T(8,128)} %bitcast_convert_fusion.1.cur_ref, bf16[4,512,512]{2,1,0:T(8,128)(2,1)} %all-gather.2.cloned.1.call-done.att_ref), custom_call_target="tpu_custom_call" | custom-call | flops 536870912 | bytes 6291456 | tf_op jit(solution)/shard_map/pallas_call | solution.py:290
  66.3 0.6 copy-done.2
  66.9 7.1 %shard_map.88 = bf16[4096,128]{1,0:T(8,128)(2,1)} custom-call(s32[4096]{0:T(1024)} %bitcast.68, f32[4104,128]{1,0:T(8,128)} %shard_map.87.src_ref, f32[8,1024]{1,0:T(8,128)} %bitcast.72), custom_call_target="tpu_custom_call" | custom-call | bytes 4194304 | tf_op jit(solution)/shard_map/pallas_call | solution.py:116
  74.0 7.4 %all-to-all-start.1 = ((bf16[32,128,128]{2,1,0:T(8,128)(2,1)}), bf16[32,128,128]{2,1,0:T(8,128)(2,1)S(1)}, u32[]{:S(2)}, u32[]{:S(2)}) async-start(bf16[32,128,128]{2,1,0:T(8,128)(2,1)} %bitcast.62), calls=%async_computation.1 | async-start | bytes 2097152 | tf_op jit(solution)/shard_map/all_to_all | solution.py:396
  81.4 0.6 fusion.8.idx_ref
  82.0 0.7 broadcast_divide_fusion
  82.7 15.6 %all-to-all-done.1 = bf16[32,128,128]{2,1,0:T(8,128)(2,1)S(1)} async-done(((bf16[32,128,128]{2,1,0:T(8,128)(2,1)}), bf16[32,128,128]{2,1,0:T(8,128)(2,1)S(1)}, u32[]{:S(2)}, u32[]{:S(2)}) %all-to-all-start.1) | async-done | bytes 1048608 | tf_op jit(solution)/shard_map/all_to_all | solution.py:396
  98.3 1.6 bitcast_convert_fusion.src_ref
  99.9 4.7 %shard_map.89 = bf16[2048,128]{1,0:T(8,128)(2,1)} custom-call(s32[2048]{0:T(1024)} %fusion.8.idx_ref, f32[4096,128]{1,0:T(8,128)} %bitcast_convert_fusion.src_ref), custom_call_target="tpu_custom_call" | custom-call | bytes 2097152 | tf_op jit(solution)/shard_map/pallas_call | solution.py:116
  104.5 11.1 %shard_map.90 = (f32[8,256,128]{2,1,0:T(8,128)}, f32[8,128,1]{2,1,0:T(8,128)}) custom-call(bf16[8,256,2048]{2,1,0:T(8,128)(2,1)} %get-tuple-element.8.basis_ref, bf16[8,256,128]{2,1,0:T(8,128)(2,1)} %bitcast.65, f32[8,1,1024]{2,1,0:T(1,128)} %get-tuple-element.21.inc_ref, f32[8,1,1024]{2,1,0:T(1,128)} %get-tuple-element.20.ins_ref), custom_call_target="tpu_custom_call" | custom-call | flops 2147483648 | bytes 8388608 | tf_op jit(solution)/shard_map/pallas_call | solution.py:249
  115.7 6.7 %shard_map.91 = bf16[4096,128]{1,0:T(8,128)(2,1)} custom-call(s32[4096]{0:T(1024)} %get-tuple-element.14.idx_ref, f32[2048,128]{1,0:T(8,128)} %bitcast.67), custom_call_target="tpu_custom_call" | custom-call | bytes 4194304 | tf_op jit(solution)/shard_map/pallas_call | solution.py:116
  122.4 20.0 %shard_map.92 = f32[32,128,128]{2,1,0:T(8,128)} custom-call(bf16[32,128,128]{2,1,0:T(8,128)(2,1)} %bitcast.61), custom_call_target="tpu_custom_call" | custom-call | tf_op jit(solution)/shard_map/pallas_call | solution.py:174
  142.4 15.9 %shard_map.93.cur_ref = f32[2048,256]{1,0:T(8,128)} custom-call(s32[4096]{0:T(1024)} %bitcast.69, f32[4096,128]{1,0:T(8,128)} %bitcast.57, f32[2048,256]{1,0:T(8,128)} %bitcast_convert_fusion.1.cur_ref), custom_call_target="tpu_custom_call" | custom-call | flops 524288 | bytes 6291456 | tf_op jit(solution)/shard_map/pallas_call | solution.py:326
  158.2 4.3 %shard_map.94.src_ref = f32[4104,128]{1,0:T(8,128)} custom-call(s32[4]{0:T(128)} %cnt_ref.3, f32[2048,256]{1,0:T(8,128)} %shard_map.93.cur_ref, bf16[4,512,512]{2,1,0:T(8,128)(2,1)} %all-gather.2.cloned.1.call-done.att_ref), custom_call_target="tpu_custom_call" | custom-call | flops 536870912 | bytes 6291456 | tf_op jit(solution)/shard_map/pallas_call | solution.py:290
  162.5 7.1 %shard_map.95 = bf16[4096,128]{1,0:T(8,128)(2,1)} custom-call(s32[4096]{0:T(1024)} %bitcast.70, f32[4104,128]{1,0:T(8,128)} %shard_map.94.src_ref, f32[8,1024]{1,0:T(8,128)} %bitcast.73), custom_call_target="tpu_custom_call" | custom-call | bytes 4194304 | tf_op jit(solution)/shard_map/pallas_call | solution.py:116
  169.6 26.4 %shard_map.96 = f32[32,128,128]{2,1,0:T(8,128)} custom-call(bf16[32,128,128]{2,1,0:T(8,128)(2,1)} %bitcast.59), custom_call_target="tpu_custom_call" | custom-call | tf_op jit(solution)/shard_map/pallas_call | solution.py:174
  196.0 4.7 %shard_map.97 = bf16[2048,128]{1,0:T(8,128)(2,1)} custom-call(s32[2048]{0:T(1024)} %fusion.8.idx_ref, f32[4096,128]{1,0:T(8,128)} %bitcast.58), custom_call_target="tpu_custom_call" | custom-call | bytes 2097152 | tf_op jit(solution)/shard_map/pallas_call | solution.py:116
  200.7 11.1 %shard_map.98 = (f32[8,256,128]{2,1,0:T(8,128)}, f32[8,128,1]{2,1,0:T(8,128)}) custom-call(bf16[8,256,2048]{2,1,0:T(8,128)(2,1)} %get-tuple-element.8.basis_ref, bf16[8,256,128]{2,1,0:T(8,128)(2,1)} %bitcast.64, f32[8,1,1024]{2,1,0:T(1,128)} %get-tuple-element.21.inc_ref, f32[8,1,1024]{2,1,0:T(1,128)} %get-tuple-element.20.ins_ref), custom_call_target="tpu_custom_call" | custom-call | flops 2147483648 | bytes 8388608 | tf_op jit(solution)/shard_map/pallas_call | solution.py:249
  211.9 6.8 %shard_map.99 = bf16[4096,128]{1,0:T(8,128)(2,1)} custom-call(s32[4096]{0:T(1024)} %get-tuple-element.14.idx_ref, f32[2048,128]{1,0:T(8,128)} %bitcast.66), custom_call_target="tpu_custom_call" | custom-call | bytes 4194304 | tf_op jit(solution)/shard_map/pallas_call | solution.py:116
  218.7 23.5 %shard_map.100 = f32[32,128,128]{2,1,0:T(8,128)} custom-call(bf16[32,128,128]{2,1,0:T(8,128)(2,1)} %bitcast.60), custom_call_target="tpu_custom_call" | custom-call | tf_op jit(solution)/shard_map/pallas_call | solution.py:174
  242.2 15.9 %shard_map.101 = f32[2048,256]{1,0:T(8,128)} custom-call(s32[4096]{0:T(1024)} %bitcast.71, f32[4096,128]{1,0:T(8,128)} %bitcast.56, f32[2048,256]{1,0:T(8,128)} %shard_map.93.cur_ref), custom_call_target="tpu_custom_call" | custom-call | flops 524288 | bytes 6291456 | tf_op jit(solution)/shard_map/pallas_call | solution.py:326
  258.1 0.8 reduce.4
  (26 shorter events, 0.1 us)
Async XLA Ops:
  7.2 4.6 %copy-start.8 = (s32[2]{0:T(128)S(1)}, s32[2]{0:T(128)}, u32[]{:S(2)}) copy-start(s32[2]{0:T(128)} %constant.65.clone) | copy-start | bytes 28
  7.2 54.7 %all-gather.2.cloned.1.call-start = ((), (), s32[]{:S(2)}) async-start(), calls=%async_computation.2 | async-start | bytes 2359296 | tf_op jit(solution)/shard_map/all_gather | solution.py:390
  18.3 11.1 %copy-start.7 = (s32[1024]{0:T(1024)S(1)}, s32[1024]{0:T(1024)}, u32[]{:S(2)}) copy-start(s32[1024]{0:T(1024)} %param.12) | copy-start | bytes 12292
  18.3 11.7 %copy-start.3 = (s32[8,256]{1,0:T(8,128)S(1)}, s32[8,256]{1,0:T(8,128)}, u32[]{:S(2)}) copy-start(s32[8,256]{1,0:T(8,128)} %param.10) | copy-start | bytes 24580
  18.3 11.7 %copy-start.5 = (s32[8,256]{1,0:T(8,128)S(1)}, s32[8,256]{1,0:T(8,128)}, u32[]{:S(2)}) copy-start(s32[8,256]{1,0:T(8,128)} %param.11) | copy-start | bytes 24580
  20.7 39.6 %copy-start = (bf16[4,512,256]{2,1,0:T(8,128)(2,1)S(1)}, bf16[4,512,256]{2,1,0:T(8,128)(2,1)}, u32[]{:S(2)}) copy-start(bf16[4,512,256]{2,1,0:T(8,128)(2,1)} %param.7) | copy-start | bytes 3145732
  20.7 45.6 %all-to-all-start = ((s32[32,1,128]{2,1,0:T(1,128)}), s32[32,1,128]{2,1,0:T(1,128)S(1)}, u32[]{:S(2)}, u32[]{:S(2)}) async-start(s32[32,1,128]{2,1,0:T(1,128)} %bitcast.4), calls=%async_computation | async-start | bytes 32768 | tf_op jit(solution)/shard_map/all_to_all | solution.py:383
  66.3 0.6 copy-start.2
  66.9 15.2 %copy-start.4 = (f32[8,1,1024]{2,1,0:T(1,128)S(1)}, f32[8,1,1024]{2,1,0:T(1,128)}, u32[]{:S(2)}) copy-start(f32[8,1,1024]{2,1,0:T(1,128)} %get-tuple-element.9) | copy-start | bytes 98308
  66.9 15.2 %copy-start.6 = (f32[8,1,1024]{2,1,0:T(1,128)S(1)}, f32[8,1,1024]{2,1,0:T(1,128)}, u32[]{:S(2)}) copy-start(f32[8,1,1024]{2,1,0:T(1,128)} %get-tuple-element.10) | copy-start | bytes 98308
  74.0 24.3 %all-to-all-start.1 = ((bf16[32,128,128]{2,1,0:T(8,128)(2,1)}), bf16[32,128,128]{2,1,0:T(8,128)(2,1)S(1)}, u32[]{:S(2)}, u32[]{:S(2)}) async-start(bf16[32,128,128]{2,1,0:T(8,128)(2,1)} %bitcast.62), calls=%async_computation.1 | async-start | bytes 2097152 | tf_op jit(solution)/shard_map/all_to_all | solution.py:396
  242.1 15.9 %copy-start.1 = (f32[8,128,1]{2,1,0:T(8,128)S(1)}, f32[8,128,1]{2,1,0:T(8,128)}, u32[]{:S(2)}) copy-start(f32[8,128,1]{2,1,0:T(8,128)} %get-tuple-element.13) | copy-start | bytes 12292
Sparse Core Ops, SparseCore 0:
  9.8 41.4 all-gather.1

commit v10 on v9

--- a/solution.py
+++ b/solution.py
@@ -185,8 +185,8 @@
     )(x)
 
 
-STREAMS = 4
-SUNROLL = 2
+STREAMS = 2
+SUNROLL = 4
 
 def scatter_add_kernel(idx_ref, src_ref, out_ref, acc_ref):
     rows = src_ref.shape[0]
@@ -392,11 +392,8 @@
         white = whiten_rows(seg_counts, current, attitude_all, SRC_GROUP)
         picked = row_gather(white, asked, jnp.bfloat16, norm_cos)
         outbound = picked.reshape(tm_count, capacity, SRC_GROUP)
-        if iteration == 0:
-            arrived = lax.all_to_all(outbound, "tm", split_axis=0, concat_axis=0, tiled=True)
-            arrived = arrived.astype(jnp.float32)
-        else:
-            arrived = tm_all_to_all(outbound, jnp.float32, 1 + 2 * iteration)
+        arrived = lax.all_to_all(outbound, "tm", split_axis=0, concat_axis=0, tiled=True)
+        arrived = arrived.astype(jnp.float32)
         observed = row_gather(arrived.reshape(-1, SRC_GROUP), slot_of, jnp.bfloat16)
         observed = observed.reshape(sched_dev, obs, SRC_GROUP)
         model, evidence = fit_fused(basis, observed, inv_cos, inv_sin)

time: 268 us -> 271 us (1.011)
  Pallas kernels: 197 us -> 168 us
  blocking collectives: 0 us -> 27.9 us
    pallas_call x3 -> x2, Pallas kernels: 69.9 us -> 40 us  [tm_all_to_all(): pl.pallas_call(a2a_kernel, in_specs=[pl.BlockSpec(memory_space=pltpu.VMEM...]
    all_to_all x0 -> x1, blocking collectives: none -> 27.9 us  [on_device(): lax.all_to_all(outbound, 'tm', split_axis=0, concat_axis=0, tiled=True)]
where the time goes in v10:
time: 271 us; the launch traced here: 267 us
  Pallas kernels  168 us (62%)
  blocking collectives  27.9 us (10%)
  waiting for transfers between devices  16.3 us (6%)
  starting transfers between devices  16.1 us (6%)
  local copies, waits for them, and re-layouts  15.2 us (6%)
  between operations  14.2 us (5%)
  other arithmetic  8.5 us (3%)
    pallas_call x2, Pallas kernels, tm_all_to_all(): pl.pallas_call(a2a_kernel, in_specs=[pl.BlockSpec(memory_space=pltpu.VMEM...  40 us
    pallas_call x6, Pallas kernels, row_gather(): pl.pallas_call(gather_kernel, in_specs=[pl.BlockSpec(memory_space=pltpu.S...  37 us
    pallas_call x2, Pallas kernels, scatter_sub(): pl.pallas_call(scatter_sub_kernel, in_specs=[pl.BlockSpec(memory_space=pl...  33.4 us
    all_to_all x1, blocking collectives, on_device(): lax.all_to_all(outbound, 'tm', split_axis=0, concat_axis=0, tiled=True)  27.9 us
    pallas_call x1, Pallas kernels, basis_and_norms(): pl.pallas_call(basis_kernel, grid=(plans,), in_specs=[pl.BlockSpec((None,...  26.9 us
    pallas_call x2, Pallas kernels, fit_fused(): pl.pallas_call(fit_kernel, grid=(plans,), in_specs=[pl.BlockSpec((None, o...  22.3 us
    all_to_all x1, waiting for transfers between devices, on_device(): lax.all_to_all(outbound, 'tm', split_axis=0, concat_axis=0, tiled=True)  15.6 us
    all_to_all x1, starting transfers between devices, on_device(): lax.all_to_all(wanted, 'tm', split_axis=0, concat_axis=0, tiled=True)  8.72 us
  transfers between devices with their start and end apart: 3, of which 1 were waited for; matrix products, arithmetic and copies ran while one was open for 7% of the time, Pallas kernels for 12%

profile of v10, /device:TPU:1, one launch (start us, length us, event | category | flops | bytes accessed | tf_op | source)
XLA Modules:
  0.0 266.7 jit_solution(14110680172411961878)
XLA Ops:
  7.2 0.0 copy-start.8
  7.2 0.0 all-gather.2.cloned.1.call-start
  7.2 0.7 all-gather.2.cloned.1.call-update
  7.9 0.1 broadcast_bitcast_fusion
  8.0 0.7 reshape.288
  8.7 0.7 copy.29
  9.4 0.7 copy.31
  10.1 0.2 convolution_bitcast_fusion
  10.3 0.1 slice.12
  10.5 0.2 copy.23
  10.7 0.2 copy.24
  10.8 0.3 subtract_reduce_fusion
  11.1 0.1 fusion.1
  11.3 0.1 fusion.11
  11.4 0.4 copy.25
  11.8 0.1 broadcast_in_dim.4
  11.9 6.4 %scatter_fusion = s32[4096,2]{1,0:T(8,128)S(1)} fusion(s32[4096,2]{1,0:T(8,128)S(1)} %broadcast_in_dim.4, s32[2048]{0:T(1024)S(1)} %bitcast.77, s32[2048,2]{1,0:T(8,128)S(1)} %copy.25), kind=kCustom, calls=%fused_computation | custom fusion | bytes 57344 | tf_op jit(solution)/shard_map/scatter | solution.py:379
  18.4 2.3 slice_reduce_fusion
  20.7 8.7 %all-to-all-start = ((s32[32,1,128]{2,1,0:T(1,128)}), s32[32,1,128]{2,1,0:T(1,128)S(1)}, u32[]{:S(2)}, u32[]{:S(2)}) async-start(s32[32,1,128]{2,1,0:T(1,128)} %bitcast.4), calls=%async_computation | async-start | bytes 32768 | tf_op jit(solution)/shard_map/all_to_all | solution.py:383
  29.4 0.6 convert_element_type.40
  30.0 1.3 copy.27.t_ref
  31.4 0.6 broadcast_divide_fusion.2
  32.0 26.9 %shard_map.86 = (bf16[8,256,2048]{2,1,0:T(8,128)(2,1)}, f32[8,1,1024]{2,1,0:T(1,128)}, f32[8,1,1024]{2,1,0:T(1,128)}) custom-call(f32[8,256,1]{2,1,0:T(8,128)} %copy.27.t_ref, f32[1,1024]{1,0:T(1,128)} %bitcast.86, f32[1,1024]{1,0:T(1,128)} %bitcast.85, f32[1,1024]{1,0:T(1,128)} %bitcast.84), custom_call_target="tpu_custom_call" | custom-call | flops 125829120 | bytes 8388608 | tf_op jit(solution)/shard_map/pallas_call | solution.py:78
  58.9 1.4 copy.34
  60.3 1.5 bitcast_convert_fusion.2.cur_ref
  61.8 4.4 %shard_map.87.src_ref = f32[4104,128]{1,0:T(8,128)} custom-call(s32[4]{0:T(128)} %cnt_ref.3, f32[2048,256]{1,0:T(8,128)} %bitcast_convert_fusion.2.cur_ref, bf16[4,512,512]{2,1,0:T(8,128)(2,1)} %all-gather.2.cloned.1.call-done.att_ref), custom_call_target="tpu_custom_call" | custom-call | flops 536870912 | bytes 6291456 | tf_op jit(solution)/shard_map/pallas_call | solution.py:290
  66.2 0.6 copy-done.2
  66.8 7.1 %shard_map.88 = bf16[4096,128]{1,0:T(8,128)(2,1)} custom-call(s32[4096]{0:T(1024)} %bitcast.69, f32[4104,128]{1,0:T(8,128)} %shard_map.87.src_ref, f32[8,1024]{1,0:T(8,128)} %bitcast.73), custom_call_target="tpu_custom_call" | custom-call | bytes 4194304 | tf_op jit(solution)/shard_map/pallas_call | solution.py:116
  73.9 7.4 %all-to-all-start.1 = ((bf16[32,128,128]{2,1,0:T(8,128)(2,1)}), bf16[32,128,128]{2,1,0:T(8,128)(2,1)S(1)}, u32[]{:S(2)}, u32[]{:S(2)}) async-start(bf16[32,128,128]{2,1,0:T(8,128)(2,1)} %bitcast.62), calls=%async_computation.1 | async-start | bytes 2097152 | tf_op jit(solution)/shard_map/all_to_all | solution.py:395
  81.3 0.6 fusion.8.idx_ref
  81.9 0.7 broadcast_divide_fusion
  82.6 15.6 %all-to-all-done.1 = bf16[32,128,128]{2,1,0:T(8,128)(2,1)S(1)} async-done(((bf16[32,128,128]{2,1,0:T(8,128)(2,1)}), bf16[32,128,128]{2,1,0:T(8,128)(2,1)S(1)}, u32[]{:S(2)}, u32[]{:S(2)}) %all-to-all-start.1) | async-done | bytes 1048608 | tf_op jit(solution)/shard_map/all_to_all | solution.py:395
  98.2 1.6 bitcast_convert_fusion.1.src_ref
  99.8 4.7 %shard_map.89 = bf16[2048,128]{1,0:T(8,128)(2,1)} custom-call(s32[2048]{0:T(1024)} %fusion.8.idx_ref, f32[4096,128]{1,0:T(8,128)} %bitcast_convert_fusion.1.src_ref), custom_call_target="tpu_custom_call" | custom-call | bytes 2097152 | tf_op jit(solution)/shard_map/pallas_call | solution.py:116
  104.5 11.1 %shard_map.90 = (f32[8,256,128]{2,1,0:T(8,128)}, f32[8,128,1]{2,1,0:T(8,128)}) custom-call(bf16[8,256,2048]{2,1,0:T(8,128)(2,1)} %get-tuple-element.8.basis_ref, bf16[8,256,128]{2,1,0:T(8,128)(2,1)} %bitcast.66, f32[8,1,1024]{2,1,0:T(1,128)} %get-tuple-element.21.inc_ref, f32[8,1,1024]{2,1,0:T(1,128)} %get-tuple-element.20.ins_ref), custom_call_target="tpu_custom_call" | custom-call | flops 2147483648 | bytes 8388608 | tf_op jit(solution)/shard_map/pallas_call | solution.py:249
  115.6 6.7 %shard_map.91 = bf16[4096,128]{1,0:T(8,128)(2,1)} custom-call(s32[4096]{0:T(1024)} %get-tuple-element.14.idx_ref, f32[2048,128]{1,0:T(8,128)} %bitcast.68), custom_call_target="tpu_custom_call" | custom-call | bytes 4194304 | tf_op jit(solution)/shard_map/pallas_call | solution.py:116
  122.3 20.0 %shard_map.92 = f32[32,128,128]{2,1,0:T(8,128)} custom-call(bf16[32,128,128]{2,1,0:T(8,128)(2,1)} %bitcast.61), custom_call_target="tpu_custom_call" | custom-call | tf_op jit(solution)/shard_map/pallas_call | solution.py:174
  142.3 16.7 %shard_map.93.cur_ref = f32[2048,256]{1,0:T(8,128)} custom-call(s32[4096]{0:T(1024)} %bitcast.70, f32[4096,128]{1,0:T(8,128)} %bitcast.59, f32[2048,256]{1,0:T(8,128)} %bitcast_convert_fusion.2.cur_ref), custom_call_target="tpu_custom_call" | custom-call | flops 524288 | bytes 6291456 | tf_op jit(solution)/shard_map/pallas_call | solution.py:326
  159.0 4.3 %shard_map.94.src_ref = f32[4104,128]{1,0:T(8,128)} custom-call(s32[4]{0:T(128)} %cnt_ref.3, f32[2048,256]{1,0:T(8,128)} %shard_map.93.cur_ref, bf16[4,512,512]{2,1,0:T(8,128)(2,1)} %all-gather.2.cloned.1.call-done.att_ref), custom_call_target="tpu_custom_call" | custom-call | flops 536870912 | bytes 6291456 | tf_op jit(solution)/shard_map/pallas_call | solution.py:290
  163.2 7.1 %shard_map.95 = bf16[4096,128]{1,0:T(8,128)(2,1)} custom-call(s32[4096]{0:T(1024)} %bitcast.71, f32[4104,128]{1,0:T(8,128)} %shard_map.94.src_ref, f32[8,1024]{1,0:T(8,128)} %bitcast.74), custom_call_target="tpu_custom_call" | custom-call | bytes 4194304 | tf_op jit(solution)/shard_map/pallas_call | solution.py:116
  170.3 27.9 %all_to_all.19 = bf16[32,128,128]{2,1,0:T(8,128)(2,1)S(1)} all-to-all(bf16[32,128,128]{2,1,0:T(8,128)(2,1)} %bitcast.63), channel_id=1, replica_groups=mesh['tm'=32,'sky'=8] {'tm'}, dimensions={0} | all-to-all | bytes 2097152 | tf_op jit(solution)/shard_map/all_to_all | solution.py:395
  198.2 1.5 bitcast_convert_fusion.src_ref
  199.7 4.7 %shard_map.96 = bf16[2048,128]{1,0:T(8,128)(2,1)} custom-call(s32[2048]{0:T(1024)} %fusion.8.idx_ref, f32[4096,128]{1,0:T(8,128)} %bitcast_convert_fusion.src_ref), custom_call_target="tpu_custom_call" | custom-call | bytes 2097152 | tf_op jit(solution)/shard_map/pallas_call | solution.py:116
  204.4 11.1 %shard_map.97 = (f32[8,256,128]{2,1,0:T(8,128)}, f32[8,128,1]{2,1,0:T(8,128)}) custom-call(bf16[8,256,2048]{2,1,0:T(8,128)(2,1)} %get-tuple-element.8.basis_ref, bf16[8,256,128]{2,1,0:T(8,128)(2,1)} %bitcast.65, f32[8,1,1024]{2,1,0:T(1,128)} %get-tuple-element.21.inc_ref, f32[8,1,1024]{2,1,0:T(1,128)} %get-tuple-element.20.ins_ref), custom_call_target="tpu_custom_call" | custom-call | flops 2147483648 | bytes 8388608 | tf_op jit(solution)/shard_map/pallas_call | solution.py:249
  215.6 6.7 %shard_map.98 = bf16[4096,128]{1,0:T(8,128)(2,1)} custom-call(s32[4096]{0:T(1024)} %get-tuple-element.14.idx_ref, f32[2048,128]{1,0:T(8,128)} %bitcast.67), custom_call_target="tpu_custom_call" | custom-call | bytes 4194304 | tf_op jit(solution)/shard_map/pallas_call | solution.py:116
  222.3 20.0 %shard_map.99 = f32[32,128,128]{2,1,0:T(8,128)} custom-call(bf16[32,128,128]{2,1,0:T(8,128)(2,1)} %bitcast.60), custom_call_target="tpu_custom_call" | custom-call | tf_op jit(solution)/shard_map/pallas_call | solution.py:174
  242.3 16.7 %shard_map.100 = f32[2048,256]{1,0:T(8,128)} custom-call(s32[4096]{0:T(1024)} %bitcast.72, f32[4096,128]{1,0:T(8,128)} %bitcast.58, f32[2048,256]{1,0:T(8,128)} %shard_map.93.cur_ref), custom_call_target="tpu_custom_call" | custom-call | flops 524288 | bytes 6291456 | tf_op jit(solution)/shard_map/pallas_call | solution.py:326
  259.1 0.8 reduce.4
  (27 shorter events, 0.1 us)
Async XLA Ops:
  7.2 4.6 %copy-start.8 = (s32[2]{0:T(128)S(1)}, s32[2]{0:T(128)}, u32[]{:S(2)}) copy-start(s32[2]{0:T(128)} %constant.65.clone) | copy-start | bytes 28
  7.2 54.6 %all-gather.2.cloned.1.call-start = ((), (), s32[]{:S(2)}) async-start(), calls=%async_computation.3 | async-start | bytes 2359296 | tf_op jit(solution)/shard_map/all_gather | solution.py:390
  18.3 11.1 %copy-start.7 = (s32[1024]{0:T(1024)S(1)}, s32[1024]{0:T(1024)}, u32[]{:S(2)}) copy-start(s32[1024]{0:T(1024)} %param.12) | copy-start | bytes 12292
  18.3 11.7 %copy-start.3 = (s32[8,256]{1,0:T(8,128)S(1)}, s32[8,256]{1,0:T(8,128)}, u32[]{:S(2)}) copy-start(s32[8,256]{1,0:T(8,128)} %param.10) | copy-start | bytes 24580
  18.3 11.7 %copy-start.5 = (s32[8,256]{1,0:T(8,128)S(1)}, s32[8,256]{1,0:T(8,128)}, u32[]{:S(2)}) copy-start(s32[8,256]{1,0:T(8,128)} %param.11) | copy-start | bytes 24580
  20.7 39.6 %copy-start = (bf16[4,512,256]{2,1,0:T(8,128)(2,1)S(1)}, bf16[4,512,256]{2,1,0:T(8,128)(2,1)}, u32[]{:S(2)}) copy-start(bf16[4,512,256]{2,1,0:T(8,128)(2,1)} %param.7) | copy-start | bytes 3145732
  20.7 45.5 %all-to-all-start = ((s32[32,1,128]{2,1,0:T(1,128)}), s32[32,1,128]{2,1,0:T(1,128)S(1)}, u32[]{:S(2)}, u32[]{:S(2)}) async-start(s32[32,1,128]{2,1,0:T(1,128)} %bitcast.4), calls=%async_computation | async-start | bytes 32768 | tf_op jit(solution)/shard_map/all_to_all | solution.py:383
  66.2 0.6 copy-start.2
  66.8 15.1 %copy-start.4 = (f32[8,1,1024]{2,1,0:T(1,128)S(1)}, f32[8,1,1024]{2,1,0:T(1,128)}, u32[]{:S(2)}) copy-start(f32[8,1,1024]{2,1,0:T(1,128)} %get-tuple-element.9) | copy-start | bytes 98308
  66.8 15.1 %copy-start.6 = (f32[8,1,1024]{2,1,0:T(1,128)S(1)}, f32[8,1,1024]{2,1,0:T(1,128)}, u32[]{:S(2)}) copy-start(f32[8,1,1024]{2,1,0:T(1,128)} %get-tuple-element.10) | copy-start | bytes 98308
  73.9 24.3 %all-to-all-start.1 = ((bf16[32,128,128]{2,1,0:T(8,128)(2,1)}), bf16[32,128,128]{2,1,0:T(8,128)(2,1)S(1)}, u32[]{:S(2)}, u32[]{:S(2)}) async-start(bf16[32,128,128]{2,1,0:T(8,128)(2,1)} %bitcast.62), calls=%async_computation.1 | async-start | bytes 2097152 | tf_op jit(solution)/shard_map/all_to_all | solution.py:395
  242.3 16.7 %copy-start.1 = (f32[8,128,1]{2,1,0:T(8,128)S(1)}, f32[8,128,1]{2,1,0:T(8,128)}, u32[]{:S(2)}) copy-start(f32[8,128,1]{2,1,0:T(8,128)} %get-tuple-element.13) | copy-start | bytes 12292
Sparse Core Ops, SparseCore 0:
  9.8 41.4 all-gather.1

commit v11 on v9

--- a/solution.py
+++ b/solution.py
@@ -221,10 +221,20 @@
     )(idx, src)
 
 
-def fit_kernel(basis_ref, obs_ref, inc_ref, ins_ref, model_ref, ev_ref):
+def fit_kernel(slot_ref, basis_ref, arrived_ref, inc_ref, ins_ref, model_ref, ev_ref, stage_ref):
     nper = inc_ref.shape[1]
+    obs = stage_ref.shape[0]
+    base = pl.program_id(0) * obs
+
+    def pick(b, carry):
+        r0 = pl.multiple_of(b * 32, 32)
+        for j in range(32):
+            stage_ref[pl.ds(r0 + j, 1), :] = arrived_ref[pl.ds(slot_ref[base + r0 + j], 1), :]
+        return carry
+
+    lax.fori_loop(0, obs // 32, pick, 0)
     basis = basis_ref[...]
-    obs_t = obs_ref[...].astype(jnp.float32).T.astype(jnp.bfloat16)
+    obs_t = stage_ref[...].T.astype(jnp.bfloat16)
     corr = jnp.dot(obs_t, basis, preferred_element_type=jnp.float32)
     cosine = corr[:, :nper]
     sine = corr[:, nper:]
@@ -241,24 +251,28 @@
     ev_ref[...] = highest + jnp.log(total)
 
 
-def fit_fused(basis, observed, inv_cos, inv_sin):
+def fit_fused(basis, arrived, slot_of, inv_cos, inv_sin):
     plans, obs, width = basis.shape
-    cols = observed.shape[2]
+    cols = arrived.shape[1]
     nper = width // 2
-    row = pl.BlockSpec((None, 1, nper), lambda g: (g, 0, 0))
+    row = pl.BlockSpec((None, 1, nper), lambda g, s: (g, 0, 0))
     model, ev = pl.pallas_call(
         fit_kernel,
-        grid=(plans,),
-        in_specs=[
-            pl.BlockSpec((None, obs, width), lambda g: (g, 0, 0)),
-            pl.BlockSpec((None, obs, cols), lambda g: (g, 0, 0)),
-            row,
-            row,
-        ],
-        out_specs=[
-            pl.BlockSpec((None, obs, cols), lambda g: (g, 0, 0)),
-            pl.BlockSpec((None, cols, 1), lambda g: (g, 0, 0)),
-        ],
+        grid_spec=pltpu.PrefetchScalarGridSpec(
+            num_scalar_prefetch=1,
+            grid=(plans,),
+            in_specs=[
+                pl.BlockSpec((None, obs, width), lambda g, s: (g, 0, 0)),
+                pl.BlockSpec(arrived.shape, lambda g, s: (0, 0)),
+                row,
+                row,
+            ],
+            out_specs=[
+                pl.BlockSpec((None, obs, cols), lambda g, s: (g, 0, 0)),
+                pl.BlockSpec((None, cols, 1), lambda g, s: (g, 0, 0)),
+            ],
+            scratch_shapes=[pltpu.VMEM((obs, cols), jnp.float32)],
+        ),
         out_shape=[
             jax.ShapeDtypeStruct((plans, obs, cols), jnp.float32),
             jax.ShapeDtypeStruct((plans, cols, 1), jnp.float32),
@@ -266,7 +280,7 @@
         cost_estimate=pl.CostEstimate(
             flops=4 * plans * obs * width * cols, transcendentals=plans * nper * cols,
             bytes_accessed=plans * obs * width * 2),
-    )(basis, observed, inv_cos, inv_sin)
+    )(slot_of, basis, arrived, inv_cos, inv_sin)
     return model, ev.reshape(plans, cols)
 
 
@@ -393,13 +407,12 @@
         picked = row_gather(white, asked, jnp.bfloat16, norm_cos)
         outbound = picked.reshape(tm_count, capacity, SRC_GROUP)
         if iteration == 0:
+            arrived = tm_all_to_all(outbound, jnp.float32, 1)
+        else:
             arrived = lax.all_to_all(outbound, "tm", split_axis=0, concat_axis=0, tiled=True)
             arrived = arrived.astype(jnp.float32)
-        else:
-            arrived = tm_all_to_all(outbound, jnp.float32, 1 + 2 * iteration)
-        observed = row_gather(arrived.reshape(-1, SRC_GROUP), slot_of, jnp.bfloat16)
-        observed = observed.reshape(sched_dev, obs, SRC_GROUP)
-        model, evidence = fit_fused(basis, observed, inv_cos, inv_sin)
+        model, evidence = fit_fused(
+            basis, arrived.reshape(-1, SRC_GROUP), slot_of, inv_cos, inv_sin)
         outgoing = row_gather(model.reshape(requests, SRC_GROUP), inverse, jnp.bfloat16)
         returned = tm_all_to_all(
             outgoing.reshape(tm_count, capacity, SRC_GROUP),

time: 268 us -> 268 us (level)
  blocking collectives: 0 us -> 24.9 us
  waiting for transfers between devices: 16.3 us -> 0.69 us
  starting transfers between devices: 16.1 us -> 8.76 us
  Pallas kernels: 197 us -> 192 us
    all_to_all x0 -> x1, blocking collectives: none -> 24.9 us  [on_device(): lax.all_to_all(outbound, 'tm', split_axis=0, concat_axis=0, tiled=True)]
    all_to_all x1 -> x0, waiting for transfers between devices: 15.6 us -> none  [on_device(): lax.all_to_all(outbound, 'tm', split_axis=0, concat_axis=0, tiled=True)]
    pallas_call x6 -> x4, Pallas kernels: 37.1 us -> 27.7 us  [row_gather(): pl.pallas_call(gather_kernel, in_specs=[pl.BlockSpec(memory_space=pltpu.S...]
    all_to_all x1 -> x0, starting transfers between devices: 7.39 us -> none  [on_device(): lax.all_to_all(outbound, 'tm', split_axis=0, concat_axis=0, tiled=True)]
    pallas_call x2, Pallas kernels: 22.3 us -> 27.4 us  [fit_fused(): pl.pallas_call(fit_kernel, grid_spec=pltpu.PrefetchScalarGridSpec(num_sca...]
  transfers between devices with their start and end apart: 3 -> 2, of which waited for: 1 -> 0; matrix products, arithmetic and copies ran while one was open for 7% -> 8% of each run, Pallas kernels for 12% -> 12%
where the time goes in v11:
time: 268 us; the launch traced here: 264 us
  Pallas kernels  192 us (72%)
  blocking collectives  24.9 us (9%)
  local copies, waits for them, and re-layouts  15.2 us (6%)
  between operations  14.2 us (5%)
  starting transfers between devices  8.76 us (3%)
  other arithmetic  7.71 us (3%)
    pallas_call x3, Pallas kernels, tm_all_to_all(): pl.pallas_call(a2a_kernel, in_specs=[pl.BlockSpec(memory_space=pltpu.VMEM...  69.4 us
    pallas_call x2, Pallas kernels, scatter_sub(): pl.pallas_call(scatter_sub_kernel, in_specs=[pl.BlockSpec(memory_space=pl...  31.8 us
    pallas_call x4, Pallas kernels, row_gather(): pl.pallas_call(gather_kernel, in_specs=[pl.BlockSpec(memory_space=pltpu.S...  27.7 us
    pallas_call x2, Pallas kernels, fit_fused(): pl.pallas_call(fit_kernel, grid_spec=pltpu.PrefetchScalarGridSpec(num_sca...  27.4 us
    pallas_call x1, Pallas kernels, basis_and_norms(): pl.pallas_call(basis_kernel, grid=(plans,), in_specs=[pl.BlockSpec((None,...  26.9 us
    all_to_all x1, blocking collectives, on_device(): lax.all_to_all(outbound, 'tm', split_axis=0, concat_axis=0, tiled=True)  24.9 us
    all_to_all x1, starting transfers between devices, on_device(): lax.all_to_all(wanted, 'tm', split_axis=0, concat_axis=0, tiled=True)  8.72 us
    pallas_call x2, Pallas kernels, whiten_rows(): pl.pallas_call(white_kernel, in_specs=[pl.BlockSpec(memory_space=pltpu.SM...  8.56 us
  transfers between devices with their start and end apart: 2, of which 0 were waited for; matrix products, arithmetic and copies ran while one was open for 8% of the time, Pallas kernels for 12%

profile of v11, /device:TPU:1, one launch (start us, length us, event | category | flops | bytes accessed | tf_op | source)
XLA Modules:
  0.0 263.6 jit_solution(3035276546487336366)
XLA Ops:
  7.2 0.0 copy-start.6
  7.2 0.0 all-gather.2.cloned.1.call-start
  7.2 0.7 all-gather.2.cloned.1.call-update
  7.9 0.1 broadcast_bitcast_fusion
  8.0 0.7 reshape.280
  8.7 0.7 copy.29
  9.4 0.7 copy.31
  10.1 0.2 convolution_bitcast_fusion
  10.3 0.1 slice.12
  10.5 0.2 copy.23
  10.7 0.2 copy.24
  10.8 0.3 subtract_reduce_fusion
  11.1 0.1 fusion.1
  11.3 0.1 fusion.11
  11.4 0.4 copy.25
  11.8 0.1 broadcast_in_dim.4
  11.9 6.4 %scatter_fusion = s32[4096,2]{1,0:T(8,128)S(1)} fusion(s32[4096,2]{1,0:T(8,128)S(1)} %broadcast_in_dim.4, s32[2048]{0:T(1024)S(1)} %bitcast.72, s32[2048,2]{1,0:T(8,128)S(1)} %copy.25), kind=kCustom, calls=%fused_computation | custom fusion | bytes 57344 | tf_op jit(solution)/shard_map/scatter | solution.py:393
  18.3 0.0 copy-start.5
  18.3 0.0 copy-start.3
  18.3 0.0 copy-start.4
  18.4 2.3 slice_reduce_fusion
  20.7 8.7 %all-to-all-start = ((s32[32,1,128]{2,1,0:T(1,128)}), s32[32,1,128]{2,1,0:T(1,128)S(1)}, u32[]{:S(2)}, u32[]{:S(2)}) async-start(s32[32,1,128]{2,1,0:T(1,128)} %bitcast.4), calls=%async_computation | async-start | bytes 32768 | tf_op jit(solution)/shard_map/all_to_all | solution.py:397
  29.4 0.6 convert_element_type.39
  30.0 1.3 copy.27.t_ref
  31.4 0.6 broadcast_divide_fusion.2
  32.0 26.9 %shard_map.86 = (bf16[8,256,2048]{2,1,0:T(8,128)(2,1)}, f32[8,1,1024]{2,1,0:T(1,128)}, f32[8,1,1024]{2,1,0:T(1,128)}) custom-call(f32[8,256,1]{2,1,0:T(8,128)} %copy.27.t_ref, f32[1,1024]{1,0:T(1,128)} %bitcast.81, f32[1,1024]{1,0:T(1,128)} %bitcast.80, f32[1,1024]{1,0:T(1,128)} %bitcast.79), custom_call_target="tpu_custom_call" | custom-call | flops 125829120 | bytes 8388608 | tf_op jit(solution)/shard_map/pallas_call | solution.py:78
  58.9 1.4 copy.34
  60.3 0.6 fusion.8.slot_ref
  60.9 1.5 broadcast_divide_fusion
  62.4 1.5 bitcast_convert_fusion.1.cur_ref
  63.9 4.3 %shard_map.87.src_ref = f32[4104,128]{1,0:T(8,128)} custom-call(s32[4]{0:T(128)} %cnt_ref.3, f32[2048,256]{1,0:T(8,128)} %bitcast_convert_fusion.1.cur_ref, bf16[4,512,512]{2,1,0:T(8,128)(2,1)} %all-gather.2.cloned.1.call-done.att_ref), custom_call_target="tpu_custom_call" | custom-call | flops 536870912 | bytes 6291456 | tf_op jit(solution)/shard_map/pallas_call | solution.py:304
  68.2 0.0 all-to-all-done
  68.2 0.6 copy-done.2
  68.8 7.2 %shard_map.88 = bf16[4096,128]{1,0:T(8,128)(2,1)} custom-call(s32[4096]{0:T(1024)} %bitcast.64, f32[4104,128]{1,0:T(8,128)} %shard_map.87.src_ref, f32[8,1024]{1,0:T(8,128)} %bitcast.68), custom_call_target="tpu_custom_call" | custom-call | bytes 4194304 | tf_op jit(solution)/shard_map/pallas_call | solution.py:116
  76.0 23.0 %shard_map.89 = f32[32,128,128]{2,1,0:T(8,128)} custom-call(bf16[32,128,128]{2,1,0:T(8,128)(2,1)} %bitcast.58), custom_call_target="tpu_custom_call" | custom-call | tf_op jit(solution)/shard_map/pallas_call | solution.py:174
  98.9 13.7 %shard_map.90 = (f32[8,256,128]{2,1,0:T(8,128)}, f32[8,128,1]{2,1,0:T(8,128)}) custom-call(s32[2048]{0:T(1024)} %fusion.8.slot_ref, bf16[8,256,2048]{2,1,0:T(8,128)(2,1)} %get-tuple-element.8.basis_ref, f32[4096,128]{1,0:T(8,128)} %bitcast.56, f32[8,1,1024]{2,1,0:T(1,128)} %get-tuple-element.21.inc_ref, f32[8,1,1024]{2,1,0:T(1,128)} %get-tuple-element.20.ins_ref), custom_call_target="tpu_custom_call" | custom-call | flops 2147483648 | bytes 8388608 | tf_op jit(solution)/shard_map/pallas_call | solution.py:259
  112.6 6.7 %shard_map.91 = bf16[4096,128]{1,0:T(8,128)(2,1)} custom-call(s32[4096]{0:T(1024)} %get-tuple-element.14.idx_ref, f32[2048,128]{1,0:T(8,128)} %bitcast.63), custom_call_target="tpu_custom_call" | custom-call | bytes 4194304 | tf_op jit(solution)/shard_map/pallas_call | solution.py:116
  119.4 26.4 %shard_map.92 = f32[32,128,128]{2,1,0:T(8,128)} custom-call(bf16[32,128,128]{2,1,0:T(8,128)(2,1)} %bitcast.59), custom_call_target="tpu_custom_call" | custom-call | tf_op jit(solution)/shard_map/pallas_call | solution.py:174
  145.8 15.9 %shard_map.93.cur_ref = f32[2048,256]{1,0:T(8,128)} custom-call(s32[4096]{0:T(1024)} %bitcast.65, f32[4096,128]{1,0:T(8,128)} %bitcast.55, f32[2048,256]{1,0:T(8,128)} %bitcast_convert_fusion.1.cur_ref), custom_call_target="tpu_custom_call" | custom-call | flops 524288 | bytes 6291456 | tf_op jit(solution)/shard_map/pallas_call | solution.py:340
  161.7 4.3 %shard_map.94.src_ref = f32[4104,128]{1,0:T(8,128)} custom-call(s32[4]{0:T(128)} %cnt_ref.3, f32[2048,256]{1,0:T(8,128)} %shard_map.93.cur_ref, bf16[4,512,512]{2,1,0:T(8,128)(2,1)} %all-gather.2.cloned.1.call-done.att_ref), custom_call_target="tpu_custom_call" | custom-call | flops 536870912 | bytes 6291456 | tf_op jit(solution)/shard_map/pallas_call | solution.py:304
  166.0 7.1 %shard_map.95 = bf16[4096,128]{1,0:T(8,128)(2,1)} custom-call(s32[4096]{0:T(1024)} %bitcast.66, f32[4104,128]{1,0:T(8,128)} %shard_map.94.src_ref, f32[8,1024]{1,0:T(8,128)} %bitcast.69), custom_call_target="tpu_custom_call" | custom-call | bytes 4194304 | tf_op jit(solution)/shard_map/pallas_call | solution.py:116
  173.1 24.9 %all_to_all.14 = bf16[32,128,128]{2,1,0:T(8,128)(2,1)S(1)} all-to-all(bf16[32,128,128]{2,1,0:T(8,128)(2,1)} %bitcast.60), channel_id=1, replica_groups=mesh['tm'=32,'sky'=8] {'tm'}, dimensions={0} | all-to-all | bytes 2097152 | tf_op jit(solution)/shard_map/all_to_all | solution.py:412
  198.0 1.5 bitcast_convert_fusion.arrived_ref
  199.5 13.7 %shard_map.96 = (f32[8,256,128]{2,1,0:T(8,128)}, f32[8,128,1]{2,1,0:T(8,128)}) custom-call(s32[2048]{0:T(1024)} %fusion.8.slot_ref, bf16[8,256,2048]{2,1,0:T(8,128)(2,1)} %get-tuple-element.8.basis_ref, f32[4096,128]{1,0:T(8,128)} %bitcast_convert_fusion.arrived_ref, f32[8,1,1024]{2,1,0:T(1,128)} %get-tuple-element.21.inc_ref, ...), custom_call_target="tpu_custom_call" | custom-call | flops 2147483648 | bytes 8388608 | tf_op jit(solution)/shard_map/pallas_call | solution.py:259
  213.2 6.7 %shard_map.97 = bf16[4096,128]{1,0:T(8,128)(2,1)} custom-call(s32[4096]{0:T(1024)} %get-tuple-element.14.idx_ref, f32[2048,128]{1,0:T(8,128)} %bitcast.62), custom_call_target="tpu_custom_call" | custom-call | bytes 4194304 | tf_op jit(solution)/shard_map/pallas_call | solution.py:116
  220.0 20.0 %shard_map.98 = f32[32,128,128]{2,1,0:T(8,128)} custom-call(bf16[32,128,128]{2,1,0:T(8,128)(2,1)} %bitcast.57), custom_call_target="tpu_custom_call" | custom-call | tf_op jit(solution)/shard_map/pallas_call | solution.py:174
  240.0 15.9 %shard_map.99 = f32[2048,256]{1,0:T(8,128)} custom-call(s32[4096]{0:T(1024)} %bitcast.67, f32[4096,128]{1,0:T(8,128)} %bitcast.54, f32[2048,256]{1,0:T(8,128)} %shard_map.93.cur_ref), custom_call_target="tpu_custom_call" | custom-call | flops 524288 | bytes 6291456 | tf_op jit(solution)/shard_map/pallas_call | solution.py:340
  255.9 0.8 reduce.4
  (19 shorter events, 0.1 us)
Async XLA Ops:
  7.2 4.6 %copy-start.6 = (s32[2]{0:T(128)S(1)}, s32[2]{0:T(128)}, u32[]{:S(2)}) copy-start(s32[2]{0:T(128)} %constant.65.clone) | copy-start | bytes 28
  7.2 56.7 %all-gather.2.cloned.1.call-start = ((), (), s32[]{:S(2)}) async-start(), calls=%async_computation.2 | async-start | bytes 2359296 | tf_op jit(solution)/shard_map/all_gather | solution.py:404
  18.3 11.1 %copy-start.5 = (s32[1024]{0:T(1024)S(1)}, s32[1024]{0:T(1024)}, u32[]{:S(2)}) copy-start(s32[1024]{0:T(1024)} %param.12) | copy-start | bytes 12292
  18.3 11.7 %copy-start.3 = (s32[8,256]{1,0:T(8,128)S(1)}, s32[8,256]{1,0:T(8,128)}, u32[]{:S(2)}) copy-start(s32[8,256]{1,0:T(8,128)} %param.10) | copy-start | bytes 24580
  18.3 11.7 %copy-start.4 = (s32[8,256]{1,0:T(8,128)S(1)}, s32[8,256]{1,0:T(8,128)}, u32[]{:S(2)}) copy-start(s32[8,256]{1,0:T(8,128)} %param.11) | copy-start | bytes 24580
  20.7 41.7 %copy-start = (bf16[4,512,256]{2,1,0:T(8,128)(2,1)S(1)}, bf16[4,512,256]{2,1,0:T(8,128)(2,1)}, u32[]{:S(2)}) copy-start(bf16[4,512,256]{2,1,0:T(8,128)(2,1)} %param.7) | copy-start | bytes 3145732
  20.7 47.5 %all-to-all-start = ((s32[32,1,128]{2,1,0:T(1,128)}), s32[32,1,128]{2,1,0:T(1,128)S(1)}, u32[]{:S(2)}, u32[]{:S(2)}) async-start(s32[32,1,128]{2,1,0:T(1,128)} %bitcast.4), calls=%async_computation | async-start | bytes 32768 | tf_op jit(solution)/shard_map/all_to_all | solution.py:397
  68.2 0.6 copy-start.2
  240.0 15.9 %copy-start.1 = (f32[8,128,1]{2,1,0:T(8,128)S(1)}, f32[8,128,1]{2,1,0:T(8,128)}, u32[]{:S(2)}) copy-start(f32[8,128,1]{2,1,0:T(8,128)} %get-tuple-element.13) | copy-start | bytes 12292
Sparse Core Ops, SparseCore 0:
  9.8 41.3 all-gather.1

commit v12 on v11

--- a/solution.py
+++ b/solution.py
@@ -154,11 +154,12 @@
             device_id_type=pl.DeviceIdType.MESH,
         )
 
-    def start(k, carry):
-        copy(k).start()
-        return carry
-
-    lax.fori_loop(1, n, start, 0)
+    def start(j, carry):
+        odd = j % 2
+        copy((1 - odd) * (j // 2 + 1) + odd * (n - 1 - j // 2)).start()
+        return carry
+
+    lax.fori_loop(0, n - 1, start, 0)
     held[pl.ds(me, 1)] = x_ref[pl.ds(me, 1)]
 
     def finish(k, carry):

time: 268 us -> 256 us (0.955); the launches traced: 264 us -> 255 us
  Pallas kernels: 192 us -> 185 us
    pallas_call x3, Pallas kernels: 69.4 us -> 62.8 us  [tm_all_to_all(): pl.pallas_call(a2a_kernel, in_specs=[pl.BlockSpec(memory_space=pltpu.VMEM...]
where the time goes in v12:
time: 256 us; the launch traced here: 255 us
  Pallas kernels  185 us (72%)
  blocking collectives  22.9 us (9%)
  local copies, waits for them, and re-layouts  15.2 us (6%)
  between operations  14.2 us (6%)
  starting transfers between devices  8.76 us (3%)
  other arithmetic  7.71 us (3%)
    pallas_call x3, Pallas kernels, tm_all_to_all(): pl.pallas_call(a2a_kernel, in_specs=[pl.BlockSpec(memory_space=pltpu.VMEM...  62.8 us
    pallas_call x2, Pallas kernels, scatter_sub(): pl.pallas_call(scatter_sub_kernel, in_specs=[pl.BlockSpec(memory_space=pl...  31.8 us
    pallas_call x4, Pallas kernels, row_gather(): pl.pallas_call(gather_kernel, in_specs=[pl.BlockSpec(memory_space=pltpu.S...  27.7 us
    pallas_call x2, Pallas kernels, fit_fused(): pl.pallas_call(fit_kernel, grid_spec=pltpu.PrefetchScalarGridSpec(num_sca...  27.4 us
    pallas_call x1, Pallas kernels, basis_and_norms(): pl.pallas_call(basis_kernel, grid=(plans,), in_specs=[pl.BlockSpec((None,...  26.9 us
    all_to_all x1, blocking collectives, on_device(): lax.all_to_all(outbound, 'tm', split_axis=0, concat_axis=0, tiled=True)  22.9 us
    all_to_all x1, starting transfers between devices, on_device(): lax.all_to_all(wanted, 'tm', split_axis=0, concat_axis=0, tiled=True)  8.72 us
    pallas_call x2, Pallas kernels, whiten_rows(): pl.pallas_call(white_kernel, in_specs=[pl.BlockSpec(memory_space=pltpu.SM...  8.56 us
  transfers between devices with their start and end apart: 2, of which 0 were waited for; matrix products, arithmetic and copies ran while one was open for 8% of the time, Pallas kernels for 12%

profile of v12, /device:TPU:1, one launch (start us, length us, event | category | flops | bytes accessed | tf_op | source)
XLA Modules:
  0.0 255.0 jit_solution(8309931169458665799)
XLA Ops:
  7.2 0.0 copy-start.6
  7.2 0.0 all-gather.2.cloned.1.call-start
  7.2 0.7 all-gather.2.cloned.1.call-update
  7.9 0.1 broadcast_bitcast_fusion
  8.0 0.7 reshape.280
  8.7 0.7 copy.29
  9.4 0.7 copy.31
  10.1 0.2 convolution_bitcast_fusion
  10.3 0.1 slice.12
  10.5 0.2 copy.23
  10.7 0.2 copy.24
  10.8 0.3 subtract_reduce_fusion
  11.1 0.1 fusion.1
  11.3 0.1 fusion.11
  11.4 0.4 copy.25
  11.8 0.1 broadcast_in_dim.4
  11.9 6.4 %scatter_fusion = s32[4096,2]{1,0:T(8,128)S(1)} fusion(s32[4096,2]{1,0:T(8,128)S(1)} %broadcast_in_dim.4, s32[2048]{0:T(1024)S(1)} %bitcast.72, s32[2048,2]{1,0:T(8,128)S(1)} %copy.25), kind=kCustom, calls=%fused_computation | custom fusion | bytes 57344 | tf_op jit(solution)/shard_map/scatter | solution.py:394
  18.3 0.0 copy-start.5
  18.3 0.0 copy-start.3
  18.3 0.0 copy-start.4
  18.4 2.3 slice_reduce_fusion
  20.7 8.7 %all-to-all-start = ((s32[32,1,128]{2,1,0:T(1,128)}), s32[32,1,128]{2,1,0:T(1,128)S(1)}, u32[]{:S(2)}, u32[]{:S(2)}) async-start(s32[32,1,128]{2,1,0:T(1,128)} %bitcast.4), calls=%async_computation | async-start | bytes 32768 | tf_op jit(solution)/shard_map/all_to_all | solution.py:398
  29.4 0.6 convert_element_type.39
  30.0 1.3 copy.27.t_ref
  31.4 0.6 broadcast_divide_fusion.2
  32.0 26.9 %shard_map.86 = (bf16[8,256,2048]{2,1,0:T(8,128)(2,1)}, f32[8,1,1024]{2,1,0:T(1,128)}, f32[8,1,1024]{2,1,0:T(1,128)}) custom-call(f32[8,256,1]{2,1,0:T(8,128)} %copy.27.t_ref, f32[1,1024]{1,0:T(1,128)} %bitcast.81, f32[1,1024]{1,0:T(1,128)} %bitcast.80, f32[1,1024]{1,0:T(1,128)} %bitcast.79), custom_call_target="tpu_custom_call" | custom-call | flops 125829120 | bytes 8388608 | tf_op jit(solution)/shard_map/pallas_call | solution.py:78
  58.9 1.4 copy.34
  60.3 0.6 fusion.8.slot_ref
  60.9 1.5 broadcast_divide_fusion
  62.4 1.5 bitcast_convert_fusion.1.cur_ref
  63.9 4.3 %shard_map.87.src_ref = f32[4104,128]{1,0:T(8,128)} custom-call(s32[4]{0:T(128)} %cnt_ref.3, f32[2048,256]{1,0:T(8,128)} %bitcast_convert_fusion.1.cur_ref, bf16[4,512,512]{2,1,0:T(8,128)(2,1)} %all-gather.2.cloned.1.call-done.att_ref), custom_call_target="tpu_custom_call" | custom-call | flops 536870912 | bytes 6291456 | tf_op jit(solution)/shard_map/pallas_call | solution.py:305
  68.2 0.0 all-to-all-done
  68.2 0.6 copy-done.2
  68.8 7.2 %shard_map.88 = bf16[4096,128]{1,0:T(8,128)(2,1)} custom-call(s32[4096]{0:T(1024)} %bitcast.64, f32[4104,128]{1,0:T(8,128)} %shard_map.87.src_ref, f32[8,1024]{1,0:T(8,128)} %bitcast.68), custom_call_target="tpu_custom_call" | custom-call | bytes 4194304 | tf_op jit(solution)/shard_map/pallas_call | solution.py:116
  76.0 22.4 %shard_map.89 = f32[32,128,128]{2,1,0:T(8,128)} custom-call(bf16[32,128,128]{2,1,0:T(8,128)(2,1)} %bitcast.58), custom_call_target="tpu_custom_call" | custom-call | tf_op jit(solution)/shard_map/pallas_call | solution.py:175
  98.4 13.7 %shard_map.90 = (f32[8,256,128]{2,1,0:T(8,128)}, f32[8,128,1]{2,1,0:T(8,128)}) custom-call(s32[2048]{0:T(1024)} %fusion.8.slot_ref, bf16[8,256,2048]{2,1,0:T(8,128)(2,1)} %get-tuple-element.8.basis_ref, f32[4096,128]{1,0:T(8,128)} %bitcast.56, f32[8,1,1024]{2,1,0:T(1,128)} %get-tuple-element.21.inc_ref, f32[8,1,1024]{2,1,0:T(1,128)} %get-tuple-element.20.ins_ref), custom_call_target="tpu_custom_call" | custom-call | flops 2147483648 | bytes 8388608 | tf_op jit(solution)/shard_map/pallas_call | solution.py:260
  112.1 6.7 %shard_map.91 = bf16[4096,128]{1,0:T(8,128)(2,1)} custom-call(s32[4096]{0:T(1024)} %get-tuple-element.14.idx_ref, f32[2048,128]{1,0:T(8,128)} %bitcast.63), custom_call_target="tpu_custom_call" | custom-call | bytes 4194304 | tf_op jit(solution)/shard_map/pallas_call | solution.py:116
  118.8 20.7 %shard_map.92 = f32[32,128,128]{2,1,0:T(8,128)} custom-call(bf16[32,128,128]{2,1,0:T(8,128)(2,1)} %bitcast.59), custom_call_target="tpu_custom_call" | custom-call | tf_op jit(solution)/shard_map/pallas_call | solution.py:175
  139.5 15.9 %shard_map.93.cur_ref = f32[2048,256]{1,0:T(8,128)} custom-call(s32[4096]{0:T(1024)} %bitcast.65, f32[4096,128]{1,0:T(8,128)} %bitcast.55, f32[2048,256]{1,0:T(8,128)} %bitcast_convert_fusion.1.cur_ref), custom_call_target="tpu_custom_call" | custom-call | flops 524288 | bytes 6291456 | tf_op jit(solution)/shard_map/pallas_call | solution.py:341
  155.4 4.3 %shard_map.94.src_ref = f32[4104,128]{1,0:T(8,128)} custom-call(s32[4]{0:T(128)} %cnt_ref.3, f32[2048,256]{1,0:T(8,128)} %shard_map.93.cur_ref, bf16[4,512,512]{2,1,0:T(8,128)(2,1)} %all-gather.2.cloned.1.call-done.att_ref), custom_call_target="tpu_custom_call" | custom-call | flops 536870912 | bytes 6291456 | tf_op jit(solution)/shard_map/pallas_call | solution.py:305
  159.7 7.1 %shard_map.95 = bf16[4096,128]{1,0:T(8,128)(2,1)} custom-call(s32[4096]{0:T(1024)} %bitcast.66, f32[4104,128]{1,0:T(8,128)} %shard_map.94.src_ref, f32[8,1024]{1,0:T(8,128)} %bitcast.69), custom_call_target="tpu_custom_call" | custom-call | bytes 4194304 | tf_op jit(solution)/shard_map/pallas_call | solution.py:116
  166.7 22.9 %all_to_all.14 = bf16[32,128,128]{2,1,0:T(8,128)(2,1)S(1)} all-to-all(bf16[32,128,128]{2,1,0:T(8,128)(2,1)} %bitcast.60), channel_id=1, replica_groups=mesh['tm'=32,'sky'=8] {'tm'}, dimensions={0} | all-to-all | bytes 2097152 | tf_op jit(solution)/shard_map/all_to_all | solution.py:413
  189.7 1.5 bitcast_convert_fusion.arrived_ref
  191.2 13.7 %shard_map.96 = (f32[8,256,128]{2,1,0:T(8,128)}, f32[8,128,1]{2,1,0:T(8,128)}) custom-call(s32[2048]{0:T(1024)} %fusion.8.slot_ref, bf16[8,256,2048]{2,1,0:T(8,128)(2,1)} %get-tuple-element.8.basis_ref, f32[4096,128]{1,0:T(8,128)} %bitcast_convert_fusion.arrived_ref, f32[8,1,1024]{2,1,0:T(1,128)} %get-tuple-element.21.inc_ref, ...), custom_call_target="tpu_custom_call" | custom-call | flops 2147483648 | bytes 8388608 | tf_op jit(solution)/shard_map/pallas_call | solution.py:260
  204.9 6.7 %shard_map.97 = bf16[4096,128]{1,0:T(8,128)(2,1)} custom-call(s32[4096]{0:T(1024)} %get-tuple-element.14.idx_ref, f32[2048,128]{1,0:T(8,128)} %bitcast.62), custom_call_target="tpu_custom_call" | custom-call | bytes 4194304 | tf_op jit(solution)/shard_map/pallas_call | solution.py:116
  211.6 19.8 %shard_map.98 = f32[32,128,128]{2,1,0:T(8,128)} custom-call(bf16[32,128,128]{2,1,0:T(8,128)(2,1)} %bitcast.57), custom_call_target="tpu_custom_call" | custom-call | tf_op jit(solution)/shard_map/pallas_call | solution.py:175
  231.4 15.9 %shard_map.99 = f32[2048,256]{1,0:T(8,128)} custom-call(s32[4096]{0:T(1024)} %bitcast.67, f32[4096,128]{1,0:T(8,128)} %bitcast.54, f32[2048,256]{1,0:T(8,128)} %shard_map.93.cur_ref), custom_call_target="tpu_custom_call" | custom-call | flops 524288 | bytes 6291456 | tf_op jit(solution)/shard_map/pallas_call | solution.py:341
  247.3 0.8 reduce.4
  (19 shorter events, 0.1 us)
Async XLA Ops:
  7.2 4.6 %copy-start.6 = (s32[2]{0:T(128)S(1)}, s32[2]{0:T(128)}, u32[]{:S(2)}) copy-start(s32[2]{0:T(128)} %constant.65.clone) | copy-start | bytes 28
  7.2 56.7 %all-gather.2.cloned.1.call-start = ((), (), s32[]{:S(2)}) async-start(), calls=%async_computation.2 | async-start | bytes 2359296 | tf_op jit(solution)/shard_map/all_gather | solution.py:405
  18.3 11.1 %copy-start.5 = (s32[1024]{0:T(1024)S(1)}, s32[1024]{0:T(1024)}, u32[]{:S(2)}) copy-start(s32[1024]{0:T(1024)} %param.12) | copy-start | bytes 12292
  18.3 11.7 %copy-start.3 = (s32[8,256]{1,0:T(8,128)S(1)}, s32[8,256]{1,0:T(8,128)}, u32[]{:S(2)}) copy-start(s32[8,256]{1,0:T(8,128)} %param.10) | copy-start | bytes 24580
  18.3 11.7 %copy-start.4 = (s32[8,256]{1,0:T(8,128)S(1)}, s32[8,256]{1,0:T(8,128)}, u32[]{:S(2)}) copy-start(s32[8,256]{1,0:T(8,128)} %param.11) | copy-start | bytes 24580
  20.7 41.7 %copy-start = (bf16[4,512,256]{2,1,0:T(8,128)(2,1)S(1)}, bf16[4,512,256]{2,1,0:T(8,128)(2,1)}, u32[]{:S(2)}) copy-start(bf16[4,512,256]{2,1,0:T(8,128)(2,1)} %param.7) | copy-start | bytes 3145732
  20.7 47.5 %all-to-all-start = ((s32[32,1,128]{2,1,0:T(1,128)}), s32[32,1,128]{2,1,0:T(1,128)S(1)}, u32[]{:S(2)}, u32[]{:S(2)}) async-start(s32[32,1,128]{2,1,0:T(1,128)} %bitcast.4), calls=%async_computation | async-start | bytes 32768 | tf_op jit(solution)/shard_map/all_to_all | solution.py:398
  68.2 0.6 copy-start.2
  231.4 15.9 %copy-start.1 = (f32[8,128,1]{2,1,0:T(8,128)S(1)}, f32[8,128,1]{2,1,0:T(8,128)}, u32[]{:S(2)}) copy-start(f32[8,128,1]{2,1,0:T(8,128)} %get-tuple-element.13) | copy-start | bytes 12292
Sparse Core Ops, SparseCore 0:
  9.8 41.3 all-gather.1

commit v13 on v12

--- a/solution.py
+++ b/solution.py
@@ -407,11 +407,7 @@
         white = whiten_rows(seg_counts, current, attitude_all, SRC_GROUP)
         picked = row_gather(white, asked, jnp.bfloat16, norm_cos)
         outbound = picked.reshape(tm_count, capacity, SRC_GROUP)
-        if iteration == 0:
-            arrived = tm_all_to_all(outbound, jnp.float32, 1)
-        else:
-            arrived = lax.all_to_all(outbound, "tm", split_axis=0, concat_axis=0, tiled=True)
-            arrived = arrived.astype(jnp.float32)
+        arrived = tm_all_to_all(outbound, jnp.float32, 1 + 2 * iteration)
         model, evidence = fit_fused(
             basis, arrived.reshape(-1, SRC_GROUP), slot_of, inv_cos, inv_sin)
         outgoing = row_gather(model.reshape(requests, SRC_GROUP), inverse, jnp.bfloat16)

time: 256 us -> 255 us (level)
  Pallas kernels: 185 us -> 209 us
  blocking collectives: 22.9 us -> 0 us
    pallas_call x3 -> x4, Pallas kernels: 62.8 us -> 86.7 us  [tm_all_to_all(): pl.pallas_call(a2a_kernel, in_specs=[pl.BlockSpec(memory_space=pltpu.VMEM...]
    all_to_all x1 -> x0, blocking collectives: 22.9 us -> none  [on_device(): lax.all_to_all(outbound, 'tm', split_axis=0, concat_axis=0, tiled=True)]
where the time goes in v13:
time: 255 us; the launch traced here: 254 us
  Pallas kernels  209 us (82%)
  local copies, waits for them, and re-layouts  15.2 us (6%)
  between operations  14.3 us (6%)
  starting transfers between devices  8.76 us (3%)
  other arithmetic  6.17 us (2%)
    pallas_call x4, Pallas kernels, tm_all_to_all(): pl.pallas_call(a2a_kernel, in_specs=[pl.BlockSpec(memory_space=pltpu.VMEM...  86.7 us
    pallas_call x2, Pallas kernels, scatter_sub(): pl.pallas_call(scatter_sub_kernel, in_specs=[pl.BlockSpec(memory_space=pl...  31.8 us
    pallas_call x4, Pallas kernels, row_gather(): pl.pallas_call(gather_kernel, in_specs=[pl.BlockSpec(memory_space=pltpu.S...  27.7 us
    pallas_call x2, Pallas kernels, fit_fused(): pl.pallas_call(fit_kernel, grid_spec=pltpu.PrefetchScalarGridSpec(num_sca...  27.4 us
    pallas_call x1, Pallas kernels, basis_and_norms(): pl.pallas_call(basis_kernel, grid=(plans,), in_specs=[pl.BlockSpec((None,...  26.9 us
    all_to_all x1, starting transfers between devices, on_device(): lax.all_to_all(wanted, 'tm', split_axis=0, concat_axis=0, tiled=True)  8.73 us
    pallas_call x2, Pallas kernels, whiten_rows(): pl.pallas_call(white_kernel, in_specs=[pl.BlockSpec(memory_space=pltpu.SM...  8.57 us
    scatter x1, local copies, waits for them, and re-layouts, on_device(): pair = jnp.broadcast_to(jnp.array([empty_row, 0], jnp.int32), (tm_count *...  6.37 us
  transfers between devices with their start and end apart: 2, of which 0 were waited for; matrix products, arithmetic and copies ran while one was open for 8% of the time, Pallas kernels for 12%

profile of v13, /device:TPU:1, one launch (start us, length us, event | category | flops | bytes accessed | tf_op | source)
XLA Modules:
  0.0 254.4 jit_solution(6674609982694953386)
XLA Ops:
  7.2 0.0 copy-start.6
  7.2 0.0 all-gather.2.cloned.1.call-start
  7.2 0.7 all-gather.2.cloned.1.call-update
  7.9 0.1 broadcast_bitcast_fusion
  8.0 0.7 reshape.278
  8.7 0.7 copy.29
  9.4 0.7 copy.31
  10.1 0.2 convolution_bitcast_fusion
  10.3 0.1 slice.12
  10.5 0.2 copy.23
  10.7 0.2 copy.24
  10.8 0.3 subtract_reduce_fusion
  11.1 0.1 fusion.1
  11.3 0.1 fusion.11
  11.4 0.4 copy.25
  11.8 0.1 broadcast_in_dim.4
  11.9 6.4 %scatter_fusion = s32[4096,2]{1,0:T(8,128)S(1)} fusion(s32[4096,2]{1,0:T(8,128)S(1)} %broadcast_in_dim.4, s32[2048]{0:T(1024)S(1)} %bitcast.71, s32[2048,2]{1,0:T(8,128)S(1)} %copy.25), kind=kCustom, calls=%fused_computation | custom fusion | bytes 57344 | tf_op jit(solution)/shard_map/scatter | solution.py:394
  18.3 0.0 copy-start.5
  18.3 0.0 copy-start.3
  18.3 0.0 copy-start.4
  18.4 2.3 slice_reduce_fusion
  20.7 8.7 %all-to-all-start = ((s32[32,1,128]{2,1,0:T(1,128)}), s32[32,1,128]{2,1,0:T(1,128)S(1)}, u32[]{:S(2)}, u32[]{:S(2)}) async-start(s32[32,1,128]{2,1,0:T(1,128)} %bitcast.4), calls=%async_computation | async-start | bytes 32768 | tf_op jit(solution)/shard_map/all_to_all | solution.py:398
  29.4 0.6 convert_element_type.38
  30.0 0.0 copy-done.3
  30.0 1.3 copy.27.t_ref
  31.4 0.6 broadcast_divide_fusion.2
  32.0 26.9 %shard_map.86 = (bf16[8,256,2048]{2,1,0:T(8,128)(2,1)}, f32[8,1,1024]{2,1,0:T(1,128)}, f32[8,1,1024]{2,1,0:T(1,128)}) custom-call(f32[8,256,1]{2,1,0:T(8,128)} %copy.27.t_ref, f32[1,1024]{1,0:T(1,128)} %bitcast.80, f32[1,1024]{1,0:T(1,128)} %bitcast.79, f32[1,1024]{1,0:T(1,128)} %bitcast.78), custom_call_target="tpu_custom_call" | custom-call | flops 125829120 | bytes 8388608 | tf_op jit(solution)/shard_map/pallas_call | solution.py:78
  58.9 1.4 copy.34
  60.3 0.6 fusion.8.slot_ref
  60.9 1.5 broadcast_divide_fusion
  62.3 1.5 bitcast_convert_fusion.cur_ref
  63.9 4.3 %shard_map.87.src_ref = f32[4104,128]{1,0:T(8,128)} custom-call(s32[4]{0:T(128)} %cnt_ref.3, f32[2048,256]{1,0:T(8,128)} %bitcast_convert_fusion.cur_ref, bf16[4,512,512]{2,1,0:T(8,128)(2,1)} %all-gather.2.cloned.1.call-done.att_ref), custom_call_target="tpu_custom_call" | custom-call | flops 536870912 | bytes 6291456 | tf_op jit(solution)/shard_map/pallas_call | solution.py:305
  68.2 0.0 all-to-all-done
  68.2 0.6 copy-done.2
  68.8 7.2 %shard_map.88 = bf16[4096,128]{1,0:T(8,128)(2,1)} custom-call(s32[4096]{0:T(1024)} %bitcast.63, f32[4104,128]{1,0:T(8,128)} %shard_map.87.src_ref, f32[8,1024]{1,0:T(8,128)} %bitcast.67), custom_call_target="tpu_custom_call" | custom-call | bytes 4194304 | tf_op jit(solution)/shard_map/pallas_call | solution.py:116
  75.9 22.4 %shard_map.89 = f32[32,128,128]{2,1,0:T(8,128)} custom-call(bf16[32,128,128]{2,1,0:T(8,128)(2,1)} %bitcast.58), custom_call_target="tpu_custom_call" | custom-call | tf_op jit(solution)/shard_map/pallas_call | solution.py:175
  98.4 13.7 %shard_map.90 = (f32[8,256,128]{2,1,0:T(8,128)}, f32[8,128,1]{2,1,0:T(8,128)}) custom-call(s32[2048]{0:T(1024)} %fusion.8.slot_ref, bf16[8,256,2048]{2,1,0:T(8,128)(2,1)} %get-tuple-element.8.basis_ref, f32[4096,128]{1,0:T(8,128)} %bitcast.55, f32[8,1,1024]{2,1,0:T(1,128)} %get-tuple-element.21.inc_ref, f32[8,1,1024]{2,1,0:T(1,128)} %get-tuple-element.20.ins_ref), custom_call_target="tpu_custom_call" | custom-call | flops 2147483648 | bytes 8388608 | tf_op jit(solution)/shard_map/pallas_call | solution.py:260
  112.1 6.7 %shard_map.91 = bf16[4096,128]{1,0:T(8,128)(2,1)} custom-call(s32[4096]{0:T(1024)} %get-tuple-element.14.idx_ref, f32[2048,128]{1,0:T(8,128)} %bitcast.62), custom_call_target="tpu_custom_call" | custom-call | bytes 4194304 | tf_op jit(solution)/shard_map/pallas_call | solution.py:116
  118.8 20.7 %shard_map.92 = f32[32,128,128]{2,1,0:T(8,128)} custom-call(bf16[32,128,128]{2,1,0:T(8,128)(2,1)} %bitcast.59), custom_call_target="tpu_custom_call" | custom-call | tf_op jit(solution)/shard_map/pallas_call | solution.py:175
  139.5 15.9 %shard_map.93.cur_ref = f32[2048,256]{1,0:T(8,128)} custom-call(s32[4096]{0:T(1024)} %bitcast.64, f32[4096,128]{1,0:T(8,128)} %bitcast.53, f32[2048,256]{1,0:T(8,128)} %bitcast_convert_fusion.cur_ref), custom_call_target="tpu_custom_call" | custom-call | flops 524288 | bytes 6291456 | tf_op jit(solution)/shard_map/pallas_call | solution.py:341
  155.4 4.3 %shard_map.94.src_ref = f32[4104,128]{1,0:T(8,128)} custom-call(s32[4]{0:T(128)} %cnt_ref.3, f32[2048,256]{1,0:T(8,128)} %shard_map.93.cur_ref, bf16[4,512,512]{2,1,0:T(8,128)(2,1)} %all-gather.2.cloned.1.call-done.att_ref), custom_call_target="tpu_custom_call" | custom-call | flops 536870912 | bytes 6291456 | tf_op jit(solution)/shard_map/pallas_call | solution.py:305
  159.6 7.1 %shard_map.95 = bf16[4096,128]{1,0:T(8,128)(2,1)} custom-call(s32[4096]{0:T(1024)} %bitcast.65, f32[4104,128]{1,0:T(8,128)} %shard_map.94.src_ref, f32[8,1024]{1,0:T(8,128)} %bitcast.68), custom_call_target="tpu_custom_call" | custom-call | bytes 4194304 | tf_op jit(solution)/shard_map/pallas_call | solution.py:116
  166.7 21.3 %shard_map.96 = f32[32,128,128]{2,1,0:T(8,128)} custom-call(bf16[32,128,128]{2,1,0:T(8,128)(2,1)} %bitcast.56), custom_call_target="tpu_custom_call" | custom-call | tf_op jit(solution)/shard_map/pallas_call | solution.py:175
  188.1 13.7 %shard_map.97 = (f32[8,256,128]{2,1,0:T(8,128)}, f32[8,128,1]{2,1,0:T(8,128)}) custom-call(s32[2048]{0:T(1024)} %fusion.8.slot_ref, bf16[8,256,2048]{2,1,0:T(8,128)(2,1)} %get-tuple-element.8.basis_ref, f32[4096,128]{1,0:T(8,128)} %bitcast.54, f32[8,1,1024]{2,1,0:T(1,128)} %get-tuple-element.21.inc_ref, f32[8,1,1024]{2,1,0:T(1,128)} %get-tuple-element.20.ins_ref), custom_call_target="tpu_custom_call" | custom-call | flops 2147483648 | bytes 8388608 | tf_op jit(solution)/shard_map/pallas_call | solution.py:260
  201.8 6.7 %shard_map.98 = bf16[4096,128]{1,0:T(8,128)(2,1)} custom-call(s32[4096]{0:T(1024)} %get-tuple-element.14.idx_ref, f32[2048,128]{1,0:T(8,128)} %bitcast.61), custom_call_target="tpu_custom_call" | custom-call | bytes 4194304 | tf_op jit(solution)/shard_map/pallas_call | solution.py:116
  208.5 22.3 %shard_map.99 = f32[32,128,128]{2,1,0:T(8,128)} custom-call(bf16[32,128,128]{2,1,0:T(8,128)(2,1)} %bitcast.57), custom_call_target="tpu_custom_call" | custom-call | tf_op jit(solution)/shard_map/pallas_call | solution.py:175
  230.9 15.9 %shard_map.100 = f32[2048,256]{1,0:T(8,128)} custom-call(s32[4096]{0:T(1024)} %bitcast.66, f32[4096,128]{1,0:T(8,128)} %bitcast.52, f32[2048,256]{1,0:T(8,128)} %shard_map.93.cur_ref), custom_call_target="tpu_custom_call" | custom-call | flops 524288 | bytes 6291456 | tf_op jit(solution)/shard_map/pallas_call | solution.py:341
  246.8 0.8 reduce.4
  (18 shorter events, 0.1 us)
Async XLA Ops:
  7.2 4.6 %copy-start.6 = (s32[2]{0:T(128)S(1)}, s32[2]{0:T(128)}, u32[]{:S(2)}) copy-start(s32[2]{0:T(128)} %constant.65.clone) | copy-start | bytes 28
  7.2 56.7 %all-gather.2.cloned.1.call-start = ((), (), s32[]{:S(2)}) async-start(), calls=%async_computation.1 | async-start | bytes 2359296 | tf_op jit(solution)/shard_map/all_gather | solution.py:405
  18.3 11.1 %copy-start.5 = (s32[1024]{0:T(1024)S(1)}, s32[1024]{0:T(1024)}, u32[]{:S(2)}) copy-start(s32[1024]{0:T(1024)} %param.12) | copy-start | bytes 12292
  18.3 11.7 %copy-start.3 = (s32[8,256]{1,0:T(8,128)S(1)}, s32[8,256]{1,0:T(8,128)}, u32[]{:S(2)}) copy-start(s32[8,256]{1,0:T(8,128)} %param.10) | copy-start | bytes 24580
  18.3 11.7 %copy-start.4 = (s32[8,256]{1,0:T(8,128)S(1)}, s32[8,256]{1,0:T(8,128)}, u32[]{:S(2)}) copy-start(s32[8,256]{1,0:T(8,128)} %param.11) | copy-start | bytes 24580
  20.7 41.7 %copy-start = (bf16[4,512,256]{2,1,0:T(8,128)(2,1)S(1)}, bf16[4,512,256]{2,1,0:T(8,128)(2,1)}, u32[]{:S(2)}) copy-start(bf16[4,512,256]{2,1,0:T(8,128)(2,1)} %param.7) | copy-start | bytes 3145732
  20.7 47.5 %all-to-all-start = ((s32[32,1,128]{2,1,0:T(1,128)}), s32[32,1,128]{2,1,0:T(1,128)S(1)}, u32[]{:S(2)}, u32[]{:S(2)}) async-start(s32[32,1,128]{2,1,0:T(1,128)} %bitcast.4), calls=%async_computation | async-start | bytes 32768 | tf_op jit(solution)/shard_map/all_to_all | solution.py:398
  68.2 0.6 copy-start.2
  230.8 15.9 %copy-start.1 = (f32[8,128,1]{2,1,0:T(8,128)S(1)}, f32[8,128,1]{2,1,0:T(8,128)}, u32[]{:S(2)}) copy-start(f32[8,128,1]{2,1,0:T(8,128)} %get-tuple-element.13) | copy-start | bytes 12292
Sparse Core Ops, SparseCore 0:
  9.8 41.2 all-gather.1

commit v14 on v13

--- a/solution.py
+++ b/solution.py
@@ -155,8 +155,8 @@
         )
 
     def start(j, carry):
-        odd = j % 2
-        copy((1 - odd) * (j // 2 + 1) + odd * (n - 1 - j // 2)).start()
+        half = (j + 1) // 2
+        copy(n // 2 + half - 2 * (j % 2) * half).start()
         return carry
 
     lax.fori_loop(0, n - 1, start, 0)

time: 255 us -> 261 us (1.024)
  Pallas kernels: 209 us -> 214 us
    pallas_call x4, Pallas kernels: 86.7 us -> 91.9 us  [tm_all_to_all(): pl.pallas_call(a2a_kernel, in_specs=[pl.BlockSpec(memory_space=pltpu.VMEM...]
where the time goes in v14:
time: 261 us; the launch traced here: 260 us
  Pallas kernels  214 us (82%)
  local copies, waits for them, and re-layouts  15.2 us (6%)
  between operations  14.3 us (5%)
  starting transfers between devices  8.76 us (3%)
  other arithmetic  6.17 us (2%)
    pallas_call x4, Pallas kernels, tm_all_to_all(): pl.pallas_call(a2a_kernel, in_specs=[pl.BlockSpec(memory_space=pltpu.VMEM...  91.9 us
    pallas_call x2, Pallas kernels, scatter_sub(): pl.pallas_call(scatter_sub_kernel, in_specs=[pl.BlockSpec(memory_space=pl...  31.8 us
    pallas_call x4, Pallas kernels, row_gather(): pl.pallas_call(gather_kernel, in_specs=[pl.BlockSpec(memory_space=pltpu.S...  27.7 us
    pallas_call x2, Pallas kernels, fit_fused(): pl.pallas_call(fit_kernel, grid_spec=pltpu.PrefetchScalarGridSpec(num_sca...  27.4 us
    pallas_call x1, Pallas kernels, basis_and_norms(): pl.pallas_call(basis_kernel, grid=(plans,), in_specs=[pl.BlockSpec((None,...  26.9 us
    all_to_all x1, starting transfers between devices, on_device(): lax.all_to_all(wanted, 'tm', split_axis=0, concat_axis=0, tiled=True)  8.73 us
    pallas_call x2, Pallas kernels, whiten_rows(): pl.pallas_call(white_kernel, in_specs=[pl.BlockSpec(memory_space=pltpu.SM...  8.57 us
    scatter x1, local copies, waits for them, and re-layouts, on_device(): pair = jnp.broadcast_to(jnp.array([empty_row, 0], jnp.int32), (tm_count *...  6.37 us
  transfers between devices with their start and end apart: 2, of which 0 were waited for; matrix products, arithmetic and copies ran while one was open for 8% of the time, Pallas kernels for 12%

profile of v14, /device:TPU:1, one launch (start us, length us, event | category | flops | bytes accessed | tf_op | source)
XLA Modules:
  0.0 259.6 jit_solution(12507892266147779931)
XLA Ops:
  7.2 0.0 copy-start.6
  7.2 0.0 all-gather.2.cloned.1.call-start
  7.2 0.7 all-gather.2.cloned.1.call-update
  7.9 0.1 broadcast_bitcast_fusion
  8.0 0.7 reshape.278
  8.7 0.7 copy.29
  9.4 0.7 copy.31
  10.1 0.2 convolution_bitcast_fusion
  10.3 0.1 slice.12
  10.5 0.2 copy.23
  10.7 0.2 copy.24
  10.8 0.3 subtract_reduce_fusion
  11.1 0.1 fusion.1
  11.3 0.1 fusion.11
  11.4 0.4 copy.25
  11.8 0.1 broadcast_in_dim.4
  11.9 6.4 %scatter_fusion = s32[4096,2]{1,0:T(8,128)S(1)} fusion(s32[4096,2]{1,0:T(8,128)S(1)} %broadcast_in_dim.4, s32[2048]{0:T(1024)S(1)} %bitcast.71, s32[2048,2]{1,0:T(8,128)S(1)} %copy.25), kind=kCustom, calls=%fused_computation | custom fusion | bytes 57344 | tf_op jit(solution)/shard_map/scatter | solution.py:394
  18.3 0.0 copy-start.5
  18.3 0.0 copy-start.3
  18.3 0.0 copy-start.4
  18.4 2.3 slice_reduce_fusion
  20.7 8.7 %all-to-all-start = ((s32[32,1,128]{2,1,0:T(1,128)}), s32[32,1,128]{2,1,0:T(1,128)S(1)}, u32[]{:S(2)}, u32[]{:S(2)}) async-start(s32[32,1,128]{2,1,0:T(1,128)} %bitcast.4), calls=%async_computation | async-start | bytes 32768 | tf_op jit(solution)/shard_map/all_to_all | solution.py:398
  29.4 0.6 convert_element_type.38
  30.0 0.0 copy-done.3
  30.0 1.3 copy.27.t_ref
  31.4 0.6 broadcast_divide_fusion.2
  32.0 26.9 %shard_map.86 = (bf16[8,256,2048]{2,1,0:T(8,128)(2,1)}, f32[8,1,1024]{2,1,0:T(1,128)}, f32[8,1,1024]{2,1,0:T(1,128)}) custom-call(f32[8,256,1]{2,1,0:T(8,128)} %copy.27.t_ref, f32[1,1024]{1,0:T(1,128)} %bitcast.80, f32[1,1024]{1,0:T(1,128)} %bitcast.79, f32[1,1024]{1,0:T(1,128)} %bitcast.78), custom_call_target="tpu_custom_call" | custom-call | flops 125829120 | bytes 8388608 | tf_op jit(solution)/shard_map/pallas_call | solution.py:78
  58.9 1.4 copy.34
  60.3 0.6 fusion.8.slot_ref
  60.9 1.5 broadcast_divide_fusion
  62.3 1.5 bitcast_convert_fusion.cur_ref
  63.9 4.3 %shard_map.87.src_ref = f32[4104,128]{1,0:T(8,128)} custom-call(s32[4]{0:T(128)} %cnt_ref.3, f32[2048,256]{1,0:T(8,128)} %bitcast_convert_fusion.cur_ref, bf16[4,512,512]{2,1,0:T(8,128)(2,1)} %all-gather.2.cloned.1.call-done.att_ref), custom_call_target="tpu_custom_call" | custom-call | flops 536870912 | bytes 6291456 | tf_op jit(solution)/shard_map/pallas_call | solution.py:305
  68.2 0.0 all-to-all-done
  68.2 0.6 copy-done.2
  68.8 7.2 %shard_map.88 = bf16[4096,128]{1,0:T(8,128)(2,1)} custom-call(s32[4096]{0:T(1024)} %bitcast.63, f32[4104,128]{1,0:T(8,128)} %shard_map.87.src_ref, f32[8,1024]{1,0:T(8,128)} %bitcast.67), custom_call_target="tpu_custom_call" | custom-call | bytes 4194304 | tf_op jit(solution)/shard_map/pallas_call | solution.py:116
  75.9 23.3 %shard_map.89 = f32[32,128,128]{2,1,0:T(8,128)} custom-call(bf16[32,128,128]{2,1,0:T(8,128)(2,1)} %bitcast.58), custom_call_target="tpu_custom_call" | custom-call | tf_op jit(solution)/shard_map/pallas_call | solution.py:175
  99.3 13.7 %shard_map.90 = (f32[8,256,128]{2,1,0:T(8,128)}, f32[8,128,1]{2,1,0:T(8,128)}) custom-call(s32[2048]{0:T(1024)} %fusion.8.slot_ref, bf16[8,256,2048]{2,1,0:T(8,128)(2,1)} %get-tuple-element.8.basis_ref, f32[4096,128]{1,0:T(8,128)} %bitcast.55, f32[8,1,1024]{2,1,0:T(1,128)} %get-tuple-element.21.inc_ref, f32[8,1,1024]{2,1,0:T(1,128)} %get-tuple-element.20.ins_ref), custom_call_target="tpu_custom_call" | custom-call | flops 2147483648 | bytes 8388608 | tf_op jit(solution)/shard_map/pallas_call | solution.py:260
  113.0 6.7 %shard_map.91 = bf16[4096,128]{1,0:T(8,128)(2,1)} custom-call(s32[4096]{0:T(1024)} %get-tuple-element.14.idx_ref, f32[2048,128]{1,0:T(8,128)} %bitcast.62), custom_call_target="tpu_custom_call" | custom-call | bytes 4194304 | tf_op jit(solution)/shard_map/pallas_call | solution.py:116
  119.7 22.8 %shard_map.92 = f32[32,128,128]{2,1,0:T(8,128)} custom-call(bf16[32,128,128]{2,1,0:T(8,128)(2,1)} %bitcast.59), custom_call_target="tpu_custom_call" | custom-call | tf_op jit(solution)/shard_map/pallas_call | solution.py:175
  142.5 15.9 %shard_map.93.cur_ref = f32[2048,256]{1,0:T(8,128)} custom-call(s32[4096]{0:T(1024)} %bitcast.64, f32[4096,128]{1,0:T(8,128)} %bitcast.53, f32[2048,256]{1,0:T(8,128)} %bitcast_convert_fusion.cur_ref), custom_call_target="tpu_custom_call" | custom-call | flops 524288 | bytes 6291456 | tf_op jit(solution)/shard_map/pallas_call | solution.py:341
  158.4 4.3 %shard_map.94.src_ref = f32[4104,128]{1,0:T(8,128)} custom-call(s32[4]{0:T(128)} %cnt_ref.3, f32[2048,256]{1,0:T(8,128)} %shard_map.93.cur_ref, bf16[4,512,512]{2,1,0:T(8,128)(2,1)} %all-gather.2.cloned.1.call-done.att_ref), custom_call_target="tpu_custom_call" | custom-call | flops 536870912 | bytes 6291456 | tf_op jit(solution)/shard_map/pallas_call | solution.py:305
  162.6 7.1 %shard_map.95 = bf16[4096,128]{1,0:T(8,128)(2,1)} custom-call(s32[4096]{0:T(1024)} %bitcast.65, f32[4104,128]{1,0:T(8,128)} %shard_map.94.src_ref, f32[8,1024]{1,0:T(8,128)} %bitcast.68), custom_call_target="tpu_custom_call" | custom-call | bytes 4194304 | tf_op jit(solution)/shard_map/pallas_call | solution.py:116
  169.7 23.2 %shard_map.96 = f32[32,128,128]{2,1,0:T(8,128)} custom-call(bf16[32,128,128]{2,1,0:T(8,128)(2,1)} %bitcast.56), custom_call_target="tpu_custom_call" | custom-call | tf_op jit(solution)/shard_map/pallas_call | solution.py:175
  192.9 13.7 %shard_map.97 = (f32[8,256,128]{2,1,0:T(8,128)}, f32[8,128,1]{2,1,0:T(8,128)}) custom-call(s32[2048]{0:T(1024)} %fusion.8.slot_ref, bf16[8,256,2048]{2,1,0:T(8,128)(2,1)} %get-tuple-element.8.basis_ref, f32[4096,128]{1,0:T(8,128)} %bitcast.54, f32[8,1,1024]{2,1,0:T(1,128)} %get-tuple-element.21.inc_ref, f32[8,1,1024]{2,1,0:T(1,128)} %get-tuple-element.20.ins_ref), custom_call_target="tpu_custom_call" | custom-call | flops 2147483648 | bytes 8388608 | tf_op jit(solution)/shard_map/pallas_call | solution.py:260
  206.6 6.7 %shard_map.98 = bf16[4096,128]{1,0:T(8,128)(2,1)} custom-call(s32[4096]{0:T(1024)} %get-tuple-element.14.idx_ref, f32[2048,128]{1,0:T(8,128)} %bitcast.61), custom_call_target="tpu_custom_call" | custom-call | bytes 4194304 | tf_op jit(solution)/shard_map/pallas_call | solution.py:116
  213.4 22.7 %shard_map.99 = f32[32,128,128]{2,1,0:T(8,128)} custom-call(bf16[32,128,128]{2,1,0:T(8,128)(2,1)} %bitcast.57), custom_call_target="tpu_custom_call" | custom-call | tf_op jit(solution)/shard_map/pallas_call | solution.py:175
  236.1 15.9 %shard_map.100 = f32[2048,256]{1,0:T(8,128)} custom-call(s32[4096]{0:T(1024)} %bitcast.66, f32[4096,128]{1,0:T(8,128)} %bitcast.52, f32[2048,256]{1,0:T(8,128)} %shard_map.93.cur_ref), custom_call_target="tpu_custom_call" | custom-call | flops 524288 | bytes 6291456 | tf_op jit(solution)/shard_map/pallas_call | solution.py:341
  252.0 0.8 reduce.4
  (18 shorter events, 0.1 us)
Async XLA Ops:
  7.2 4.6 %copy-start.6 = (s32[2]{0:T(128)S(1)}, s32[2]{0:T(128)}, u32[]{:S(2)}) copy-start(s32[2]{0:T(128)} %constant.65.clone) | copy-start | bytes 28
  7.2 56.7 %all-gather.2.cloned.1.call-start = ((), (), s32[]{:S(2)}) async-start(), calls=%async_computation.1 | async-start | bytes 2359296 | tf_op jit(solution)/shard_map/all_gather | solution.py:405
  18.3 11.1 %copy-start.5 = (s32[1024]{0:T(1024)S(1)}, s32[1024]{0:T(1024)}, u32[]{:S(2)}) copy-start(s32[1024]{0:T(1024)} %param.12) | copy-start | bytes 12292
  18.3 11.7 %copy-start.3 = (s32[8,256]{1,0:T(8,128)S(1)}, s32[8,256]{1,0:T(8,128)}, u32[]{:S(2)}) copy-start(s32[8,256]{1,0:T(8,128)} %param.10) | copy-start | bytes 24580
  18.3 11.7 %copy-start.4 = (s32[8,256]{1,0:T(8,128)S(1)}, s32[8,256]{1,0:T(8,128)}, u32[]{:S(2)}) copy-start(s32[8,256]{1,0:T(8,128)} %param.11) | copy-start | bytes 24580
  20.7 41.7 %copy-start = (bf16[4,512,256]{2,1,0:T(8,128)(2,1)S(1)}, bf16[4,512,256]{2,1,0:T(8,128)(2,1)}, u32[]{:S(2)}) copy-start(bf16[4,512,256]{2,1,0:T(8,128)(2,1)} %param.7) | copy-start | bytes 3145732
  20.7 47.5 %all-to-all-start = ((s32[32,1,128]{2,1,0:T(1,128)}), s32[32,1,128]{2,1,0:T(1,128)S(1)}, u32[]{:S(2)}, u32[]{:S(2)}) async-start(s32[32,1,128]{2,1,0:T(1,128)} %bitcast.4), calls=%async_computation | async-start | bytes 32768 | tf_op jit(solution)/shard_map/all_to_all | solution.py:398
  68.2 0.6 copy-start.2
  236.0 15.9 %copy-start.1 = (f32[8,128,1]{2,1,0:T(8,128)S(1)}, f32[8,128,1]{2,1,0:T(8,128)}, u32[]{:S(2)}) copy-start(f32[8,128,1]{2,1,0:T(8,128)} %get-tuple-element.13) | copy-start | bytes 12292
Sparse Core Ops, SparseCore 0:
  9.8 41.2 all-gather.1

commit v15 on v13

--- a/solution.py
+++ b/solution.py
@@ -129,7 +129,7 @@
     return jnp.concatenate([flat, jnp.zeros((8, flat.shape[1]), flat.dtype)], axis=0)
 
 
-def a2a_kernel(x_ref, out_ref, held, send_sem, recv_sem):
+def a2a_kernel(x_ref, out_ref, held, send_sem, recv_sem, own_sem):
     n = x_ref.shape[0]
     me = lax.axis_index("tm")
     sky = lax.axis_index("sky")
@@ -160,13 +160,15 @@
         return carry
 
     lax.fori_loop(0, n - 1, start, 0)
-    held[pl.ds(me, 1)] = x_ref[pl.ds(me, 1)]
+    own = pltpu.make_async_copy(x_ref.at[me], held.at[me], own_sem.at[0])
+    own.start()
 
     def finish(k, carry):
         copy(k).wait()
         return carry
 
     lax.fori_loop(1, n, finish, 0)
+    own.wait()
     out_ref[...] = held[...].astype(out_ref.dtype)
 
 
@@ -174,13 +176,14 @@
     n, rows, width = x.shape
     return pl.pallas_call(
         a2a_kernel,
-        in_specs=[pl.BlockSpec(memory_space=pltpu.VMEM)],
+        in_specs=[pl.BlockSpec(memory_space=pl.ANY)],
         out_specs=pl.BlockSpec(memory_space=pltpu.VMEM),
         out_shape=jax.ShapeDtypeStruct((n, rows, width), out_dtype),
         scratch_shapes=[
             pltpu.VMEM((n, rows, width), x.dtype),
             pltpu.SemaphoreType.DMA((n,)),
             pltpu.SemaphoreType.DMA((n,)),
+            pltpu.SemaphoreType.DMA((1,)),
         ],
         compiler_params=pltpu.CompilerParams(collective_id=collective_id, has_side_effects=True),
     )(x)

time: 255 us -> 252 us (0.988)
  Pallas kernels: 209 us -> 206 us
    pallas_call x4, Pallas kernels: 86.7 us -> 83.5 us  [tm_all_to_all(): pl.pallas_call(a2a_kernel, in_specs=[pl.BlockSpec(memory_space=pl.ANY)],...]
where the time goes in v15:
time: 252 us; the launch traced here: 251 us
  Pallas kernels  206 us (82%)
  local copies, waits for them, and re-layouts  15.2 us (6%)
  between operations  14.3 us (6%)
  starting transfers between devices  8.76 us (3%)
  other arithmetic  6.17 us (2%)
    pallas_call x4, Pallas kernels, tm_all_to_all(): pl.pallas_call(a2a_kernel, in_specs=[pl.BlockSpec(memory_space=pl.ANY)],...  83.5 us
    pallas_call x2, Pallas kernels, scatter_sub(): pl.pallas_call(scatter_sub_kernel, in_specs=[pl.BlockSpec(memory_space=pl...  31.8 us
    pallas_call x4, Pallas kernels, row_gather(): pl.pallas_call(gather_kernel, in_specs=[pl.BlockSpec(memory_space=pltpu.S...  27.7 us
    pallas_call x2, Pallas kernels, fit_fused(): pl.pallas_call(fit_kernel, grid_spec=pltpu.PrefetchScalarGridSpec(num_sca...  27.4 us
    pallas_call x1, Pallas kernels, basis_and_norms(): pl.pallas_call(basis_kernel, grid=(plans,), in_specs=[pl.BlockSpec((None,...  26.9 us
    all_to_all x1, starting transfers between devices, on_device(): lax.all_to_all(wanted, 'tm', split_axis=0, concat_axis=0, tiled=True)  8.73 us
    pallas_call x2, Pallas kernels, whiten_rows(): pl.pallas_call(white_kernel, in_specs=[pl.BlockSpec(memory_space=pltpu.SM...  8.57 us
    scatter x1, local copies, waits for them, and re-layouts, on_device(): pair = jnp.broadcast_to(jnp.array([empty_row, 0], jnp.int32), (tm_count *...  6.37 us
  transfers between devices with their start and end apart: 2, of which 0 were waited for; matrix products, arithmetic and copies ran while one was open for 8% of the time, Pallas kernels for 12%

profile of v15, /device:TPU:1, one launch (start us, length us, event | category | flops | bytes accessed | tf_op | source)
XLA Modules:
  0.0 251.2 jit_solution(16012213148421284882)
XLA Ops:
  7.2 0.0 copy-start.6
  7.2 0.0 all-gather.2.cloned.1.call-start
  7.2 0.7 all-gather.2.cloned.1.call-update
  7.9 0.1 broadcast_bitcast_fusion
  8.0 0.7 reshape.278
  8.7 0.7 copy.29
  9.4 0.7 copy.31
  10.1 0.2 convolution_bitcast_fusion
  10.3 0.1 slice.12
  10.5 0.2 copy.23
  10.7 0.2 copy.24
  10.8 0.3 subtract_reduce_fusion
  11.1 0.1 fusion.1
  11.3 0.1 fusion.11
  11.4 0.4 copy.25
  11.8 0.1 broadcast_in_dim.4
  11.9 6.4 %scatter_fusion = s32[4096,2]{1,0:T(8,128)S(1)} fusion(s32[4096,2]{1,0:T(8,128)S(1)} %broadcast_in_dim.4, s32[2048]{0:T(1024)S(1)} %bitcast.71, s32[2048,2]{1,0:T(8,128)S(1)} %copy.25), kind=kCustom, calls=%fused_computation | custom fusion | bytes 57344 | tf_op jit(solution)/shard_map/scatter | solution.py:397
  18.3 0.0 copy-start.5
  18.3 0.0 copy-start.3
  18.3 0.0 copy-start.4
  18.4 2.3 slice_reduce_fusion
  20.7 8.7 %all-to-all-start = ((s32[32,1,128]{2,1,0:T(1,128)}), s32[32,1,128]{2,1,0:T(1,128)S(1)}, u32[]{:S(2)}, u32[]{:S(2)}) async-start(s32[32,1,128]{2,1,0:T(1,128)} %bitcast.4), calls=%async_computation | async-start | bytes 32768 | tf_op jit(solution)/shard_map/all_to_all | solution.py:401
  29.4 0.6 convert_element_type.38
  30.0 0.0 copy-done.3
  30.0 1.3 copy.27.t_ref
  31.4 0.6 broadcast_divide_fusion.2
  32.0 26.9 %shard_map.86 = (bf16[8,256,2048]{2,1,0:T(8,128)(2,1)}, f32[8,1,1024]{2,1,0:T(1,128)}, f32[8,1,1024]{2,1,0:T(1,128)}) custom-call(f32[8,256,1]{2,1,0:T(8,128)} %copy.27.t_ref, f32[1,1024]{1,0:T(1,128)} %bitcast.80, f32[1,1024]{1,0:T(1,128)} %bitcast.79, f32[1,1024]{1,0:T(1,128)} %bitcast.78), custom_call_target="tpu_custom_call" | custom-call | flops 125829120 | bytes 8388608 | tf_op jit(solution)/shard_map/pallas_call | solution.py:78
  58.9 1.4 copy.34
  60.3 0.6 fusion.8.slot_ref
  60.9 1.5 broadcast_divide_fusion
  62.3 1.5 bitcast_convert_fusion.cur_ref
  63.9 4.3 %shard_map.87.src_ref = f32[4104,128]{1,0:T(8,128)} custom-call(s32[4]{0:T(128)} %cnt_ref.3, f32[2048,256]{1,0:T(8,128)} %bitcast_convert_fusion.cur_ref, bf16[4,512,512]{2,1,0:T(8,128)(2,1)} %all-gather.2.cloned.1.call-done.att_ref), custom_call_target="tpu_custom_call" | custom-call | flops 536870912 | bytes 6291456 | tf_op jit(solution)/shard_map/pallas_call | solution.py:308
  68.2 0.0 all-to-all-done
  68.2 0.6 copy-done.2
  68.8 7.2 %shard_map.88 = bf16[4096,128]{1,0:T(8,128)(2,1)} custom-call(s32[4096]{0:T(1024)} %bitcast.63, f32[4104,128]{1,0:T(8,128)} %shard_map.87.src_ref, f32[8,1024]{1,0:T(8,128)} %bitcast.67), custom_call_target="tpu_custom_call" | custom-call | bytes 4194304 | tf_op jit(solution)/shard_map/pallas_call | solution.py:116
  75.9 21.5 %shard_map.89 = f32[32,128,128]{2,1,0:T(8,128)} custom-call(bf16[32,128,128]{2,1,0:T(8,128)(2,1)} %bitcast.58), custom_call_target="tpu_custom_call" | custom-call | tf_op jit(solution)/shard_map/pallas_call | solution.py:177
  97.4 13.7 %shard_map.90 = (f32[8,256,128]{2,1,0:T(8,128)}, f32[8,128,1]{2,1,0:T(8,128)}) custom-call(s32[2048]{0:T(1024)} %fusion.8.slot_ref, bf16[8,256,2048]{2,1,0:T(8,128)(2,1)} %get-tuple-element.8.basis_ref, f32[4096,128]{1,0:T(8,128)} %bitcast.55, f32[8,1,1024]{2,1,0:T(1,128)} %get-tuple-element.21.inc_ref, f32[8,1,1024]{2,1,0:T(1,128)} %get-tuple-element.20.ins_ref), custom_call_target="tpu_custom_call" | custom-call | flops 2147483648 | bytes 8388608 | tf_op jit(solution)/shard_map/pallas_call | solution.py:263
  111.1 6.7 %shard_map.91 = bf16[4096,128]{1,0:T(8,128)(2,1)} custom-call(s32[4096]{0:T(1024)} %get-tuple-element.14.idx_ref, f32[2048,128]{1,0:T(8,128)} %bitcast.62), custom_call_target="tpu_custom_call" | custom-call | bytes 4194304 | tf_op jit(solution)/shard_map/pallas_call | solution.py:116
  117.9 19.7 %shard_map.92 = f32[32,128,128]{2,1,0:T(8,128)} custom-call(bf16[32,128,128]{2,1,0:T(8,128)(2,1)} %bitcast.59), custom_call_target="tpu_custom_call" | custom-call | tf_op jit(solution)/shard_map/pallas_call | solution.py:177
  137.6 15.9 %shard_map.93.cur_ref = f32[2048,256]{1,0:T(8,128)} custom-call(s32[4096]{0:T(1024)} %bitcast.64, f32[4096,128]{1,0:T(8,128)} %bitcast.53, f32[2048,256]{1,0:T(8,128)} %bitcast_convert_fusion.cur_ref), custom_call_target="tpu_custom_call" | custom-call | flops 524288 | bytes 6291456 | tf_op jit(solution)/shard_map/pallas_call | solution.py:344
  153.5 4.3 %shard_map.94.src_ref = f32[4104,128]{1,0:T(8,128)} custom-call(s32[4]{0:T(128)} %cnt_ref.3, f32[2048,256]{1,0:T(8,128)} %shard_map.93.cur_ref, bf16[4,512,512]{2,1,0:T(8,128)(2,1)} %all-gather.2.cloned.1.call-done.att_ref), custom_call_target="tpu_custom_call" | custom-call | flops 536870912 | bytes 6291456 | tf_op jit(solution)/shard_map/pallas_call | solution.py:308
  157.7 7.1 %shard_map.95 = bf16[4096,128]{1,0:T(8,128)(2,1)} custom-call(s32[4096]{0:T(1024)} %bitcast.65, f32[4104,128]{1,0:T(8,128)} %shard_map.94.src_ref, f32[8,1024]{1,0:T(8,128)} %bitcast.68), custom_call_target="tpu_custom_call" | custom-call | bytes 4194304 | tf_op jit(solution)/shard_map/pallas_call | solution.py:116
  164.8 20.2 %shard_map.96 = f32[32,128,128]{2,1,0:T(8,128)} custom-call(bf16[32,128,128]{2,1,0:T(8,128)(2,1)} %bitcast.56), custom_call_target="tpu_custom_call" | custom-call | tf_op jit(solution)/shard_map/pallas_call | solution.py:177
  185.1 13.7 %shard_map.97 = (f32[8,256,128]{2,1,0:T(8,128)}, f32[8,128,1]{2,1,0:T(8,128)}) custom-call(s32[2048]{0:T(1024)} %fusion.8.slot_ref, bf16[8,256,2048]{2,1,0:T(8,128)(2,1)} %get-tuple-element.8.basis_ref, f32[4096,128]{1,0:T(8,128)} %bitcast.54, f32[8,1,1024]{2,1,0:T(1,128)} %get-tuple-element.21.inc_ref, f32[8,1,1024]{2,1,0:T(1,128)} %get-tuple-element.20.ins_ref), custom_call_target="tpu_custom_call" | custom-call | flops 2147483648 | bytes 8388608 | tf_op jit(solution)/shard_map/pallas_call | solution.py:263
  198.8 6.7 %shard_map.98 = bf16[4096,128]{1,0:T(8,128)(2,1)} custom-call(s32[4096]{0:T(1024)} %get-tuple-element.14.idx_ref, f32[2048,128]{1,0:T(8,128)} %bitcast.61), custom_call_target="tpu_custom_call" | custom-call | bytes 4194304 | tf_op jit(solution)/shard_map/pallas_call | solution.py:116
  205.6 22.0 %shard_map.99 = f32[32,128,128]{2,1,0:T(8,128)} custom-call(bf16[32,128,128]{2,1,0:T(8,128)(2,1)} %bitcast.57), custom_call_target="tpu_custom_call" | custom-call | tf_op jit(solution)/shard_map/pallas_call | solution.py:177
  227.6 15.9 %shard_map.100 = f32[2048,256]{1,0:T(8,128)} custom-call(s32[4096]{0:T(1024)} %bitcast.66, f32[4096,128]{1,0:T(8,128)} %bitcast.52, f32[2048,256]{1,0:T(8,128)} %shard_map.93.cur_ref), custom_call_target="tpu_custom_call" | custom-call | flops 524288 | bytes 6291456 | tf_op jit(solution)/shard_map/pallas_call | solution.py:344
  243.5 0.8 reduce.4
  (18 shorter events, 0.1 us)
Async XLA Ops:
  7.2 4.6 %copy-start.6 = (s32[2]{0:T(128)S(1)}, s32[2]{0:T(128)}, u32[]{:S(2)}) copy-start(s32[2]{0:T(128)} %constant.65.clone) | copy-start | bytes 28
  7.2 56.7 %all-gather.2.cloned.1.call-start = ((), (), s32[]{:S(2)}) async-start(), calls=%async_computation.1 | async-start | bytes 2359296 | tf_op jit(solution)/shard_map/all_gather | solution.py:408
  18.3 11.1 %copy-start.5 = (s32[1024]{0:T(1024)S(1)}, s32[1024]{0:T(1024)}, u32[]{:S(2)}) copy-start(s32[1024]{0:T(1024)} %param.12) | copy-start | bytes 12292
  18.3 11.7 %copy-start.3 = (s32[8,256]{1,0:T(8,128)S(1)}, s32[8,256]{1,0:T(8,128)}, u32[]{:S(2)}) copy-start(s32[8,256]{1,0:T(8,128)} %param.10) | copy-start | bytes 24580
  18.3 11.7 %copy-start.4 = (s32[8,256]{1,0:T(8,128)S(1)}, s32[8,256]{1,0:T(8,128)}, u32[]{:S(2)}) copy-start(s32[8,256]{1,0:T(8,128)} %param.11) | copy-start | bytes 24580
  20.7 41.7 %copy-start = (bf16[4,512,256]{2,1,0:T(8,128)(2,1)S(1)}, bf16[4,512,256]{2,1,0:T(8,128)(2,1)}, u32[]{:S(2)}) copy-start(bf16[4,512,256]{2,1,0:T(8,128)(2,1)} %param.7) | copy-start | bytes 3145732
  20.7 47.5 %all-to-all-start = ((s32[32,1,128]{2,1,0:T(1,128)}), s32[32,1,128]{2,1,0:T(1,128)S(1)}, u32[]{:S(2)}, u32[]{:S(2)}) async-start(s32[32,1,128]{2,1,0:T(1,128)} %bitcast.4), calls=%async_computation | async-start | bytes 32768 | tf_op jit(solution)/shard_map/all_to_all | solution.py:401
  68.2 0.6 copy-start.2
  227.6 15.9 %copy-start.1 = (f32[8,128,1]{2,1,0:T(8,128)S(1)}, f32[8,128,1]{2,1,0:T(8,128)}, u32[]{:S(2)}) copy-start(f32[8,128,1]{2,1,0:T(8,128)} %get-tuple-element.13) | copy-start | bytes 12292
Sparse Core Ops, SparseCore 0:
  9.8 41.2 all-gather.1

commit v16 on v15

--- a/solution.py
+++ b/solution.py
@@ -316,11 +316,16 @@
     )(counts, current, attitude_all)
 
 
-def scatter_sub_kernel(idx_ref, src_ref, cur_ref, out_ref, acc_ref):
+def scatter_sub_kernel(idx_ref, src_hbm, cur_hbm, out_ref, acc_ref, src_ref, cur_ref, sems):
     rows, width = src_ref.shape
     streams = acc_ref.shape[0]
     n = cur_ref.shape[0]
+    src_copy = pltpu.make_async_copy(src_hbm, src_ref, sems.at[0])
+    cur_copy = pltpu.make_async_copy(cur_hbm, cur_ref, sems.at[1])
+    src_copy.start()
+    cur_copy.start()
     acc_ref[...] = jnp.zeros_like(acc_ref)
+    src_copy.wait()
 
     def body(step, carry):
         base = step * streams
@@ -331,6 +336,7 @@
         return carry
 
     lax.fori_loop(0, rows // streams, body, 0, unroll=SUNROLL)
+    cur_copy.wait()
     for b in range(cur_ref.shape[1] // width):
         total = acc_ref[0, pl.ds(b * n, n), :]
         for s in range(1, streams):
@@ -343,10 +349,15 @@
     blocks = current.shape[1] // width
     return pl.pallas_call(
         scatter_sub_kernel,
-        in_specs=[pl.BlockSpec(memory_space=pltpu.SMEM)] + [pl.BlockSpec(memory_space=pltpu.VMEM)] * 2,
+        in_specs=[pl.BlockSpec(memory_space=pltpu.SMEM)] + [pl.BlockSpec(memory_space=pl.ANY)] * 2,
         out_specs=pl.BlockSpec(memory_space=pltpu.VMEM),
         out_shape=jax.ShapeDtypeStruct(current.shape, jnp.float32),
-        scratch_shapes=[pltpu.VMEM((STREAMS, blocks * current.shape[0] + 8, width), jnp.float32)],
+        scratch_shapes=[
+            pltpu.VMEM((STREAMS, blocks * current.shape[0] + 8, width), jnp.float32),
+            pltpu.VMEM(src.shape, src.dtype),
+            pltpu.VMEM(current.shape, current.dtype),
+            pltpu.SemaphoreType.DMA((2,)),
+        ],
         cost_estimate=pl.CostEstimate(
             flops=rows * width, transcendentals=0, bytes_accessed=(rows * width + 2 * current.size) * 4),
     )(idx, src, current)

time: 252 us -> 252 us (level)
  no operation moved by 1% of the time
where the time goes in v16:
time: 252 us; the launch traced here: 250 us
  Pallas kernels  205 us (81%)
  local copies, waits for them, and re-layouts  15.2 us (6%)
  between operations  14.3 us (6%)
  starting transfers between devices  8.76 us (3%)
  other arithmetic  6.17 us (2%)
    pallas_call x4, Pallas kernels, tm_all_to_all(): pl.pallas_call(a2a_kernel, in_specs=[pl.BlockSpec(memory_space=pl.ANY)],...  83 us
    pallas_call x2, Pallas kernels, scatter_sub(): pl.pallas_call(scatter_sub_kernel, in_specs=[pl.BlockSpec(memory_space=pl...  31.4 us
    pallas_call x4, Pallas kernels, row_gather(): pl.pallas_call(gather_kernel, in_specs=[pl.BlockSpec(memory_space=pltpu.S...  27.7 us
    pallas_call x2, Pallas kernels, fit_fused(): pl.pallas_call(fit_kernel, grid_spec=pltpu.PrefetchScalarGridSpec(num_sca...  27.4 us
    pallas_call x1, Pallas kernels, basis_and_norms(): pl.pallas_call(basis_kernel, grid=(plans,), in_specs=[pl.BlockSpec((None,...  26.9 us
    all_to_all x1, starting transfers between devices, on_device(): lax.all_to_all(wanted, 'tm', split_axis=0, concat_axis=0, tiled=True)  8.73 us
    pallas_call x2, Pallas kernels, whiten_rows(): pl.pallas_call(white_kernel, in_specs=[pl.BlockSpec(memory_space=pltpu.SM...  8.57 us
    scatter x1, local copies, waits for them, and re-layouts, on_device(): pair = jnp.broadcast_to(jnp.array([empty_row, 0], jnp.int32), (tm_count *...  6.37 us
  transfers between devices with their start and end apart: 2, of which 0 were waited for; matrix products, arithmetic and copies ran while one was open for 8% of the time, Pallas kernels for 12%

profile of v16, /device:TPU:1, one launch (start us, length us, event | category | flops | bytes accessed | tf_op | source)
XLA Modules:
  0.0 250.3 jit_solution(197446992315746868)
XLA Ops:
  7.2 0.0 copy-start.6
  7.2 0.0 all-gather.2.cloned.1.call-start
  7.2 0.7 all-gather.2.cloned.1.call-update
  7.9 0.1 broadcast_bitcast_fusion
  8.0 0.7 reshape.278
  8.7 0.7 copy.29
  9.4 0.7 copy.31
  10.1 0.2 convolution_bitcast_fusion
  10.3 0.1 slice.12
  10.5 0.2 copy.23
  10.7 0.2 copy.24
  10.8 0.3 subtract_reduce_fusion
  11.1 0.1 fusion.1
  11.3 0.1 fusion.11
  11.4 0.4 copy.25
  11.8 0.1 broadcast_in_dim.4
  11.9 6.4 %scatter_fusion = s32[4096,2]{1,0:T(8,128)S(1)} fusion(s32[4096,2]{1,0:T(8,128)S(1)} %broadcast_in_dim.4, s32[2048]{0:T(1024)S(1)} %bitcast.71, s32[2048,2]{1,0:T(8,128)S(1)} %copy.25), kind=kCustom, calls=%fused_computation | custom fusion | bytes 57344 | tf_op jit(solution)/shard_map/scatter | solution.py:408
  18.3 0.0 copy-start.5
  18.3 0.0 copy-start.3
  18.3 0.0 copy-start.4
  18.4 2.3 slice_reduce_fusion
  20.7 8.7 %all-to-all-start = ((s32[32,1,128]{2,1,0:T(1,128)}), s32[32,1,128]{2,1,0:T(1,128)S(1)}, u32[]{:S(2)}, u32[]{:S(2)}) async-start(s32[32,1,128]{2,1,0:T(1,128)} %bitcast.4), calls=%async_computation | async-start | bytes 32768 | tf_op jit(solution)/shard_map/all_to_all | solution.py:412
  29.4 0.6 convert_element_type.38
  30.0 0.0 copy-done.3
  30.0 1.3 copy.27.t_ref
  31.4 0.6 broadcast_divide_fusion.2
  32.0 26.9 %shard_map.86 = (bf16[8,256,2048]{2,1,0:T(8,128)(2,1)}, f32[8,1,1024]{2,1,0:T(1,128)}, f32[8,1,1024]{2,1,0:T(1,128)}) custom-call(f32[8,256,1]{2,1,0:T(8,128)} %copy.27.t_ref, f32[1,1024]{1,0:T(1,128)} %bitcast.80, f32[1,1024]{1,0:T(1,128)} %bitcast.79, f32[1,1024]{1,0:T(1,128)} %bitcast.78), custom_call_target="tpu_custom_call" | custom-call | flops 125829120 | bytes 8388608 | tf_op jit(solution)/shard_map/pallas_call | solution.py:78
  58.9 1.4 copy.34
  60.3 0.6 fusion.8.slot_ref
  60.9 1.5 broadcast_divide_fusion
  62.3 1.5 bitcast_convert_fusion.cur_ref.cur_hbm
  63.9 4.3 %shard_map.87.src_ref = f32[4104,128]{1,0:T(8,128)} custom-call(s32[4]{0:T(128)} %cnt_ref.3, f32[2048,256]{1,0:T(8,128)} %bitcast_convert_fusion.cur_ref.cur_hbm, bf16[4,512,512]{2,1,0:T(8,128)(2,1)} %all-gather.2.cloned.1.call-done.att_ref), custom_call_target="tpu_custom_call" | custom-call | flops 536870912 | bytes 6291456 | tf_op jit(solution)/shard_map/pallas_call | solution.py:308
  68.2 0.0 all-to-all-done
  68.2 0.6 copy-done.2
  68.8 7.2 %shard_map.88 = bf16[4096,128]{1,0:T(8,128)(2,1)} custom-call(s32[4096]{0:T(1024)} %bitcast.63, f32[4104,128]{1,0:T(8,128)} %shard_map.87.src_ref, f32[8,1024]{1,0:T(8,128)} %bitcast.67), custom_call_target="tpu_custom_call" | custom-call | bytes 4194304 | tf_op jit(solution)/shard_map/pallas_call | solution.py:116
  75.9 21.5 %shard_map.89 = f32[32,128,128]{2,1,0:T(8,128)} custom-call(bf16[32,128,128]{2,1,0:T(8,128)(2,1)} %bitcast.58), custom_call_target="tpu_custom_call" | custom-call | tf_op jit(solution)/shard_map/pallas_call | solution.py:177
  97.4 13.7 %shard_map.90 = (f32[8,256,128]{2,1,0:T(8,128)}, f32[8,128,1]{2,1,0:T(8,128)}) custom-call(s32[2048]{0:T(1024)} %fusion.8.slot_ref, bf16[8,256,2048]{2,1,0:T(8,128)(2,1)} %get-tuple-element.8.basis_ref, f32[4096,128]{1,0:T(8,128)} %bitcast.55, f32[8,1,1024]{2,1,0:T(1,128)} %get-tuple-element.21.inc_ref, f32[8,1,1024]{2,1,0:T(1,128)} %get-tuple-element.20.ins_ref), custom_call_target="tpu_custom_call" | custom-call | flops 2147483648 | bytes 8388608 | tf_op jit(solution)/shard_map/pallas_call | solution.py:263
  111.1 6.7 %shard_map.91 = bf16[4096,128]{1,0:T(8,128)(2,1)} custom-call(s32[4096]{0:T(1024)} %get-tuple-element.14.idx_ref, f32[2048,128]{1,0:T(8,128)} %bitcast.62), custom_call_target="tpu_custom_call" | custom-call | bytes 4194304 | tf_op jit(solution)/shard_map/pallas_call | solution.py:116
  117.9 19.8 %shard_map.92 = f32[32,128,128]{2,1,0:T(8,128)} custom-call(bf16[32,128,128]{2,1,0:T(8,128)(2,1)} %bitcast.59), custom_call_target="tpu_custom_call" | custom-call | tf_op jit(solution)/shard_map/pallas_call | solution.py:177
  137.6 15.6 %shard_map.93.cur_ref.cur_hbm = f32[2048,256]{1,0:T(8,128)} custom-call(s32[4096]{0:T(1024)} %bitcast.64, f32[4096,128]{1,0:T(8,128)} %bitcast.53, f32[2048,256]{1,0:T(8,128)} %bitcast_convert_fusion.cur_ref.cur_hbm), custom_call_target="tpu_custom_call" | custom-call | flops 524288 | bytes 6291456 | tf_op jit(solution)/shard_map/pallas_call | solution.py:350
  153.2 4.3 %shard_map.94.src_ref = f32[4104,128]{1,0:T(8,128)} custom-call(s32[4]{0:T(128)} %cnt_ref.3, f32[2048,256]{1,0:T(8,128)} %shard_map.93.cur_ref.cur_hbm, bf16[4,512,512]{2,1,0:T(8,128)(2,1)} %all-gather.2.cloned.1.call-done.att_ref), custom_call_target="tpu_custom_call" | custom-call | flops 536870912 | bytes 6291456 | tf_op jit(solution)/shard_map/pallas_call | solution.py:308
  157.5 7.1 %shard_map.95 = bf16[4096,128]{1,0:T(8,128)(2,1)} custom-call(s32[4096]{0:T(1024)} %bitcast.65, f32[4104,128]{1,0:T(8,128)} %shard_map.94.src_ref, f32[8,1024]{1,0:T(8,128)} %bitcast.68), custom_call_target="tpu_custom_call" | custom-call | bytes 4194304 | tf_op jit(solution)/shard_map/pallas_call | solution.py:116
  164.6 20.2 %shard_map.96 = f32[32,128,128]{2,1,0:T(8,128)} custom-call(bf16[32,128,128]{2,1,0:T(8,128)(2,1)} %bitcast.56), custom_call_target="tpu_custom_call" | custom-call | tf_op jit(solution)/shard_map/pallas_call | solution.py:177
  184.9 13.7 %shard_map.97 = (f32[8,256,128]{2,1,0:T(8,128)}, f32[8,128,1]{2,1,0:T(8,128)}) custom-call(s32[2048]{0:T(1024)} %fusion.8.slot_ref, bf16[8,256,2048]{2,1,0:T(8,128)(2,1)} %get-tuple-element.8.basis_ref, f32[4096,128]{1,0:T(8,128)} %bitcast.54, f32[8,1,1024]{2,1,0:T(1,128)} %get-tuple-element.21.inc_ref, f32[8,1,1024]{2,1,0:T(1,128)} %get-tuple-element.20.ins_ref), custom_call_target="tpu_custom_call" | custom-call | flops 2147483648 | bytes 8388608 | tf_op jit(solution)/shard_map/pallas_call | solution.py:263
  198.6 6.7 %shard_map.98 = bf16[4096,128]{1,0:T(8,128)(2,1)} custom-call(s32[4096]{0:T(1024)} %get-tuple-element.14.idx_ref, f32[2048,128]{1,0:T(8,128)} %bitcast.61), custom_call_target="tpu_custom_call" | custom-call | bytes 4194304 | tf_op jit(solution)/shard_map/pallas_call | solution.py:116
  205.3 21.6 %shard_map.99 = f32[32,128,128]{2,1,0:T(8,128)} custom-call(bf16[32,128,128]{2,1,0:T(8,128)(2,1)} %bitcast.57), custom_call_target="tpu_custom_call" | custom-call | tf_op jit(solution)/shard_map/pallas_call | solution.py:177
  226.9 15.7 %shard_map.100 = f32[2048,256]{1,0:T(8,128)} custom-call(s32[4096]{0:T(1024)} %bitcast.66, f32[4096,128]{1,0:T(8,128)} %bitcast.52, f32[2048,256]{1,0:T(8,128)} %shard_map.93.cur_ref.cur_hbm), custom_call_target="tpu_custom_call" | custom-call | flops 524288 | bytes 6291456 | tf_op jit(solution)/shard_map/pallas_call | solution.py:350
  242.7 0.8 reduce.4
  (18 shorter events, 0.1 us)
Async XLA Ops:
  7.2 4.6 %copy-start.6 = (s32[2]{0:T(128)S(1)}, s32[2]{0:T(128)}, u32[]{:S(2)}) copy-start(s32[2]{0:T(128)} %constant.65.clone) | copy-start | bytes 28
  7.2 56.7 %all-gather.2.cloned.1.call-start = ((), (), s32[]{:S(2)}) async-start(), calls=%async_computation.1 | async-start | bytes 2359296 | tf_op jit(solution)/shard_map/all_gather | solution.py:419
  18.3 11.1 %copy-start.5 = (s32[1024]{0:T(1024)S(1)}, s32[1024]{0:T(1024)}, u32[]{:S(2)}) copy-start(s32[1024]{0:T(1024)} %param.12) | copy-start | bytes 12292
  18.3 11.7 %copy-start.3 = (s32[8,256]{1,0:T(8,128)S(1)}, s32[8,256]{1,0:T(8,128)}, u32[]{:S(2)}) copy-start(s32[8,256]{1,0:T(8,128)} %param.10) | copy-start | bytes 24580
  18.3 11.7 %copy-start.4 = (s32[8,256]{1,0:T(8,128)S(1)}, s32[8,256]{1,0:T(8,128)}, u32[]{:S(2)}) copy-start(s32[8,256]{1,0:T(8,128)} %param.11) | copy-start | bytes 24580
  20.7 41.7 %copy-start = (bf16[4,512,256]{2,1,0:T(8,128)(2,1)S(1)}, bf16[4,512,256]{2,1,0:T(8,128)(2,1)}, u32[]{:S(2)}) copy-start(bf16[4,512,256]{2,1,0:T(8,128)(2,1)} %param.7) | copy-start | bytes 3145732
  20.7 47.5 %all-to-all-start = ((s32[32,1,128]{2,1,0:T(1,128)}), s32[32,1,128]{2,1,0:T(1,128)S(1)}, u32[]{:S(2)}, u32[]{:S(2)}) async-start(s32[32,1,128]{2,1,0:T(1,128)} %bitcast.4), calls=%async_computation | async-start | bytes 32768 | tf_op jit(solution)/shard_map/all_to_all | solution.py:412
  68.2 0.6 copy-start.2
  226.9 15.8 %copy-start.1 = (f32[8,128,1]{2,1,0:T(8,128)S(1)}, f32[8,128,1]{2,1,0:T(8,128)}, u32[]{:S(2)}) copy-start(f32[8,128,1]{2,1,0:T(8,128)} %get-tuple-element.13) | copy-start | bytes 12292
Sparse Core Ops, SparseCore 0:
  9.8 41.2 all-gather.1

commit v17 on v15

--- a/solution.py
+++ b/solution.py
@@ -225,10 +225,14 @@
     )(idx, src)
 
 
-def fit_kernel(slot_ref, basis_ref, arrived_ref, inc_ref, ins_ref, model_ref, ev_ref, stage_ref):
+def fit_kernel(slot_ref, basis_ref, arrived_in, inc_ref, ins_ref, model_ref, ev_ref, stage_ref, arrived_ref):
     nper = inc_ref.shape[1]
     obs = stage_ref.shape[0]
     base = pl.program_id(0) * obs
+
+    @pl.when(pl.program_id(0) == 0)
+    def _():
+        arrived_ref[...] = arrived_in[...].astype(jnp.float32)
 
     def pick(b, carry):
         r0 = pl.multiple_of(b * 32, 32)
@@ -275,7 +279,7 @@
                 pl.BlockSpec((None, obs, cols), lambda g, s: (g, 0, 0)),
                 pl.BlockSpec((None, cols, 1), lambda g, s: (g, 0, 0)),
             ],
-            scratch_shapes=[pltpu.VMEM((obs, cols), jnp.float32)],
+            scratch_shapes=[pltpu.VMEM((obs, cols), jnp.float32), pltpu.VMEM(arrived.shape, jnp.float32)],
         ),
         out_shape=[
             jax.ShapeDtypeStruct((plans, obs, cols), jnp.float32),
@@ -316,10 +320,11 @@
     )(counts, current, attitude_all)
 
 
-def scatter_sub_kernel(idx_ref, src_ref, cur_ref, out_ref, acc_ref):
+def scatter_sub_kernel(idx_ref, src_in, cur_ref, out_ref, acc_ref, src_ref):
     rows, width = src_ref.shape
     streams = acc_ref.shape[0]
     n = cur_ref.shape[0]
+    src_ref[...] = src_in[...].astype(jnp.float32)
     acc_ref[...] = jnp.zeros_like(acc_ref)
 
     def body(step, carry):
@@ -346,7 +351,8 @@
         in_specs=[pl.BlockSpec(memory_space=pltpu.SMEM)] + [pl.BlockSpec(memory_space=pltpu.VMEM)] * 2,
         out_specs=pl.BlockSpec(memory_space=pltpu.VMEM),
         out_shape=jax.ShapeDtypeStruct(current.shape, jnp.float32),
-        scratch_shapes=[pltpu.VMEM((STREAMS, blocks * current.shape[0] + 8, width), jnp.float32)],
+        scratch_shapes=[pltpu.VMEM((STREAMS, blocks * current.shape[0] + 8, width), jnp.float32),
+                        pltpu.VMEM(src.shape, jnp.float32)],
         cost_estimate=pl.CostEstimate(
             flops=rows * width, transcendentals=0, bytes_accessed=(rows * width + 2 * current.size) * 4),
     )(idx, src, current)
@@ -410,13 +416,13 @@
         white = whiten_rows(seg_counts, current, attitude_all, SRC_GROUP)
         picked = row_gather(white, asked, jnp.bfloat16, norm_cos)
         outbound = picked.reshape(tm_count, capacity, SRC_GROUP)
-        arrived = tm_all_to_all(outbound, jnp.float32, 1 + 2 * iteration)
+        arrived = tm_all_to_all(outbound, jnp.bfloat16, 1 + 2 * iteration)
         model, evidence = fit_fused(
             basis, arrived.reshape(-1, SRC_GROUP), slot_of, inv_cos, inv_sin)
         outgoing = row_gather(model.reshape(requests, SRC_GROUP), inverse, jnp.bfloat16)
         returned = tm_all_to_all(
             outgoing.reshape(tm_count, capacity, SRC_GROUP),
-            jnp.float32, 2 + 2 * iteration)
+            jnp.bfloat16, 2 + 2 * iteration)
         current = scatter_sub(returned.reshape(-1, SRC_GROUP), asked, current)
     current = current.reshape(seg_dev, slots, width)
     return (current, evidence)

time: 252 us -> 250 us (level)
  transfers between devices with their start and end apart: 2 -> 2, of which waited for: 0 -> 0; matrix products, arithmetic and copies ran while one was open for 8% -> 8% of each run, Pallas kernels for 12% -> 13%
where the time goes in v17:
time: 250 us; the launch traced here: 249 us
  Pallas kernels  204 us (82%)
  local copies, waits for them, and re-layouts  15.2 us (6%)
  between operations  14.3 us (6%)
  starting transfers between devices  8.76 us (4%)
  other arithmetic  6.17 us (2%)
    pallas_call x4, Pallas kernels, tm_all_to_all(): pl.pallas_call(a2a_kernel, in_specs=[pl.BlockSpec(memory_space=pl.ANY)],...  81.4 us
    pallas_call x2, Pallas kernels, scatter_sub(): pl.pallas_call(scatter_sub_kernel, in_specs=[pl.BlockSpec(memory_space=pl...  31.4 us
    pallas_call x4, Pallas kernels, row_gather(): pl.pallas_call(gather_kernel, in_specs=[pl.BlockSpec(memory_space=pltpu.S...  27.7 us
    pallas_call x2, Pallas kernels, fit_fused(): pl.pallas_call(fit_kernel, grid_spec=pltpu.PrefetchScalarGridSpec(num_sca...  27.7 us
    pallas_call x1, Pallas kernels, basis_and_norms(): pl.pallas_call(basis_kernel, grid=(plans,), in_specs=[pl.BlockSpec((None,...  26.9 us
    all_to_all x1, starting transfers between devices, on_device(): lax.all_to_all(wanted, 'tm', split_axis=0, concat_axis=0, tiled=True)  8.73 us
    pallas_call x2, Pallas kernels, whiten_rows(): pl.pallas_call(white_kernel, in_specs=[pl.BlockSpec(memory_space=pltpu.SM...  8.56 us
    scatter x1, local copies, waits for them, and re-layouts, on_device(): pair = jnp.broadcast_to(jnp.array([empty_row, 0], jnp.int32), (tm_count *...  6.37 us
  transfers between devices with their start and end apart: 2, of which 0 were waited for; matrix products, arithmetic and copies ran while one was open for 8% of the time, Pallas kernels for 13%

profile of v17, /device:TPU:1, one launch (start us, length us, event | category | flops | bytes accessed | tf_op | source)
XLA Modules:
  0.0 248.9 jit_solution(5732046092845397401)
XLA Ops:
  7.2 0.0 copy-start.6
  7.2 0.0 all-gather.2.cloned.1.call-start
  7.2 0.7 all-gather.2.cloned.1.call-update
  7.9 0.1 broadcast_bitcast_fusion
  8.0 0.7 reshape.278
  8.7 0.7 copy.29
  9.4 0.7 copy.31
  10.1 0.2 convolution_bitcast_fusion
  10.3 0.1 slice.12
  10.5 0.2 copy.23
  10.7 0.2 copy.24
  10.8 0.3 subtract_reduce_fusion
  11.1 0.1 fusion.1
  11.3 0.1 fusion.11
  11.4 0.4 copy.25
  11.8 0.1 broadcast_in_dim.4
  11.9 6.4 %scatter_fusion = s32[4096,2]{1,0:T(8,128)S(1)} fusion(s32[4096,2]{1,0:T(8,128)S(1)} %broadcast_in_dim.4, s32[2048]{0:T(1024)S(1)} %bitcast.71, s32[2048,2]{1,0:T(8,128)S(1)} %copy.25), kind=kCustom, calls=%fused_computation | custom fusion | bytes 57344 | tf_op jit(solution)/shard_map/scatter | solution.py:403
  18.3 0.0 copy-start.5
  18.3 0.0 copy-start.3
  18.3 0.0 copy-start.4
  18.4 2.3 slice_reduce_fusion
  20.7 8.7 %all-to-all-start = ((s32[32,1,128]{2,1,0:T(1,128)}), s32[32,1,128]{2,1,0:T(1,128)S(1)}, u32[]{:S(2)}, u32[]{:S(2)}) async-start(s32[32,1,128]{2,1,0:T(1,128)} %bitcast.4), calls=%async_computation | async-start | bytes 32768 | tf_op jit(solution)/shard_map/all_to_all | solution.py:407
  29.4 0.0 copy-done.5
  29.4 0.6 convert_element_type.38
  30.0 1.3 copy.27.t_ref
  31.4 0.6 broadcast_divide_fusion.2
  32.0 26.9 %shard_map.86 = (bf16[8,256,2048]{2,1,0:T(8,128)(2,1)}, f32[8,1,1024]{2,1,0:T(1,128)}, f32[8,1,1024]{2,1,0:T(1,128)}) custom-call(f32[8,256,1]{2,1,0:T(8,128)} %copy.27.t_ref, f32[1,1024]{1,0:T(1,128)} %bitcast.80, f32[1,1024]{1,0:T(1,128)} %bitcast.79, f32[1,1024]{1,0:T(1,128)} %bitcast.78), custom_call_target="tpu_custom_call" | custom-call | flops 125829120 | bytes 8388608 | tf_op jit(solution)/shard_map/pallas_call | solution.py:78
  58.9 1.4 copy.34
  60.3 0.6 fusion.8.slot_ref
  60.9 1.5 broadcast_divide_fusion
  62.3 1.5 bitcast_convert_fusion.cur_ref
  63.9 4.3 %shard_map.87.src_ref = f32[4104,128]{1,0:T(8,128)} custom-call(s32[4]{0:T(128)} %cnt_ref.3, f32[2048,256]{1,0:T(8,128)} %bitcast_convert_fusion.cur_ref, bf16[4,512,512]{2,1,0:T(8,128)(2,1)} %all-gather.2.cloned.1.call-done.att_ref), custom_call_target="tpu_custom_call" | custom-call | flops 536870912 | bytes 6291456 | tf_op jit(solution)/shard_map/pallas_call | solution.py:312
  68.2 0.0 all-to-all-done
  68.2 0.6 copy-done.2
  68.8 7.2 %shard_map.88 = bf16[4096,128]{1,0:T(8,128)(2,1)} custom-call(s32[4096]{0:T(1024)} %bitcast.63, f32[4104,128]{1,0:T(8,128)} %shard_map.87.src_ref, f32[8,1024]{1,0:T(8,128)} %bitcast.67), custom_call_target="tpu_custom_call" | custom-call | bytes 4194304 | tf_op jit(solution)/shard_map/pallas_call | solution.py:116
  75.9 21.1 %shard_map.89 = bf16[32,128,128]{2,1,0:T(8,128)(2,1)} custom-call(bf16[32,128,128]{2,1,0:T(8,128)(2,1)} %bitcast.56), custom_call_target="tpu_custom_call" | custom-call | tf_op jit(solution)/shard_map/pallas_call | solution.py:177
  97.0 13.8 %shard_map.90 = (f32[8,256,128]{2,1,0:T(8,128)}, f32[8,128,1]{2,1,0:T(8,128)}) custom-call(s32[2048]{0:T(1024)} %fusion.8.slot_ref, bf16[8,256,2048]{2,1,0:T(8,128)(2,1)} %get-tuple-element.8.basis_ref, bf16[4096,128]{1,0:T(8,128)(2,1)} %bitcast.59, f32[8,1,1024]{2,1,0:T(1,128)} %get-tuple-element.21.inc_ref, f32[8,1,1024]{2,1,0:T(1,128)} %get-tuple-element.20.ins_ref), custom_call_target="tpu_custom_call" | custom-call | flops 2147483648 | bytes 8388608 | tf_op jit(solution)/shard_map/pallas_call | solution.py:267
  110.8 6.7 %shard_map.91 = bf16[4096,128]{1,0:T(8,128)(2,1)} custom-call(s32[4096]{0:T(1024)} %get-tuple-element.14.idx_ref, f32[2048,128]{1,0:T(8,128)} %bitcast.62), custom_call_target="tpu_custom_call" | custom-call | bytes 4194304 | tf_op jit(solution)/shard_map/pallas_call | solution.py:116
  117.6 19.4 %shard_map.92 = bf16[32,128,128]{2,1,0:T(8,128)(2,1)} custom-call(bf16[32,128,128]{2,1,0:T(8,128)(2,1)} %bitcast.57), custom_call_target="tpu_custom_call" | custom-call | tf_op jit(solution)/shard_map/pallas_call | solution.py:177
  137.0 15.7 %shard_map.93.cur_ref = f32[2048,256]{1,0:T(8,128)} custom-call(s32[4096]{0:T(1024)} %bitcast.64, bf16[4096,128]{1,0:T(8,128)(2,1)} %bitcast.53, f32[2048,256]{1,0:T(8,128)} %bitcast_convert_fusion.cur_ref), custom_call_target="tpu_custom_call" | custom-call | flops 524288 | bytes 6291456 | tf_op jit(solution)/shard_map/pallas_call | solution.py:349
  152.7 4.3 %shard_map.94.src_ref = f32[4104,128]{1,0:T(8,128)} custom-call(s32[4]{0:T(128)} %cnt_ref.3, f32[2048,256]{1,0:T(8,128)} %shard_map.93.cur_ref, bf16[4,512,512]{2,1,0:T(8,128)(2,1)} %all-gather.2.cloned.1.call-done.att_ref), custom_call_target="tpu_custom_call" | custom-call | flops 536870912 | bytes 6291456 | tf_op jit(solution)/shard_map/pallas_call | solution.py:312
  156.9 7.1 %shard_map.95 = bf16[4096,128]{1,0:T(8,128)(2,1)} custom-call(s32[4096]{0:T(1024)} %bitcast.65, f32[4104,128]{1,0:T(8,128)} %shard_map.94.src_ref, f32[8,1024]{1,0:T(8,128)} %bitcast.68), custom_call_target="tpu_custom_call" | custom-call | bytes 4194304 | tf_op jit(solution)/shard_map/pallas_call | solution.py:116
  164.0 19.8 %shard_map.96 = bf16[32,128,128]{2,1,0:T(8,128)(2,1)} custom-call(bf16[32,128,128]{2,1,0:T(8,128)(2,1)} %bitcast.54), custom_call_target="tpu_custom_call" | custom-call | tf_op jit(solution)/shard_map/pallas_call | solution.py:177
  183.9 13.8 %shard_map.97 = (f32[8,256,128]{2,1,0:T(8,128)}, f32[8,128,1]{2,1,0:T(8,128)}) custom-call(s32[2048]{0:T(1024)} %fusion.8.slot_ref, bf16[8,256,2048]{2,1,0:T(8,128)(2,1)} %get-tuple-element.8.basis_ref, bf16[4096,128]{1,0:T(8,128)(2,1)} %bitcast.58, f32[8,1,1024]{2,1,0:T(1,128)} %get-tuple-element.21.inc_ref, f32[8,1,1024]{2,1,0:T(1,128)} %get-tuple-element.20.ins_ref), custom_call_target="tpu_custom_call" | custom-call | flops 2147483648 | bytes 8388608 | tf_op jit(solution)/shard_map/pallas_call | solution.py:267
  197.7 6.7 %shard_map.98 = bf16[4096,128]{1,0:T(8,128)(2,1)} custom-call(s32[4096]{0:T(1024)} %get-tuple-element.14.idx_ref, f32[2048,128]{1,0:T(8,128)} %bitcast.61), custom_call_target="tpu_custom_call" | custom-call | bytes 4194304 | tf_op jit(solution)/shard_map/pallas_call | solution.py:116
  204.4 21.1 %shard_map.99 = bf16[32,128,128]{2,1,0:T(8,128)(2,1)} custom-call(bf16[32,128,128]{2,1,0:T(8,128)(2,1)} %bitcast.55), custom_call_target="tpu_custom_call" | custom-call | tf_op jit(solution)/shard_map/pallas_call | solution.py:177
  225.5 15.7 %shard_map.100 = f32[2048,256]{1,0:T(8,128)} custom-call(s32[4096]{0:T(1024)} %bitcast.66, bf16[4096,128]{1,0:T(8,128)(2,1)} %bitcast.52, f32[2048,256]{1,0:T(8,128)} %shard_map.93.cur_ref), custom_call_target="tpu_custom_call" | custom-call | flops 524288 | bytes 6291456 | tf_op jit(solution)/shard_map/pallas_call | solution.py:349
  241.3 0.8 reduce.4
  (18 shorter events, 0.1 us)
Async XLA Ops:
  7.2 4.6 %copy-start.6 = (s32[2]{0:T(128)S(1)}, s32[2]{0:T(128)}, u32[]{:S(2)}) copy-start(s32[2]{0:T(128)} %constant.65.clone) | copy-start | bytes 28
  7.2 56.7 %all-gather.2.cloned.1.call-start = ((), (), s32[]{:S(2)}) async-start(), calls=%async_computation.1 | async-start | bytes 2359296 | tf_op jit(solution)/shard_map/all_gather | solution.py:414
  18.3 11.1 %copy-start.5 = (s32[1024]{0:T(1024)S(1)}, s32[1024]{0:T(1024)}, u32[]{:S(2)}) copy-start(s32[1024]{0:T(1024)} %param.12) | copy-start | bytes 12292
  18.3 11.7 %copy-start.3 = (s32[8,256]{1,0:T(8,128)S(1)}, s32[8,256]{1,0:T(8,128)}, u32[]{:S(2)}) copy-start(s32[8,256]{1,0:T(8,128)} %param.10) | copy-start | bytes 24580
  18.3 11.7 %copy-start.4 = (s32[8,256]{1,0:T(8,128)S(1)}, s32[8,256]{1,0:T(8,128)}, u32[]{:S(2)}) copy-start(s32[8,256]{1,0:T(8,128)} %param.11) | copy-start | bytes 24580
  20.7 41.7 %copy-start = (bf16[4,512,256]{2,1,0:T(8,128)(2,1)S(1)}, bf16[4,512,256]{2,1,0:T(8,128)(2,1)}, u32[]{:S(2)}) copy-start(bf16[4,512,256]{2,1,0:T(8,128)(2,1)} %param.7) | copy-start | bytes 3145732
  20.7 47.5 %all-to-all-start = ((s32[32,1,128]{2,1,0:T(1,128)}), s32[32,1,128]{2,1,0:T(1,128)S(1)}, u32[]{:S(2)}, u32[]{:S(2)}) async-start(s32[32,1,128]{2,1,0:T(1,128)} %bitcast.4), calls=%async_computation | async-start | bytes 32768 | tf_op jit(solution)/shard_map/all_to_all | solution.py:407
  68.2 0.6 copy-start.2
  225.5 15.8 %copy-start.1 = (f32[8,128,1]{2,1,0:T(8,128)S(1)}, f32[8,128,1]{2,1,0:T(8,128)}, u32[]{:S(2)}) copy-start(f32[8,128,1]{2,1,0:T(8,128)} %get-tuple-element.13) | copy-start | bytes 12292
Sparse Core Ops, SparseCore 0:
  9.8 41.2 all-gather.1

commit v18 on v17

--- a/solution.py
+++ b/solution.py
@@ -292,11 +292,24 @@
     return model, ev.reshape(plans, cols)
 
 
-def white_kernel(cnt_ref, cur_ref, att_ref, out_ref):
+def white_kernel(cnt_ref, cur_hbm, att_hbm, out_ref, cur_ref, att_ref, sems):
     segs, slots, _ = att_ref.shape
     width = out_ref.shape[1]
     blocks = cur_ref.shape[1] // width
+
+    def copies(s):
+        rows = pl.ds(s * slots, slots)
+        return (
+            pltpu.make_async_copy(cur_hbm.at[rows], cur_ref.at[rows], sems.at[0, s]),
+            pltpu.make_async_copy(att_hbm.at[s], att_ref.at[s], sems.at[1, s]),
+        )
+
     for s in range(segs):
+        for c in copies(s):
+            c.start()
+    for s in range(segs):
+        for c in copies(s):
+            c.wait()
         cur = cur_ref[pl.ds(s * slots, slots), :]
         slot = lax.broadcasted_iota(jnp.int32, cur.shape, 0)
         masked = jnp.where(slot < cnt_ref[s], cur, 0.0).astype(jnp.bfloat16)
@@ -311,9 +324,14 @@
     rows = current.shape[0] * current.shape[1] // width
     return pl.pallas_call(
         white_kernel,
-        in_specs=[pl.BlockSpec(memory_space=pltpu.SMEM)] + [pl.BlockSpec(memory_space=pltpu.VMEM)] * 2,
+        in_specs=[pl.BlockSpec(memory_space=pltpu.SMEM)] + [pl.BlockSpec(memory_space=pl.ANY)] * 2,
         out_specs=pl.BlockSpec(memory_space=pltpu.VMEM),
         out_shape=jax.ShapeDtypeStruct((rows + 8, width), jnp.float32),
+        scratch_shapes=[
+            pltpu.VMEM(current.shape, current.dtype),
+            pltpu.VMEM(attitude_all.shape, attitude_all.dtype),
+            pltpu.SemaphoreType.DMA((2, segs)),
+        ],
         cost_estimate=pl.CostEstimate(
             flops=2 * segs * slots * slots * current.shape[1], transcendentals=0,
             bytes_accessed=current.size * 8 + attitude_all.size * 2),

time: 250 us -> 252 us (level)
  no operation moved by 1% of the time
where the time goes in v18:
time: 252 us; the launch traced here: 251 us
  Pallas kernels  206 us (82%)
  local copies, waits for them, and re-layouts  15.2 us (6%)
  between operations  14.3 us (6%)
  starting transfers between devices  8.76 us (3%)
  other arithmetic  6.17 us (2%)
    pallas_call x4, Pallas kernels, tm_all_to_all(): pl.pallas_call(a2a_kernel, in_specs=[pl.BlockSpec(memory_space=pl.ANY)],...  81.9 us
    pallas_call x2, Pallas kernels, scatter_sub(): pl.pallas_call(scatter_sub_kernel, in_specs=[pl.BlockSpec(memory_space=pl...  31.4 us
    pallas_call x4, Pallas kernels, row_gather(): pl.pallas_call(gather_kernel, in_specs=[pl.BlockSpec(memory_space=pltpu.S...  27.7 us
    pallas_call x2, Pallas kernels, fit_fused(): pl.pallas_call(fit_kernel, grid_spec=pltpu.PrefetchScalarGridSpec(num_sca...  27.6 us
    pallas_call x1, Pallas kernels, basis_and_norms(): pl.pallas_call(basis_kernel, grid=(plans,), in_specs=[pl.BlockSpec((None,...  26.9 us
    pallas_call x2, Pallas kernels, whiten_rows(): pl.pallas_call(white_kernel, in_specs=[pl.BlockSpec(memory_space=pltpu.SM...  9.93 us
    all_to_all x1, starting transfers between devices, on_device(): lax.all_to_all(wanted, 'tm', split_axis=0, concat_axis=0, tiled=True)  8.73 us
    scatter x1, local copies, waits for them, and re-layouts, on_device(): pair = jnp.broadcast_to(jnp.array([empty_row, 0], jnp.int32), (tm_count *...  6.37 us
  transfers between devices with their start and end apart: 2, of which 0 were waited for; matrix products, arithmetic and copies ran while one was open for 8% of the time, Pallas kernels for 13%

profile of v18, /device:TPU:1, one launch (start us, length us, event | category | flops | bytes accessed | tf_op | source)
XLA Modules:
  0.0 250.8 jit_solution(17648670398201882309)
XLA Ops:
  7.2 0.0 copy-start.6
  7.2 0.0 all-gather.2.cloned.1.call-start
  7.2 0.7 all-gather.2.cloned.1.call-update
  7.9 0.1 broadcast_bitcast_fusion
  8.0 0.7 reshape.278
  8.7 0.7 copy.29
  9.4 0.7 copy.31
  10.1 0.2 convolution_bitcast_fusion
  10.3 0.1 slice.12
  10.5 0.2 copy.23
  10.7 0.2 copy.24
  10.8 0.3 subtract_reduce_fusion
  11.1 0.1 fusion.1
  11.3 0.1 fusion.11
  11.4 0.4 copy.25
  11.8 0.1 broadcast_in_dim.4
  11.9 6.4 %scatter_fusion = s32[4096,2]{1,0:T(8,128)S(1)} fusion(s32[4096,2]{1,0:T(8,128)S(1)} %broadcast_in_dim.4, s32[2048]{0:T(1024)S(1)} %bitcast.71, s32[2048,2]{1,0:T(8,128)S(1)} %copy.25), kind=kCustom, calls=%fused_computation | custom fusion | bytes 57344 | tf_op jit(solution)/shard_map/scatter | solution.py:421
  18.3 0.0 copy-start.5
  18.3 0.0 copy-start.3
  18.3 0.0 copy-start.4
  18.4 2.3 slice_reduce_fusion
  20.7 8.7 %all-to-all-start = ((s32[32,1,128]{2,1,0:T(1,128)}), s32[32,1,128]{2,1,0:T(1,128)S(1)}, u32[]{:S(2)}, u32[]{:S(2)}) async-start(s32[32,1,128]{2,1,0:T(1,128)} %bitcast.4), calls=%async_computation | async-start | bytes 32768 | tf_op jit(solution)/shard_map/all_to_all | solution.py:425
  29.4 0.6 convert_element_type.38
  30.0 0.0 copy-done.3
  30.0 1.3 copy.27.t_ref
  31.4 0.6 broadcast_divide_fusion.2
  32.0 26.9 %shard_map.86 = (bf16[8,256,2048]{2,1,0:T(8,128)(2,1)}, f32[8,1,1024]{2,1,0:T(1,128)}, f32[8,1,1024]{2,1,0:T(1,128)}) custom-call(f32[8,256,1]{2,1,0:T(8,128)} %copy.27.t_ref, f32[1,1024]{1,0:T(1,128)} %bitcast.80, f32[1,1024]{1,0:T(1,128)} %bitcast.79, f32[1,1024]{1,0:T(1,128)} %bitcast.78), custom_call_target="tpu_custom_call" | custom-call | flops 125829120 | bytes 8388608 | tf_op jit(solution)/shard_map/pallas_call | solution.py:78
  58.9 1.4 copy.34
  60.3 0.6 fusion.8.slot_ref
  60.9 1.5 broadcast_divide_fusion
  62.3 1.5 bitcast_convert_fusion.cur_hbm.cur_ref
  63.9 5.0 %shard_map.87.src_ref = f32[4104,128]{1,0:T(8,128)} custom-call(s32[4]{0:T(128)} %cnt_ref.3, f32[2048,256]{1,0:T(8,128)} %bitcast_convert_fusion.cur_hbm.cur_ref, bf16[4,512,512]{2,1,0:T(8,128)(2,1)} %all-gather.2.cloned.1.call-done.att_hbm), custom_call_target="tpu_custom_call" | custom-call | flops 536870912 | bytes 6291456 | tf_op jit(solution)/shard_map/pallas_call | solution.py:325
  68.9 0.0 all-to-all-done
  68.9 0.6 copy-done.2
  69.5 7.2 %shard_map.88 = bf16[4096,128]{1,0:T(8,128)(2,1)} custom-call(s32[4096]{0:T(1024)} %bitcast.63, f32[4104,128]{1,0:T(8,128)} %shard_map.87.src_ref, f32[8,1024]{1,0:T(8,128)} %bitcast.67), custom_call_target="tpu_custom_call" | custom-call | bytes 4194304 | tf_op jit(solution)/shard_map/pallas_call | solution.py:116
  76.6 21.1 %shard_map.89 = bf16[32,128,128]{2,1,0:T(8,128)(2,1)} custom-call(bf16[32,128,128]{2,1,0:T(8,128)(2,1)} %bitcast.56), custom_call_target="tpu_custom_call" | custom-call | tf_op jit(solution)/shard_map/pallas_call | solution.py:177
  97.7 13.8 %shard_map.90 = (f32[8,256,128]{2,1,0:T(8,128)}, f32[8,128,1]{2,1,0:T(8,128)}) custom-call(s32[2048]{0:T(1024)} %fusion.8.slot_ref, bf16[8,256,2048]{2,1,0:T(8,128)(2,1)} %get-tuple-element.8.basis_ref, bf16[4096,128]{1,0:T(8,128)(2,1)} %bitcast.59, f32[8,1,1024]{2,1,0:T(1,128)} %get-tuple-element.21.inc_ref, f32[8,1,1024]{2,1,0:T(1,128)} %get-tuple-element.20.ins_ref), custom_call_target="tpu_custom_call" | custom-call | flops 2147483648 | bytes 8388608 | tf_op jit(solution)/shard_map/pallas_call | solution.py:267
  111.5 6.7 %shard_map.91 = bf16[4096,128]{1,0:T(8,128)(2,1)} custom-call(s32[4096]{0:T(1024)} %get-tuple-element.14.idx_ref, f32[2048,128]{1,0:T(8,128)} %bitcast.62), custom_call_target="tpu_custom_call" | custom-call | bytes 4194304 | tf_op jit(solution)/shard_map/pallas_call | solution.py:116
  118.3 19.4 %shard_map.92 = bf16[32,128,128]{2,1,0:T(8,128)(2,1)} custom-call(bf16[32,128,128]{2,1,0:T(8,128)(2,1)} %bitcast.57), custom_call_target="tpu_custom_call" | custom-call | tf_op jit(solution)/shard_map/pallas_call | solution.py:177
  137.7 15.7 %shard_map.93.cur_hbm.cur_ref = f32[2048,256]{1,0:T(8,128)} custom-call(s32[4096]{0:T(1024)} %bitcast.64, bf16[4096,128]{1,0:T(8,128)(2,1)} %bitcast.53, f32[2048,256]{1,0:T(8,128)} %bitcast_convert_fusion.cur_hbm.cur_ref), custom_call_target="tpu_custom_call" | custom-call | flops 524288 | bytes 6291456 | tf_op jit(solution)/shard_map/pallas_call | solution.py:367
  153.4 5.0 %shard_map.94.src_ref = f32[4104,128]{1,0:T(8,128)} custom-call(s32[4]{0:T(128)} %cnt_ref.3, f32[2048,256]{1,0:T(8,128)} %shard_map.93.cur_hbm.cur_ref, bf16[4,512,512]{2,1,0:T(8,128)(2,1)} %all-gather.2.cloned.1.call-done.att_hbm), custom_call_target="tpu_custom_call" | custom-call | flops 536870912 | bytes 6291456 | tf_op jit(solution)/shard_map/pallas_call | solution.py:325
  158.3 7.1 %shard_map.95 = bf16[4096,128]{1,0:T(8,128)(2,1)} custom-call(s32[4096]{0:T(1024)} %bitcast.65, f32[4104,128]{1,0:T(8,128)} %shard_map.94.src_ref, f32[8,1024]{1,0:T(8,128)} %bitcast.68), custom_call_target="tpu_custom_call" | custom-call | bytes 4194304 | tf_op jit(solution)/shard_map/pallas_call | solution.py:116
  165.4 19.8 %shard_map.96 = bf16[32,128,128]{2,1,0:T(8,128)(2,1)} custom-call(bf16[32,128,128]{2,1,0:T(8,128)(2,1)} %bitcast.54), custom_call_target="tpu_custom_call" | custom-call | tf_op jit(solution)/shard_map/pallas_call | solution.py:177
  185.3 13.8 %shard_map.97 = (f32[8,256,128]{2,1,0:T(8,128)}, f32[8,128,1]{2,1,0:T(8,128)}) custom-call(s32[2048]{0:T(1024)} %fusion.8.slot_ref, bf16[8,256,2048]{2,1,0:T(8,128)(2,1)} %get-tuple-element.8.basis_ref, bf16[4096,128]{1,0:T(8,128)(2,1)} %bitcast.58, f32[8,1,1024]{2,1,0:T(1,128)} %get-tuple-element.21.inc_ref, f32[8,1,1024]{2,1,0:T(1,128)} %get-tuple-element.20.ins_ref), custom_call_target="tpu_custom_call" | custom-call | flops 2147483648 | bytes 8388608 | tf_op jit(solution)/shard_map/pallas_call | solution.py:267
  199.1 6.7 %shard_map.98 = bf16[4096,128]{1,0:T(8,128)(2,1)} custom-call(s32[4096]{0:T(1024)} %get-tuple-element.14.idx_ref, f32[2048,128]{1,0:T(8,128)} %bitcast.61), custom_call_target="tpu_custom_call" | custom-call | bytes 4194304 | tf_op jit(solution)/shard_map/pallas_call | solution.py:116
  205.8 21.6 %shard_map.99 = bf16[32,128,128]{2,1,0:T(8,128)(2,1)} custom-call(bf16[32,128,128]{2,1,0:T(8,128)(2,1)} %bitcast.55), custom_call_target="tpu_custom_call" | custom-call | tf_op jit(solution)/shard_map/pallas_call | solution.py:177
  227.4 15.7 %shard_map.100 = f32[2048,256]{1,0:T(8,128)} custom-call(s32[4096]{0:T(1024)} %bitcast.66, bf16[4096,128]{1,0:T(8,128)(2,1)} %bitcast.52, f32[2048,256]{1,0:T(8,128)} %shard_map.93.cur_hbm.cur_ref), custom_call_target="tpu_custom_call" | custom-call | flops 524288 | bytes 6291456 | tf_op jit(solution)/shard_map/pallas_call | solution.py:367
  243.2 0.8 reduce.4
  (18 shorter events, 0.1 us)
Async XLA Ops:
  7.2 4.6 %copy-start.6 = (s32[2]{0:T(128)S(1)}, s32[2]{0:T(128)}, u32[]{:S(2)}) copy-start(s32[2]{0:T(128)} %constant.65.clone) | copy-start | bytes 28
  7.2 56.7 %all-gather.2.cloned.1.call-start = ((), (), s32[]{:S(2)}) async-start(), calls=%async_computation.1 | async-start | bytes 2359296 | tf_op jit(solution)/shard_map/all_gather | solution.py:432
  18.3 11.1 %copy-start.5 = (s32[1024]{0:T(1024)S(1)}, s32[1024]{0:T(1024)}, u32[]{:S(2)}) copy-start(s32[1024]{0:T(1024)} %param.12) | copy-start | bytes 12292
  18.3 11.7 %copy-start.3 = (s32[8,256]{1,0:T(8,128)S(1)}, s32[8,256]{1,0:T(8,128)}, u32[]{:S(2)}) copy-start(s32[8,256]{1,0:T(8,128)} %param.10) | copy-start | bytes 24580
  18.3 11.7 %copy-start.4 = (s32[8,256]{1,0:T(8,128)S(1)}, s32[8,256]{1,0:T(8,128)}, u32[]{:S(2)}) copy-start(s32[8,256]{1,0:T(8,128)} %param.11) | copy-start | bytes 24580
  20.7 41.7 %copy-start = (bf16[4,512,256]{2,1,0:T(8,128)(2,1)S(1)}, bf16[4,512,256]{2,1,0:T(8,128)(2,1)}, u32[]{:S(2)}) copy-start(bf16[4,512,256]{2,1,0:T(8,128)(2,1)} %param.7) | copy-start | bytes 3145732
  20.7 48.2 %all-to-all-start = ((s32[32,1,128]{2,1,0:T(1,128)}), s32[32,1,128]{2,1,0:T(1,128)S(1)}, u32[]{:S(2)}, u32[]{:S(2)}) async-start(s32[32,1,128]{2,1,0:T(1,128)} %bitcast.4), calls=%async_computation | async-start | bytes 32768 | tf_op jit(solution)/shard_map/all_to_all | solution.py:425
  68.9 0.6 copy-start.2
  227.4 15.8 %copy-start.1 = (f32[8,128,1]{2,1,0:T(8,128)S(1)}, f32[8,128,1]{2,1,0:T(8,128)}, u32[]{:S(2)}) copy-start(f32[8,128,1]{2,1,0:T(8,128)} %get-tuple-element.13) | copy-start | bytes 12292
Sparse Core Ops, SparseCore 0:
  9.8 41.2 all-gather.1

commit v19 on v17

--- a/solution.py
+++ b/solution.py
@@ -320,12 +320,17 @@
     )(counts, current, attitude_all)
 
 
-def scatter_sub_kernel(idx_ref, src_in, cur_ref, out_ref, acc_ref, src_ref):
+def scatter_sub_kernel(idx_ref, src_hbm, cur_hbm, out_ref, acc_ref, src_ref, src_in, cur_ref, sems):
     rows, width = src_ref.shape
     streams = acc_ref.shape[0]
     n = cur_ref.shape[0]
+    src_copy = pltpu.make_async_copy(src_hbm, src_in, sems.at[0])
+    cur_copy = pltpu.make_async_copy(cur_hbm, cur_ref, sems.at[1])
+    src_copy.start()
+    cur_copy.start()
+    acc_ref[...] = jnp.zeros_like(acc_ref)
+    src_copy.wait()
     src_ref[...] = src_in[...].astype(jnp.float32)
-    acc_ref[...] = jnp.zeros_like(acc_ref)
 
     def body(step, carry):
         base = step * streams
@@ -336,6 +341,7 @@
         return carry
 
     lax.fori_loop(0, rows // streams, body, 0, unroll=SUNROLL)
+    cur_copy.wait()
     for b in range(cur_ref.shape[1] // width):
         total = acc_ref[0, pl.ds(b * n, n), :]
         for s in range(1, streams):
@@ -348,11 +354,12 @@
     blocks = current.shape[1] // width
     return pl.pallas_call(
         scatter_sub_kernel,
-        in_specs=[pl.BlockSpec(memory_space=pltpu.SMEM)] + [pl.BlockSpec(memory_space=pltpu.VMEM)] * 2,
+        in_specs=[pl.BlockSpec(memory_space=pltpu.SMEM)] + [pl.BlockSpec(memory_space=pl.ANY)] * 2,
         out_specs=pl.BlockSpec(memory_space=pltpu.VMEM),
         out_shape=jax.ShapeDtypeStruct(current.shape, jnp.float32),
         scratch_shapes=[pltpu.VMEM((STREAMS, blocks * current.shape[0] + 8, width), jnp.float32),
-                        pltpu.VMEM(src.shape, jnp.float32)],
+                        pltpu.VMEM(src.shape, jnp.float32), pltpu.VMEM(src.shape, src.dtype),
+                        pltpu.VMEM(current.shape, current.dtype), pltpu.SemaphoreType.DMA((2,))],
         cost_estimate=pl.CostEstimate(
             flops=rows * width, transcendentals=0, bytes_accessed=(rows * width + 2 * current.size) * 4),
     )(idx, src, current)

time: 250 us -> 250 us (level)
  no operation moved by 1% of the time
where the time goes in v19:
time: 250 us; the launch traced here: 249 us
  Pallas kernels  204 us (82%)
  local copies, waits for them, and re-layouts  15.2 us (6%)
  between operations  14.3 us (6%)
  starting transfers between devices  8.76 us (4%)
  other arithmetic  6.17 us (2%)
    pallas_call x4, Pallas kernels, tm_all_to_all(): pl.pallas_call(a2a_kernel, in_specs=[pl.BlockSpec(memory_space=pl.ANY)],...  81.9 us
    pallas_call x2, Pallas kernels, scatter_sub(): pl.pallas_call(scatter_sub_kernel, in_specs=[pl.BlockSpec(memory_space=pl...  31.5 us
    pallas_call x4, Pallas kernels, row_gather(): pl.pallas_call(gather_kernel, in_specs=[pl.BlockSpec(memory_space=pltpu.S...  27.7 us
    pallas_call x2, Pallas kernels, fit_fused(): pl.pallas_call(fit_kernel, grid_spec=pltpu.PrefetchScalarGridSpec(num_sca...  27.6 us
    pallas_call x1, Pallas kernels, basis_and_norms(): pl.pallas_call(basis_kernel, grid=(plans,), in_specs=[pl.BlockSpec((None,...  26.9 us
    all_to_all x1, starting transfers between devices, on_device(): lax.all_to_all(wanted, 'tm', split_axis=0, concat_axis=0, tiled=True)  8.73 us
    pallas_call x2, Pallas kernels, whiten_rows(): pl.pallas_call(white_kernel, in_specs=[pl.BlockSpec(memory_space=pltpu.SM...  8.57 us
    scatter x1, local copies, waits for them, and re-layouts, on_device(): pair = jnp.broadcast_to(jnp.array([empty_row, 0], jnp.int32), (tm_count *...  6.37 us
  transfers between devices with their start and end apart: 2, of which 0 were waited for; matrix products, arithmetic and copies ran while one was open for 8% of the time, Pallas kernels for 13%

profile of v19, /device:TPU:1, one launch (start us, length us, event | category | flops | bytes accessed | tf_op | source)
XLA Modules:
  0.0 249.4 jit_solution(15933358719028685518)
XLA Ops:
  7.2 0.0 copy-start.6
  7.2 0.0 all-gather.2.cloned.1.call-start
  7.2 0.7 all-gather.2.cloned.1.call-update
  7.9 0.1 broadcast_bitcast_fusion
  8.0 0.7 reshape.278
  8.7 0.7 copy.29
  9.4 0.7 copy.31
  10.1 0.2 convolution_bitcast_fusion
  10.3 0.1 slice.12
  10.5 0.2 copy.23
  10.7 0.2 copy.24
  10.8 0.3 subtract_reduce_fusion
  11.1 0.1 fusion.1
  11.3 0.1 fusion.11
  11.4 0.4 copy.25
  11.8 0.1 broadcast_in_dim.4
  11.9 6.4 %scatter_fusion = s32[4096,2]{1,0:T(8,128)S(1)} fusion(s32[4096,2]{1,0:T(8,128)S(1)} %broadcast_in_dim.4, s32[2048]{0:T(1024)S(1)} %bitcast.71, s32[2048,2]{1,0:T(8,128)S(1)} %copy.25), kind=kCustom, calls=%fused_computation | custom fusion | bytes 57344 | tf_op jit(solution)/shard_map/scatter | solution.py:410
  18.3 0.0 copy-start.5
  18.3 0.0 copy-start.3
  18.3 0.0 copy-start.4
  18.4 2.3 slice_reduce_fusion
  20.7 8.7 %all-to-all-start = ((s32[32,1,128]{2,1,0:T(1,128)}), s32[32,1,128]{2,1,0:T(1,128)S(1)}, u32[]{:S(2)}, u32[]{:S(2)}) async-start(s32[32,1,128]{2,1,0:T(1,128)} %bitcast.4), calls=%async_computation | async-start | bytes 32768 | tf_op jit(solution)/shard_map/all_to_all | solution.py:414
  29.4 0.0 copy-done.5
  29.4 0.6 convert_element_type.38
  30.0 1.3 copy.27.t_ref
  31.4 0.6 broadcast_divide_fusion.2
  32.0 26.9 %shard_map.86 = (bf16[8,256,2048]{2,1,0:T(8,128)(2,1)}, f32[8,1,1024]{2,1,0:T(1,128)}, f32[8,1,1024]{2,1,0:T(1,128)}) custom-call(f32[8,256,1]{2,1,0:T(8,128)} %copy.27.t_ref, f32[1,1024]{1,0:T(1,128)} %bitcast.80, f32[1,1024]{1,0:T(1,128)} %bitcast.79, f32[1,1024]{1,0:T(1,128)} %bitcast.78), custom_call_target="tpu_custom_call" | custom-call | flops 125829120 | bytes 8388608 | tf_op jit(solution)/shard_map/pallas_call | solution.py:78
  58.9 1.4 copy.34
  60.3 0.6 fusion.8.slot_ref
  60.9 1.5 broadcast_divide_fusion
  62.3 1.5 bitcast_convert_fusion.cur_ref.cur_hbm
  63.9 4.3 %shard_map.87.src_ref = f32[4104,128]{1,0:T(8,128)} custom-call(s32[4]{0:T(128)} %cnt_ref.3, f32[2048,256]{1,0:T(8,128)} %bitcast_convert_fusion.cur_ref.cur_hbm, bf16[4,512,512]{2,1,0:T(8,128)(2,1)} %all-gather.2.cloned.1.call-done.att_ref), custom_call_target="tpu_custom_call" | custom-call | flops 536870912 | bytes 6291456 | tf_op jit(solution)/shard_map/pallas_call | solution.py:312
  68.2 0.0 all-to-all-done
  68.2 0.6 copy-done.2
  68.8 7.2 %shard_map.88 = bf16[4096,128]{1,0:T(8,128)(2,1)} custom-call(s32[4096]{0:T(1024)} %bitcast.63, f32[4104,128]{1,0:T(8,128)} %shard_map.87.src_ref, f32[8,1024]{1,0:T(8,128)} %bitcast.67), custom_call_target="tpu_custom_call" | custom-call | bytes 4194304 | tf_op jit(solution)/shard_map/pallas_call | solution.py:116
  75.9 21.1 %shard_map.89 = bf16[32,128,128]{2,1,0:T(8,128)(2,1)} custom-call(bf16[32,128,128]{2,1,0:T(8,128)(2,1)} %bitcast.56), custom_call_target="tpu_custom_call" | custom-call | tf_op jit(solution)/shard_map/pallas_call | solution.py:177
  97.0 13.8 %shard_map.90 = (f32[8,256,128]{2,1,0:T(8,128)}, f32[8,128,1]{2,1,0:T(8,128)}) custom-call(s32[2048]{0:T(1024)} %fusion.8.slot_ref, bf16[8,256,2048]{2,1,0:T(8,128)(2,1)} %get-tuple-element.8.basis_ref, bf16[4096,128]{1,0:T(8,128)(2,1)} %bitcast.59, f32[8,1,1024]{2,1,0:T(1,128)} %get-tuple-element.21.inc_ref, f32[8,1,1024]{2,1,0:T(1,128)} %get-tuple-element.20.ins_ref), custom_call_target="tpu_custom_call" | custom-call | flops 2147483648 | bytes 8388608 | tf_op jit(solution)/shard_map/pallas_call | solution.py:267
  110.8 6.7 %shard_map.91 = bf16[4096,128]{1,0:T(8,128)(2,1)} custom-call(s32[4096]{0:T(1024)} %get-tuple-element.14.idx_ref, f32[2048,128]{1,0:T(8,128)} %bitcast.62), custom_call_target="tpu_custom_call" | custom-call | bytes 4194304 | tf_op jit(solution)/shard_map/pallas_call | solution.py:116
  117.6 19.4 %shard_map.92 = bf16[32,128,128]{2,1,0:T(8,128)(2,1)} custom-call(bf16[32,128,128]{2,1,0:T(8,128)(2,1)} %bitcast.57), custom_call_target="tpu_custom_call" | custom-call | tf_op jit(solution)/shard_map/pallas_call | solution.py:177
  136.9 15.7 %shard_map.93.cur_ref.cur_hbm = f32[2048,256]{1,0:T(8,128)} custom-call(s32[4096]{0:T(1024)} %bitcast.64, bf16[4096,128]{1,0:T(8,128)(2,1)} %bitcast.53, f32[2048,256]{1,0:T(8,128)} %bitcast_convert_fusion.cur_ref.cur_hbm), custom_call_target="tpu_custom_call" | custom-call | flops 524288 | bytes 6291456 | tf_op jit(solution)/shard_map/pallas_call | solution.py:355
  152.6 4.3 %shard_map.94.src_ref = f32[4104,128]{1,0:T(8,128)} custom-call(s32[4]{0:T(128)} %cnt_ref.3, f32[2048,256]{1,0:T(8,128)} %shard_map.93.cur_ref.cur_hbm, bf16[4,512,512]{2,1,0:T(8,128)(2,1)} %all-gather.2.cloned.1.call-done.att_ref), custom_call_target="tpu_custom_call" | custom-call | flops 536870912 | bytes 6291456 | tf_op jit(solution)/shard_map/pallas_call | solution.py:312
  156.9 7.1 %shard_map.95 = bf16[4096,128]{1,0:T(8,128)(2,1)} custom-call(s32[4096]{0:T(1024)} %bitcast.65, f32[4104,128]{1,0:T(8,128)} %shard_map.94.src_ref, f32[8,1024]{1,0:T(8,128)} %bitcast.68), custom_call_target="tpu_custom_call" | custom-call | bytes 4194304 | tf_op jit(solution)/shard_map/pallas_call | solution.py:116
  164.0 19.8 %shard_map.96 = bf16[32,128,128]{2,1,0:T(8,128)(2,1)} custom-call(bf16[32,128,128]{2,1,0:T(8,128)(2,1)} %bitcast.54), custom_call_target="tpu_custom_call" | custom-call | tf_op jit(solution)/shard_map/pallas_call | solution.py:177
  183.8 13.8 %shard_map.97 = (f32[8,256,128]{2,1,0:T(8,128)}, f32[8,128,1]{2,1,0:T(8,128)}) custom-call(s32[2048]{0:T(1024)} %fusion.8.slot_ref, bf16[8,256,2048]{2,1,0:T(8,128)(2,1)} %get-tuple-element.8.basis_ref, bf16[4096,128]{1,0:T(8,128)(2,1)} %bitcast.58, f32[8,1,1024]{2,1,0:T(1,128)} %get-tuple-element.21.inc_ref, f32[8,1,1024]{2,1,0:T(1,128)} %get-tuple-element.20.ins_ref), custom_call_target="tpu_custom_call" | custom-call | flops 2147483648 | bytes 8388608 | tf_op jit(solution)/shard_map/pallas_call | solution.py:267
  197.6 6.7 %shard_map.98 = bf16[4096,128]{1,0:T(8,128)(2,1)} custom-call(s32[4096]{0:T(1024)} %get-tuple-element.14.idx_ref, f32[2048,128]{1,0:T(8,128)} %bitcast.61), custom_call_target="tpu_custom_call" | custom-call | bytes 4194304 | tf_op jit(solution)/shard_map/pallas_call | solution.py:116
  204.4 21.6 %shard_map.99 = bf16[32,128,128]{2,1,0:T(8,128)(2,1)} custom-call(bf16[32,128,128]{2,1,0:T(8,128)(2,1)} %bitcast.55), custom_call_target="tpu_custom_call" | custom-call | tf_op jit(solution)/shard_map/pallas_call | solution.py:177
  226.0 15.8 %shard_map.100 = f32[2048,256]{1,0:T(8,128)} custom-call(s32[4096]{0:T(1024)} %bitcast.66, bf16[4096,128]{1,0:T(8,128)(2,1)} %bitcast.52, f32[2048,256]{1,0:T(8,128)} %shard_map.93.cur_ref.cur_hbm), custom_call_target="tpu_custom_call" | custom-call | flops 524288 | bytes 6291456 | tf_op jit(solution)/shard_map/pallas_call | solution.py:355
  241.8 0.8 reduce.4
  (18 shorter events, 0.1 us)
Async XLA Ops:
  7.2 4.6 %copy-start.6 = (s32[2]{0:T(128)S(1)}, s32[2]{0:T(128)}, u32[]{:S(2)}) copy-start(s32[2]{0:T(128)} %constant.65.clone) | copy-start | bytes 28
  7.2 56.7 %all-gather.2.cloned.1.call-start = ((), (), s32[]{:S(2)}) async-start(), calls=%async_computation.1 | async-start | bytes 2359296 | tf_op jit(solution)/shard_map/all_gather | solution.py:421
  18.3 11.1 %copy-start.5 = (s32[1024]{0:T(1024)S(1)}, s32[1024]{0:T(1024)}, u32[]{:S(2)}) copy-start(s32[1024]{0:T(1024)} %param.12) | copy-start | bytes 12292
  18.3 11.7 %copy-start.3 = (s32[8,256]{1,0:T(8,128)S(1)}, s32[8,256]{1,0:T(8,128)}, u32[]{:S(2)}) copy-start(s32[8,256]{1,0:T(8,128)} %param.10) | copy-start | bytes 24580
  18.3 11.7 %copy-start.4 = (s32[8,256]{1,0:T(8,128)S(1)}, s32[8,256]{1,0:T(8,128)}, u32[]{:S(2)}) copy-start(s32[8,256]{1,0:T(8,128)} %param.11) | copy-start | bytes 24580
  20.7 41.7 %copy-start = (bf16[4,512,256]{2,1,0:T(8,128)(2,1)S(1)}, bf16[4,512,256]{2,1,0:T(8,128)(2,1)}, u32[]{:S(2)}) copy-start(bf16[4,512,256]{2,1,0:T(8,128)(2,1)} %param.7) | copy-start | bytes 3145732
  20.7 47.5 %all-to-all-start = ((s32[32,1,128]{2,1,0:T(1,128)}), s32[32,1,128]{2,1,0:T(1,128)S(1)}, u32[]{:S(2)}, u32[]{:S(2)}) async-start(s32[32,1,128]{2,1,0:T(1,128)} %bitcast.4), calls=%async_computation | async-start | bytes 32768 | tf_op jit(solution)/shard_map/all_to_all | solution.py:414
  68.2 0.6 copy-start.2
  226.0 15.8 %copy-start.1 = (f32[8,128,1]{2,1,0:T(8,128)S(1)}, f32[8,128,1]{2,1,0:T(8,128)}, u32[]{:S(2)}) copy-start(f32[8,128,1]{2,1,0:T(8,128)} %get-tuple-element.13) | copy-start | bytes 12292
Sparse Core Ops, SparseCore 0:
  9.8 41.2 all-gather.1
